TPU v7x, 128 devices: a whole 4x4x4 slice. The times are simulated.
128 devices in a mesh: leaf: 4 (over y), front: 32 (over x, z, core).
Axes of the slice: x: 4, y: 4, z: 4, core: 2. Of those that a mesh axis runs over, the one named last changes fastest.
Arguments:
- child_rhs: bfloat16 [4, 2, 32, 64, 128], P('leaf', None, 'front'), may hold values from -6 to 6
- child_lower: bfloat16 [4, 2, 32, 64, 4096], P('leaf', None, 'front'), may hold values from -0.046875 to 0.046875
- child_inverse: bfloat16 [4, 2, 32, 64, 2048], P('leaf', None, 'front'), may hold values from -0.125 to 0.125
- child_upper: bfloat16 [4, 2, 32, 64, 4096], P('leaf', None, 'front'), may hold values from -0.046875 to 0.046875
- child_coupling: bfloat16 [4, 2, 32, 64, 4096], P('leaf', None, 'front'), may hold values from -0.046875 to 0.046875
- child_update: bfloat16 [4, 4096, 4096], P('leaf', 'front'), may hold values from -0.09375 to 0.09375
- update_owner: int32 [4, 4096, 1], P('leaf', 'front'), may hold values from 0 to 127; in each aligned block of 128 rows (0 to 127, 128 to 255, ..., all dimensions but the last counted through in order) at most 2 rows name the same one
- update_slot: int32 [4, 4096], P('leaf', 'front'), may hold values from 0 to 127
- root_rhs: bfloat16 [2, 128, 64, 128], P(None, ('leaf', 'front')), may hold values from -6 to 6
- root_lower: bfloat16 [2, 128, 64, 16384], P(None, ('leaf', 'front')), may hold values from -0.0234375 to 0.0234375
- root_inverse: bfloat16 [2, 128, 64, 8192], P(None, ('leaf', 'front')), may hold values from -0.0625 to 0.0625
- root_upper: bfloat16 [2, 128, 64, 16384], P(None, ('leaf', 'front')), may hold values from -0.0234375 to 0.0234375
Outputs:
- child_solution: bfloat16 [4, 2, 32, 64, 128], P('leaf', None, 'front')
- root_solution: bfloat16 [2, 128, 64, 128], P(None, ('leaf', 'front'))
Inputs may be any that keep to these rules, and one draw needn't show every extreme that they name: `update_owner`: among the contribution rows that one device holds (aligned blocks of 128 rows), at most 2 name the same owner, a bound that some block reaches.
All inputs are finite; a program needn't handle non-finite values.
Results may differ from a plain program's by a relative error of at most 0.014.
Values may be sent and summed in bfloat16 or wider, within the bound.
No kernel may reach another device: no remote copies, remote signals or barrier semaphores. Data moves between devices by JAX's collectives and lax.ppermute only.
A program may use at most 64 MiB of HBM per device.

v0:
```python
import jax
import jax.numpy as jnp
from jax import lax
from jax.sharding import PartitionSpec as P


def gather_child(own_piece):
    return lax.all_gather(own_piece, "front", axis=0, tiled=True)


def gather_root(own_piece):
    return lax.all_gather(own_piece, ("leaf", "front"), axis=0, tiled=True)


def block_chain(right_side, own_rows, backward, gather_rows):
    step_count = right_side.shape[0]
    block_rows = own_rows.shape[2] // step_count
    blocks_full = [None] * step_count
    own_pieces = [None] * step_count
    if backward:
        block_order = range(step_count - 1, -1, -1)
    else:
        block_order = range(step_count)
    for block_id in block_order:
        partial_sum = right_side[block_id]
        if backward:
            known_blocks = blocks_full[block_id + 1 :]
            column_start = (block_id + 1) * block_rows
        else:
            known_blocks = blocks_full[:block_id]
            column_start = 0
        if len(known_blocks) > 0:
            stacked = known_blocks[0]
            columns = own_rows[block_id][:, column_start : column_start + stacked.shape[0]]
            partial_sum = partial_sum - jnp.dot(
                columns, stacked, preferred_element_type=jnp.float32
            )
        own_piece = partial_sum.astype(jnp.bfloat16)
        own_pieces[block_id] = own_piece
        blocks_full[block_id] = gather_rows(own_piece)
    return (blocks_full, jnp.stack(own_pieces))


def apply_inverse(inverse_rows, blocks_full):
    return jnp.stack(
        [
            jnp.dot(inverse_rows[i], blocks_full[i], preferred_element_type=jnp.float32).astype(
                jnp.bfloat16
            )
            for i in range(len(blocks_full))
        ]
    )


def body(
    child_rhs,
    child_lower,
    child_inverse,
    child_upper,
    child_coupling,
    child_update,
    update_owner,
    update_slot,
    root_rhs,
    root_lower,
    root_inverse,
    root_upper,
):
    child_forward, unused_pieces = block_chain(
        child_rhs[0, :, 0].astype(jnp.float32), child_lower[0, :, 0], False, gather_child
    )
    child_diag = apply_inverse(child_inverse[0, :, 0], child_forward)
    pivot_values = jnp.concatenate(child_forward, axis=0)
    contribution = -jnp.dot(child_update[0], pivot_values, preferred_element_type=jnp.float32)
    owner_ids = update_owner[0, :, 0]
    slot_ids = update_slot[0]
    stripe_rows = root_rhs.shape[2]
    root_slots = root_rhs.shape[0] * stripe_rows
    devices = lax.axis_size("leaf") * lax.axis_size("front")
    right_count = contribution.shape[1]
    dense_buffer = (
        jnp.zeros((devices, root_slots, right_count), jnp.float32)
        .at[owner_ids, slot_ids]
        .add(contribution)
    )
    received = lax.psum_scatter(dense_buffer, ("leaf", "front"), scatter_dimension=0, tiled=True)[0]
    root_right = root_rhs[:, 0].astype(jnp.float32) + received.reshape(
        root_rhs.shape[0], stripe_rows, right_count
    )
    root_forward, unused_root = block_chain(root_right, root_lower[:, 0], False, gather_root)
    root_diag = apply_inverse(root_inverse[:, 0], root_forward)
    root_backward, root_pieces = block_chain(
        root_diag.astype(jnp.float32), root_upper[:, 0], True, gather_root
    )
    root_values = jnp.concatenate(root_backward, axis=0)
    block_span = devices * stripe_rows
    root_index = (
        slot_ids // stripe_rows * block_span + owner_ids * stripe_rows + slot_ids % stripe_rows
    )
    update_x = lax.all_gather(root_values[root_index], "front", axis=0, tiled=True)
    coupling_rows = child_coupling[0, :, 0]
    coupled = jnp.dot(
        coupling_rows.reshape(-1, update_x.shape[0]), update_x, preferred_element_type=jnp.float32
    ).reshape(child_diag.shape)
    child_backward, child_pieces = block_chain(
        child_diag.astype(jnp.float32) - coupled, child_upper[0, :, 0], True, gather_child
    )
    return (child_pieces[None, :, None], root_pieces[:, None])


def solution(mesh):
    in_specs = (
        P("leaf", None, "front", None, None),
        P("leaf", None, "front", None, None),
        P("leaf", None, "front", None, None),
        P("leaf", None, "front", None, None),
        P("leaf", None, "front", None, None),
        P("leaf", "front", None),
        P("leaf", "front", None),
        P("leaf", "front"),
        P(None, ("leaf", "front"), None, None),
        P(None, ("leaf", "front"), None, None),
        P(None, ("leaf", "front"), None, None),
        P(None, ("leaf", "front"), None, None),
    )
    out_specs = (P("leaf", None, "front", None, None), P(None, ("leaf", "front"), None, None))
    return jax.shard_map(body, mesh=mesh, in_specs=in_specs, out_specs=out_specs, check_vma=False)
```

profile of v0, /device:TPU:1, one launch (start us, length us, event | category | flops | bytes accessed | tf_op | source)
XLA Modules:
  0.0 1082.6 jit_solution(4324055462776083758)
XLA Ops:
  8.1 27.4 %all-gather = bf16[1,1,1,2048,128]{4,3,2,1,0:T(8,128)(2,1)S(1)} all-gather(bf16[1,1,1,64,128]{4,3,2,1,0:T(8,128)(2,1)S(1)} %slice.74), channel_id=2, replica_groups=mesh['leaf'=4,'front'=32] {'front'}, dimensions={3}, use_global_device_ids=true | all-gather | bytes 540672 | tf_op jit(solution)/shard_map/all_gather | solution.py:8
  35.5 1.3 slice_bitcast_fusion.3
  36.8 1.0 fusion.13
  37.8 24.1 %all_gather.25 = bf16[2048,128]{1,0:T(8,128)(2,1)S(1)} all-gather(bf16[64,128]{1,0:T(8,128)(2,1)S(1)} %fusion.13), channel_id=1, replica_groups=mesh['leaf'=4,'front'=32] {'front'}, dimensions={0}, use_global_device_ids=true | all-gather | bytes 540672 | tf_op jit(solution)/shard_map/all_gather | solution.py:8
  63.4 4.3 broadcast_in_dim.12
  67.7 13.4 %scatter_fusion = f32[128,128,128]{2,1,0:T(8,128)} fusion(f32[128,128,128]{2,1,0:T(8,128)} %broadcast_in_dim.12, s32[128]{0:T(128)S(1)} %get-tuple-element.5, f32[128,128]{1,0:T(8,128)S(1)} %copy.14), kind=kCustom, calls=%fused_computation.1 | custom fusion | flops 16384 | bytes 197632 | tf_op jit(solution)/shard_map/scatter-add | solution.py:84
  81.2 641.7 %reduce-scatter.2.cloned.1.call-done = f32[1,128,128]{2,1,0:T(8,128)} async-done(((f32[128,128,128]{2,1,0:T(8,128)}), f32[1,128,128]{2,1,0:T(8,128)}) %reduce-scatter.2.cloned.1.call-update) | async-done | bytes 65552 | tf_op jit(solution)/shard_map/reduce_scatter | solution.py:86
  724.5 3.0 slice_bitcast_fusion.1
  727.5 65.9 %all-gather.15.cloned.1.call-done = bf16[1,8192,128]{2,1,0:T(8,128)(2,1)} async-done(((bf16[1,64,128]{2,1,0:T(8,128)(2,1)}), bf16[1,8192,128]{2,1,0:T(8,128)(2,1)}) %all-gather.15.cloned.1.call-update) | async-done | bytes 2097168 | tf_op jit(solution)/shard_map/all_gather | solution.py:12
  793.4 3.2 fusion.16
  796.6 1.7 fusion.25
  798.4 62.0 %all-gather.11.cloned.1.call-done = bf16[8192,128]{1,0:T(8,128)(2,1)} async-done(((bf16[64,128]{1,0:T(8,128)(2,1)}), bf16[8192,128]{1,0:T(8,128)(2,1)}) %all-gather.11.cloned.1.call-update) | async-done | bytes 2097168 | tf_op jit(solution)/shard_map/all_gather | solution.py:12
  860.4 2.4 fusion.24
  863.5 3.0 slice_bitcast_fusion
  866.5 60.7 %all-gather.17.cloned.1.call-done = bf16[1,8192,128]{2,1,0:T(8,128)(2,1)} async-done(((bf16[1,64,128]{2,1,0:T(8,128)(2,1)}), bf16[1,8192,128]{2,1,0:T(8,128)(2,1)}) %all-gather.17.cloned.1.call-update) | async-done | bytes 2097168 | tf_op jit(solution)/shard_map/all_gather | solution.py:12
  927.2 3.2 fusion.14
  930.6 62.8 %all-gather.13.cloned.1.call-done = bf16[8192,128]{1,0:T(8,128)(2,1)} async-done(((bf16[64,128]{1,0:T(8,128)(2,1)}), bf16[8192,128]{1,0:T(8,128)(2,1)}) %all-gather.13.cloned.1.call-update) | async-done | bytes 2097168 | tf_op jit(solution)/shard_map/all_gather | solution.py:12
  993.4 11.0 %pad_maximum_fusion = bf16[16384,128]{1,0:T(8,128)(2,1)} fusion(bf16[8192,128]{1,0:T(8,128)(2,1)S(1)} %bitcast.157, bf16[8192,128]{1,0:T(8,128)(2,1)} %all-gather.13.cloned.1.call-done), kind=kLoop, calls=%fused_computation.2 | loop fusion | flops 8388608 | bytes 8388608 | tf_op jit(solution)/shard_map/concatenate | solution.py:95
  1004.4 4.1 gather_fusion
  1008.5 1.3 fusion.23
  1009.9 1.3 fusion.22
  1011.9 37.1 %all-gather.19.cloned.1.call-done = bf16[4096,128]{1,0:T(8,128)(2,1)} async-done(((bf16[128,128]{1,0:T(8,128)(2,1)}), bf16[4096,128]{1,0:T(8,128)(2,1)}) %all-gather.19.cloned.1.call-update) | async-done | bytes 1048592 | tf_op jit(solution)/shard_map/all_gather | solution.py:100
  1049.0 1.6 fusion.55
  1050.7 24.2 %all-gather.4 = bf16[1,2048,128]{2,1,0:T(8,128)(2,1)S(1)} all-gather(bf16[1,64,128]{2,1,0:T(8,128)(2,1)S(1)} %slice.148), channel_id=6, replica_groups=mesh['leaf'=4,'front'=32] {'front'}, dimensions={1}, use_global_device_ids=true | all-gather | bytes 540672 | tf_op jit(solution)/shard_map/all_gather | solution.py:8
  (51 shorter events, 6.4 us)
Async XLA Ops:
  7.2 1041.8 %copy-start = (bf16[1,2,1,64,4096]{4,3,2,1,0:T(8,128)(2,1)S(1)}, bf16[1,2,1,64,4096]{4,3,2,1,0:T(8,128)(2,1)}, u32[]{:S(2)}) copy-start(bf16[1,2,1,64,4096]{4,3,2,1,0:T(8,128)(2,1)} %param.16) | copy-start | bytes 3145732
  7.2 55.6 %copy-start.11 = (bf16[1,128,4096]{2,1,0:T(8,128)(2,1)S(1)}, bf16[1,128,4096]{2,1,0:T(8,128)(2,1)}, u32[]{:S(2)}) copy-start(bf16[1,128,4096]{2,1,0:T(8,128)(2,1)} %param.17) | copy-start | bytes 3145732
  7.2 715.7 %reduce-scatter.2.cloned.1.call-start = ((), (), s32[]{:S(2)}) async-start(), calls=%async_computation.1 | async-start | bytes 8454144 | tf_op jit(solution)/shard_map/reduce_scatter | solution.py:86
  35.5 26.4 %copy-start.3 = (bf16[1,1,1,2048,128]{4,3,2,1,0:T(8,128)(2,1)}, bf16[1,1,1,2048,128]{4,3,2,1,0:T(8,128)(2,1)S(1)}, u32[]{:S(2)}) copy-start(bf16[1,1,1,2048,128]{4,3,2,1,0:T(8,128)(2,1)S(1)} %all-gather) | copy-start | bytes 1572868
  36.8 26.5 %copy-start.9 = (s32[1,128,1]{1,2,0:T(1,128)S(1)}, s32[1,128,1]{1,2,0:T(1,128)}, u32[]{:S(2)}) copy-start(s32[1,128,1]{1,2,0:T(1,128)} %param.18) | copy-start | bytes 1540
  36.8 26.5 %copy-start.10 = (s32[1,128]{1,0:T(1,128)S(1)}, s32[1,128]{1,0:T(1,128)}, u32[]{:S(2)}) copy-start(s32[1,128]{1,0:T(1,128)} %param.19) | copy-start | bytes 1540
  61.9 0.8 copy-start.4
  81.1 641.8 %copy-start.8 = (bf16[2,1,64,128]{3,2,1,0:T(8,128)(2,1)S(1)}, bf16[2,1,64,128]{3,2,1,0:T(8,128)(2,1)}, u32[]{:S(2)}) copy-start(bf16[2,1,64,128]{3,2,1,0:T(8,128)(2,1)} %param.20) | copy-start | bytes 98308
  81.2 712.2 %all-gather.15.cloned.1.call-start = ((), (), s32[]{:S(2)}) async-start(), calls=%async_computation.4 | async-start | bytes 2113536 | tf_op jit(solution)/shard_map/all_gather | solution.py:12
  724.4 136.0 %all-gather.11.cloned.1.call-start = ((), (), s32[]{:S(2)}) async-start(), calls=%async_computation.2 | async-start | bytes 2113536 | tf_op jit(solution)/shard_map/all_gather | solution.py:12
  793.4 3.2 copy-start.1
  796.6 130.6 %all-gather.17.cloned.1.call-start = ((), (), s32[]{:S(2)}) async-start(), calls=%async_computation.5 | async-start | bytes 2113536 | tf_op jit(solution)/shard_map/all_gather | solution.py:12
  863.4 130.0 %all-gather.13.cloned.1.call-start = ((), (), s32[]{:S(2)}) async-start(), calls=%async_computation.3 | async-start | bytes 2113536 | tf_op jit(solution)/shard_map/all_gather | solution.py:12
  927.2 66.2 %copy-start.2 = (bf16[1,8192,128]{2,1,0:T(8,128)(2,1)S(1)}, bf16[1,8192,128]{2,1,0:T(8,128)(2,1)}, u32[]{:S(2)}) copy-start(bf16[1,8192,128]{2,1,0:T(8,128)(2,1)} %all-gather.17.cloned.1.call-done) | copy-start | bytes 6291460
  930.4 118.6 %all-gather.19.cloned.1.call-start = ((), (), s32[]{:S(2)}) async-start(), calls=%async_computation.6 | async-start | bytes 1081344 | tf_op jit(solution)/shard_map/all_gather | solution.py:100
  1004.4 6.8 copy-start.5
  1004.4 6.9 copy-start.6
  1004.4 6.9 copy-start.7
Sparse Core Ops, SparseCore 0:
  81.3 641.6 reduce-scatter.1
  727.1 66.2 all-gather.14
  797.6 62.7 all-gather.10
  864.4 62.7 all-gather.16
  930.6 62.7 all-gather.12
  1008.7 40.3 all-gather.18
where the time goes:
time: 1080 us
  waiting for transfers between devices  930 us (86%)
  blocking collectives  75.8 us (7%)
  other arithmetic  26.6 us (2%)
  local copies, waits for them, and re-layouts  18.8 us (2%)
  matrix products  16.5 us (2%)
  between operations  14.3 us (1%)
    reduce_scatter x1, waiting for transfers between devices, body(): lax.psum_scatter(dense_buffer, ('leaf', 'front'), scatter_dimension=0, ti...  642 us
    all_gather x4, waiting for transfers between devices, gather_root(): return lax.all_gather(own_piece, ('leaf', 'front'), axis=0, tiled=True)  251 us
    all_gather x3, blocking collectives, gather_child(): return lax.all_gather(own_piece, 'front', axis=0, tiled=True)  75.8 us
    all_gather x1, waiting for transfers between devices, body(): lax.all_gather(root_values[root_index], 'front', axis=0, tiled=True)  37.1 us
  transfers between devices with their start and end apart: 6, of which 6 were waited for; matrix products, arithmetic and copies ran while one was open for 1% of the time, Pallas kernels for 0%

commit v1 on v0

v1 whole, which is shorter than its diff:
```python
import functools

import jax
import jax.numpy as jnp
from jax import lax
from jax.experimental import pallas as pl
from jax.experimental.pallas import tpu as pltpu
from jax.sharding import Mesh
from jax.sharding import PartitionSpec as P

F32 = jnp.float32
BF16 = jnp.bfloat16
ALL = ("y", "x", "z", "c")
PLANE = ("x", "z")
CUBE = ("y", "x", "z")


def gather_rows(piece, axes, count):
    own = lax.all_to_all(jnp.broadcast_to(piece, (count,) + piece.shape), axes, 0, 0)
    other = lax.ppermute(own, "c", [(0, 1), (1, 0)])
    first = lax.axis_index("c") == 0
    return jnp.stack([jnp.where(first, own, other), jnp.where(first, other, own)], axis=1)


def flat(gathered):
    return gathered.reshape(-1, gathered.shape[-1])


def dot(a, b):
    return jnp.dot(a, b, preferred_element_type=F32)


def rows_of(array, block, first, last):
    lead = array.ndim - 4
    start = (0,) * lead + (block, 0, 0, first)
    stop = (1,) * lead + (block + 1, 1, array.shape[-2], last)
    return lax.slice(array, start, stop).reshape(array.shape[-2], last - first)


def pick_kernel(index_ref, x0_ref, x1_ref, coupling_ref, out_ref, wide_ref, picked_ref):
    half = x0_ref.shape[0]
    wide_ref[0:half, :] = x0_ref[...].astype(F32)
    wide_ref[half : 2 * half, :] = x1_ref[...].astype(F32)

    def body(group, carry):
        base = group * 8
        rows = [wide_ref[pl.ds(index_ref[base + j], 1), :] for j in range(8)]
        picked_ref[pl.ds(pl.multiple_of(base, 8), 8), :] = jnp.concatenate(rows, axis=0)
        return carry

    lax.fori_loop(0, picked_ref.shape[0] // 8, body, 0, unroll=4)
    out_ref[...] = jnp.dot(
        coupling_ref[...], picked_ref[...].astype(BF16), preferred_element_type=F32
    )


def pick_and_couple(index, x0, x1, coupling):
    vmem = pl.BlockSpec(memory_space=pltpu.VMEM)
    return pl.pallas_call(
        pick_kernel,
        out_shape=jax.ShapeDtypeStruct((coupling.shape[0], x0.shape[1]), F32),
        in_specs=[pl.BlockSpec(memory_space=pltpu.SMEM), vmem, vmem, vmem],
        out_specs=vmem,
        scratch_shapes=[
            pltpu.VMEM((x0.shape[0] + x1.shape[0], x0.shape[1]), F32),
            pltpu.VMEM((index.shape[0], x0.shape[1]), F32),
        ],
        compiler_params=pltpu.CompilerParams(vmem_limit_bytes=40 << 20),
    )(index, x0, x1, coupling)


def body(
    child_rhs,
    child_lower,
    child_inverse,
    child_upper,
    child_coupling,
    child_update,
    update_owner,
    update_slot,
    root_rhs,
    root_lower,
    root_inverse,
    root_upper,
):
    planes = lax.axis_size("x") * lax.axis_size("z")
    cubes = planes * lax.axis_size("y")
    devices = cubes * lax.axis_size("c")
    stripe = root_rhs.shape[2]
    rhs = root_rhs.shape[3]
    kc = child_inverse.shape[-1]
    kr = root_inverse.shape[-1]
    nc = child_lower.shape[-1]
    owner = update_owner[0, :, 0]
    slot = update_slot[0]
    held = owner.shape[0]

    same = (owner[:, None] == owner[None, :]) & (
        jnp.arange(held)[None, :] < jnp.arange(held)[:, None]
    )
    rank = jnp.sum(same.astype(jnp.int32), axis=1)
    place = owner * 2 + rank
    select = (jnp.arange(devices * 2)[:, None] == place[None, :]).astype(BF16)
    slot_lanes = jnp.where(
        jnp.arange(rhs)[None, :] == 0, (slot + 1)[:, None], 0
    ).astype(BF16)

    marks = jnp.concatenate(
        [owner[None], slot[None], jnp.zeros((6, held), jnp.int32)], axis=0
    ).astype(BF16)
    first_piece = jnp.concatenate([child_rhs[0, 0, 0], marks], axis=0)
    first = gather_rows(first_piece, PLANE, planes)
    y0 = flat(first[:, :, :stripe])
    owners = first[:, :, stripe].astype(jnp.int32).reshape(-1)
    slots = first[:, :, stripe + 1].astype(jnp.int32).reshape(-1)
    index = slots // stripe * kr + owners * stripe + slots % stripe
    y1_own = (
        child_rhs[0, 1, 0].astype(F32) - dot(rows_of(child_lower, 1, 0, kc), y0)
    ).astype(BF16)
    y1 = flat(gather_rows(y1_own, PLANE, planes))
    update = child_update[0]
    contribution = -(dot(update[:, :kc], y0) + dot(update[:, kc:], y1))

    packed = dot(
        select, jnp.concatenate([contribution.astype(BF16), slot_lanes], axis=1)
    ).astype(BF16)
    arrived = lax.all_to_all(packed.reshape(devices, 2, 2 * rhs), ALL, 0, 0)
    arrived = arrived.reshape(devices * 2, 2 * rhs)
    lands = (
        arrived[:, rhs : rhs + 1].astype(jnp.int32) == jnp.arange(1, 2 * stripe + 1)[None, :]
    ).astype(BF16)
    received = lax.dot_general(
        lands, arrived[:, :rhs], (((0,), (0,)), ((), ())), preferred_element_type=F32
    )
    right = root_rhs[:, 0].astype(F32) + received.reshape(2, stripe, rhs)

    r0 = flat(gather_rows(right[0].astype(BF16), CUBE, cubes))
    r1_own = (right[1] - dot(rows_of(root_lower, 1, 0, kr), r0)).astype(BF16)
    r1 = flat(gather_rows(r1_own, CUBE, cubes))
    x1_own = dot(rows_of(root_inverse, 1, 0, kr), r1).astype(BF16)
    x1 = flat(gather_rows(x1_own, CUBE, cubes))
    z0_own = dot(rows_of(root_inverse, 0, 0, kr), r0).astype(BF16)
    x0_own = (
        z0_own.astype(F32) - dot(rows_of(root_upper, 0, kr, 2 * kr), x1)
    ).astype(BF16)
    x0 = flat(gather_rows(x0_own, CUBE, cubes))

    coupling = child_coupling.reshape(2 * stripe, -1)
    coupled = pick_and_couple(index, x0, x1, coupling)
    z0c = dot(rows_of(child_inverse, 0, 0, kc), y0).astype(BF16).astype(F32)
    z1c = dot(rows_of(child_inverse, 1, 0, kc), y1).astype(BF16).astype(F32)
    c1_own = (z1c - coupled[stripe:]).astype(BF16)
    c1 = flat(gather_rows(c1_own, PLANE, planes))
    c0_own = (
        z0c - coupled[:stripe] - dot(rows_of(child_upper, 0, kc, nc), c1)
    ).astype(BF16)
    child_solution = jnp.stack([c0_own, c1_own])[None, :, None]
    root_solution = jnp.stack([x0_own, x1_own])[:, None]
    return child_solution, root_solution


def solution(mesh):
    leaf, front = mesh.devices.shape
    side = {32: (4, 4, 2)}[front]
    fine = Mesh(mesh.devices.reshape((leaf,) + side), ALL)
    subtree = P("y", None, ("x", "z", "c"), None, None)
    ancestor = P(None, ALL, None, None)
    in_specs = (
        subtree,
        subtree,
        subtree,
        subtree,
        subtree,
        P("y", ("x", "z", "c"), None),
        P("y", ("x", "z", "c"), None),
        P("y", ("x", "z", "c")),
        ancestor,
        ancestor,
        ancestor,
        ancestor,
    )
    return jax.shard_map(
        body, mesh=fine, in_specs=in_specs, out_specs=(subtree, ancestor), check_vma=False
    )
```

time: 1080 us -> 193 us (0.18)
  waiting for transfers between devices: 930 us -> 27.3 us
  blocking collectives: 75.8 us -> 113 us
  starting transfers between devices: 0.43 us -> 24.4 us
  other arithmetic: 26.6 us -> 5.53 us
  between operations: 14.3 us -> 1.02 us
  local copies, waits for them, and re-layouts: 18.8 us -> 6.39 us
    reduce_scatter x1 -> x0, waiting for transfers between devices: 642 us -> none  [body(): lax.psum_scatter(dense_buffer, ('leaf', 'front'), scatter_dimension=0, ti...]
    all_gather x5 -> x0, waiting for transfers between devices: 288 us -> none  [the longest x4 251 us: gather_root(): return lax.all_gather(own_piece, ('leaf', 'front'), axis=0, tiled=True)]
    all_to_all x0 -> x6, blocking collectives: none -> 113 us  [gather_rows(): lax.all_to_all(jnp.broadcast_to(piece, (count,) + piece.shape), axes, 0, 0)]
    all_gather x3 -> x0, blocking collectives: 75.8 us -> none  [gather_child(): return lax.all_gather(own_piece, 'front', axis=0, tiled=True)]
    all_to_all x0 -> x2, waiting for transfers between devices: none -> 17.3 us  [the longest x1 9.81 us: body(): arrived = lax.all_to_all(packed.reshape(devices, 2, 2 * rhs), ALL, 0, 0)]
    ppermute x0 -> x7, starting transfers between devices: none -> 14.7 us  [gather_rows(): other = lax.ppermute(own, 'c', [(0, 1), (1, 0)])]
    scatter-add x1 -> x0, other arithmetic: 13.4 us -> none  [body(): dense_buffer = jnp.zeros((devices, root_slots, right_count), jnp.float32)...]
    concatenate x1, other arithmetic: 11 us -> 0.08 us  [body(): first_piece = jnp.concatenate([child_rhs[0, 0, 0], marks], axis=0)]
  transfers between devices with their start and end apart: 6 -> 9, of which waited for: 6 -> 9; matrix products, arithmetic and copies ran while one was open for 1% -> 1% of each run, Pallas kernels for 0% -> 0%
where the time goes in v1:
time: 193 us; the launch traced here: 192 us
  blocking collectives  113 us (59%)
  waiting for transfers between devices  27.3 us (14%)
  starting transfers between devices  24.4 us (13%)
  matrix products  8.36 us (4%)
  local copies, waits for them, and re-layouts  6.39 us (3%)
  Pallas kernels  5.74 us (3%)
  other arithmetic  5.53 us (3%)
    all_to_all x6, blocking collectives, gather_rows(): lax.all_to_all(jnp.broadcast_to(piece, (count,) + piece.shape), axes, 0, 0)  113 us
    ppermute x7, starting transfers between devices, gather_rows(): other = lax.ppermute(own, 'c', [(0, 1), (1, 0)])  14.7 us
    ppermute x7, waiting for transfers between devices, gather_rows(): other = lax.ppermute(own, 'c', [(0, 1), (1, 0)])  9.98 us
    all_to_all x1, waiting for transfers between devices, body(): arrived = lax.all_to_all(packed.reshape(devices, 2, 2 * rhs), ALL, 0, 0)  9.81 us
    dot_general x11, matrix products, dot(): return jnp.dot(a, b, preferred_element_type=F32)  8.08 us
    all_to_all x1, waiting for transfers between devices, gather_rows(): lax.all_to_all(jnp.broadcast_to(piece, (count,) + piece.shape), axes, 0, 0)  7.47 us
    all_to_all x1, starting transfers between devices, body(): arrived = lax.all_to_all(packed.reshape(devices, 2, 2 * rhs), ALL, 0, 0)  6.14 us
    pallas_call x1, Pallas kernels, pick_and_couple(): pl.pallas_call(pick_kernel, out_shape=jax.ShapeDtypeStruct((coupling.shap...  5.74 us
  transfers between devices with their start and end apart: 9, of which 9 were waited for; matrix products, arithmetic and copies ran while one was open for 1% of the time, Pallas kernels for 0%

profile of v1, /device:TPU:1, one launch (start us, length us, event | category | flops | bytes accessed | tf_op | source)
XLA Modules:
  0.0 191.9 jit_solution(12413233912852970795)
XLA Ops:
  3.0 15.8 %all_to_all.40 = bf16[16,72,128]{2,1,0:T(8,128)(2,1)S(1)} all-to-all(bf16[16,72,128]{2,1,0:T(8,128)(2,1)S(1)} %broadcast_in_dim.58), channel_id=1, replica_groups=mesh['y'=4,'x'=4,'z'=4,'c'=2] {'x','z'}, dimensions={0} | all-to-all | bytes 589824 | tf_op jit(solution)/shard_map/all_to_all | solution.py:19
  18.8 2.2 %collective-permute-start = (bf16[16,72,128]{2,1,0:T(8,128)(2,1)S(1)}, bf16[16,72,128]{2,1,0:T(8,128)(2,1)S(1)}, u32[]{:S(2)}, u32[]{:S(2)}) collective-permute-start(bf16[16,72,128]{2,1,0:T(8,128)(2,1)S(1)} %all_to_all.40), channel_id=1, source_target_pairs={{0,1},{1,0},{2,3},{3,2},{4,5},{5,4},{6,7},{7,6},{8,9},{9,8},{10,11... | collective-permute-start | bytes 884744 | tf_op jit(solution)/shard_map/ppermute | solution.py:20
  24.2 3.5 %all-to-all-start.1 = ((bf16[16,64,128]{2,1,0:T(8,128)(2,1)}), bf16[16,64,128]{2,1,0:T(8,128)(2,1)S(1)}, u32[]{:S(2)}, u32[]{:S(2)}) async-start(bf16[16,64,128]{2,1,0:T(8,128)(2,1)} %broadcast_in_dim.59), calls=%async_computation.1 | async-start | bytes 524288 | tf_op jit(solution)/shard_map/all_to_all | solution.py:19
  27.9 7.5 %all-to-all-done.1 = bf16[16,64,128]{2,1,0:T(8,128)(2,1)S(1)} async-done(((bf16[16,64,128]{2,1,0:T(8,128)(2,1)}), bf16[16,64,128]{2,1,0:T(8,128)(2,1)S(1)}, u32[]{:S(2)}, u32[]{:S(2)}) %all-to-all-start.1) | async-done | bytes 262176 | tf_op jit(solution)/shard_map/all_to_all | solution.py:19
  35.4 1.8 collective-permute-start.1
  39.7 6.1 %all-to-all-start.2 = ((bf16[128,2,256]{2,1,0:T(2,128)(2,1)}), bf16[128,2,256]{2,1,0:T(2,128)(2,1)S(1)}, u32[]{:S(2)}, u32[]{:S(2)}) async-start(bf16[128,2,256]{2,1,0:T(2,128)(2,1)} %reshape.105), calls=%async_computation.2 | async-start | bytes 262144 | tf_op jit(solution)/shard_map/all_to_all | solution.py:127
  45.9 9.8 %all-to-all-done.2 = bf16[128,2,256]{2,1,0:T(2,128)(2,1)S(1)} async-done(((bf16[128,2,256]{2,1,0:T(2,128)(2,1)}), bf16[128,2,256]{2,1,0:T(2,128)(2,1)S(1)}, u32[]{:S(2)}, u32[]{:S(2)}) %all-to-all-start.2) | async-done | bytes 131104 | tf_op jit(solution)/shard_map/all_to_all | solution.py:127
  56.4 22.1 %all_to_all.41 = bf16[64,64,128]{2,1,0:T(8,128)(2,1)S(1)} all-to-all(bf16[64,64,128]{2,1,0:T(8,128)(2,1)S(1)} %broadcast_in_dim.63), channel_id=1, replica_groups=mesh['y'=4,'x'=4,'z'=4,'c'=2] {'y','x','z'}, dimensions={0} | all-to-all | bytes 2097152 | tf_op jit(solution)/shard_map/all_to_all | solution.py:19
  78.5 2.3 %collective-permute-start.2 = (bf16[64,64,128]{2,1,0:T(8,128)(2,1)S(1)}, bf16[64,64,128]{2,1,0:T(8,128)(2,1)S(1)}, u32[]{:S(2)}, u32[]{:S(2)}) collective-permute-start(bf16[64,64,128]{2,1,0:T(8,128)(2,1)S(1)} %all_to_all.41), channel_id=1, source_target_pairs={{0,1},{1,0},{2,3},{3,2},{4,5},{5,4},{6,7},{7,6},{8,9},{9,8},{10,11... | collective-permute-start | bytes 3145736 | tf_op jit(solution)/shard_map/ppermute | solution.py:20
  80.8 2.3 %collective-permute-done.2 = bf16[64,64,128]{2,1,0:T(8,128)(2,1)S(1)} collective-permute-done((bf16[64,64,128]{2,1,0:T(8,128)(2,1)S(1)}, bf16[64,64,128]{2,1,0:T(8,128)(2,1)S(1)}, u32[]{:S(2)}, u32[]{:S(2)}) %collective-permute-start.2) | collective-permute-done | bytes 1048608 | tf_op jit(solution)/shard_map/ppermute | solution.py:20
  83.5 1.7 fusion.7
  85.5 21.7 %all_to_all.42 = bf16[64,64,128]{2,1,0:T(8,128)(2,1)S(1)} all-to-all(bf16[64,64,128]{2,1,0:T(8,128)(2,1)S(1)} %broadcast_in_dim.64), channel_id=1, replica_groups=mesh['y'=4,'x'=4,'z'=4,'c'=2] {'y','x','z'}, dimensions={0} | all-to-all | bytes 2097152 | tf_op jit(solution)/shard_map/all_to_all | solution.py:19
  107.2 2.2 %collective-permute-start.3 = (bf16[64,64,128]{2,1,0:T(8,128)(2,1)S(1)}, bf16[64,64,128]{2,1,0:T(8,128)(2,1)S(1)}, u32[]{:S(2)}, u32[]{:S(2)}) collective-permute-start(bf16[64,64,128]{2,1,0:T(8,128)(2,1)S(1)} %all_to_all.42), channel_id=1, source_target_pairs={{0,1},{1,0},{2,3},{3,2},{4,5},{5,4},{6,7},{7,6},{8,9},{9,8},{10,11... | collective-permute-start | bytes 3145736 | tf_op jit(solution)/shard_map/ppermute | solution.py:20
  109.3 2.3 %collective-permute-done.3 = bf16[64,64,128]{2,1,0:T(8,128)(2,1)S(1)} collective-permute-done((bf16[64,64,128]{2,1,0:T(8,128)(2,1)S(1)}, bf16[64,64,128]{2,1,0:T(8,128)(2,1)S(1)}, u32[]{:S(2)}, u32[]{:S(2)}) %collective-permute-start.3) | collective-permute-done | bytes 1048608 | tf_op jit(solution)/shard_map/ppermute | solution.py:20
  114.3 21.7 %all_to_all.43 = bf16[64,64,128]{2,1,0:T(8,128)(2,1)S(1)} all-to-all(bf16[64,64,128]{2,1,0:T(8,128)(2,1)S(1)} %broadcast_in_dim.65), channel_id=1, replica_groups=mesh['y'=4,'x'=4,'z'=4,'c'=2] {'y','x','z'}, dimensions={0} | all-to-all | bytes 2097152 | tf_op jit(solution)/shard_map/all_to_all | solution.py:19
  136.0 2.2 %collective-permute-start.4 = (bf16[64,64,128]{2,1,0:T(8,128)(2,1)S(1)}, bf16[64,64,128]{2,1,0:T(8,128)(2,1)S(1)}, u32[]{:S(2)}, u32[]{:S(2)}) collective-permute-start(bf16[64,64,128]{2,1,0:T(8,128)(2,1)S(1)} %all_to_all.43), channel_id=1, source_target_pairs={{0,1},{1,0},{2,3},{3,2},{4,5},{5,4},{6,7},{7,6},{8,9},{9,8},{10,11... | collective-permute-start | bytes 3145736 | tf_op jit(solution)/shard_map/ppermute | solution.py:20
  138.7 1.8 collective-permute-done.4
  141.0 1.7 fusion.8
  143.0 21.7 %all_to_all.44 = bf16[64,64,128]{2,1,0:T(8,128)(2,1)S(1)} all-to-all(bf16[64,64,128]{2,1,0:T(8,128)(2,1)S(1)} %broadcast_in_dim.66), channel_id=1, replica_groups=mesh['y'=4,'x'=4,'z'=4,'c'=2] {'y','x','z'}, dimensions={0} | all-to-all | bytes 2097152 | tf_op jit(solution)/shard_map/all_to_all | solution.py:19
  164.6 2.2 %collective-permute-start.5 = (bf16[64,64,128]{2,1,0:T(8,128)(2,1)S(1)}, bf16[64,64,128]{2,1,0:T(8,128)(2,1)S(1)}, u32[]{:S(2)}, u32[]{:S(2)}) collective-permute-start(bf16[64,64,128]{2,1,0:T(8,128)(2,1)S(1)} %all_to_all.44), channel_id=1, source_target_pairs={{0,1},{1,0},{2,3},{3,2},{4,5},{5,4},{6,7},{7,6},{8,9},{9,8},{10,11... | collective-permute-start | bytes 3145736 | tf_op jit(solution)/shard_map/ppermute | solution.py:20
  166.9 2.2 %collective-permute-done.5 = bf16[64,64,128]{2,1,0:T(8,128)(2,1)S(1)} collective-permute-done((bf16[64,64,128]{2,1,0:T(8,128)(2,1)S(1)}, bf16[64,64,128]{2,1,0:T(8,128)(2,1)S(1)}, u32[]{:S(2)}, u32[]{:S(2)}) %collective-permute-start.5) | collective-permute-done | bytes 1048608 | tf_op jit(solution)/shard_map/ppermute | solution.py:20
  170.7 5.7 %shard_map.131 = f32[128,128]{1,0:T(8,128)S(1)} custom-call(s32[4096]{0:T(1024)S(1)} %fusion.52.index_ref, bf16[8192,128]{1,0:T(8,128)(2,1)S(1)} %bitcast.153, bf16[8192,128]{1,0:T(8,128)(2,1)S(1)} %bitcast.152, bf16[128,4096]{1,0:T(8,128)(2,1)S(1)} %bitcast.154), custom_call_target="tpu_custom_call" | custom-call | tf_op jit(solution)/shard_map/pallas_call | solution.py:59
  176.7 10.2 %all_to_all.45 = bf16[16,64,128]{2,1,0:T(8,128)(2,1)S(1)} all-to-all(bf16[16,64,128]{2,1,0:T(8,128)(2,1)S(1)} %broadcast_in_dim.67), channel_id=1, replica_groups=mesh['y'=4,'x'=4,'z'=4,'c'=2] {'x','z'}, dimensions={0} | all-to-all | bytes 524288 | tf_op jit(solution)/shard_map/all_to_all | solution.py:19
  186.9 1.9 collective-permute-start.6
  (73 shorter events, 18.3 us)
Async XLA Ops:
  0.6 21.7 %copy-start.5 = (bf16[1,2,1,64,128]{4,3,2,1,0:T(8,128)(2,1)S(1)}, bf16[1,2,1,64,128]{4,3,2,1,0:T(8,128)(2,1)}, u32[]{:S(2)}) copy-start(bf16[1,2,1,64,128]{4,3,2,1,0:T(8,128)(2,1)} %param.12) | copy-start | bytes 98308
  18.8 18.4 %copy-start.6 = (s32[1,128,1]{1,2,0:T(1,128)S(1)}, s32[1,128,1]{1,2,0:T(1,128)}, u32[]{:S(2)}) copy-start(s32[1,128,1]{1,2,0:T(1,128)} %param.18) | copy-start | bytes 1540
  18.8 18.4 %copy-start.2 = (bf16[1,128,4096]{2,1,0:T(8,128)(2,1)S(1)}, bf16[1,128,4096]{2,1,0:T(8,128)(2,1)}, u32[]{:S(2)}) copy-start(bf16[1,128,4096]{2,1,0:T(8,128)(2,1)} %param.17) | copy-start | bytes 3145732
  18.8 3.4 %collective-permute-start = (bf16[16,72,128]{2,1,0:T(8,128)(2,1)S(1)}, bf16[16,72,128]{2,1,0:T(8,128)(2,1)S(1)}, u32[]{:S(2)}, u32[]{:S(2)}) collective-permute-start(bf16[16,72,128]{2,1,0:T(8,128)(2,1)S(1)} %all_to_all.40), channel_id=1, source_target_pairs={{0,1},{1,0},{2,3},{3,2},{4,5},{5,4},{6,7},{7,6},{8,9},{9,8},{10,11... | collective-permute-start | bytes 884744 | tf_op jit(solution)/shard_map/ppermute | solution.py:20
  24.2 11.1 %all-to-all-start.1 = ((bf16[16,64,128]{2,1,0:T(8,128)(2,1)}), bf16[16,64,128]{2,1,0:T(8,128)(2,1)S(1)}, u32[]{:S(2)}, u32[]{:S(2)}) async-start(bf16[16,64,128]{2,1,0:T(8,128)(2,1)} %broadcast_in_dim.59), calls=%async_computation.1 | async-start | bytes 524288 | tf_op jit(solution)/shard_map/all_to_all | solution.py:19
  35.4 3.0 %collective-permute-start.1 = (bf16[16,64,128]{2,1,0:T(8,128)(2,1)S(1)}, bf16[16,64,128]{2,1,0:T(8,128)(2,1)S(1)}, u32[]{:S(2)}, u32[]{:S(2)}) collective-permute-start(bf16[16,64,128]{2,1,0:T(8,128)(2,1)S(1)} %all-to-all-done.1), channel_id=1, source_target_pairs={{0,1},{1,0},{2,3},{3,2},{4,5},{5,4},{6,7},{7,6},{8,9},{9,8},{10,11... | collective-permute-start | bytes 786440 | tf_op jit(solution)/shard_map/ppermute | solution.py:20
  37.5 18.6 %copy-start.4 = (bf16[2,1,64,128]{3,2,1,0:T(8,128)(2,1)S(1)}, bf16[2,1,64,128]{3,2,1,0:T(8,128)(2,1)}, u32[]{:S(2)}) copy-start(bf16[2,1,64,128]{3,2,1,0:T(8,128)(2,1)} %param.20) | copy-start | bytes 98308
  39.7 16.0 %all-to-all-start.2 = ((bf16[128,2,256]{2,1,0:T(2,128)(2,1)}), bf16[128,2,256]{2,1,0:T(2,128)(2,1)S(1)}, u32[]{:S(2)}, u32[]{:S(2)}) async-start(bf16[128,2,256]{2,1,0:T(2,128)(2,1)} %reshape.105), calls=%async_computation.2 | async-start | bytes 262144 | tf_op jit(solution)/shard_map/all_to_all | solution.py:127
  78.5 4.6 %collective-permute-start.2 = (bf16[64,64,128]{2,1,0:T(8,128)(2,1)S(1)}, bf16[64,64,128]{2,1,0:T(8,128)(2,1)S(1)}, u32[]{:S(2)}, u32[]{:S(2)}) collective-permute-start(bf16[64,64,128]{2,1,0:T(8,128)(2,1)S(1)} %all_to_all.41), channel_id=1, source_target_pairs={{0,1},{1,0},{2,3},{3,2},{4,5},{5,4},{6,7},{7,6},{8,9},{9,8},{10,11... | collective-permute-start | bytes 3145736 | tf_op jit(solution)/shard_map/ppermute | solution.py:20
  107.2 4.5 %collective-permute-start.3 = (bf16[64,64,128]{2,1,0:T(8,128)(2,1)S(1)}, bf16[64,64,128]{2,1,0:T(8,128)(2,1)S(1)}, u32[]{:S(2)}, u32[]{:S(2)}) collective-permute-start(bf16[64,64,128]{2,1,0:T(8,128)(2,1)S(1)} %all_to_all.42), channel_id=1, source_target_pairs={{0,1},{1,0},{2,3},{3,2},{4,5},{5,4},{6,7},{7,6},{8,9},{9,8},{10,11... | collective-permute-start | bytes 3145736 | tf_op jit(solution)/shard_map/ppermute | solution.py:20
  112.0 1.6 copy-start.1
  136.0 4.5 %collective-permute-start.4 = (bf16[64,64,128]{2,1,0:T(8,128)(2,1)S(1)}, bf16[64,64,128]{2,1,0:T(8,128)(2,1)S(1)}, u32[]{:S(2)}, u32[]{:S(2)}) collective-permute-start(bf16[64,64,128]{2,1,0:T(8,128)(2,1)S(1)} %all_to_all.43), channel_id=1, source_target_pairs={{0,1},{1,0},{2,3},{3,2},{4,5},{5,4},{6,7},{7,6},{8,9},{9,8},{10,11... | collective-permute-start | bytes 3145736 | tf_op jit(solution)/shard_map/ppermute | solution.py:20
  164.6 4.5 %collective-permute-start.5 = (bf16[64,64,128]{2,1,0:T(8,128)(2,1)S(1)}, bf16[64,64,128]{2,1,0:T(8,128)(2,1)S(1)}, u32[]{:S(2)}, u32[]{:S(2)}) collective-permute-start(bf16[64,64,128]{2,1,0:T(8,128)(2,1)S(1)} %all_to_all.44), channel_id=1, source_target_pairs={{0,1},{1,0},{2,3},{3,2},{4,5},{5,4},{6,7},{7,6},{8,9},{9,8},{10,11... | collective-permute-start | bytes 3145736 | tf_op jit(solution)/shard_map/ppermute | solution.py:20
  169.5 1.2 copy-start
  170.7 5.7 %copy-start.3 = (bf16[1,2,1,64,2048]{4,3,2,1,0:T(8,128)(2,1)S(1)}, bf16[1,2,1,64,2048]{4,3,2,1,0:T(8,128)(2,1)}, u32[]{:S(2)}) copy-start(bf16[1,2,1,64,2048]{4,3,2,1,0:T(8,128)(2,1)} %param.14) | copy-start | bytes 1572868
  186.9 3.0 %collective-permute-start.6 = (bf16[16,64,128]{2,1,0:T(8,128)(2,1)S(1)}, bf16[16,64,128]{2,1,0:T(8,128)(2,1)S(1)}, u32[]{:S(2)}, u32[]{:S(2)}) collective-permute-start(bf16[16,64,128]{2,1,0:T(8,128)(2,1)S(1)} %all_to_all.45), channel_id=1, source_target_pairs={{0,1},{1,0},{2,3},{3,2},{4,5},{5,4},{6,7},{7,6},{8,9},{9,8},{10,11... | collective-permute-start | bytes 786440 | tf_op jit(solution)/shard_map/ppermute | solution.py:20

commit v2 on v1

v2 whole, which is shorter than its diff:
```python
import functools

import jax
import jax.numpy as jnp
from jax import lax
from jax.experimental import pallas as pl
from jax.experimental.pallas import tpu as pltpu
from jax.sharding import Mesh
from jax.sharding import PartitionSpec as P

F32 = jnp.float32
BF16 = jnp.bfloat16
ALL = ("y", "x", "z", "c")
PLANE = ("x", "z")
CUBE = ("y", "x", "z")
VMEM = pl.BlockSpec(memory_space=pltpu.VMEM)
SMEM = pl.BlockSpec(memory_space=pltpu.SMEM)
MIB = 1 << 20


def swap(array):
    return lax.ppermute(array, "c", [(0, 1), (1, 0)])


def spread(copies, axes):
    return lax.all_to_all(copies, axes, 0, 0)


def in_core_order(own, other, axis):
    first = lax.axis_index("c") == 0
    return jnp.stack([jnp.where(first, own, other), jnp.where(first, other, own)], axis=axis)


def gather_plane(copies):
    own = spread(copies, PLANE)
    return in_core_order(own, swap(own), 1)


def flat(gathered):
    return gathered.reshape(-1, gathered.shape[-1])


def dot(a, b):
    return jnp.dot(a, b, preferred_element_type=F32)


def rows_of(array, block, first, last):
    lead = array.ndim - 4
    start = (0,) * lead + (block, 0, 0, first)
    stop = (1,) * lead + (block + 1, 1, array.shape[-2], last)
    return lax.slice(array, start, stop).reshape(array.shape[-2], last - first)


def product_kernel(subtract, core_ref, blocks_ref, own_ref, other_ref, *refs):
    if subtract:
        base_ref, out_ref = refs
    else:
        (out_ref,) = refs
    count, half, lanes = blocks_ref.shape
    total = jnp.zeros((half, lanes), F32)
    for i in range(count // 2):
        columns = slice(i * 2 * lanes, (i + 1) * 2 * lanes)
        left = jnp.concatenate([blocks_ref[2 * i], blocks_ref[2 * i + 1]], axis=1)
        right = jnp.concatenate([own_ref[0, :, columns], other_ref[0, :, columns]], axis=0)
        total = total + lax.dot_general(
            left, right, (((1,), (1,)), ((), ())), preferred_element_type=F32
        )
    total = jnp.where(core_ref[0] == 0, total, pltpu.roll(total, lanes // 2, 1))
    if subtract:
        total = base_ref[...] - total
    value = total.astype(BF16)
    if len(out_ref.shape) == 2:
        out_ref[...] = value
    else:
        for j in range(out_ref.shape[0]):
            out_ref[j] = value


def product(core, blocks, own, other, which, base, copies):
    count, half, lanes = blocks.shape
    shape = (copies, half, lanes) if copies else (half, lanes)
    matrix = pl.BlockSpec((1,) + own.shape[1:], lambda i: (which, 0, 0))
    args = (core, blocks, own, other) + (() if base is None else (base,))
    whole = lambda a: pl.BlockSpec(a.shape, lambda i: (0,) * a.ndim)
    specs = [SMEM, whole(blocks), matrix, matrix] + ([] if base is None else [whole(base)])
    return pl.pallas_call(
        functools.partial(product_kernel, base is not None),
        grid=(1,),
        out_shape=jax.ShapeDtypeStruct(shape, BF16),
        in_specs=specs,
        out_specs=pl.BlockSpec(shape, lambda i: (0,) * len(shape)),
        compiler_params=pltpu.CompilerParams(vmem_limit_bytes=14 * MIB),
        cost_estimate=pl.CostEstimate(
            flops=2 * count * half * lanes * lanes, bytes_accessed=4 * MIB, transcendentals=0
        ),
    )(*args)


def build_kernel(index_ref, coupling_ref, out_ref, sums_ref, turned_ref):
    def clear(i, carry):
        sums_ref[pl.ds(pl.multiple_of(i * 64, 64), 64), :] = jnp.zeros((64, 128), F32)
        return carry

    lax.fori_loop(0, sums_ref.shape[0] // 64, clear, 0, unroll=4)

    for i in range(turned_ref.shape[0] // 128):
        block = coupling_ref[:, i * 128 : (i + 1) * 128].astype(F32)
        turned_ref[i * 128 : (i + 1) * 128, :] = block.T

    def add(group, carry):
        base = pl.multiple_of(group * 8, 8)
        block = turned_ref[pl.ds(base, 8), :]
        for part in range(2):
            at = [index_ref[base + part * 4 + j] for j in range(4)]
            terms = [block[part * 4 + j : part * 4 + j + 1] for j in range(4)]
            old = [sums_ref[pl.ds(at[j], 1), :] for j in range(4)]
            for j in range(4):
                value = old[j] + terms[j]
                for m in range(j):
                    value = value + jnp.where(at[m] == at[j], terms[m], 0.0)
                sums_ref[pl.ds(at[j], 1), :] = value
        return carry

    lax.fori_loop(0, turned_ref.shape[0] // 8, add, 0, unroll=2)

    def settle(i, carry):
        rows = pl.ds(pl.multiple_of(i * 64, 64), 64)
        out_ref[rows, :] = sums_ref[rows, :].astype(BF16)
        return carry

    lax.fori_loop(0, sums_ref.shape[0] // 64, settle, 0, unroll=4)


def build_coupling(index, coupling, root_rows):
    rows, columns = coupling.shape
    return pl.pallas_call(
        build_kernel,
        out_shape=jax.ShapeDtypeStruct((root_rows, rows), BF16),
        in_specs=[SMEM, VMEM],
        out_specs=VMEM,
        scratch_shapes=[
            pltpu.VMEM((root_rows, rows), F32),
            pltpu.VMEM((columns, rows), F32),
        ],
        compiler_params=pltpu.CompilerParams(vmem_limit_bytes=20 * MIB),
        cost_estimate=pl.CostEstimate(flops=0, bytes_accessed=40 * MIB, transcendentals=0),
    )(index, coupling)


def couple_kernel(blocks_ref, matrix_ref, *refs):
    out_ref = refs[-1]
    count, half, lanes = blocks_ref.shape
    total = refs[0][...] if len(refs) == 2 else jnp.zeros((half, matrix_ref.shape[1]), F32)
    for i in range(count // 2):
        left = jnp.concatenate([blocks_ref[2 * i], blocks_ref[2 * i + 1]], axis=1)
        right = matrix_ref[i * 2 * lanes : (i + 1) * 2 * lanes, :]
        total = total + jnp.dot(left, right, preferred_element_type=F32)
    out_ref[...] = total


def couple(blocks, matrix, which, base):
    count, half, lanes = blocks.shape
    whole = lambda a: pl.BlockSpec(a.shape, lambda i: (0,) * a.ndim)
    args = (blocks, matrix) + (() if base is None else (base,))
    shape = (half, matrix.shape[1])
    return pl.pallas_call(
        couple_kernel,
        grid=(1,),
        out_shape=jax.ShapeDtypeStruct(shape, F32),
        in_specs=[whole(blocks), pl.BlockSpec((count * lanes, shape[1]), lambda i: (which, 0))]
        + ([] if base is None else [whole(base)]),
        out_specs=pl.BlockSpec(shape, lambda i: (0, 0)),
        compiler_params=pltpu.CompilerParams(vmem_limit_bytes=14 * MIB),
        cost_estimate=pl.CostEstimate(
            flops=2 * count * half * lanes * lanes, bytes_accessed=3 * MIB, transcendentals=0
        ),
    )(*args)


def body(
    child_rhs,
    child_lower,
    child_inverse,
    child_upper,
    child_coupling,
    child_update,
    update_owner,
    update_slot,
    root_rhs,
    root_lower,
    root_inverse,
    root_upper,
):
    planes = lax.axis_size("x") * lax.axis_size("z")
    cubes = planes * lax.axis_size("y")
    devices = cubes * 2
    stripe, rhs = root_rhs.shape[2:]
    half = rhs // 2
    kc = child_inverse.shape[-1]
    kr = root_inverse.shape[-1]
    nc = child_lower.shape[-1]
    owner = update_owner[0, :, 0]
    slot = update_slot[0]
    held = owner.shape[0]
    me = lax.axis_index("c")
    core = me.astype(jnp.int32).reshape(1)

    own = jnp.stack(
        [
            rows_of(root_lower, 1, 0, kr),
            rows_of(root_inverse, 1, 0, kr),
            rows_of(root_inverse, 0, 0, kr),
            rows_of(root_upper, 0, kr, 2 * kr),
        ]
    )
    other = swap(own)

    turned = jnp.transpose(root_rhs[:, 0], (2, 0, 1)).reshape(2, half, 2, stripe)
    kept = lax.dynamic_index_in_dim(turned, me, 0, keepdims=False)
    given = lax.dynamic_index_in_dim(turned, 1 - me, 0, keepdims=False)
    right_base = in_core_order(kept, swap(given), 2).reshape(half, -1).astype(F32)

    same = (owner[:, None] == owner[None, :]) & (
        jnp.arange(held)[None, :] < jnp.arange(held)[:, None]
    )
    rank = jnp.sum(same.astype(jnp.int32), axis=1)
    place = owner * 2 + rank
    select = (jnp.arange(devices * 2)[:, None] == place[None, :]).astype(BF16)
    target = slot // stripe * (2 * stripe) + owner % 2 * stripe + slot % stripe + 1
    target_lanes = jnp.where(jnp.arange(half)[None, :] == 0, target[:, None], 0).astype(BF16)

    marks = jnp.concatenate(
        [owner[None], slot[None], jnp.zeros((6, held), jnp.int32)], axis=0
    ).astype(BF16)
    first_piece = jnp.concatenate([child_rhs[0, 0, 0], marks], axis=0)
    first = gather_plane(jnp.broadcast_to(first_piece, (planes,) + first_piece.shape))
    y0 = flat(first[:, :, :stripe])
    owners = first[:, :, stripe].astype(jnp.int32).reshape(-1)
    slots = first[:, :, stripe + 1].astype(jnp.int32).reshape(-1)
    index = slots // stripe * kr + owners * stripe + slots % stripe
    y1_own = (
        child_rhs[0, 1, 0].astype(F32) - dot(rows_of(child_lower, 1, 0, kc), y0)
    ).astype(BF16)
    y1 = flat(gather_plane(jnp.broadcast_to(y1_own, (planes,) + y1_own.shape)))
    update = child_update[0]
    contribution = (-(dot(update[:, :kc], y0) + dot(update[:, kc:], y1))).astype(BF16)

    packed = [
        dot(
            select,
            jnp.concatenate([contribution[:, h * half : (h + 1) * half], target_lanes], axis=1),
        )
        .astype(BF16)
        .reshape(cubes, 1, 4, rhs)
        for h in range(2)
    ]
    arrived = spread(jnp.concatenate(packed, axis=1).reshape(devices, 4, rhs), ALL)
    arrived = arrived.reshape(devices * 4, rhs)
    lands = (
        arrived[:, half : half + 1].astype(jnp.int32)
        == jnp.arange(1, 4 * stripe + 1)[None, :]
    ).astype(BF16)
    received = lax.dot_general(
        arrived, lands, (((0,), (0,)), ((), ())), preferred_element_type=F32
    )[:half]
    right = right_base + received

    r0_own = right[:, : 2 * stripe].astype(BF16)
    r0 = spread(jnp.broadcast_to(r0_own, (cubes,) + r0_own.shape), CUBE)
    r1 = spread(product(core, r0, own, other, 0, right[:, 2 * stripe :], cubes), CUBE)
    x1 = spread(product(core, r1, own, other, 1, None, cubes), CUBE)
    z0_own = product(core, r0, own, other, 2, None, 0).astype(F32)
    x0_copies = product(core, x1, own, other, 3, z0_own, cubes)
    x0 = spread(x0_copies, CUBE)

    summed = build_coupling(index, child_coupling.reshape(2 * stripe, -1), 2 * kr)
    x1_other = swap(x1)
    x0_other = swap(x0)
    coupled_own = couple(x0, summed, 0, couple(x1, summed, 1, None))
    coupled_other = couple(x0_other, summed, 0, couple(x1_other, summed, 1, None))
    coupled = in_core_order(coupled_own, coupled_other, 0).reshape(rhs, 2 * stripe).T
    z0c = dot(rows_of(child_inverse, 0, 0, kc), y0).astype(BF16).astype(F32)
    z1c = dot(rows_of(child_inverse, 1, 0, kc), y1).astype(BF16).astype(F32)
    c1_own = (z1c - coupled[stripe:]).astype(BF16)
    c1 = flat(gather_plane(jnp.broadcast_to(c1_own, (planes,) + c1_own.shape)))
    c0_own = (
        z0c - coupled[:stripe] - dot(rows_of(child_upper, 0, kc, nc), c1)
    ).astype(BF16)
    child_solution = jnp.stack([c0_own, c1_own])[None, :, None]

    chip = (lax.axis_index("y") * planes + lax.axis_index("x") * lax.axis_size("z")) + (
        lax.axis_index("z")
    )

    def own_rows(mine, others):
        pair = in_core_order(
            lax.dynamic_index_in_dim(mine, chip, 0, keepdims=False),
            lax.dynamic_index_in_dim(others, chip, 0, keepdims=False),
            0,
        ).reshape(rhs, 2 * stripe)
        return lax.dynamic_slice_in_dim(pair.T, me * stripe, stripe, 0)

    root_solution = jnp.stack([own_rows(x0, x0_other), own_rows(x1, x1_other)])[:, None]
    return child_solution, root_solution


def solution(mesh):
    leaf, front = mesh.devices.shape
    fine = Mesh(mesh.devices.reshape((leaf, 4, front // 8, 2)), ALL)
    subtree = P("y", None, ("x", "z", "c"), None, None)
    ancestor = P(None, ALL, None, None)
    in_specs = (
        subtree,
        subtree,
        subtree,
        subtree,
        subtree,
        P("y", ("x", "z", "c"), None),
        P("y", ("x", "z", "c"), None),
        P("y", ("x", "z", "c")),
        ancestor,
        ancestor,
        ancestor,
        ancestor,
    )
    return jax.shard_map(
        body, mesh=fine, in_specs=in_specs, out_specs=(subtree, ancestor), check_vma=False
    )
```

time: 193 us -> 210 us (1.088)
  blocking collectives: 113 us -> 21.2 us
  waiting for transfers between devices: 27.3 us -> 75.7 us
  starting transfers between devices: 24.4 us -> 52.4 us
  Pallas kernels: 5.74 us -> 28.8 us
  local copies, waits for them, and re-layouts: 6.39 us -> 16.5 us
  matrix products: 8.36 us -> 4.29 us
  other arithmetic: 5.53 us -> 8.43 us
    all_to_all x6 -> x1, blocking collectives: 113 us -> 21.2 us  [spread(): return lax.all_to_all(copies, axes, 0, 0)]
    all_to_all x2 -> x7, waiting for transfers between devices: 17.3 us -> 69.2 us  [spread(): return lax.all_to_all(copies, axes, 0, 0)]
    all_to_all x2 -> x7, starting transfers between devices: 9.67 us -> 40.5 us  [spread(): return lax.all_to_all(copies, axes, 0, 0)]
    pallas_call x1 -> x9, Pallas kernels: 5.74 us -> 28.8 us  [the longest x1 13.4 us: build_coupling(): pl.pallas_call(build_kernel, out_shape=jax.ShapeDtypeStruct((root_rows, r...]
    dot_general x11 -> x8, matrix products: 8.08 us -> 3.99 us  [dot(): return jnp.dot(a, b, preferred_element_type=F32)]
    unnamed x14 -> x30, local copies, waits for them, and re-layouts: 2.34 us -> 6.29 us
    ppermute x7, waiting for transfers between devices: 9.98 us -> 6.5 us  [swap(): return lax.ppermute(array, 'c', [(0, 1), (1, 0)])]
    another operation x4 -> x5, local copies, waits for them, and re-layouts: 0.68 us -> 3.57 us  [the longest x2 3.36 us: body(): jnp.stack([rows_of(root_lower, 1, 0, kr), rows_of(root_inverse, 1, 0, kr)...]
  transfers between devices with their start and end apart: 9 -> 14, of which waited for: 9 -> 9; matrix products, arithmetic and copies ran while one was open for 1% -> 8% of each run, Pallas kernels for 0% -> 8%
where the time goes in v2:
time: 210 us; the launch traced here: 209 us
  waiting for transfers between devices  75.7 us (36%)
  starting transfers between devices  52.4 us (25%)
  Pallas kernels  28.8 us (14%)
  blocking collectives  21.2 us (10%)
  local copies, waits for them, and re-layouts  16.5 us (8%)
  other arithmetic  8.43 us (4%)
  matrix products  4.29 us (2%)
    all_to_all x7, waiting for transfers between devices, spread(): return lax.all_to_all(copies, axes, 0, 0)  69.2 us
    all_to_all x7, starting transfers between devices, spread(): return lax.all_to_all(copies, axes, 0, 0)  40.5 us
    all_to_all x1, blocking collectives, spread(): return lax.all_to_all(copies, axes, 0, 0)  21.2 us
    pallas_call x1, Pallas kernels, build_coupling(): pl.pallas_call(build_kernel, out_shape=jax.ShapeDtypeStruct((root_rows, r...  13.4 us
    pallas_call x4, Pallas kernels, product(): pl.pallas_call(functools.partial(product_kernel, base is not None), grid=...  12.1 us
    ppermute x7, starting transfers between devices, swap(): return lax.ppermute(array, 'c', [(0, 1), (1, 0)])  11.9 us
    ppermute x7, waiting for transfers between devices, swap(): return lax.ppermute(array, 'c', [(0, 1), (1, 0)])  6.5 us
    unnamed x30, local copies, waits for them, and re-layouts  6.29 us
  transfers between devices with their start and end apart: 14, of which 9 were waited for; matrix products, arithmetic and copies ran while one was open for 8% of the time, Pallas kernels for 8%

profile of v2, /device:TPU:1, one launch (start us, length us, event | category | flops | bytes accessed | tf_op | source)
XLA Modules:
  0.0 208.5 jit_solution(8849833251009831460)
XLA Ops:
  3.6 8.4 %all-to-all-start = ((bf16[16,72,128]{2,1,0:T(8,128)(2,1)}), bf16[16,72,128]{2,1,0:T(8,128)(2,1)S(1)}, u32[]{:S(2)}, u32[]{:S(2)}) async-start(bf16[16,72,128]{2,1,0:T(8,128)(2,1)} %broadcast_in_dim.49), calls=%async_computation | async-start | bytes 589824 | tf_op jit(solution)/shard_map/all_to_all | solution.py:26
  17.6 2.3 %pad_maximum_fusion.own_ref = bf16[4,64,8192]{2,1,0:T(8,128)(2,1)} fusion(bf16[1,64,8192]{2,1,0:T(8,128)(2,1)S(1)} %get-tuple-element.34, bf16[1,64,8192]{2,1,0:T(8,128)(2,1)S(1)} %get-tuple-element.17, bf16[1,64,8192]{2,1,0:T(8,128)(2,1)S(1)} %get-tuple-element.16, bf16[1,64,8192]{2,1,0:T(8,128)(2,1)S(1)} %get-tuple-element.35), kind=kLoop, calls=%fused_computation | loop fusion | flops 6291456 | bytes 8388608 | tf_op jit(solution)/shard_map/stack | solution.py:208
  22.0 5.5 %collective-permute-done = bf16[16,72,128]{2,1,0:T(8,128)(2,1)S(1)} collective-permute-done((bf16[16,72,128]{2,1,0:T(8,128)(2,1)S(1)}, bf16[16,72,128]{2,1,0:T(8,128)(2,1)S(1)}, u32[]{:S(2)}, u32[]{:S(2)}) %collective-permute-start) | collective-permute-done | bytes 294944 | tf_op jit(solution)/shard_map/ppermute | solution.py:22
  30.5 6.0 %all-to-all-start.1 = ((bf16[16,64,128]{2,1,0:T(8,128)(2,1)}), bf16[16,64,128]{2,1,0:T(8,128)(2,1)S(1)}, u32[]{:S(2)}, u32[]{:S(2)}) async-start(bf16[16,64,128]{2,1,0:T(8,128)(2,1)} %broadcast_in_dim.50), calls=%async_computation.1 | async-start | bytes 524288 | tf_op jit(solution)/shard_map/all_to_all | solution.py:26
  36.6 7.5 %all-to-all-done.1 = bf16[16,64,128]{2,1,0:T(8,128)(2,1)S(1)} async-done(((bf16[16,64,128]{2,1,0:T(8,128)(2,1)}), bf16[16,64,128]{2,1,0:T(8,128)(2,1)S(1)}, u32[]{:S(2)}, u32[]{:S(2)}) %all-to-all-start.1) | async-done | bytes 262176 | tf_op jit(solution)/shard_map/all_to_all | solution.py:26
  50.0 6.1 %all-to-all-start.2 = ((bf16[128,4,128]{2,1,0:T(4,128)(2,1)}), bf16[128,4,128]{2,1,0:T(4,128)(2,1)S(1)}, u32[]{:S(2)}, u32[]{:S(2)}) async-start(bf16[128,4,128]{2,1,0:T(4,128)(2,1)} %copy.66), calls=%async_computation.2 | async-start | bytes 262144 | tf_op jit(solution)/shard_map/all_to_all | solution.py:26
  56.4 9.5 %all-to-all-done.2 = bf16[128,4,128]{2,1,0:T(4,128)(2,1)S(1)} async-done(((bf16[128,4,128]{2,1,0:T(4,128)(2,1)}), bf16[128,4,128]{2,1,0:T(4,128)(2,1)S(1)}, u32[]{:S(2)}, u32[]{:S(2)}) %all-to-all-start.2) | async-done | bytes 131104 | tf_op jit(solution)/shard_map/all_to_all | solution.py:26
  67.7 4.9 %all-to-all-start.3 = ((bf16[64,64,128]{2,1,0:T(8,128)(2,1)}), bf16[64,64,128]{2,1,0:T(8,128)(2,1)S(1)}, u32[]{:S(2)}, u32[]{:S(2)}) async-start(bf16[64,64,128]{2,1,0:T(8,128)(2,1)} %broadcast_in_dim.54), calls=%async_computation.3 | async-start | bytes 2097152 | tf_op jit(solution)/shard_map/all_to_all | solution.py:26
  72.7 17.4 %all-to-all-done.3.blocks_ref = bf16[64,64,128]{2,1,0:T(8,128)(2,1)S(1)} async-done(((bf16[64,64,128]{2,1,0:T(8,128)(2,1)}), bf16[64,64,128]{2,1,0:T(8,128)(2,1)S(1)}, u32[]{:S(2)}, u32[]{:S(2)}) %all-to-all-start.3) | async-done | bytes 1048608 | tf_op jit(solution)/shard_map/all_to_all | solution.py:26
  90.0 2.5 %shard_map.131 = bf16[64,64,128]{2,1,0:T(8,128)(2,1)S(1)} custom-call(s32[1]{0:T(128)} %bitcast.8.core_ref, bf16[64,64,128]{2,1,0:T(8,128)(2,1)S(1)} %all-to-all-done.3.blocks_ref, bf16[4,64,8192]{2,1,0:T(8,128)(2,1)} %pad_maximum_fusion.own_ref, bf16[4,64,8192]{2,1,0:T(8,128)(2,1)} %collective-permute-done.3.other_ref, f32[64,128]{1,0:T(8,128)S(1)} %slice.103.refs_0_), custom_call_target="tpu_custom_call" | custom-call | flops 134217728 | bytes 4194304 | tf_op jit(solution)/shard_map/pallas_call | solution.py:86
  92.6 21.2 %all_to_all.40.blocks_ref = bf16[64,64,128]{2,1,0:T(8,128)(2,1)S(1)} all-to-all(bf16[64,64,128]{2,1,0:T(8,128)(2,1)S(1)} %shard_map.131), channel_id=1, replica_groups=mesh['y'=4,'x'=4,'z'=4,'c'=2] {'y','x','z'}, dimensions={0} | all-to-all | bytes 2097152 | tf_op jit(solution)/shard_map/all_to_all | solution.py:26
  113.8 3.5 %shard_map.132 = bf16[64,64,128]{2,1,0:T(8,128)(2,1)} custom-call(s32[1]{0:T(128)} %bitcast.8.core_ref, bf16[64,64,128]{2,1,0:T(8,128)(2,1)S(1)} %all_to_all.40.blocks_ref, bf16[4,64,8192]{2,1,0:T(8,128)(2,1)} %pad_maximum_fusion.own_ref, bf16[4,64,8192]{2,1,0:T(8,128)(2,1)} %collective-permute-done.3.other_ref), custom_call_target="tpu_custom_call" | custom-call | flops 134217728 | bytes 4194304 | tf_op jit(solution)/shard_map/pallas_call | solution.py:86
  117.3 5.7 %all-to-all-start.5 = ((bf16[64,64,128]{2,1,0:T(8,128)(2,1)}), bf16[64,64,128]{2,1,0:T(8,128)(2,1)S(1)}, u32[]{:S(2)}, u32[]{:S(2)}) async-start(bf16[64,64,128]{2,1,0:T(8,128)(2,1)} %shard_map.132), calls=%async_computation.5 | async-start | bytes 2097152 | tf_op jit(solution)/shard_map/all_to_all | solution.py:26
  123.1 2.4 %shard_map.133 = bf16[64,128]{1,0:T(8,128)(2,1)S(1)} custom-call(s32[1]{0:T(128)} %bitcast.8.core_ref, bf16[64,64,128]{2,1,0:T(8,128)(2,1)S(1)} %all-to-all-done.3.blocks_ref, bf16[4,64,8192]{2,1,0:T(8,128)(2,1)} %pad_maximum_fusion.own_ref, bf16[4,64,8192]{2,1,0:T(8,128)(2,1)} %collective-permute-done.3.other_ref), custom_call_target="tpu_custom_call" | custom-call | flops 134217728 | bytes 4194304 | tf_op jit(solution)/shard_map/pallas_call | solution.py:86
  125.5 13.8 %all-to-all-done.5.blocks_ref = bf16[64,64,128]{2,1,0:T(8,128)(2,1)S(1)} async-done(((bf16[64,64,128]{2,1,0:T(8,128)(2,1)}), bf16[64,64,128]{2,1,0:T(8,128)(2,1)S(1)}, u32[]{:S(2)}, u32[]{:S(2)}) %all-to-all-start.5) | async-done | bytes 1048608 | tf_op jit(solution)/shard_map/all_to_all | solution.py:26
  139.4 3.5 %shard_map.134 = bf16[64,64,128]{2,1,0:T(8,128)(2,1)} custom-call(s32[1]{0:T(128)} %bitcast.8.core_ref, bf16[64,64,128]{2,1,0:T(8,128)(2,1)S(1)} %all-to-all-done.5.blocks_ref, bf16[4,64,8192]{2,1,0:T(8,128)(2,1)} %pad_maximum_fusion.own_ref, bf16[4,64,8192]{2,1,0:T(8,128)(2,1)} %collective-permute-done.3.other_ref, f32[64,128]{1,0:T(8,128)S(1)} %convert_element_type.93.refs_0_), custom_call_target="tpu_custom_call" | custom-call | flops 134217728 | bytes 4194304 | tf_op jit(solution)/shard_map/pallas_call | solution.py:86
  142.9 5.8 %all-to-all-start.6 = ((bf16[64,64,128]{2,1,0:T(8,128)(2,1)}), bf16[64,64,128]{2,1,0:T(8,128)(2,1)S(1)}, u32[]{:S(2)}, u32[]{:S(2)}) async-start(bf16[64,64,128]{2,1,0:T(8,128)(2,1)} %shard_map.134), calls=%async_computation.6 | async-start | bytes 2097152 | tf_op jit(solution)/shard_map/all_to_all | solution.py:26
  148.7 2.3 %collective-permute-start.5 = (bf16[64,64,128]{2,1,0:T(8,128)(2,1)S(1)}, bf16[64,64,128]{2,1,0:T(8,128)(2,1)S(1)}, u32[]{:S(2)}, u32[]{:S(2)}) collective-permute-start(bf16[64,64,128]{2,1,0:T(8,128)(2,1)S(1)} %all-to-all-done.5.blocks_ref), channel_id=1, source_target_pairs={{0,1},{1,0},{2,3},{3,2},{4,5},{5,4},{6,7},{7,6},{8,9},{9,8},{10,11... | collective-permute-start | bytes 3145736 | tf_op jit(solution)/shard_map/ppermute | solution.py:22
  151.0 14.0 %all-to-all-done.6.blocks_ref = bf16[64,64,128]{2,1,0:T(8,128)(2,1)S(1)} async-done(((bf16[64,64,128]{2,1,0:T(8,128)(2,1)}), bf16[64,64,128]{2,1,0:T(8,128)(2,1)S(1)}, u32[]{:S(2)}, u32[]{:S(2)}) %all-to-all-start.6) | async-done | bytes 1048608 | tf_op jit(solution)/shard_map/all_to_all | solution.py:26
  165.0 3.4 %collective-permute-start.4 = (bf16[64,64,128]{2,1,0:T(8,128)(2,1)S(1)}, bf16[64,64,128]{2,1,0:T(8,128)(2,1)}, u32[]{:S(2)}, u32[]{:S(2)}) collective-permute-start(bf16[64,64,128]{2,1,0:T(8,128)(2,1)S(1)} %all-to-all-done.6.blocks_ref), channel_id=1, source_target_pairs={{0,1},{1,0},{2,3},{3,2},{4,5},{5,4},{6,7},{7,6},{8,9},{9,8},{10,11... | collective-permute-start | bytes 3145736 | tf_op jit(solution)/shard_map/ppermute | solution.py:22
  171.2 13.4 %shard_map.135.matrix_ref = bf16[16384,128]{1,0:T(8,128)(2,1)S(1)} custom-call(s32[4096]{0:T(1024)S(1)} %fusion.41.index_ref, bf16[128,4096]{1,0:T(8,128)(2,1)S(1)} %bitcast.145), custom_call_target="tpu_custom_call" | custom-call | bytes 41943040 | tf_op jit(solution)/shard_map/pallas_call | solution.py:136
  186.8 2.2 %copy-done.1 = bf16[16384,128]{1,0:T(8,128)(2,1)S(1)} copy-done((bf16[16384,128]{1,0:T(8,128)(2,1)S(1)}, bf16[16384,128]{1,0:T(8,128)(2,1)}, u32[]{:S(2)}) %copy-start.1) | copy-done | bytes 4194328
  192.5 3.5 %all-to-all-start.7 = ((bf16[16,64,128]{2,1,0:T(8,128)(2,1)}), bf16[16,64,128]{2,1,0:T(8,128)(2,1)S(1)}, u32[]{:S(2)}, u32[]{:S(2)}) async-start(bf16[16,64,128]{2,1,0:T(8,128)(2,1)} %broadcast_in_dim.55), calls=%async_computation.7 | async-start | bytes 524288 | tf_op jit(solution)/shard_map/all_to_all | solution.py:26
  197.0 7.0 %all-to-all-done.7 = bf16[16,64,128]{2,1,0:T(8,128)(2,1)S(1)} async-done(((bf16[16,64,128]{2,1,0:T(8,128)(2,1)}), bf16[16,64,128]{2,1,0:T(8,128)(2,1)S(1)}, u32[]{:S(2)}, u32[]{:S(2)}) %all-to-all-start.7) | async-done | bytes 262176 | tf_op jit(solution)/shard_map/all_to_all | solution.py:26
  (107 shorter events, 35.5 us)
Async XLA Ops:
  3.6 16.3 %all-to-all-start = ((bf16[16,72,128]{2,1,0:T(8,128)(2,1)}), bf16[16,72,128]{2,1,0:T(8,128)(2,1)S(1)}, u32[]{:S(2)}, u32[]{:S(2)}) async-start(bf16[16,72,128]{2,1,0:T(8,128)(2,1)} %broadcast_in_dim.49), calls=%async_computation | async-start | bytes 589824 | tf_op jit(solution)/shard_map/all_to_all | solution.py:26
  13.2 42.9 %collective-permute-start.1 = (bf16[64,2,64]{2,0,1:T(8,128)(2,1)S(1)}, bf16[64,2,64]{2,0,1:T(8,128)(2,1)S(1)}, u32[]{:S(2)}, u32[]{:S(2)}) collective-permute-start(bf16[64,2,64]{2,0,1:T(8,128)(2,1)S(1)} %bitcast.170), channel_id=1, source_target_pairs={{0,1},{1,0},{2,3},{3,2},{4,5},{5,4},{6,7},{7,6},{8,9},{9,8},{10,11... | collective-permute-start | bytes 49160 | tf_op jit(solution)/shard_map/ppermute | solution.py:22
  17.6 4.3 %copy-start.12 = (s32[1,128,1]{1,2,0:T(1,128)S(1)}, s32[1,128,1]{1,2,0:T(1,128)}, u32[]{:S(2)}) copy-start(s32[1,128,1]{1,2,0:T(1,128)} %param.18) | copy-start | bytes 1540
  17.6 4.4 %copy-start.11 = (s32[1,128]{1,0:T(1,128)S(1)}, s32[1,128]{1,0:T(1,128)}, u32[]{:S(2)}) copy-start(s32[1,128]{1,0:T(1,128)} %param.19) | copy-start | bytes 1540
  17.6 10.8 %copy-start.10 = (bf16[1,2,1,64,128]{4,3,2,1,0:T(8,128)(2,1)S(1)}, bf16[1,2,1,64,128]{4,3,2,1,0:T(8,128)(2,1)}, u32[]{:S(2)}) copy-start(bf16[1,2,1,64,128]{4,3,2,1,0:T(8,128)(2,1)} %param.12) | copy-start | bytes 98308
  17.6 28.4 %copy-start.8 = (bf16[1,128,4096]{2,1,0:T(8,128)(2,1)S(1)}, bf16[1,128,4096]{2,1,0:T(8,128)(2,1)}, u32[]{:S(2)}) copy-start(bf16[1,128,4096]{2,1,0:T(8,128)(2,1)} %param.17) | copy-start | bytes 3145732
  19.9 70.1 %collective-permute-start.3 = (bf16[4,64,8192]{2,1,0:T(8,128)(2,1)}, bf16[4,64,8192]{2,1,0:T(8,128)(2,1)}, u32[]{:S(2)}, u32[]{:S(2)}) collective-permute-start(bf16[4,64,8192]{2,1,0:T(8,128)(2,1)} %pad_maximum_fusion.own_ref), channel_id=1, source_target_pairs={{0,1},{1,0},{2,3},{3,2},{4,5},{5,4},{6,7},{7,6},{8,9},{9,8},{10,11... | collective-permute-start | bytes 12582920 | tf_op jit(solution)/shard_map/ppermute | solution.py:22
  19.9 7.6 %collective-permute-start = (bf16[16,72,128]{2,1,0:T(8,128)(2,1)S(1)}, bf16[16,72,128]{2,1,0:T(8,128)(2,1)S(1)}, u32[]{:S(2)}, u32[]{:S(2)}) collective-permute-start(bf16[16,72,128]{2,1,0:T(8,128)(2,1)S(1)} %all-to-all-done), channel_id=1, source_target_pairs={{0,1},{1,0},{2,3},{3,2},{4,5},{5,4},{6,7},{7,6},{8,9},{9,8},{10,11... | collective-permute-start | bytes 884744 | tf_op jit(solution)/shard_map/ppermute | solution.py:22
  28.4 28.1 %copy-start.3 = (bf16[16,2,64,128]{3,2,1,0:T(8,128)(2,1)}, bf16[16,2,64,128]{3,2,1,0:T(8,128)(2,1)S(1)}, u32[]{:S(2)}) copy-start(bf16[16,2,64,128]{3,2,1,0:T(8,128)(2,1)S(1)} %fusion.15) | copy-start | bytes 1572868
  30.5 13.5 %all-to-all-start.1 = ((bf16[16,64,128]{2,1,0:T(8,128)(2,1)}), bf16[16,64,128]{2,1,0:T(8,128)(2,1)S(1)}, u32[]{:S(2)}, u32[]{:S(2)}) async-start(bf16[16,64,128]{2,1,0:T(8,128)(2,1)} %broadcast_in_dim.50), calls=%async_computation.1 | async-start | bytes 524288 | tf_op jit(solution)/shard_map/all_to_all | solution.py:26
  44.0 3.1 %collective-permute-start.2 = (bf16[16,64,128]{2,1,0:T(8,128)(2,1)S(1)}, bf16[16,64,128]{2,1,0:T(8,128)(2,1)S(1)}, u32[]{:S(2)}, u32[]{:S(2)}) collective-permute-start(bf16[16,64,128]{2,1,0:T(8,128)(2,1)S(1)} %all-to-all-done.1), channel_id=1, source_target_pairs={{0,1},{1,0},{2,3},{3,2},{4,5},{5,4},{6,7},{7,6},{8,9},{9,8},{10,11... | collective-permute-start | bytes 786440 | tf_op jit(solution)/shard_map/ppermute | solution.py:22
  50.0 15.9 %all-to-all-start.2 = ((bf16[128,4,128]{2,1,0:T(4,128)(2,1)}), bf16[128,4,128]{2,1,0:T(4,128)(2,1)S(1)}, u32[]{:S(2)}, u32[]{:S(2)}) async-start(bf16[128,4,128]{2,1,0:T(4,128)(2,1)} %copy.66), calls=%async_computation.2 | async-start | bytes 262144 | tf_op jit(solution)/shard_map/all_to_all | solution.py:26
  67.7 22.3 %all-to-all-start.3 = ((bf16[64,64,128]{2,1,0:T(8,128)(2,1)}), bf16[64,64,128]{2,1,0:T(8,128)(2,1)S(1)}, u32[]{:S(2)}, u32[]{:S(2)}) async-start(bf16[64,64,128]{2,1,0:T(8,128)(2,1)} %broadcast_in_dim.54), calls=%async_computation.3 | async-start | bytes 2097152 | tf_op jit(solution)/shard_map/all_to_all | solution.py:26
  117.3 22.0 %all-to-all-start.5 = ((bf16[64,64,128]{2,1,0:T(8,128)(2,1)}), bf16[64,64,128]{2,1,0:T(8,128)(2,1)S(1)}, u32[]{:S(2)}, u32[]{:S(2)}) async-start(bf16[64,64,128]{2,1,0:T(8,128)(2,1)} %shard_map.132), calls=%async_computation.5 | async-start | bytes 2097152 | tf_op jit(solution)/shard_map/all_to_all | solution.py:26
  142.9 22.1 %all-to-all-start.6 = ((bf16[64,64,128]{2,1,0:T(8,128)(2,1)}), bf16[64,64,128]{2,1,0:T(8,128)(2,1)S(1)}, u32[]{:S(2)}, u32[]{:S(2)}) async-start(bf16[64,64,128]{2,1,0:T(8,128)(2,1)} %shard_map.134), calls=%async_computation.6 | async-start | bytes 2097152 | tf_op jit(solution)/shard_map/all_to_all | solution.py:26
  148.7 37.9 %collective-permute-start.5 = (bf16[64,64,128]{2,1,0:T(8,128)(2,1)S(1)}, bf16[64,64,128]{2,1,0:T(8,128)(2,1)S(1)}, u32[]{:S(2)}, u32[]{:S(2)}) collective-permute-start(bf16[64,64,128]{2,1,0:T(8,128)(2,1)S(1)} %all-to-all-done.5.blocks_ref), channel_id=1, source_target_pairs={{0,1},{1,0},{2,3},{3,2},{4,5},{5,4},{6,7},{7,6},{8,9},{9,8},{10,11... | collective-permute-start | bytes 3145736 | tf_op jit(solution)/shard_map/ppermute | solution.py:22
  165.0 24.5 %collective-permute-start.4 = (bf16[64,64,128]{2,1,0:T(8,128)(2,1)S(1)}, bf16[64,64,128]{2,1,0:T(8,128)(2,1)}, u32[]{:S(2)}, u32[]{:S(2)}) collective-permute-start(bf16[64,64,128]{2,1,0:T(8,128)(2,1)S(1)} %all-to-all-done.6.blocks_ref), channel_id=1, source_target_pairs={{0,1},{1,0},{2,3},{3,2},{4,5},{5,4},{6,7},{7,6},{8,9},{9,8},{10,11... | collective-permute-start | bytes 3145736 | tf_op jit(solution)/shard_map/ppermute | solution.py:22
  184.6 2.0 copy-start
  186.8 2.2 %copy-start.1 = (bf16[16384,128]{1,0:T(8,128)(2,1)S(1)}, bf16[16384,128]{1,0:T(8,128)(2,1)}, u32[]{:S(2)}) copy-start(bf16[16384,128]{1,0:T(8,128)(2,1)} %copy-done) | copy-start | bytes 12582916
  189.0 2.5 %copy-start.6 = (bf16[16,2,64,128]{3,2,1,0:T(8,128)(2,1)S(1)}, bf16[16,2,64,128]{3,2,1,0:T(8,128)(2,1)}, u32[]{:S(2)}) copy-start(bf16[16,2,64,128]{3,2,1,0:T(8,128)(2,1)} %copy-done.5) | copy-start | bytes 1572868
  189.5 2.0 copy-start.9
  189.5 16.5 %copy-start.4 = (bf16[16,2,64,128]{3,2,1,0:T(8,128)(2,1)S(1)}, bf16[16,2,64,128]{3,2,1,0:T(8,128)(2,1)}, u32[]{:S(2)}) copy-start(bf16[16,2,64,128]{3,2,1,0:T(8,128)(2,1)} %copy-done.3) | copy-start | bytes 1572868
  192.5 11.4 %all-to-all-start.7 = ((bf16[16,64,128]{2,1,0:T(8,128)(2,1)}), bf16[16,64,128]{2,1,0:T(8,128)(2,1)S(1)}, u32[]{:S(2)}, u32[]{:S(2)}) async-start(bf16[16,64,128]{2,1,0:T(8,128)(2,1)} %broadcast_in_dim.55), calls=%async_computation.7 | async-start | bytes 524288 | tf_op jit(solution)/shard_map/all_to_all | solution.py:26
  204.0 2.6 %collective-permute-start.6 = (bf16[16,64,128]{2,1,0:T(8,128)(2,1)S(1)}, bf16[16,64,128]{2,1,0:T(8,128)(2,1)S(1)}, u32[]{:S(2)}, u32[]{:S(2)}) collective-permute-start(bf16[16,64,128]{2,1,0:T(8,128)(2,1)S(1)} %all-to-all-done.7), channel_id=1, source_target_pairs={{0,1},{1,0},{2,3},{3,2},{4,5},{5,4},{6,7},{7,6},{8,9},{9,8},{10,11... | collective-permute-start | bytes 786440 | tf_op jit(solution)/shard_map/ppermute | solution.py:22
  (3 other events, 2.8 us)

commit v3 on v2

v3 whole, which is shorter than its diff:
```python
import functools

import jax
import jax.numpy as jnp
from jax import lax
from jax.experimental import pallas as pl
from jax.experimental.pallas import tpu as pltpu
from jax.sharding import Mesh
from jax.sharding import PartitionSpec as P

F32 = jnp.float32
BF16 = jnp.bfloat16
ALL = ("y", "x", "z", "c")
PLANE = ("x", "z")
CUBE = ("y", "x", "z")
VMEM = pl.BlockSpec(memory_space=pltpu.VMEM)
SMEM = pl.BlockSpec(memory_space=pltpu.SMEM)
MIB = 1 << 20
SMALL = 4 * MIB


def swap(array):
    return lax.ppermute(array, "c", [(0, 1), (1, 0)])


def spread(copies, axes):
    return lax.all_to_all(copies, axes, 0, 0)


def in_core_order(own, other, axis):
    first = lax.axis_index("c") == 0
    return jnp.stack([jnp.where(first, own, other), jnp.where(first, other, own)], axis=axis)


def flat(gathered):
    return gathered.reshape(-1, gathered.shape[-1])


def dot(a, b):
    return jnp.dot(a, b, preferred_element_type=F32)


def rows_of(array, block, first, last):
    lead = array.ndim - 4
    start = (0,) * lead + (block, 0, 0, first)
    stop = (1,) * lead + (block + 1, 1, array.shape[-2], last)
    return lax.slice(array, start, stop).reshape(array.shape[-2], last - first)


def opening_kernel(rhs_ref, owner_ref, slot_ref, out_ref):
    row = lax.broadcasted_iota(jnp.int32, (8, 128), 0)
    marks = jnp.where(row == 0, owner_ref[...], jnp.where(row == 1, slot_ref[...], 0))
    marks = marks.astype(F32).astype(BF16)
    rows = rhs_ref.shape[3]
    for j in range(out_ref.shape[0]):
        out_ref[j, 0:rows] = rhs_ref[0, 0, 0]
        out_ref[j, rows : rows + 8] = marks


def opening(child_rhs, owner, slot, copies):
    rows, lanes = child_rhs.shape[3:]
    return pl.pallas_call(
        opening_kernel,
        out_shape=jax.ShapeDtypeStruct((copies, rows + 8, lanes), BF16),
        in_specs=[VMEM] * 3,
        out_specs=VMEM,
        compiler_params=pltpu.CompilerParams(vmem_limit_bytes=SMALL),
    )(child_rhs, owner, slot)


def pair_dot(blocks_ref, rights):
    count, half, lanes = blocks_ref.shape
    total = None
    for i in range(count // 2):
        left = jnp.concatenate([blocks_ref[2 * i], blocks_ref[2 * i + 1]], axis=1)
        term = rights(left, slice(i * 2 * lanes, (i + 1) * 2 * lanes))
        total = term if total is None else total + term
    return total


def product_kernel(number, subtract, core_ref, blocks_ref, *refs):
    matrices, outs = refs[: 2 * number], refs[2 * number :]
    if subtract:
        base_ref, outs = outs[0], outs[1:]
    lanes = blocks_ref.shape[2]
    rights = lambda left, columns: lax.dot_general(
        left,
        jnp.concatenate([m[:, columns] for m in matrices], axis=0),
        (((1,), (1,)), ((), ())),
        preferred_element_type=F32,
    )
    both = pair_dot(blocks_ref, rights)
    for n, out_ref in enumerate(outs):
        total = both[:, n * lanes : (n + 1) * lanes]
        total = jnp.where(core_ref[0] == 0, total, pltpu.roll(total, lanes // 2, 1))
        if n == 0:
            if subtract:
                total = base_ref[...] - total
            value = total.astype(BF16)
            for j in range(out_ref.shape[0]):
                out_ref[j] = value
        else:
            out_ref[...] = total.astype(BF16).astype(F32)


def product(core, blocks, matrices, base):
    count, half, lanes = blocks.shape
    number = len(matrices) // 2
    args = (core, blocks, *matrices) + (() if base is None else (base,))
    shapes = [jax.ShapeDtypeStruct((count, half, lanes), BF16)]
    shapes += [jax.ShapeDtypeStruct((half, lanes), F32)] * (number - 1)
    return pl.pallas_call(
        functools.partial(product_kernel, number, base is not None),
        out_shape=shapes,
        in_specs=[SMEM] + [VMEM] * (len(args) - 1),
        out_specs=[VMEM] * len(shapes),
        compiler_params=pltpu.CompilerParams(vmem_limit_bytes=SMALL),
        cost_estimate=pl.CostEstimate(
            flops=2 * number * count * half * lanes * lanes,
            bytes_accessed=(2 + 2 * number) * MIB,
            transcendentals=0,
        ),
    )(*args)


def build_kernel(index_ref, own_ref, other_ref, out_ref, sums_ref, turned_ref):
    width = out_ref.shape[1]
    half = width // 2

    def clear(i, carry):
        sums_ref[pl.ds(pl.multiple_of(i * 64, 64), 64), :] = jnp.zeros((64, width), F32)
        return carry

    lax.fori_loop(0, sums_ref.shape[0] // 64, clear, 0, unroll=4)

    for i in range(turned_ref.shape[0] // 128):
        rows = slice(i * 128, (i + 1) * 128)
        turned_ref[rows, 0:half] = own_ref[:, rows].astype(F32).T
        turned_ref[rows, half:width] = other_ref[:, rows].astype(F32).T

    def add(group, carry):
        base = pl.multiple_of(group * 8, 8)
        block = turned_ref[pl.ds(base, 8), :]
        for part in range(2):
            at = [index_ref[base + part * 4 + j] for j in range(4)]
            terms = [block[part * 4 + j : part * 4 + j + 1] for j in range(4)]
            old = [sums_ref[pl.ds(at[j], 1), :] for j in range(4)]
            for j in range(4):
                value = old[j] + terms[j]
                for m in range(j):
                    value = value + jnp.where(at[m] == at[j], terms[m], 0.0)
                sums_ref[pl.ds(at[j], 1), :] = value
        return carry

    lax.fori_loop(0, turned_ref.shape[0] // 8, add, 0, unroll=2)

    def settle(i, carry):
        rows = pl.ds(pl.multiple_of(i * 64, 64), 64)
        out_ref[rows, :] = sums_ref[rows, :].astype(BF16)
        return carry

    lax.fori_loop(0, sums_ref.shape[0] // 64, settle, 0, unroll=4)


def build_coupling(index, own, other, root_rows):
    rows, columns = own.shape
    return pl.pallas_call(
        build_kernel,
        out_shape=jax.ShapeDtypeStruct((root_rows, 2 * rows), BF16),
        in_specs=[SMEM, VMEM, VMEM],
        out_specs=VMEM,
        scratch_shapes=[
            pltpu.VMEM((root_rows, 2 * rows), F32),
            pltpu.VMEM((columns, 2 * rows), F32),
        ],
        compiler_params=pltpu.CompilerParams(vmem_limit_bytes=32 * MIB),
        cost_estimate=pl.CostEstimate(flops=0, bytes_accessed=40 * MIB, transcendentals=0),
    )(index, own, other)


def couple_kernel(x0_ref, x1_ref, matrix_ref, own_ref, other_ref):
    count, half, lanes = x0_ref.shape

    def product_with(blocks_ref, start):
        return pair_dot(
            blocks_ref,
            lambda left, columns: jnp.dot(
                left,
                matrix_ref[start + columns.start : start + columns.stop, :],
                preferred_element_type=F32,
            ),
        )

    total = product_with(x0_ref, 0) + product_with(x1_ref, count * lanes)
    own_ref[...] = total[:, : total.shape[1] // 2]
    other_ref[...] = total[:, total.shape[1] // 2 :]


def couple(x0, x1, matrix):
    count, half, lanes = x0.shape
    width = matrix.shape[1]
    return pl.pallas_call(
        couple_kernel,
        out_shape=[jax.ShapeDtypeStruct((half, width // 2), F32)] * 2,
        in_specs=[VMEM] * 3,
        out_specs=[VMEM] * 2,
        compiler_params=pltpu.CompilerParams(vmem_limit_bytes=SMALL),
        cost_estimate=pl.CostEstimate(
            flops=4 * count * half * lanes * width, bytes_accessed=10 * MIB, transcendentals=0
        ),
    )(x0, x1, matrix)


def settle_kernel(core_ref, mine_ref, theirs_ref, z0_ref, z1_ref, copies_ref, rest_ref):
    mine, theirs = mine_ref[...], theirs_ref[...]
    first = core_ref[0] == 0
    both = jnp.concatenate(
        [jnp.where(first, mine, theirs), jnp.where(first, theirs, mine)], axis=0
    ).T
    stripe = z0_ref.shape[0]
    rest_ref[...] = z0_ref[...] - both[:stripe]
    value = (z1_ref[...] - both[stripe:]).astype(BF16)
    for j in range(copies_ref.shape[0]):
        copies_ref[j] = value


def settle_coupling(core, mine, theirs, z0, z1, copies):
    return pl.pallas_call(
        settle_kernel,
        out_shape=[
            jax.ShapeDtypeStruct((copies,) + z1.shape, BF16),
            jax.ShapeDtypeStruct(z0.shape, F32),
        ],
        in_specs=[SMEM] + [VMEM] * 4,
        out_specs=[VMEM] * 2,
        compiler_params=pltpu.CompilerParams(vmem_limit_bytes=SMALL),
    )(core, mine, theirs, z0, z1)


def body(
    child_rhs,
    child_lower,
    child_inverse,
    child_upper,
    child_coupling,
    child_update,
    update_owner,
    update_slot,
    root_rhs,
    root_lower,
    root_inverse,
    root_upper,
):
    planes = lax.axis_size("x") * lax.axis_size("z")
    cubes = planes * lax.axis_size("y")
    devices = cubes * 2
    stripe, rhs = root_rhs.shape[2:]
    half = rhs // 2
    kc = child_inverse.shape[-1]
    kr = root_inverse.shape[-1]
    nc = child_lower.shape[-1]
    owner = update_owner[0, :, 0]
    slot = update_slot[0]
    held = owner.shape[0]
    me = lax.axis_index("c")
    core = me.astype(jnp.int32).reshape(1)

    tie = lax.optimization_barrier

    own_first = spread(opening(child_rhs, owner[None], slot[None], planes), PLANE)
    own = [
        rows_of(root_lower, 1, 0, kr),
        rows_of(root_inverse, 0, 0, kr),
        rows_of(root_inverse, 1, 0, kr),
        rows_of(root_upper, 0, kr, 2 * kr),
    ]
    own_first, own = tie((own_first, own))
    first = in_core_order(own_first, swap(own_first), 1)
    y0 = flat(first[:, :, :stripe])
    y1_own = (child_rhs[0, 1, 0].astype(F32) - dot(rows_of(child_lower, 1, 0, kc), y0)).astype(BF16)
    own_second = spread(jnp.broadcast_to(y1_own, (planes,) + y1_own.shape), PLANE)

    own, coupling, first = tie((own, child_coupling.reshape(2 * stripe, -1), first))
    lower, low_inverse, high_inverse, upper = [(m, swap(m)) for m in own]
    coupling_other = swap(coupling)
    turned = jnp.transpose(root_rhs[:, 0], (2, 0, 1)).reshape(2, half, 2, stripe)
    kept = jnp.where(me == 0, turned[0], turned[1])
    given = jnp.where(me == 0, turned[1], turned[0])
    right_base = in_core_order(kept, swap(given), 2).reshape(half, -1).astype(F32)
    z0c = dot(rows_of(child_inverse, 0, 0, kc), y0).astype(BF16).astype(F32)
    owners = first[:, :, stripe].astype(jnp.int32).reshape(-1)
    slots = first[:, :, stripe + 1].astype(jnp.int32).reshape(-1)
    index = slots // stripe * kr + owners * stripe + slots % stripe
    same = (owner[:, None] == owner[None, :]) & (
        jnp.arange(held)[None, :] < jnp.arange(held)[:, None]
    )
    rank = jnp.sum(same.astype(jnp.int32), axis=1)
    place = owner * 2 + rank
    select = (jnp.arange(devices * 2)[:, None] == place[None, :]).astype(BF16)
    target = slot // stripe * (2 * stripe) + owner % 2 * stripe + slot % stripe + 1
    target_lanes = jnp.where(jnp.arange(half)[None, :] == 0, target[:, None], 0).astype(BF16)
    update = child_update[0]
    part = dot(update[:, :kc], y0)
    own_second, z0c, index, select, target_lanes, part = tie(
        (own_second, z0c, index, select, target_lanes, part)
    )
    y1 = flat(in_core_order(own_second, swap(own_second), 1))
    contribution = (-(part + dot(update[:, kc:], y1))).astype(BF16)

    packed = [
        dot(
            select,
            jnp.concatenate([contribution[:, h * half : (h + 1) * half], target_lanes], axis=1),
        )
        .astype(BF16)
        .reshape(cubes, 1, 4, rhs)
        for h in range(2)
    ]
    arrived = spread(jnp.concatenate(packed, axis=1).reshape(devices, 4, rhs), ALL)
    z1c = dot(rows_of(child_inverse, 1, 0, kc), y1).astype(BF16).astype(F32)
    arrived, z1c, right_base, coupling_other, lower, low_inverse = tie(
        (arrived, z1c, right_base, coupling_other, lower, low_inverse)
    )
    arrived = arrived.reshape(devices * 4, rhs)
    lands = (
        arrived[:, half : half + 1].astype(jnp.int32)
        == jnp.arange(1, 4 * stripe + 1)[None, :]
    ).astype(BF16)
    received = lax.dot_general(
        arrived, lands, (((0,), (0,)), ((), ())), preferred_element_type=F32
    )[:half]
    right = right_base + received

    r0_own = right[:, : 2 * stripe].astype(BF16)
    r0 = spread(jnp.broadcast_to(r0_own, (cubes,) + r0_own.shape), CUBE)
    summed = build_coupling(index, coupling, coupling_other, 2 * kr)
    r0, summed, high_inverse, upper = tie((r0, summed, high_inverse, upper))
    r1_copies, z0_own = product(core, r0, lower + low_inverse, right[:, 2 * stripe :])
    r1 = spread(r1_copies, CUBE)
    (x1_copies,) = product(core, r1, high_inverse, None)
    x1 = spread(x1_copies, CUBE)
    (x0_copies,) = product(core, x1, upper, z0_own)
    x0 = spread(x0_copies, CUBE)

    x0, x0_copies, x1_copies = tie((x0, x0_copies, x1_copies))
    mine, given = couple(x0, x1, summed)
    c1_copies, rest = settle_coupling(core, mine, swap(given), z0c, z1c, planes)
    c1_copies, x0_own, x1_own = tie((c1_copies, x0_copies[0], x1_copies[0]))
    own_c1 = spread(c1_copies, PLANE)

    def own_rows(half_rows):
        pair = in_core_order(half_rows, swap(half_rows), 0).reshape(rhs, 2 * stripe)
        rows = pair.T
        return jnp.where(me == 0, rows[:stripe], rows[stripe:])

    root_solution = jnp.stack([own_rows(x0_own), own_rows(x1_own)])[:, None]
    own_c1, root_solution = tie((own_c1, root_solution))
    c1 = flat(in_core_order(own_c1, swap(own_c1), 1))
    c0_own = (rest - dot(rows_of(child_upper, 0, kc, nc), c1)).astype(BF16)
    child_solution = jnp.stack([c0_own, c1_copies[0]])[None, :, None]
    return child_solution, root_solution


def solution(mesh):
    leaf, front = mesh.devices.shape
    fine = Mesh(mesh.devices.reshape((leaf, 4, front // 8, 2)), ALL)
    subtree = P("y", None, ("x", "z", "c"), None, None)
    ancestor = P(None, ALL, None, None)
    in_specs = (
        subtree,
        subtree,
        subtree,
        subtree,
        subtree,
        P("y", ("x", "z", "c"), None),
        P("y", ("x", "z", "c"), None),
        P("y", ("x", "z", "c")),
        ancestor,
        ancestor,
        ancestor,
        ancestor,
    )
    return jax.shard_map(
        body, mesh=fine, in_specs=in_specs, out_specs=(subtree, ancestor), check_vma=False
    )
```

time: 210 us -> 205 us (0.976)
  waiting for transfers between devices: 75.7 us -> 25.5 us
  blocking collectives: 21.2 us -> 69.7 us
  starting transfers between devices: 52.4 us -> 37.9 us
  local copies, waits for them, and re-layouts: 16.5 us -> 21.2 us
  matrix products: 4.29 us -> 7.57 us
  Pallas kernels: 28.8 us -> 31.3 us
    all_to_all x1 -> x3, blocking collectives: 21.2 us -> 69.7 us  [spread(): return lax.all_to_all(copies, axes, 0, 0)]
    all_to_all x7 -> x5, waiting for transfers between devices: 69.2 us -> 23.3 us  [spread(): return lax.all_to_all(copies, axes, 0, 0)]
    all_to_all x7 -> x5, starting transfers between devices: 40.5 us -> 26.5 us  [spread(): return lax.all_to_all(copies, axes, 0, 0)]
    ppermute x7 -> x12, waiting for transfers between devices: 6.5 us -> 2.19 us  [swap(): return lax.ppermute(array, 'c', [(0, 1), (1, 0)])]
    reshape x2 -> x4, local copies, waits for them, and re-layouts: 0.93 us -> 4.66 us  [the longest x2 4.44 us: rows_of(): return lax.slice(array, start, stop).reshape(array.shape[-2], last - first)]
    another operation x3, other arithmetic: 3.62 us -> 0.02 us  [the longest x2 0.02 us: body(): root_solution = jnp.stack([own_rows(x0_own), own_rows(x1_own)])[:, None]]
    another operation x4 -> x0, local copies, waits for them, and re-layouts: 3.53 us -> none  [the longest x2 3.36 us: body(): jnp.stack([rows_of(root_lower, 1, 0, kr), rows_of(root_inverse, 1, 0, kr)...]
    convert_element_type x2, local copies, waits for them, and re-layouts: 0.27 us -> 3.35 us  [body(): in_core_order(kept, swap(given), 2).reshape(half, -1).astype(F32)]
  transfers between devices with their start and end apart: 14 -> 17, of which waited for: 9 -> 7; matrix products, arithmetic and copies ran while one was open for 8% -> 13% of each run, Pallas kernels for 8% -> 10%
where the time goes in v3:
time: 205 us; the launch traced here: 204 us
  blocking collectives  69.7 us (34%)
  starting transfers between devices  37.9 us (18%)
  Pallas kernels  31.3 us (15%)
  waiting for transfers between devices  25.5 us (12%)
  local copies, waits for them, and re-layouts  21.2 us (10%)
  other arithmetic  9.87 us (5%)
  matrix products  7.57 us (4%)
    all_to_all x3, blocking collectives, spread(): return lax.all_to_all(copies, axes, 0, 0)  69.7 us
    all_to_all x5, starting transfers between devices, spread(): return lax.all_to_all(copies, axes, 0, 0)  26.5 us
    all_to_all x5, waiting for transfers between devices, spread(): return lax.all_to_all(copies, axes, 0, 0)  23.3 us
    pallas_call x1, Pallas kernels, build_coupling(): pl.pallas_call(build_kernel, out_shape=jax.ShapeDtypeStruct((root_rows, 2...  20 us
    ppermute x12, starting transfers between devices, swap(): return lax.ppermute(array, 'c', [(0, 1), (1, 0)])  11.3 us
    unnamed x28, local copies, waits for them, and re-layouts  8.61 us
    pallas_call x3, Pallas kernels, product(): pl.pallas_call(functools.partial(product_kernel, number, base is not None...  8.16 us
    dot_general x8, matrix products, dot(): return jnp.dot(a, b, preferred_element_type=F32)  6.6 us
  transfers between devices with their start and end apart: 17, of which 7 were waited for; matrix products, arithmetic and copies ran while one was open for 13% of the time, Pallas kernels for 10%

profile of v3, /device:TPU:1, one launch (start us, length us, event | category | flops | bytes accessed | tf_op | source)
XLA Modules:
  0.0 204.0 jit_solution(3544727193256187890)
XLA Ops:
  6.4 7.7 %all-to-all-start = ((bf16[16,72,128]{2,1,0:T(8,128)(2,1)}), bf16[16,72,128]{2,1,0:T(8,128)(2,1)S(1)}, u32[]{:S(2)}, u32[]{:S(2)}) async-start(bf16[16,72,128]{2,1,0:T(8,128)(2,1)} %shard_map.131), calls=%async_computation | async-start | bytes 589824 | tf_op jit(solution)/shard_map/all_to_all | solution.py:27
  16.1 3.1 %slice_bitcast_fusion.1 = (bf16[64,8192]{1,0:T(8,128)(2,1)S(1)}, bf16[64,8192]{1,0:T(8,128)(2,1)}, bf16[64,8192]{1,0:T(8,128)(2,1)S(1)}) fusion(bf16[2,1,64,8192]{3,2,1,0:T(8,128)(2,1)} %param.22, bf16[2,1,64,16384]{3,2,1,0:T(8,128)(2,1)} %param.23), kind=kLoop, calls=%fused_computation.18 | loop fusion | bytes 6291456 | tf_op jit(solution)/shard_map/reshape | solution.py:47
  19.4 2.9 %all-to-all-done = bf16[16,72,128]{2,1,0:T(8,128)(2,1)S(1)} async-done(((bf16[16,72,128]{2,1,0:T(8,128)(2,1)}), bf16[16,72,128]{2,1,0:T(8,128)(2,1)S(1)}, u32[]{:S(2)}, u32[]{:S(2)}) %all-to-all-start) | async-done | bytes 294944 | tf_op jit(solution)/shard_map/all_to_all | solution.py:27
  22.2 1.7 collective-permute-start
  29.3 3.5 %all-to-all-start.1 = ((bf16[16,64,128]{2,1,0:T(8,128)(2,1)}), bf16[16,64,128]{2,1,0:T(8,128)(2,1)S(1)}, u32[]{:S(2)}, u32[]{:S(2)}) async-start(bf16[16,64,128]{2,1,0:T(8,128)(2,1)} %broadcast_in_dim.39), calls=%async_computation.1 | async-start | bytes 524288 | tf_op jit(solution)/shard_map/all_to_all | solution.py:27
  34.5 6.1 %all-to-all-done.1 = bf16[16,64,128]{2,1,0:T(8,128)(2,1)S(1)} async-done(((bf16[16,64,128]{2,1,0:T(8,128)(2,1)}), bf16[16,64,128]{2,1,0:T(8,128)(2,1)S(1)}, u32[]{:S(2)}, u32[]{:S(2)}) %all-to-all-start.1) | async-done | bytes 262176 | tf_op jit(solution)/shard_map/all_to_all | solution.py:27
  40.6 1.7 collective-permute-start.1
  43.9 1.7 copy.77
  45.5 1.7 reshape.194
  53.1 6.3 %all-to-all-start.2 = ((bf16[128,4,128]{2,1,0:T(4,128)(2,1)}), bf16[128,4,128]{2,1,0:T(4,128)(2,1)S(1)}, u32[]{:S(2)}, u32[]{:S(2)}) async-start(bf16[128,4,128]{2,1,0:T(4,128)(2,1)} %copy.76), calls=%async_computation.2 | async-start | bytes 262144 | tf_op jit(solution)/shard_map/all_to_all | solution.py:27
  60.8 8.5 %all-to-all-done.2 = bf16[128,4,128]{2,1,0:T(4,128)(2,1)S(1)} async-done(((bf16[128,4,128]{2,1,0:T(4,128)(2,1)}), bf16[128,4,128]{2,1,0:T(4,128)(2,1)S(1)}, u32[]{:S(2)}, u32[]{:S(2)}) %all-to-all-start.2) | async-done | bytes 131104 | tf_op jit(solution)/shard_map/all_to_all | solution.py:27
  71.8 5.5 %all-to-all-start.3 = ((bf16[64,64,128]{2,1,0:T(8,128)(2,1)}), bf16[64,64,128]{2,1,0:T(8,128)(2,1)}, u32[]{:S(2)}, u32[]{:S(2)}) async-start(bf16[64,64,128]{2,1,0:T(8,128)(2,1)} %broadcast_in_dim.43), calls=%async_computation.3 | async-start | bytes 2097152 | tf_op jit(solution)/shard_map/all_to_all | solution.py:27
  78.5 20.0 %shard_map.132.matrix_ref = bf16[16384,256]{1,0:T(8,128)(2,1)S(1)} custom-call(s32[4096]{0:T(1024)S(1)} %fusion.31.index_ref, bf16[128,4096]{1,0:T(8,128)(2,1)S(1)} %bitcast.135, bf16[128,4096]{1,0:T(8,128)(2,1)} %collective-permute-done.3.other_ref), custom_call_target="tpu_custom_call" | custom-call | bytes 41943040 | tf_op jit(solution)/shard_map/pallas_call | solution.py:167
  98.5 3.3 %copy-done = bf16[16384,256]{1,0:T(8,128)(2,1)} copy-done((bf16[16384,256]{1,0:T(8,128)(2,1)}, bf16[16384,256]{1,0:T(8,128)(2,1)S(1)}, u32[]{:S(2)}) %copy-start) | copy-done | bytes 8388632
  103.1 3.6 %shard_map.133 = (bf16[64,64,128]{2,1,0:T(8,128)(2,1)S(1)}, f32[64,128]{1,0:T(8,128)S(1)}) custom-call(s32[1]{0:T(128)} %bitcast.core_ref, bf16[64,64,128]{2,1,0:T(8,128)(2,1)} %all-to-all-done.3.blocks_ref, bf16[64,8192]{1,0:T(8,128)(2,1)S(1)} %slice_bitcast_fusion.3.refs_0_, bf16[64,8192]{1,0:T(8,128)(2,1)} %collective-permute-done.4.refs_1_, ...), custom_call_target="tpu_custom_call" | custom-call | flops 268435456 | bytes 6291456 | tf_op jit(solution)/shard_map/pallas_call | solution.py:112
  106.6 26.2 %all_to_all.40.blocks_ref = bf16[64,64,128]{2,1,0:T(8,128)(2,1)S(1)} all-to-all(bf16[64,64,128]{2,1,0:T(8,128)(2,1)S(1)} %get-tuple-element.71), channel_id=1, replica_groups=mesh['y'=4,'x'=4,'z'=4,'c'=2] {'y','x','z'}, dimensions={0} | all-to-all | bytes 2097152 | tf_op jit(solution)/shard_map/all_to_all | solution.py:27
  132.9 2.4 %shard_map.134 = bf16[64,64,128]{2,1,0:T(8,128)(2,1)S(1)} custom-call(s32[1]{0:T(128)} %bitcast.core_ref, bf16[64,64,128]{2,1,0:T(8,128)(2,1)S(1)} %all_to_all.40.blocks_ref, bf16[64,8192]{1,0:T(8,128)(2,1)S(1)} %get-tuple-element.72.refs_0_, bf16[64,8192]{1,0:T(8,128)(2,1)} %collective-permute-done.6.refs_1_), custom_call_target="tpu_custom_call" | custom-call | flops 134217728 | bytes 4194304 | tf_op jit(solution)/shard_map/pallas_call | solution.py:112
  135.2 21.5 %all_to_all.41.blocks_ref.x1_ref = bf16[64,64,128]{2,1,0:T(8,128)(2,1)S(1)} all-to-all(bf16[64,64,128]{2,1,0:T(8,128)(2,1)S(1)} %shard_map.134), channel_id=1, replica_groups=mesh['y'=4,'x'=4,'z'=4,'c'=2] {'y','x','z'}, dimensions={0} | all-to-all | bytes 2097152 | tf_op jit(solution)/shard_map/all_to_all | solution.py:27
  156.7 2.2 %shard_map.135 = bf16[64,64,128]{2,1,0:T(8,128)(2,1)S(1)} custom-call(s32[1]{0:T(128)} %bitcast.core_ref, bf16[64,64,128]{2,1,0:T(8,128)(2,1)S(1)} %all_to_all.41.blocks_ref.x1_ref, bf16[64,8192]{1,0:T(8,128)(2,1)S(1)} %get-tuple-element.74.refs_0_, bf16[64,8192]{1,0:T(8,128)(2,1)} %collective-permute-done.7.refs_1_, f32[64,128]{1,0:T(8,128)S(1)} %get-tuple-element.76.refs_2_), custom_call_target="tpu_custom_call" | custom-call | flops 134217728 | bytes 4194304 | tf_op jit(solution)/shard_map/pallas_call | solution.py:112
  159.0 21.9 %all_to_all.42.x0_ref = bf16[64,64,128]{2,1,0:T(8,128)(2,1)S(1)} all-to-all(bf16[64,64,128]{2,1,0:T(8,128)(2,1)S(1)} %shard_map.135), channel_id=1, replica_groups=mesh['y'=4,'x'=4,'z'=4,'c'=2] {'y','x','z'}, dimensions={0} | all-to-all | bytes 2097152 | tf_op jit(solution)/shard_map/all_to_all | solution.py:27
  180.9 1.6 shard_map.136
  182.5 3.4 %collective-permute-start.8 = (f32[64,128]{1,0:T(8,128)S(1)}, f32[64,128]{1,0:T(8,128)S(1)}, u32[]{:S(2)}, u32[]{:S(2)}) collective-permute-start(f32[64,128]{1,0:T(8,128)S(1)} %get-tuple-element.80), channel_id=1, source_target_pairs={{0,1},{1,0},{2,3},{3,2},{4,5},{5,4},{6,7},{7,6},{8,9},{9,8},{10,11... | collective-permute-start | bytes 98312 | tf_op jit(solution)/shard_map/ppermute | solution.py:23
  188.0 3.5 %all-to-all-start.7 = ((bf16[16,64,128]{2,1,0:T(8,128)(2,1)}), bf16[16,64,128]{2,1,0:T(8,128)(2,1)S(1)}, u32[]{:S(2)}, u32[]{:S(2)}) async-start(bf16[16,64,128]{2,1,0:T(8,128)(2,1)} %get-tuple-element.87), calls=%async_computation.7 | async-start | bytes 524288 | tf_op jit(solution)/shard_map/all_to_all | solution.py:27
  193.5 5.9 %all-to-all-done.7 = bf16[16,64,128]{2,1,0:T(8,128)(2,1)S(1)} async-done(((bf16[16,64,128]{2,1,0:T(8,128)(2,1)}), bf16[16,64,128]{2,1,0:T(8,128)(2,1)S(1)}, u32[]{:S(2)}, u32[]{:S(2)}) %all-to-all-start.7) | async-done | bytes 262176 | tf_op jit(solution)/shard_map/all_to_all | solution.py:27
  (111 shorter events, 37.2 us)
Async XLA Ops:
  2.2 40.1 %collective-permute-start.2 = (bf16[64,2,64]{0,2,1:T(8,128)(2,1)}, bf16[64,2,64]{0,2,1:T(8,128)(2,1)}, u32[]{:S(2)}, u32[]{:S(2)}) collective-permute-start(bf16[64,2,64]{0,2,1:T(8,128)(2,1)} %broadcast_select_fusion), channel_id=1, source_target_pairs={{0,1},{1,0},{2,3},{3,2},{4,5},{5,4},{6,7},{7,6},{8,9},{9,8},{10,11... | collective-permute-start | bytes 49160 | tf_op jit(solution)/shard_map/ppermute | solution.py:23
  6.4 15.8 %all-to-all-start = ((bf16[16,72,128]{2,1,0:T(8,128)(2,1)}), bf16[16,72,128]{2,1,0:T(8,128)(2,1)S(1)}, u32[]{:S(2)}, u32[]{:S(2)}) async-start(bf16[16,72,128]{2,1,0:T(8,128)(2,1)} %shard_map.131), calls=%async_computation | async-start | bytes 589824 | tf_op jit(solution)/shard_map/all_to_all | solution.py:27
  16.1 10.0 %copy-start.4 = (bf16[1,2,1,64,128]{4,3,2,1,0:T(8,128)(2,1)S(1)}, bf16[1,2,1,64,128]{4,3,2,1,0:T(8,128)(2,1)}, u32[]{:S(2)}) copy-start(bf16[1,2,1,64,128]{4,3,2,1,0:T(8,128)(2,1)} %rhs_ref.1) | copy-start | bytes 98308
  22.2 5.1 %copy-start.10 = (bf16[1,2,1,64,2048]{4,3,2,1,0:T(8,128)(2,1)S(1)}, bf16[1,2,1,64,2048]{4,3,2,1,0:T(8,128)(2,1)}, u32[]{:S(2)}) copy-start(bf16[1,2,1,64,2048]{4,3,2,1,0:T(8,128)(2,1)} %param.14) | copy-start | bytes 1572868
  22.2 5.4 %copy-start.8 = (bf16[1,128,4096]{2,1,0:T(8,128)(2,1)S(1)}, bf16[1,128,4096]{2,1,0:T(8,128)(2,1)}, u32[]{:S(2)}) copy-start(bf16[1,128,4096]{2,1,0:T(8,128)(2,1)} %param.17) | copy-start | bytes 3145732
  22.2 3.0 %collective-permute-start = (bf16[16,72,128]{2,1,0:T(8,128)(2,1)S(1)}, bf16[16,72,128]{2,1,0:T(8,128)(2,1)S(1)}, u32[]{:S(2)}, u32[]{:S(2)}) collective-permute-start(bf16[16,72,128]{2,1,0:T(8,128)(2,1)S(1)} %all-to-all-done), channel_id=1, source_target_pairs={{0,1},{1,0},{2,3},{3,2},{4,5},{5,4},{6,7},{7,6},{8,9},{9,8},{10,11... | collective-permute-start | bytes 884744 | tf_op jit(solution)/shard_map/ppermute | solution.py:23
  29.3 11.3 %all-to-all-start.1 = ((bf16[16,64,128]{2,1,0:T(8,128)(2,1)}), bf16[16,64,128]{2,1,0:T(8,128)(2,1)S(1)}, u32[]{:S(2)}, u32[]{:S(2)}) async-start(bf16[16,64,128]{2,1,0:T(8,128)(2,1)} %broadcast_in_dim.39), calls=%async_computation.1 | async-start | bytes 524288 | tf_op jit(solution)/shard_map/all_to_all | solution.py:27
  40.6 7.7 %collective-permute-start.1 = (bf16[16,64,128]{2,1,0:T(8,128)(2,1)S(1)}, bf16[16,64,128]{2,1,0:T(8,128)(2,1)}, u32[]{:S(2)}, u32[]{:S(2)}) collective-permute-start(bf16[16,64,128]{2,1,0:T(8,128)(2,1)S(1)} %all-to-all-done.1), channel_id=1, source_target_pairs={{0,1},{1,0},{2,3},{3,2},{4,5},{5,4},{6,7},{7,6},{8,9},{9,8},{10,11... | collective-permute-start | bytes 786440 | tf_op jit(solution)/shard_map/ppermute | solution.py:23
  47.2 22.0 %collective-permute-start.3 = (bf16[128,4096]{1,0:T(8,128)(2,1)}, bf16[128,4096]{1,0:T(8,128)(2,1)}, u32[]{:S(2)}, u32[]{:S(2)}) collective-permute-start(bf16[128,4096]{1,0:T(8,128)(2,1)} %bitcast.134), channel_id=1, source_target_pairs={{0,1},{1,0},{2,3},{3,2},{4,5},{5,4},{6,7},{7,6},{8,9},{9,8},{10,11... | collective-permute-start | bytes 3145736 | tf_op jit(solution)/shard_map/ppermute | solution.py:23
  47.2 22.0 %collective-permute-start.4 = (bf16[64,8192]{1,0:T(8,128)(2,1)S(1)}, bf16[64,8192]{1,0:T(8,128)(2,1)}, u32[]{:S(2)}, u32[]{:S(2)}) collective-permute-start(bf16[64,8192]{1,0:T(8,128)(2,1)S(1)} %slice_bitcast_fusion.3.refs_0_), channel_id=1, source_target_pairs={{0,1},{1,0},{2,3},{3,2},{4,5},{5,4},{6,7},{7,6},{8,9},{9,8},{10,11... | collective-permute-start | bytes 3145736 | tf_op jit(solution)/shard_map/ppermute | solution.py:23
  47.7 21.5 %collective-permute-start.5 = (bf16[64,8192]{1,0:T(8,128)(2,1)}, bf16[64,8192]{1,0:T(8,128)(2,1)}, u32[]{:S(2)}, u32[]{:S(2)}) collective-permute-start(bf16[64,8192]{1,0:T(8,128)(2,1)} %get-tuple-element.69.refs_2_), channel_id=1, source_target_pairs={{0,1},{1,0},{2,3},{3,2},{4,5},{5,4},{6,7},{7,6},{8,9},{9,8},{10,11... | collective-permute-start | bytes 3145736 | tf_op jit(solution)/shard_map/ppermute | solution.py:23
  47.7 54.1 %collective-permute-start.6 = (bf16[64,8192]{1,0:T(8,128)(2,1)S(1)}, bf16[64,8192]{1,0:T(8,128)(2,1)}, u32[]{:S(2)}, u32[]{:S(2)}) collective-permute-start(bf16[64,8192]{1,0:T(8,128)(2,1)S(1)} %get-tuple-element.72.refs_0_), channel_id=1, source_target_pairs={{0,1},{1,0},{2,3},{3,2},{4,5},{5,4},{6,7},{7,6},{8,9},{9,8},{10,11... | collective-permute-start | bytes 3145736 | tf_op jit(solution)/shard_map/ppermute | solution.py:23
  48.2 53.6 %collective-permute-start.7 = (bf16[64,8192]{1,0:T(8,128)(2,1)S(1)}, bf16[64,8192]{1,0:T(8,128)(2,1)}, u32[]{:S(2)}, u32[]{:S(2)}) collective-permute-start(bf16[64,8192]{1,0:T(8,128)(2,1)S(1)} %get-tuple-element.74.refs_0_), channel_id=1, source_target_pairs={{0,1},{1,0},{2,3},{3,2},{4,5},{5,4},{6,7},{7,6},{8,9},{9,8},{10,11... | collective-permute-start | bytes 3145736 | tf_op jit(solution)/shard_map/ppermute | solution.py:23
  49.2 21.2 %copy-start.11 = (f32[64,256]{1,0:T(8,128)S(1)}, f32[64,256]{1,0:T(8,128)}, u32[]{:S(2)}) copy-start(f32[64,256]{1,0:T(8,128)} %reshape.194) | copy-start | bytes 196612
  53.1 16.1 %all-to-all-start.2 = ((bf16[128,4,128]{2,1,0:T(4,128)(2,1)}), bf16[128,4,128]{2,1,0:T(4,128)(2,1)S(1)}, u32[]{:S(2)}, u32[]{:S(2)}) async-start(bf16[128,4,128]{2,1,0:T(4,128)(2,1)} %copy.76), calls=%async_computation.2 | async-start | bytes 262144 | tf_op jit(solution)/shard_map/all_to_all | solution.py:27
  71.8 30.0 %all-to-all-start.3 = ((bf16[64,64,128]{2,1,0:T(8,128)(2,1)}), bf16[64,64,128]{2,1,0:T(8,128)(2,1)}, u32[]{:S(2)}, u32[]{:S(2)}) async-start(bf16[64,64,128]{2,1,0:T(8,128)(2,1)} %broadcast_in_dim.43), calls=%async_computation.3 | async-start | bytes 2097152 | tf_op jit(solution)/shard_map/all_to_all | solution.py:27
  98.5 3.3 %copy-start = (bf16[16384,256]{1,0:T(8,128)(2,1)}, bf16[16384,256]{1,0:T(8,128)(2,1)S(1)}, u32[]{:S(2)}) copy-start(bf16[16384,256]{1,0:T(8,128)(2,1)S(1)} %shard_map.132.matrix_ref) | copy-start | bytes 25165828
  103.1 77.8 %slice-start = ((s8[8388608]{0:T(1024)(128)(4,1)}), s8[4194304]{0:T(1024)(128)(4,1)S(1)}, s32[]{:S(2)}) async-start(s8[8388608]{0:T(1024)(128)(4,1)} %bitcast.132), calls=%async_computation.8 | async-start | bytes 8388608
  132.9 48.0 %slice-start.1 = ((s8[8388608]{0:T(1024)(128)(4,1)}), s8[4194304]{0:T(1024)(128)(4,1)S(1)}, s32[]{:S(2)}) async-start(s8[8388608]{0:T(1024)(128)(4,1)} %bitcast.132), calls=%async_computation.9 | async-start | bytes 8388608
  182.5 4.3 %collective-permute-start.8 = (f32[64,128]{1,0:T(8,128)S(1)}, f32[64,128]{1,0:T(8,128)S(1)}, u32[]{:S(2)}, u32[]{:S(2)}) collective-permute-start(f32[64,128]{1,0:T(8,128)S(1)} %get-tuple-element.80), channel_id=1, source_target_pairs={{0,1},{1,0},{2,3},{3,2},{4,5},{5,4},{6,7},{7,6},{8,9},{9,8},{10,11... | collective-permute-start | bytes 98312 | tf_op jit(solution)/shard_map/ppermute | solution.py:23
  187.6 4.1 %collective-permute-start.9 = (bf16[64,128]{1,0:T(8,128)(2,1)S(1)}, bf16[64,128]{1,0:T(8,128)(2,1)S(1)}, u32[]{:S(2)}, u32[]{:S(2)}) collective-permute-start(bf16[64,128]{1,0:T(8,128)(2,1)S(1)} %slice_bitcast_fusion.5), channel_id=1, source_target_pairs={{0,1},{1,0},{2,3},{3,2},{4,5},{5,4},{6,7},{7,6},{8,9},{9,8},{10,11... | collective-permute-start | bytes 49160 | tf_op jit(solution)/shard_map/ppermute | solution.py:23
  188.0 11.4 %all-to-all-start.7 = ((bf16[16,64,128]{2,1,0:T(8,128)(2,1)}), bf16[16,64,128]{2,1,0:T(8,128)(2,1)S(1)}, u32[]{:S(2)}, u32[]{:S(2)}) async-start(bf16[16,64,128]{2,1,0:T(8,128)(2,1)} %get-tuple-element.87), calls=%async_computation.7 | async-start | bytes 524288 | tf_op jit(solution)/shard_map/all_to_all | solution.py:27
  191.5 1.3 collective-permute-start.10
  199.4 2.7 %collective-permute-start.11 = (bf16[16,64,128]{2,1,0:T(8,128)(2,1)S(1)}, bf16[16,64,128]{2,1,0:T(8,128)(2,1)S(1)}, u32[]{:S(2)}, u32[]{:S(2)}) collective-permute-start(bf16[16,64,128]{2,1,0:T(8,128)(2,1)S(1)} %all-to-all-done.7), channel_id=1, source_target_pairs={{0,1},{1,0},{2,3},{3,2},{4,5},{5,4},{6,7},{7,6},{8,9},{9,8},{10,11... | collective-permute-start | bytes 786440 | tf_op jit(solution)/shard_map/ppermute | solution.py:23
  (7 other events, 8.5 us)

commit v4 on v1

v4 whole, which is shorter than its diff:
```python
import functools

import jax
import jax.numpy as jnp
from jax import lax
from jax.experimental import pallas as pl
from jax.experimental.pallas import tpu as pltpu
from jax.sharding import Mesh
from jax.sharding import PartitionSpec as P

F32 = jnp.float32
BF16 = jnp.bfloat16
ALL = ("y", "x", "z", "c")
PLANE = ("x", "z")
CUBE = ("y", "x", "z")
VMEM = pl.BlockSpec(memory_space=pltpu.VMEM)
SMEM = pl.BlockSpec(memory_space=pltpu.SMEM)
HBM = pl.BlockSpec(memory_space=pltpu.HBM)
DMA = pltpu.SemaphoreType.DMA
MIB = 1 << 20
tie = lax.optimization_barrier


def swap(array):
    return lax.ppermute(array, "c", [(0, 1), (1, 0)])


def spread(copies, axes):
    return lax.all_to_all(copies, axes, 0, 0)


def in_core_order(own, other, axis):
    first = lax.axis_index("c") == 0
    return jnp.stack([jnp.where(first, own, other), jnp.where(first, other, own)], axis=axis)


def rows_of(array, block, first, last):
    lead = array.ndim - 4
    start = (0,) * lead + (block, 0, 0, first)
    stop = (1,) * lead + (block + 1, 1, array.shape[-2], last)
    return lax.slice(array, start, stop).reshape(array.shape[-2], last - first)


def like(shape, dtype=BF16):
    return jax.ShapeDtypeStruct(shape, dtype)


def kernel_call(body, args, specs, shapes, out_specs, scratch=(), limit=None, flops=0, moved=0):
    return pl.pallas_call(
        body,
        out_shape=shapes,
        in_specs=specs,
        out_specs=out_specs,
        scratch_shapes=list(scratch),
        compiler_params=pltpu.CompilerParams(
            vmem_limit_bytes=None if limit is None else limit * MIB
        ),
        cost_estimate=pl.CostEstimate(flops=flops, bytes_accessed=moved, transcendentals=0),
    )(*args)


def by_core(core_ref, own_refs, other_refs, work):
    @pl.when(core_ref[0] == 0)
    def _():
        work(own_refs, other_refs)

    @pl.when(core_ref[0] != 0)
    def _():
        work(other_refs, own_refs)


def plane_dot(matrix_ref, first_ref, second_ref, rows):
    total = None
    for p in range(first_ref.shape[0] // 2):
        block = jnp.concatenate(
            [
                first_ref[2 * p, 0:rows],
                second_ref[2 * p, 0:rows],
                first_ref[2 * p + 1, 0:rows],
                second_ref[2 * p + 1, 0:rows],
            ],
            axis=0,
        )
        term = jnp.dot(
            matrix_ref[:, p * 4 * rows : (p + 1) * 4 * rows], block, preferred_element_type=F32
        )
        total = term if total is None else total + term
    return total


def opening_kernel(rhs_ref, owner_ref, slot_ref, out_ref):
    row = lax.broadcasted_iota(jnp.int32, (8, 128), 0)
    marks = jnp.where(row == 0, owner_ref[...], jnp.where(row == 1, slot_ref[...], 0))
    marks = marks.astype(F32).astype(BF16)
    rows = rhs_ref.shape[3]
    for j in range(out_ref.shape[0]):
        out_ref[j, 0:rows] = rhs_ref[0, 0, 0]
        out_ref[j, rows : rows + 8] = marks


def turn_kernel(core_ref, rhs_ref, lower_ref, kept_ref, given_ref, low_ref, sem):
    copy = pltpu.make_async_copy(
        lower_ref.at[0, 1, 0, :, pl.ds(0, low_ref.shape[1])], low_ref, sem
    )
    copy.start()
    both = jnp.concatenate(
        [rhs_ref[0, 0].astype(F32).T, rhs_ref[1, 0].astype(F32).T], axis=1
    ).astype(BF16)
    half = both.shape[0] // 2

    @pl.when(core_ref[0] == 0)
    def _():
        kept_ref[...] = both[:half]
        given_ref[...] = both[half:]

    @pl.when(core_ref[0] != 0)
    def _():
        kept_ref[...] = both[half:]
        given_ref[...] = both[:half]

    copy.wait()


def advance_kernel(core_ref, own_ref, other_ref, low_ref, rhs_ref, out_ref):
    rows = out_ref.shape[1]

    def work(first, second):
        total = rhs_ref[0, 1, 0].astype(F32) - plane_dot(low_ref, first, second, rows)
        value = total.astype(BF16)
        for j in range(out_ref.shape[0]):
            out_ref[j] = value

    by_core(core_ref, own_ref, other_ref, work)


def aside_kernel(
    rows, kr, core_ref, own_ref, other_ref, update_ref, inverse_ref,
    part_ref, z0_ref, index_ref, low_ref, diag_ref, sems
):
    kc = low_ref.shape[1]
    copies = [
        pltpu.make_async_copy(update_ref.at[0, :, pl.ds(0, kc)], low_ref, sems.at[0]),
        pltpu.make_async_copy(inverse_ref.at[0, 0, 0], diag_ref, sems.at[1]),
    ]
    for copy in copies:
        copy.start()

    def work(first, second):
        for j in range(own_ref.shape[0]):
            for c, source in enumerate((first, second)):
                marks = source[j, rows : rows + 8].astype(F32).astype(jnp.int32)
                owner, slot = marks[0:1], marks[1:2]
                index_ref[2 * j + c : 2 * j + c + 1, :] = (
                    (slot // rows) * kr + owner * rows + slot % rows
                )
        copies[0].wait()
        part_ref[...] = plane_dot(low_ref, first, second, rows)
        copies[1].wait()
        z0_ref[...] = plane_dot(diag_ref, first, second, rows).astype(BF16).astype(F32)

    by_core(core_ref, own_ref, other_ref, work)


def contribute_kernel(
    core_ref, own_ref, other_ref, update_ref, part_ref, owner_ref, slot_ref, out_ref, high_ref, sem
):
    kc = high_ref.shape[1]
    copy = pltpu.make_async_copy(update_ref.at[0, :, pl.ds(kc, kc)], high_ref, sem)
    copy.start()
    rows = own_ref.shape[1]
    held = owner_ref.shape[1]
    owner = owner_ref[...].astype(F32)
    owners = jnp.broadcast_to(owner, (held, held))
    above = lax.broadcasted_iota(jnp.int32, (held, held), 0) < lax.broadcasted_iota(
        jnp.int32, (held, held), 1
    )
    same = jnp.where((owners == owners.T) & above, 1.0, 0.0)
    place = owner * 2.0 + jnp.sum(same, axis=0, keepdims=True)
    row = lax.broadcasted_iota(jnp.int32, (out_ref.shape[0], held), 0)
    wanted = (row // 8 * 4 + row % 4).astype(F32)
    select = jnp.where(wanted == place, 1.0, 0.0).astype(BF16)
    slot = slot_ref[...]
    target = slot // rows * (2 * rows) + owner_ref[...] % 2 * rows + slot % rows + 1
    targets = jnp.broadcast_to(target.astype(F32), (held, held)).T[:, :rows].astype(BF16)

    copy.wait()

    def work(first, second):
        contribution = -(part_ref[...] + plane_dot(high_ref, first, second, rows))
        contribution = contribution.astype(BF16)
        half = contribution.shape[1] // 2
        source = jnp.concatenate(
            [contribution[:, :half], targets, contribution[:, half:], targets], axis=1
        )
        both = jnp.dot(select, source, preferred_element_type=F32)
        lanes = 2 * half
        upper = lax.broadcasted_iota(jnp.int32, (both.shape[0], lanes), 0) % 8 >= 4
        out_ref[...] = jnp.where(upper, both[:, lanes:], both[:, :lanes]).astype(BF16)

    by_core(core_ref, own_ref, other_ref, work)


def diagonal_kernel(core_ref, own_ref, other_ref, inverse_ref, z1_ref, diag_ref, sem):
    copy = pltpu.make_async_copy(inverse_ref.at[0, 1, 0], diag_ref, sem)
    copy.start()
    copy.wait()

    def work(first, second):
        total = plane_dot(diag_ref, first, second, own_ref.shape[1])
        z1_ref[...] = total.astype(BF16).astype(F32)

    by_core(core_ref, own_ref, other_ref, work)


def unpack_kernel(core_ref, arrived_ref, kept_ref, got_ref, copies_ref, right_ref):
    half, lanes = right_ref.shape
    arrived = arrived_ref[...]
    code = arrived[:, half : half + 1].astype(F32)
    lane = lax.broadcasted_iota(jnp.int32, (arrived.shape[0], 2 * lanes), 1).astype(F32)
    lands = jnp.where(code == lane + 1.0, 1.0, 0.0).astype(BF16)
    received = lax.dot_general(
        arrived, lands, (((0,), (0,)), ((), ())), preferred_element_type=F32
    )[:half]

    def work(first, second):
        bases = [
            jnp.concatenate(
                [first[:, r * half : (r + 1) * half], second[:, r * half : (r + 1) * half]], axis=1
            ).astype(F32)
            for r in range(2)
        ]
        value = (bases[0] + received[:, :lanes]).astype(BF16)
        for j in range(copies_ref.shape[0]):
            copies_ref[j] = value
        right_ref[...] = bases[1] + received[:, lanes:]

    by_core(core_ref, kept_ref, got_ref, work)


def build_kernel(index_ref, coupling_ref, out_ref, raw_ref, turned_ref, sums_ref, done_ref, sems):
    rows, width = sums_ref.shape
    half = width // 2
    loads = [
        pltpu.make_async_copy(
            coupling_ref.at[0, r, 0], raw_ref.at[pl.ds(r * half, half)], sems.at[r]
        )
        for r in range(2)
    ]
    for load in loads:
        load.start()

    def clear(i, carry):
        sums_ref[pl.ds(pl.multiple_of(i * 128, 128), 128), :] = jnp.zeros((128, width), F32)
        return carry

    lax.fori_loop(0, rows // 128, clear, 0, unroll=4)
    for load in loads:
        load.wait()
    for i in range(turned_ref.shape[0] // 128):
        part = slice(i * 128, (i + 1) * 128)
        turned_ref[part, :] = raw_ref[:, part].astype(F32).T

    def add(group, carry):
        base = pl.multiple_of(group * 8, 8)
        block = turned_ref[pl.ds(base, 8), :]
        for part in range(2):
            at = []
            for j in range(4):
                u = base + part * 4 + j
                at.append(index_ref[u // 128, u % 128])
            terms = [block[part * 4 + j : part * 4 + j + 1] for j in range(4)]
            old = [sums_ref[pl.ds(at[j], 1), :] for j in range(4)]
            for j in range(4):
                value = old[j] + terms[j]
                for m in range(j):
                    value = value + jnp.where(at[m] == at[j], terms[m], 0.0)
                sums_ref[pl.ds(at[j], 1), :] = value
        return carry

    lax.fori_loop(0, turned_ref.shape[0] // 8, add, 0, unroll=2)
    parts = sems.shape[0] - 2
    size = rows // parts
    stores = []
    for i in range(parts):
        part = pl.ds(i * size, size)
        done_ref[part, :] = sums_ref[part, :].astype(BF16)
        store = pltpu.make_async_copy(done_ref.at[part], out_ref.at[part], sems.at[2 + i])
        store.start()
        stores.append(store)
    for store in stores:
        store.wait()


def build_coupling(index, coupling, root_rows):
    rows, columns = 2 * coupling.shape[-2], coupling.shape[-1]
    return kernel_call(
        build_kernel,
        (index, coupling),
        [SMEM, HBM],
        like((root_rows, rows)),
        HBM,
        scratch=[
            pltpu.VMEM((rows, columns), BF16),
            pltpu.VMEM((columns, rows), F32),
            pltpu.VMEM((root_rows, rows), F32),
            pltpu.VMEM((root_rows, rows), BF16),
            DMA((10,)),
        ],
        limit=61,
        moved=30 * MIB,
    )


def pair_dot(blocks_ref, start, stop, rights):
    lanes = blocks_ref.shape[2]
    total = None
    for i in range(start // 2, stop // 2):
        left = jnp.concatenate([blocks_ref[2 * i], blocks_ref[2 * i + 1]], axis=1)
        term = rights(left, slice(i * 2 * lanes, (i + 1) * 2 * lanes))
        total = term if total is None else total + term
    return total


def against(*parts):
    return lambda left, columns: lax.dot_general(
        left,
        jnp.concatenate([part[:, columns] for part in parts], axis=0),
        (((1,), (1,)), ((), ())),
        preferred_element_type=F32,
    )


def ordered(core_ref, total):
    return jnp.where(core_ref[0] == 0, total, pltpu.roll(total, total.shape[1] // 2, 1))


def write_copies(copies_ref, value):
    for j in range(copies_ref.shape[0]):
        copies_ref[j] = value


def first_product_kernel(
    core_ref, blocks_ref, lower_ref, inverse_ref, upper_ref,
    lower_other, low_other, high_other, upper_other, base_ref,
    copies_ref, z0_ref, high_ref, top_ref, held_ref, sems
):
    kr = held_ref.shape[2]
    chips, half, lanes = blocks_ref.shape
    steps = 4
    width, span = kr // steps, chips // steps
    copies = []
    for i in range(steps):
        columns = pl.ds(i * width, width)
        pairs = [
            (lower_ref.at[1, 0, :, columns], held_ref.at[0, :, columns]),
            (lower_other.at[:, columns], held_ref.at[1, :, columns]),
            (inverse_ref.at[0, 0, :, columns], held_ref.at[2, :, columns]),
            (low_other.at[:, columns], held_ref.at[3, :, columns]),
        ]
        copies.append(
            [pltpu.make_async_copy(a, b, sems.at[i, n]) for n, (a, b) in enumerate(pairs)]
        )
    later = [
        (inverse_ref.at[1, 0], high_ref.at[0]),
        (high_other, high_ref.at[1]),
        (upper_ref.at[0, 0, :, pl.ds(kr, kr)], top_ref.at[0]),
        (upper_other, top_ref.at[1]),
    ]
    later = [pltpu.make_async_copy(a, b, sems.at[steps, n]) for n, (a, b) in enumerate(later)]
    for group in copies:
        for copy in group:
            copy.start()
    for copy in later:
        copy.start()
    rights = against(*(held_ref.at[n] for n in range(4)))
    both = None
    for i, group in enumerate(copies):
        for copy in group:
            copy.wait()
        term = pair_dot(blocks_ref, i * span, (i + 1) * span, rights)
        both = term if both is None else both + term
    total = base_ref[...] - ordered(core_ref, both[:, :lanes])
    write_copies(copies_ref, total.astype(BF16))
    z0_ref[...] = ordered(core_ref, both[:, lanes:]).astype(BF16).astype(F32)
    for copy in later:
        copy.wait()


def product_kernel(subtract, core_ref, blocks_ref, matrix_ref, *refs):
    copies_ref = refs[-1]
    total = pair_dot(
        blocks_ref, 0, blocks_ref.shape[0], against(matrix_ref.at[0], matrix_ref.at[1])
    )
    total = ordered(core_ref, total)
    if subtract:
        total = refs[0][...] - total
    write_copies(copies_ref, total.astype(BF16))


def product(core, blocks, matrix, base):
    args = (core, blocks, matrix) + (() if base is None else (base,))
    count, half, lanes = blocks.shape
    return kernel_call(
        functools.partial(product_kernel, base is not None),
        args,
        [SMEM] + [VMEM] * (len(args) - 1),
        like(blocks.shape),
        VMEM,
        limit=6,
        flops=2 * count * half * lanes * lanes,
        moved=4 * MIB,
    )


def couple_kernel(x0_ref, x1_ref, own_ref, other_ref, mine_ref, theirs_ref):
    count, half, lanes = x0_ref.shape
    total = None
    for start, blocks_ref in ((0, x0_ref), (count * lanes, x1_ref)):

        def rights(left, columns):
            rows = slice(start + columns.start, start + columns.stop)
            return jnp.dot(
                left,
                jnp.concatenate([own_ref[rows, :], other_ref[rows, :]], axis=1),
                preferred_element_type=F32,
            )

        term = pair_dot(blocks_ref, 0, count, rights)
        total = term if total is None else total + term
    width = mine_ref.shape[1]
    mine_ref[...] = total[:, :width]
    theirs_ref[...] = total[:, width:]


def settle_kernel(core_ref, mine_ref, got_ref, z0_ref, z1_ref, upper_ref,
                  copies_ref, rest_ref, top_ref, sem):
    width = top_ref.shape[1]
    copy = pltpu.make_async_copy(upper_ref.at[0, 0, 0, :, pl.ds(width, width)], top_ref, sem)
    copy.start()
    stripe = z0_ref.shape[0]

    def work(first, second):
        both = jnp.concatenate([first[...], second[...]], axis=0).T
        rest_ref[...] = z0_ref[...] - both[:stripe]
        write_copies(copies_ref, (z1_ref[...] - both[stripe:]).astype(BF16))

    by_core(core_ref, mine_ref, got_ref, work)
    copy.wait()


def closing_kernel(core_ref, own_ref, other_ref, top_ref, rest_ref, copies_ref, out_ref):
    out_ref[0, 1, 0] = copies_ref[0]

    def work(first, second):
        total = rest_ref[...] - plane_dot(top_ref, first, second, own_ref.shape[1])
        out_ref[0, 0, 0] = total.astype(BF16)

    by_core(core_ref, own_ref, other_ref, work)


def body(
    child_rhs,
    child_lower,
    child_inverse,
    child_upper,
    child_coupling,
    child_update,
    update_owner,
    update_slot,
    root_rhs,
    root_lower,
    root_inverse,
    root_upper,
):
    planes = lax.axis_size("x") * lax.axis_size("z")
    cubes = planes * lax.axis_size("y")
    devices = cubes * 2
    stripe, rhs = root_rhs.shape[2:]
    half = rhs // 2
    kc = child_inverse.shape[-1]
    kr = root_inverse.shape[-1]
    held = update_slot.shape[1]
    owner = update_owner.reshape(1, held)
    slot = update_slot
    me = lax.axis_index("c")
    core = me.astype(jnp.int32).reshape(1)
    piece = (planes, stripe, rhs)

    opened = kernel_call(
        opening_kernel, (child_rhs, owner, slot), [VMEM] * 3,
        like((planes, stripe + 8, rhs)), VMEM,
    )
    opened, root_rhs, child_lower, root_lower, root_inverse, root_upper = tie(
        (opened, root_rhs, child_lower, root_lower, root_inverse, root_upper)
    )
    own_first = spread(opened, PLANE)
    kept, given, low = kernel_call(
        turn_kernel, (core, root_rhs, child_lower), [SMEM, VMEM, HBM],
        [like((half, rhs)), like((half, rhs)), pltpu.VMEM((stripe, kc), BF16)], [VMEM] * 3,
        scratch=[DMA], limit=2, moved=MIB,
    )
    own = [
        rows_of(root_lower, 1, 0, kr),
        rows_of(root_inverse, 0, 0, kr),
        rows_of(root_inverse, 1, 0, kr),
        rows_of(root_upper, 0, kr, 2 * kr),
    ]
    own_first, own, kept, given, low = tie((own_first, own, kept, given, low))
    other_first = swap(own_first)
    y1_copies = kernel_call(
        advance_kernel, (core, own_first, other_first, low, child_rhs), [SMEM] + [VMEM] * 4,
        like(piece), VMEM, limit=2, moved=MIB,
    )
    y1_copies, own, given = tie((y1_copies, own, given))
    own_second = spread(y1_copies, PLANE)

    lower_other, low_other, high_other, upper_other = [swap(m) for m in own]
    got = swap(given)
    part, z0c, index = kernel_call(
        functools.partial(aside_kernel, stripe, kr),
        (core, own_first, other_first, child_update, child_inverse),
        [SMEM, VMEM, VMEM, HBM, HBM],
        [
            like((held, rhs), F32),
            like((stripe, rhs), F32),
            like((2 * planes, held), jnp.int32),
        ],
        [VMEM] * 3,
        scratch=[pltpu.VMEM((held, kc), BF16), pltpu.VMEM((stripe, kc), BF16), DMA((2,))],
        limit=4, moved=2 * MIB,
    )
    own_second, part, z0c, index, got = tie((own_second, part, z0c, index, got))
    other_second = swap(own_second)

    packed = kernel_call(
        contribute_kernel, (core, own_second, other_second, child_update, part, owner, slot),
        [SMEM, VMEM, VMEM, HBM] + [VMEM] * 3, like((devices * 4, rhs)), VMEM,
        scratch=[pltpu.VMEM((held, kc), BF16), DMA], limit=4, moved=MIB,
    )
    arrived = spread(packed.reshape(devices, 4, rhs), ALL)
    z1c = kernel_call(
        diagonal_kernel, (core, own_second, other_second, child_inverse),
        [SMEM, VMEM, VMEM, HBM], like((stripe, rhs), F32), VMEM,
        scratch=[pltpu.VMEM((stripe, kc), BF16), DMA], limit=2, moved=MIB,
    )
    arrived, z1c, lower_other, low_other, high_other, upper_other = tie(
        (arrived, z1c, lower_other, low_other, high_other, upper_other)
    )

    r0_copies, right = kernel_call(
        unpack_kernel, (core, arrived.reshape(devices * 4, rhs), kept, got), [SMEM] + [VMEM] * 3,
        [like((cubes, half, rhs)), like((half, rhs), F32)], [VMEM] * 2, limit=4, moved=MIB,
    )
    r0 = spread(r0_copies, CUBE)
    summed = build_coupling(index, child_coupling, 2 * kr)
    r0, summed = tie((r0, summed))
    whole = (cubes, half, rhs)
    r1_copies, z0_own, high_inverse, top = kernel_call(
        first_product_kernel,
        (core, r0, root_lower, root_inverse, root_upper,
         lower_other, low_other, high_other, upper_other, right),
        [SMEM, VMEM] + [HBM] * 7 + [VMEM],
        [
            like(whole),
            like((half, rhs), F32),
            pltpu.VMEM((2, stripe, kr), BF16),
            pltpu.VMEM((2, stripe, kr), BF16),
        ],
        [VMEM] * 4,
        scratch=[pltpu.VMEM((4, stripe, kr), BF16), DMA((5, 4))],
        limit=57, moved=10 * MIB,
    )
    r1_copies, summed = tie((r1_copies, summed))
    summed_other = swap(summed)
    r1 = spread(r1_copies, CUBE)
    x1_copies = product(core, r1, high_inverse, None)
    x1 = spread(x1_copies, CUBE)
    x1, summed_other = tie((x1, summed_other))
    x0_copies = product(core, x1, top, z0_own)
    x0, x0_copies, x1_copies = tie((spread(x0_copies, CUBE), x0_copies, x1_copies))

    mine, given = kernel_call(
        couple_kernel, (x0, x1, summed, summed_other), [VMEM] * 4,
        [like((half, 2 * stripe), F32)] * 2, [VMEM] * 2,
        limit=4, flops=8 * cubes * half * rhs * rhs, moved=10 * MIB,
    )
    c1_copies, rest, top_child = kernel_call(
        settle_kernel, (core, mine, swap(given), z0c, z1c, child_upper),
        [SMEM] + [VMEM] * 4 + [HBM],
        [like(piece), like((stripe, rhs), F32), pltpu.VMEM((stripe, kc), BF16)], [VMEM] * 3,
        scratch=[DMA], limit=2, moved=MIB,
    )
    c1_copies, x0_own, x1_own = tie((c1_copies, x0_copies[0], x1_copies[0]))
    own_c1 = spread(c1_copies, PLANE)

    def own_rows(half_rows):
        pair = in_core_order(half_rows, swap(half_rows), 0).reshape(rhs, 2 * stripe)
        rows = pair.T
        return jnp.where(me == 0, rows[:stripe], rows[stripe:])

    root_solution = jnp.stack([own_rows(x0_own), own_rows(x1_own)])[:, None]
    own_c1, root_solution = tie((own_c1, root_solution))
    child_solution = kernel_call(
        closing_kernel, (core, own_c1, swap(own_c1), top_child, rest, c1_copies),
        [SMEM] + [VMEM] * 5, like(child_rhs.shape), VMEM, limit=2, moved=MIB,
    )
    return child_solution, root_solution


def solution(mesh):
    leaf, front = mesh.devices.shape
    fine = Mesh(mesh.devices.reshape((leaf, 4, front // 8, 2)), ALL)
    subtree = P("y", None, ("x", "z", "c"), None, None)
    ancestor = P(None, ALL, None, None)
    in_specs = (
        subtree,
        subtree,
        subtree,
        subtree,
        subtree,
        P("y", ("x", "z", "c"), None),
        P("y", ("x", "z", "c"), None),
        P("y", ("x", "z", "c")),
        ancestor,
        ancestor,
        ancestor,
        ancestor,
    )
    return jax.shard_map(
        body, mesh=fine, in_specs=in_specs, out_specs=(subtree, ancestor), check_vma=False
    )
```

time: 193 us -> 209 us (1.083)
  Pallas kernels: 5.74 us -> 59.7 us
  blocking collectives: 113 us -> 71.3 us
  starting transfers between devices: 24.4 us -> 40 us
  matrix products: 8.36 us -> 0 us
  other arithmetic: 5.53 us -> 0.67 us
  local copies, waits for them, and re-layouts: 6.39 us -> 8.48 us
    pallas_call x1 -> x14, Pallas kernels: 5.74 us -> 59.7 us  [kernel_call(): pl.pallas_call(body, out_shape=shapes, in_specs=specs, out_specs=out_spec...]
    all_to_all x6 -> x3, blocking collectives: 113 us -> 71.3 us  [spread(): return lax.all_to_all(copies, axes, 0, 0)]
    all_to_all x2 -> x5, starting transfers between devices: 9.67 us -> 27.5 us  [spread(): return lax.all_to_all(copies, axes, 0, 0)]
    dot_general x12 -> x0, matrix products: 8.36 us -> none  [the longest x11 8.08 us: dot(): return jnp.dot(a, b, preferred_element_type=F32)]
    all_to_all x2 -> x5, waiting for transfers between devices: 17.3 us -> 23 us  [spread(): return lax.all_to_all(copies, axes, 0, 0)]
    ppermute x7 -> x12, waiting for transfers between devices: 9.98 us -> 4.41 us  [swap(): return lax.ppermute(array, 'c', [(0, 1), (1, 0)])]
    reshape x2 -> x4, local copies, waits for them, and re-layouts: 0.76 us -> 6.25 us  [the longest x2 6.03 us: rows_of(): return lax.slice(array, start, stop).reshape(array.shape[-2], last - first)]
    ppermute x7 -> x12, starting transfers between devices: 14.7 us -> 12.4 us  [swap(): return lax.ppermute(array, 'c', [(0, 1), (1, 0)])]
  transfers between devices with their start and end apart: 9 -> 17, of which waited for: 9 -> 8; matrix products, arithmetic and copies ran while one was open for 1% -> 3% of each run, Pallas kernels for 0% -> 21%
where the time goes in v4:
time: 209 us; the launch traced here: 208 us
  blocking collectives  71.3 us (34%)
  Pallas kernels  59.7 us (29%)
  starting transfers between devices  40 us (19%)
  waiting for transfers between devices  27.4 us (13%)
  local copies, waits for them, and re-layouts  8.48 us (4%)
    all_to_all x3, blocking collectives, spread(): return lax.all_to_all(copies, axes, 0, 0)  71.3 us
    pallas_call x14, Pallas kernels, kernel_call(): pl.pallas_call(body, out_shape=shapes, in_specs=specs, out_specs=out_spec...  59.7 us
    all_to_all x5, starting transfers between devices, spread(): return lax.all_to_all(copies, axes, 0, 0)  27.5 us
    all_to_all x5, waiting for transfers between devices, spread(): return lax.all_to_all(copies, axes, 0, 0)  23 us
    ppermute x12, starting transfers between devices, swap(): return lax.ppermute(array, 'c', [(0, 1), (1, 0)])  12.4 us
    reshape x2, local copies, waits for them, and re-layouts, rows_of(): return lax.slice(array, start, stop).reshape(array.shape[-2], last - first)  6.03 us
    ppermute x12, waiting for transfers between devices, swap(): return lax.ppermute(array, 'c', [(0, 1), (1, 0)])  4.41 us
  transfers between devices with their start and end apart: 17, of which 8 were waited for; matrix products, arithmetic and copies ran while one was open for 3% of the time, Pallas kernels for 21%

profile of v4, /device:TPU:1, one launch (start us, length us, event | category | flops | bytes accessed | tf_op | source)
XLA Modules:
  0.0 208.4 jit_solution(16122054988504424622)
XLA Ops:
  0.6 1.5 shard_map.131
  2.2 8.4 %all-to-all-start = ((bf16[16,72,128]{2,1,0:T(8,128)(2,1)}), bf16[16,72,128]{2,1,0:T(8,128)(2,1)S(1)}, u32[]{:S(2)}, u32[]{:S(2)}) async-start(bf16[16,72,128]{2,1,0:T(8,128)(2,1)} %shard_map.131), calls=%async_computation | async-start | bytes 589824 | tf_op jit(solution)/shard_map/all_to_all | solution.py:29
  10.7 3.7 %slice_bitcast_fusion.1 = (bf16[64,8192]{1,0:T(8,128)(2,1)}, bf16[64,8192]{1,0:T(8,128)(2,1)}, bf16[64,8192]{1,0:T(8,128)(2,1)}) fusion(bf16[2,1,64,8192]{3,2,1,0:T(8,128)(2,1)} %inverse_ref.4, bf16[2,1,64,16384]{3,2,1,0:T(8,128)(2,1)} %upper_ref.1), kind=kLoop, calls=%fused_computation.1 | loop fusion | bytes 6291456 | tf_op jit(solution)/shard_map/reshape | solution.py:41
  14.4 2.3 %slice_bitcast_fusion.3 = bf16[64,8192]{1,0:T(8,128)(2,1)} fusion(bf16[2,1,64,16384]{3,2,1,0:T(8,128)(2,1)} %lower_ref.1), kind=kLoop, calls=%fused_computation.3 | loop fusion | bytes 2097152 | tf_op jit(solution)/shard_map/reshape | solution.py:41
  18.2 2.2 %collective-permute-start = (bf16[16,72,128]{2,1,0:T(8,128)(2,1)S(1)}, bf16[16,72,128]{2,1,0:T(8,128)(2,1)S(1)}, u32[]{:S(2)}, u32[]{:S(2)}) collective-permute-start(bf16[16,72,128]{2,1,0:T(8,128)(2,1)S(1)} %all-to-all-done.own_ref), channel_id=1, source_target_pairs={{0,1},{1,0},{2,3},{3,2},{4,5},{5,4},{6,7},{7,6},{8,9},{9,8},{10,11... | collective-permute-start | bytes 884744 | tf_op jit(solution)/shard_map/ppermute | solution.py:25
  23.6 4.5 %all-to-all-start.1 = ((bf16[16,64,128]{2,1,0:T(8,128)(2,1)}), bf16[16,64,128]{2,1,0:T(8,128)(2,1)S(1)}, u32[]{:S(2)}, u32[]{:S(2)}) async-start(bf16[16,64,128]{2,1,0:T(8,128)(2,1)} %shard_map.133), calls=%async_computation.1 | async-start | bytes 524288 | tf_op jit(solution)/shard_map/all_to_all | solution.py:29
  30.2 5.5 %all-to-all-done.1.own_ref = bf16[16,64,128]{2,1,0:T(8,128)(2,1)S(1)} async-done(((bf16[16,64,128]{2,1,0:T(8,128)(2,1)}), bf16[16,64,128]{2,1,0:T(8,128)(2,1)S(1)}, u32[]{:S(2)}, u32[]{:S(2)}) %all-to-all-start.1) | async-done | bytes 262176 | tf_op jit(solution)/shard_map/all_to_all | solution.py:29
  35.6 1.9 collective-permute-start.2
  38.7 1.4 shard_map.135
  40.1 6.1 %all-to-all-start.2 = ((bf16[128,4,128]{2,1,0:T(4,128)(2,1)}), bf16[128,4,128]{2,1,0:T(4,128)(2,1)S(1)}, u32[]{:S(2)}, u32[]{:S(2)}) async-start(bf16[128,4,128]{2,1,0:T(4,128)(2,1)} %bitcast.6), calls=%async_computation.2 | async-start | bytes 262144 | tf_op jit(solution)/shard_map/all_to_all | solution.py:29
  46.6 9.5 %all-to-all-done.2 = bf16[128,4,128]{2,1,0:T(4,128)(2,1)S(1)} async-done(((bf16[128,4,128]{2,1,0:T(4,128)(2,1)}), bf16[128,4,128]{2,1,0:T(4,128)(2,1)S(1)}, u32[]{:S(2)}, u32[]{:S(2)}) %all-to-all-start.2) | async-done | bytes 131104 | tf_op jit(solution)/shard_map/all_to_all | solution.py:29
  56.1 1.5 shard_map.137
  58.2 5.0 %all-to-all-start.3 = ((bf16[64,64,128]{2,1,0:T(8,128)(2,1)}), bf16[64,64,128]{2,1,0:T(8,128)(2,1)S(1)}, u32[]{:S(2)}, u32[]{:S(2)}) async-start(bf16[64,64,128]{2,1,0:T(8,128)(2,1)} %get-tuple-element.94), calls=%async_computation.3 | async-start | bytes 2097152 | tf_op jit(solution)/shard_map/all_to_all | solution.py:29
  63.1 40.6 %shard_map.138.own_ref = bf16[16384,128]{1,0:T(8,128)(2,1)} custom-call(s32[32,128]{1,0:T(8,128)} %copy-done.9, bf16[1,2,1,64,4096]{4,3,2,1,0:T(8,128)(2,1)} %coupling_ref.1), custom_call_target="tpu_custom_call" | custom-call | bytes 31457280 | tf_op jit(solution)/shard_map/pallas_call | solution.py:49
  104.7 6.2 %shard_map.139 = (bf16[64,64,128]{2,1,0:T(8,128)(2,1)}, f32[64,128]{1,0:T(8,128)}, bf16[2,64,8192]{2,1,0:T(8,128)(2,1)S(1)}, bf16[2,64,8192]{2,1,0:T(8,128)(2,1)S(1)}) custom-call(s32[1]{0:T(128)} %bitcast.core_ref, bf16[64,64,128]{2,1,0:T(8,128)(2,1)} %copy-done.12, bf16[2,1,64,16384]{3,2,1,0:T(8,128)(2,1)} %lower_ref.1, ...), custom_call_target="tpu_custom_call" | custom-call | bytes 10485760 | tf_op jit(solution)/shard_map/pallas_call | solution.py:49
  111.7 28.0 %all_to_all.40.blocks_ref = bf16[64,64,128]{2,1,0:T(8,128)(2,1)S(1)} all-to-all(bf16[64,64,128]{2,1,0:T(8,128)(2,1)} %get-tuple-element.104), channel_id=1, replica_groups=mesh['y'=4,'x'=4,'z'=4,'c'=2] {'y','x','z'}, dimensions={0} | all-to-all | bytes 2097152 | tf_op jit(solution)/shard_map/all_to_all | solution.py:29
  140.7 21.8 %all_to_all.41.blocks_ref.x1_ref = bf16[64,64,128]{2,1,0:T(8,128)(2,1)S(1)} all-to-all(bf16[64,64,128]{2,1,0:T(8,128)(2,1)S(1)} %shard_map.140), channel_id=1, replica_groups=mesh['y'=4,'x'=4,'z'=4,'c'=2] {'y','x','z'}, dimensions={0} | all-to-all | bytes 2097152 | tf_op jit(solution)/shard_map/all_to_all | solution.py:29
  163.5 21.5 %all_to_all.42.x0_ref = bf16[64,64,128]{2,1,0:T(8,128)(2,1)S(1)} all-to-all(bf16[64,64,128]{2,1,0:T(8,128)(2,1)S(1)} %shard_map.141), channel_id=1, replica_groups=mesh['y'=4,'x'=4,'z'=4,'c'=2] {'y','x','z'}, dimensions={0} | all-to-all | bytes 2097152 | tf_op jit(solution)/shard_map/all_to_all | solution.py:29
  185.1 1.7 shard_map.142
  186.7 3.4 %collective-permute-start.8 = (f32[64,128]{1,0:T(8,128)S(1)}, f32[64,128]{1,0:T(8,128)S(1)}, u32[]{:S(2)}, u32[]{:S(2)}) collective-permute-start(f32[64,128]{1,0:T(8,128)S(1)} %get-tuple-element.113), channel_id=1, source_target_pairs={{0,1},{1,0},{2,3},{3,2},{4,5},{5,4},{6,7},{7,6},{8,9},{9,8},{10,11... | collective-permute-start | bytes 98312 | tf_op jit(solution)/shard_map/ppermute | solution.py:25
  192.5 3.5 %all-to-all-start.7 = ((bf16[16,64,128]{2,1,0:T(8,128)(2,1)}), bf16[16,64,128]{2,1,0:T(8,128)(2,1)S(1)}, u32[]{:S(2)}, u32[]{:S(2)}) async-start(bf16[16,64,128]{2,1,0:T(8,128)(2,1)} %get-tuple-element.119.copies_ref), calls=%async_computation.7 | async-start | bytes 524288 | tf_op jit(solution)/shard_map/all_to_all | solution.py:29
  197.0 6.7 %all-to-all-done.7.own_ref = bf16[16,64,128]{2,1,0:T(8,128)(2,1)S(1)} async-done(((bf16[16,64,128]{2,1,0:T(8,128)(2,1)}), bf16[16,64,128]{2,1,0:T(8,128)(2,1)S(1)}, u32[]{:S(2)}, u32[]{:S(2)}) %all-to-all-start.7) | async-done | bytes 262176 | tf_op jit(solution)/shard_map/all_to_all | solution.py:29
  203.7 1.7 collective-permute-start.11
  206.6 1.8 shard_map.144
  (66 shorter events, 17.0 us)
Async XLA Ops:
  2.2 16.0 %all-to-all-start = ((bf16[16,72,128]{2,1,0:T(8,128)(2,1)}), bf16[16,72,128]{2,1,0:T(8,128)(2,1)S(1)}, u32[]{:S(2)}, u32[]{:S(2)}) async-start(bf16[16,72,128]{2,1,0:T(8,128)(2,1)} %shard_map.131), calls=%async_computation | async-start | bytes 589824 | tf_op jit(solution)/shard_map/all_to_all | solution.py:29
  10.6 11.0 %copy-start.5 = (bf16[1,2,1,64,128]{4,3,2,1,0:T(8,128)(2,1)S(1)}, bf16[1,2,1,64,128]{4,3,2,1,0:T(8,128)(2,1)}, u32[]{:S(2)}) copy-start(bf16[1,2,1,64,128]{4,3,2,1,0:T(8,128)(2,1)} %rhs_ref.4) | copy-start | bytes 98308
  10.6 18.2 %copy-start.1 = (bf16[1,128,4096]{2,1,0:T(8,128)(2,1)S(1)}, bf16[1,128,4096]{2,1,0:T(8,128)(2,1)}, u32[]{:S(2)}) copy-start(bf16[1,128,4096]{2,1,0:T(8,128)(2,1)} %update_ref.3) | copy-start | bytes 3145732
  10.7 18.2 %copy-start.2 = (bf16[1,2,1,64,2048]{4,3,2,1,0:T(8,128)(2,1)S(1)}, bf16[1,2,1,64,2048]{4,3,2,1,0:T(8,128)(2,1)}, u32[]{:S(2)}) copy-start(bf16[1,2,1,64,2048]{4,3,2,1,0:T(8,128)(2,1)} %inverse_ref.3) | copy-start | bytes 1572868
  14.4 24.3 %copy-start.10 = (s32[1,128,1]{1,2,0:T(1,128)S(1)}, s32[1,128,1]{1,2,0:T(1,128)}, u32[]{:S(2)}) copy-start(s32[1,128,1]{1,2,0:T(1,128)} %param.18) | copy-start | bytes 1540
  14.4 24.3 %copy-start.11 = (s32[1,128]{1,0:T(1,128)S(1)}, s32[1,128]{1,0:T(1,128)}, u32[]{:S(2)}) copy-start(s32[1,128]{1,0:T(1,128)} %slot_ref.3) | copy-start | bytes 1540
  18.2 3.4 %collective-permute-start = (bf16[16,72,128]{2,1,0:T(8,128)(2,1)S(1)}, bf16[16,72,128]{2,1,0:T(8,128)(2,1)S(1)}, u32[]{:S(2)}, u32[]{:S(2)}) collective-permute-start(bf16[16,72,128]{2,1,0:T(8,128)(2,1)S(1)} %all-to-all-done.own_ref), channel_id=1, source_target_pairs={{0,1},{1,0},{2,3},{3,2},{4,5},{5,4},{6,7},{7,6},{8,9},{9,8},{10,11... | collective-permute-start | bytes 884744 | tf_op jit(solution)/shard_map/ppermute | solution.py:25
  22.6 33.5 %collective-permute-start.3 = (bf16[64,8192]{1,0:T(8,128)(2,1)}, bf16[64,8192]{1,0:T(8,128)(2,1)}, u32[]{:S(2)}, u32[]{:S(2)}) collective-permute-start(bf16[64,8192]{1,0:T(8,128)(2,1)} %slice_bitcast_fusion.3), channel_id=1, source_target_pairs={{0,1},{1,0},{2,3},{3,2},{4,5},{5,4},{6,7},{7,6},{8,9},{9,8},{10,11... | collective-permute-start | bytes 3145736 | tf_op jit(solution)/shard_map/ppermute | solution.py:25
  22.9 33.1 %collective-permute-start.4 = (bf16[64,8192]{1,0:T(8,128)(2,1)}, bf16[64,8192]{1,0:T(8,128)(2,1)}, u32[]{:S(2)}, u32[]{:S(2)}) collective-permute-start(bf16[64,8192]{1,0:T(8,128)(2,1)} %get-tuple-element.88), channel_id=1, source_target_pairs={{0,1},{1,0},{2,3},{3,2},{4,5},{5,4},{6,7},{7,6},{8,9},{9,8},{10,11... | collective-permute-start | bytes 3145736 | tf_op jit(solution)/shard_map/ppermute | solution.py:25
  23.1 33.0 %collective-permute-start.5 = (bf16[64,8192]{1,0:T(8,128)(2,1)}, bf16[64,8192]{1,0:T(8,128)(2,1)}, u32[]{:S(2)}, u32[]{:S(2)}) collective-permute-start(bf16[64,8192]{1,0:T(8,128)(2,1)} %get-tuple-element.89), channel_id=1, source_target_pairs={{0,1},{1,0},{2,3},{3,2},{4,5},{5,4},{6,7},{7,6},{8,9},{9,8},{10,11... | collective-permute-start | bytes 3145736 | tf_op jit(solution)/shard_map/ppermute | solution.py:25
  23.4 32.6 %collective-permute-start.6 = (bf16[64,8192]{1,0:T(8,128)(2,1)}, bf16[64,8192]{1,0:T(8,128)(2,1)}, u32[]{:S(2)}, u32[]{:S(2)}) collective-permute-start(bf16[64,8192]{1,0:T(8,128)(2,1)} %get-tuple-element.90), channel_id=1, source_target_pairs={{0,1},{1,0},{2,3},{3,2},{4,5},{5,4},{6,7},{7,6},{8,9},{9,8},{10,11... | collective-permute-start | bytes 3145736 | tf_op jit(solution)/shard_map/ppermute | solution.py:25
  23.6 12.1 %all-to-all-start.1 = ((bf16[16,64,128]{2,1,0:T(8,128)(2,1)}), bf16[16,64,128]{2,1,0:T(8,128)(2,1)S(1)}, u32[]{:S(2)}, u32[]{:S(2)}) async-start(bf16[16,64,128]{2,1,0:T(8,128)(2,1)} %shard_map.133), calls=%async_computation.1 | async-start | bytes 524288 | tf_op jit(solution)/shard_map/all_to_all | solution.py:29
  28.1 2.1 %collective-permute-start.1 = (bf16[64,128]{1,0:T(8,128)(2,1)S(1)}, bf16[64,128]{1,0:T(8,128)(2,1)S(1)}, u32[]{:S(2)}, u32[]{:S(2)}) collective-permute-start(bf16[64,128]{1,0:T(8,128)(2,1)S(1)} %get-tuple-element.84), channel_id=1, source_target_pairs={{0,1},{1,0},{2,3},{3,2},{4,5},{5,4},{6,7},{7,6},{8,9},{9,8},{10,11... | collective-permute-start | bytes 49160 | tf_op jit(solution)/shard_map/ppermute | solution.py:25
  35.6 3.1 %collective-permute-start.2 = (bf16[16,64,128]{2,1,0:T(8,128)(2,1)S(1)}, bf16[16,64,128]{2,1,0:T(8,128)(2,1)S(1)}, u32[]{:S(2)}, u32[]{:S(2)}) collective-permute-start(bf16[16,64,128]{2,1,0:T(8,128)(2,1)S(1)} %all-to-all-done.1.own_ref), channel_id=1, source_target_pairs={{0,1},{1,0},{2,3},{3,2},{4,5},{5,4},{6,7},{7,6},{8,9},{9,8},{10,11... | collective-permute-start | bytes 786440 | tf_op jit(solution)/shard_map/ppermute | solution.py:25
  40.1 15.9 %all-to-all-start.2 = ((bf16[128,4,128]{2,1,0:T(4,128)(2,1)}), bf16[128,4,128]{2,1,0:T(4,128)(2,1)S(1)}, u32[]{:S(2)}, u32[]{:S(2)}) async-start(bf16[128,4,128]{2,1,0:T(4,128)(2,1)} %bitcast.6), calls=%async_computation.2 | async-start | bytes 262144 | tf_op jit(solution)/shard_map/all_to_all | solution.py:29
  58.2 45.5 %all-to-all-start.3 = ((bf16[64,64,128]{2,1,0:T(8,128)(2,1)}), bf16[64,64,128]{2,1,0:T(8,128)(2,1)S(1)}, u32[]{:S(2)}, u32[]{:S(2)}) async-start(bf16[64,64,128]{2,1,0:T(8,128)(2,1)} %get-tuple-element.94), calls=%async_computation.3 | async-start | bytes 2097152 | tf_op jit(solution)/shard_map/all_to_all | solution.py:29
  110.9 51.6 %copy-start.7 = (f32[64,128]{1,0:T(8,128)S(1)}, f32[64,128]{1,0:T(8,128)}, u32[]{:S(2)}) copy-start(f32[64,128]{1,0:T(8,128)} %get-tuple-element.109.refs_0_) | copy-start | bytes 98308
  110.9 51.6 %collective-permute-start.7 = (bf16[16384,128]{1,0:T(8,128)(2,1)}, bf16[16384,128]{1,0:T(8,128)(2,1)S(1)}, u32[]{:S(2)}, u32[]{:S(2)}) collective-permute-start(bf16[16384,128]{1,0:T(8,128)(2,1)} %shard_map.138.own_ref), channel_id=1, source_target_pairs={{0,1},{1,0},{2,3},{3,2},{4,5},{5,4},{6,7},{7,6},{8,9},{9,8},{10,11... | collective-permute-start | bytes 12582920 | tf_op jit(solution)/shard_map/ppermute | solution.py:25
  140.7 44.4 %copy-start = (bf16[16384,128]{1,0:T(8,128)(2,1)S(1)}, bf16[16384,128]{1,0:T(8,128)(2,1)}, u32[]{:S(2)}) copy-start(bf16[16384,128]{1,0:T(8,128)(2,1)} %shard_map.138.own_ref) | copy-start | bytes 12582916
  186.7 4.3 %collective-permute-start.8 = (f32[64,128]{1,0:T(8,128)S(1)}, f32[64,128]{1,0:T(8,128)S(1)}, u32[]{:S(2)}, u32[]{:S(2)}) collective-permute-start(f32[64,128]{1,0:T(8,128)S(1)} %get-tuple-element.113), channel_id=1, source_target_pairs={{0,1},{1,0},{2,3},{3,2},{4,5},{5,4},{6,7},{7,6},{8,9},{9,8},{10,11... | collective-permute-start | bytes 98312 | tf_op jit(solution)/shard_map/ppermute | solution.py:25
  191.9 4.1 %collective-permute-start.9 = (bf16[64,128]{1,0:T(8,128)(2,1)S(1)}, bf16[64,128]{1,0:T(8,128)(2,1)S(1)}, u32[]{:S(2)}, u32[]{:S(2)}) collective-permute-start(bf16[64,128]{1,0:T(8,128)(2,1)S(1)} %slice_bitcast_fusion.5), channel_id=1, source_target_pairs={{0,1},{1,0},{2,3},{3,2},{4,5},{5,4},{6,7},{7,6},{8,9},{9,8},{10,11... | collective-permute-start | bytes 49160 | tf_op jit(solution)/shard_map/ppermute | solution.py:25
  192.3 3.9 %collective-permute-start.10 = (bf16[64,128]{1,0:T(8,128)(2,1)S(1)}, bf16[64,128]{1,0:T(8,128)(2,1)S(1)}, u32[]{:S(2)}, u32[]{:S(2)}) collective-permute-start(bf16[64,128]{1,0:T(8,128)(2,1)S(1)} %slice_bitcast_fusion.4), channel_id=1, source_target_pairs={{0,1},{1,0},{2,3},{3,2},{4,5},{5,4},{6,7},{7,6},{8,9},{9,8},{10,11... | collective-permute-start | bytes 49160 | tf_op jit(solution)/shard_map/ppermute | solution.py:25
  192.5 11.2 %all-to-all-start.7 = ((bf16[16,64,128]{2,1,0:T(8,128)(2,1)}), bf16[16,64,128]{2,1,0:T(8,128)(2,1)S(1)}, u32[]{:S(2)}, u32[]{:S(2)}) async-start(bf16[16,64,128]{2,1,0:T(8,128)(2,1)} %get-tuple-element.119.copies_ref), calls=%async_computation.7 | async-start | bytes 524288 | tf_op jit(solution)/shard_map/all_to_all | solution.py:29
  203.7 2.9 %collective-permute-start.11 = (bf16[16,64,128]{2,1,0:T(8,128)(2,1)S(1)}, bf16[16,64,128]{2,1,0:T(8,128)(2,1)S(1)}, u32[]{:S(2)}, u32[]{:S(2)}) collective-permute-start(bf16[16,64,128]{2,1,0:T(8,128)(2,1)S(1)} %all-to-all-done.7.own_ref), channel_id=1, source_target_pairs={{0,1},{1,0},{2,3},{3,2},{4,5},{5,4},{6,7},{7,6},{8,9},{9,8},{10,11... | collective-permute-start | bytes 786440 | tf_op jit(solution)/shard_map/ppermute | solution.py:25
  (6 other events, 20.3 us)

commit v5 on v4

--- a/solution.py
+++ b/solution.py
@@ -18,6 +18,7 @@
 HBM = pl.BlockSpec(memory_space=pltpu.HBM)
 DMA = pltpu.SemaphoreType.DMA
 MIB = 1 << 20
+BATCH = 8
 tie = lax.optimization_barrier
 
 
@@ -135,7 +136,7 @@
 
 def aside_kernel(
     rows, kr, core_ref, own_ref, other_ref, update_ref, inverse_ref,
-    part_ref, z0_ref, index_ref, low_ref, diag_ref, sems
+    part_ref, z0_ref, index_ref, repeats_ref, low_ref, diag_ref, sems
 ):
     kc = low_ref.shape[1]
     copies = [
@@ -153,6 +154,15 @@
                 index_ref[2 * j + c : 2 * j + c + 1, :] = (
                     (slot // rows) * kr + owner * rows + slot % rows
                 )
+        index = index_ref[...]
+        lane = lax.broadcasted_iota(jnp.int32, index.shape, 1) % BATCH
+        found = jnp.zeros(index.shape, jnp.int32)
+        for d in range(1, BATCH):
+            again = (pltpu.roll(index, d, 1) == index) & (lane >= d)
+            found = jnp.maximum(found, jnp.where(again, 1, 0))
+        repeats_ref[...] = jnp.broadcast_to(
+            jnp.max(found, axis=1, keepdims=True), repeats_ref.shape
+        )
         copies[0].wait()
         part_ref[...] = plane_dot(low_ref, first, second, rows)
         copies[1].wait()
@@ -237,7 +247,7 @@
     by_core(core_ref, kept_ref, got_ref, work)
 
 
-def build_kernel(index_ref, coupling_ref, out_ref, raw_ref, turned_ref, sums_ref, done_ref, sems):
+def build_kernel(index_ref, repeats_ref, coupling_ref, out_ref, raw_ref, turned_ref, sums_ref, done_ref, sems):
     rows, width = sums_ref.shape
     half = width // 2
     loads = [
@@ -260,24 +270,37 @@
         part = slice(i * 128, (i + 1) * 128)
         turned_ref[part, :] = raw_ref[:, part].astype(F32).T
 
-    def add(group, carry):
-        base = pl.multiple_of(group * 8, 8)
-        block = turned_ref[pl.ds(base, 8), :]
-        for part in range(2):
-            at = []
-            for j in range(4):
-                u = base + part * 4 + j
-                at.append(index_ref[u // 128, u % 128])
-            terms = [block[part * 4 + j : part * 4 + j + 1] for j in range(4)]
-            old = [sums_ref[pl.ds(at[j], 1), :] for j in range(4)]
-            for j in range(4):
-                value = old[j] + terms[j]
-                for m in range(j):
-                    value = value + jnp.where(at[m] == at[j], terms[m], 0.0)
-                sums_ref[pl.ds(at[j], 1), :] = value
+    def add_line(line, carry):
+        start = pl.multiple_of(line * 128, 128)
+
+        def add_apart(group, carry):
+            base = pl.multiple_of(start + group * BATCH, BATCH)
+            block = turned_ref[pl.ds(base, BATCH), :]
+            at = [pl.ds(index_ref[base + j], 1) for j in range(BATCH)]
+            values = [sums_ref[at[j], :] + block[j : j + 1] for j in range(BATCH)]
+            for j in range(BATCH):
+                sums_ref[at[j], :] = values[j]
+            return carry
+
+        def add_in_turn(group, carry):
+            base = pl.multiple_of(start + group * BATCH, BATCH)
+            block = turned_ref[pl.ds(base, BATCH), :]
+            for j in range(BATCH):
+                at = pl.ds(index_ref[base + j], 1)
+                sums_ref[at, :] = sums_ref[at, :] + block[j : j + 1]
+            return carry
+
+        @pl.when(repeats_ref[line] == 0)
+        def _():
+            lax.fori_loop(0, 128 // BATCH, add_apart, 0, unroll=4)
+
+        @pl.when(repeats_ref[line] != 0)
+        def _():
+            lax.fori_loop(0, 128 // BATCH, add_in_turn, 0)
+
         return carry
 
-    lax.fori_loop(0, turned_ref.shape[0] // 8, add, 0, unroll=2)
+    lax.fori_loop(0, turned_ref.shape[0] // 128, add_line, 0)
     parts = sems.shape[0] - 2
     size = rows // parts
     stores = []
@@ -291,12 +314,12 @@
         store.wait()
 
 
-def build_coupling(index, coupling, root_rows):
+def build_coupling(index, repeats, coupling, root_rows):
     rows, columns = 2 * coupling.shape[-2], coupling.shape[-1]
     return kernel_call(
         build_kernel,
-        (index, coupling),
-        [SMEM, HBM],
+        (index, repeats, coupling),
+        [SMEM, SMEM, HBM],
         like((root_rows, rows)),
         HBM,
         scratch=[
@@ -306,7 +329,7 @@
             pltpu.VMEM((root_rows, rows), BF16),
             DMA((10,)),
         ],
-        limit=61,
+        limit=60,
         moved=30 * MIB,
     )
 
@@ -340,76 +363,49 @@
 
 
 def first_product_kernel(
-    core_ref, blocks_ref, lower_ref, inverse_ref, upper_ref,
-    lower_other, low_other, high_other, upper_other, base_ref,
-    copies_ref, z0_ref, high_ref, top_ref, held_ref, sems
+    core_ref, blocks_ref, lower_ref, other_ref, base_ref, copies_ref, held_ref, sems
 ):
     kr = held_ref.shape[2]
-    chips, half, lanes = blocks_ref.shape
-    steps = 4
+    chips = blocks_ref.shape[0]
+    steps = sems.shape[0]
     width, span = kr // steps, chips // steps
     copies = []
     for i in range(steps):
         columns = pl.ds(i * width, width)
         pairs = [
-            (lower_ref.at[1, 0, :, columns], held_ref.at[0, :, columns]),
-            (lower_other.at[:, columns], held_ref.at[1, :, columns]),
-            (inverse_ref.at[0, 0, :, columns], held_ref.at[2, :, columns]),
-            (low_other.at[:, columns], held_ref.at[3, :, columns]),
+            (lower_ref.at[:, columns], held_ref.at[0, :, columns]),
+            (other_ref.at[:, columns], held_ref.at[1, :, columns]),
         ]
         copies.append(
             [pltpu.make_async_copy(a, b, sems.at[i, n]) for n, (a, b) in enumerate(pairs)]
         )
-    later = [
-        (inverse_ref.at[1, 0], high_ref.at[0]),
-        (high_other, high_ref.at[1]),
-        (upper_ref.at[0, 0, :, pl.ds(kr, kr)], top_ref.at[0]),
-        (upper_other, top_ref.at[1]),
-    ]
-    later = [pltpu.make_async_copy(a, b, sems.at[steps, n]) for n, (a, b) in enumerate(later)]
     for group in copies:
         for copy in group:
             copy.start()
-    for copy in later:
-        copy.start()
-    rights = against(*(held_ref.at[n] for n in range(4)))
-    both = None
+    total = base_ref[...]
     for i, group in enumerate(copies):
         for copy in group:
             copy.wait()
-        term = pair_dot(blocks_ref, i * span, (i + 1) * span, rights)
-        both = term if both is None else both + term
-    total = base_ref[...] - ordered(core_ref, both[:, :lanes])
+        term = pair_dot(
+            blocks_ref, i * span, (i + 1) * span, against(held_ref.at[0], held_ref.at[1])
+        )
+        total = total - ordered(core_ref, term)
     write_copies(copies_ref, total.astype(BF16))
-    z0_ref[...] = ordered(core_ref, both[:, lanes:]).astype(BF16).astype(F32)
-    for copy in later:
-        copy.wait()
-
-
-def product_kernel(subtract, core_ref, blocks_ref, matrix_ref, *refs):
-    copies_ref = refs[-1]
-    total = pair_dot(
-        blocks_ref, 0, blocks_ref.shape[0], against(matrix_ref.at[0], matrix_ref.at[1])
-    )
-    total = ordered(core_ref, total)
-    if subtract:
-        total = refs[0][...] - total
-    write_copies(copies_ref, total.astype(BF16))
-
-
-def product(core, blocks, matrix, base):
-    args = (core, blocks, matrix) + (() if base is None else (base,))
-    count, half, lanes = blocks.shape
-    return kernel_call(
-        functools.partial(product_kernel, base is not None),
-        args,
-        [SMEM] + [VMEM] * (len(args) - 1),
-        like(blocks.shape),
-        VMEM,
-        limit=6,
-        flops=2 * count * half * lanes * lanes,
-        moved=4 * MIB,
-    )
+
+
+def product_kernel(core_ref, blocks_ref, own_ref, other_ref, copies_ref):
+    total = pair_dot(blocks_ref, 0, blocks_ref.shape[0], against(own_ref, other_ref))
+    write_copies(copies_ref, ordered(core_ref, total).astype(BF16))
+
+
+def last_product_kernel(
+    core_ref, r0_ref, low_own_ref, low_other_ref, x1_ref, top_own_ref, top_other_ref, copies_ref
+):
+    chips = x1_ref.shape[0]
+    diagonal = pair_dot(r0_ref, 0, chips, against(low_own_ref, low_other_ref))
+    diagonal = diagonal.astype(BF16).astype(F32)
+    total = diagonal - pair_dot(x1_ref, 0, chips, against(top_own_ref, top_other_ref))
+    write_copies(copies_ref, ordered(core_ref, total).astype(BF16))
 
 
 def couple_kernel(x0_ref, x1_ref, own_ref, other_ref, mine_ref, theirs_ref):
@@ -516,7 +512,7 @@
 
     lower_other, low_other, high_other, upper_other = [swap(m) for m in own]
     got = swap(given)
-    part, z0c, index = kernel_call(
+    part, z0c, index, repeats = kernel_call(
         functools.partial(aside_kernel, stripe, kr),
         (core, own_first, other_first, child_update, child_inverse),
         [SMEM, VMEM, VMEM, HBM, HBM],
@@ -524,12 +520,16 @@
             like((held, rhs), F32),
             like((stripe, rhs), F32),
             like((2 * planes, held), jnp.int32),
+            like((2 * planes, held), jnp.int32),
         ],
-        [VMEM] * 3,
+        [VMEM] * 4,
         scratch=[pltpu.VMEM((held, kc), BF16), pltpu.VMEM((stripe, kc), BF16), DMA((2,))],
         limit=4, moved=2 * MIB,
     )
-    own_second, part, z0c, index, got = tie((own_second, part, z0c, index, got))
+    index, repeats = index.reshape(-1), repeats[:, 0]
+    own_second, part, z0c, index, repeats, got = tie(
+        (own_second, part, z0c, index, repeats, got)
+    )
     other_second = swap(own_second)
 
     packed = kernel_call(
@@ -552,31 +552,27 @@
         [like((cubes, half, rhs)), like((half, rhs), F32)], [VMEM] * 2, limit=4, moved=MIB,
     )
     r0 = spread(r0_copies, CUBE)
-    summed = build_coupling(index, child_coupling, 2 * kr)
+    summed = build_coupling(index, repeats, child_coupling, 2 * kr)
+    summed_other = swap(summed)
     r0, summed = tie((r0, summed))
     whole = (cubes, half, rhs)
-    r1_copies, z0_own, high_inverse, top = kernel_call(
-        first_product_kernel,
-        (core, r0, root_lower, root_inverse, root_upper,
-         lower_other, low_other, high_other, upper_other, right),
-        [SMEM, VMEM] + [HBM] * 7 + [VMEM],
-        [
-            like(whole),
-            like((half, rhs), F32),
-            pltpu.VMEM((2, stripe, kr), BF16),
-            pltpu.VMEM((2, stripe, kr), BF16),
-        ],
-        [VMEM] * 4,
-        scratch=[pltpu.VMEM((4, stripe, kr), BF16), DMA((5, 4))],
-        limit=57, moved=10 * MIB,
-    )
-    r1_copies, summed = tie((r1_copies, summed))
-    summed_other = swap(summed)
+    r1_copies = kernel_call(
+        first_product_kernel, (core, r0, own[0], lower_other, right),
+        [SMEM, VMEM, HBM, HBM, VMEM], like(whole), VMEM,
+        scratch=[pltpu.VMEM((2, stripe, kr), BF16), DMA((4, 2))], limit=50, moved=4 * MIB,
+    )
     r1 = spread(r1_copies, CUBE)
-    x1_copies = product(core, r1, high_inverse, None)
+    x1_copies = kernel_call(
+        product_kernel, (core, r1, own[2], high_other), [SMEM] + [VMEM] * 3, like(whole), VMEM,
+        limit=4, flops=2 * cubes * half * rhs * rhs, moved=4 * MIB,
+    )
     x1 = spread(x1_copies, CUBE)
     x1, summed_other = tie((x1, summed_other))
-    x0_copies = product(core, x1, top, z0_own)
+    x0_copies = kernel_call(
+        last_product_kernel, (core, r0, own[1], low_other, x1, own[3], upper_other),
+        [SMEM] + [VMEM] * 6, like(whole), VMEM,
+        limit=4, flops=4 * cubes * half * rhs * rhs, moved=7 * MIB,
+    )
     x0, x0_copies, x1_copies = tie((spread(x0_copies, CUBE), x0_copies, x1_copies))
 
     mine, given = kernel_call(

time: 209 us -> 194 us (0.928)
  Pallas kernels: 59.7 us -> 33.8 us
  blocking collectives: 71.3 us -> 87.2 us
  waiting for transfers between devices: 27.4 us -> 19.5 us
  local copies, waits for them, and re-layouts: 8.48 us -> 15.7 us
  starting transfers between devices: 40 us -> 35.5 us
    pallas_call x14, Pallas kernels: 59.7 us -> 33.8 us  [kernel_call(): pl.pallas_call(body, out_shape=shapes, in_specs=specs, out_specs=out_spec...]
    all_to_all x3 -> x4, blocking collectives: 71.3 us -> 87.2 us  [spread(): return lax.all_to_all(copies, axes, 0, 0)]
    unnamed x26 -> x40, local copies, waits for them, and re-layouts: 2.23 us -> 9.9 us
    all_to_all x5 -> x4, waiting for transfers between devices: 23 us -> 15.4 us  [spread(): return lax.all_to_all(copies, axes, 0, 0)]
    all_to_all x5 -> x4, starting transfers between devices: 27.5 us -> 23.9 us  [spread(): return lax.all_to_all(copies, axes, 0, 0)]
  transfers between devices with their start and end apart: 17 -> 16, of which waited for: 8 -> 7; matrix products, arithmetic and copies ran while one was open for 3% -> 3% of each run, Pallas kernels for 21% -> 11%
where the time goes in v5:
time: 194 us; the launch traced here: 193 us
  blocking collectives  87.2 us (45%)
  starting transfers between devices  35.5 us (18%)
  Pallas kernels  33.8 us (17%)
  waiting for transfers between devices  19.5 us (10%)
  local copies, waits for them, and re-layouts  15.7 us (8%)
    all_to_all x4, blocking collectives, spread(): return lax.all_to_all(copies, axes, 0, 0)  87.2 us
    pallas_call x14, Pallas kernels, kernel_call(): pl.pallas_call(body, out_shape=shapes, in_specs=specs, out_specs=out_spec...  33.8 us
    all_to_all x4, starting transfers between devices, spread(): return lax.all_to_all(copies, axes, 0, 0)  23.9 us
    all_to_all x4, waiting for transfers between devices, spread(): return lax.all_to_all(copies, axes, 0, 0)  15.4 us
    ppermute x12, starting transfers between devices, swap(): return lax.ppermute(array, 'c', [(0, 1), (1, 0)])  11.6 us
    unnamed x40, local copies, waits for them, and re-layouts  9.9 us
    reshape x2, local copies, waits for them, and re-layouts, rows_of(): return lax.slice(array, start, stop).reshape(array.shape[-2], last - first)  4.84 us
    ppermute x12, waiting for transfers between devices, swap(): return lax.ppermute(array, 'c', [(0, 1), (1, 0)])  4.1 us
  transfers between devices with their start and end apart: 16, of which 7 were waited for; matrix products, arithmetic and copies ran while one was open for 3% of the time, Pallas kernels for 11%

profile of v5, /device:TPU:1, one launch (start us, length us, event | category | flops | bytes accessed | tf_op | source)
XLA Modules:
  0.0 193.3 jit_solution(274738853901148009)
XLA Ops:
  0.6 1.5 shard_map.131
  2.2 8.4 %all-to-all-start = ((bf16[16,72,128]{2,1,0:T(8,128)(2,1)}), bf16[16,72,128]{2,1,0:T(8,128)(2,1)S(1)}, u32[]{:S(2)}, u32[]{:S(2)}) async-start(bf16[16,72,128]{2,1,0:T(8,128)(2,1)} %shard_map.131), calls=%async_computation | async-start | bytes 589824 | tf_op jit(solution)/shard_map/all_to_all | solution.py:30
  10.6 3.6 %slice_bitcast_fusion.1 = (bf16[64,8192]{1,0:T(8,128)(2,1)S(1)}, bf16[64,8192]{1,0:T(8,128)(2,1)}, bf16[64,8192]{1,0:T(8,128)(2,1)}) fusion(bf16[2,1,64,8192]{3,2,1,0:T(8,128)(2,1)} %param.22, bf16[2,1,64,16384]{3,2,1,0:T(8,128)(2,1)} %param.23), kind=kLoop, calls=%fused_computation.1 | loop fusion | bytes 6291456 | tf_op jit(solution)/shard_map/reshape | solution.py:42
  18.3 2.1 %collective-permute-start = (bf16[16,72,128]{2,1,0:T(8,128)(2,1)S(1)}, bf16[16,72,128]{2,1,0:T(8,128)(2,1)S(1)}, u32[]{:S(2)}, u32[]{:S(2)}) collective-permute-start(bf16[16,72,128]{2,1,0:T(8,128)(2,1)S(1)} %all-to-all-done.own_ref), channel_id=1, source_target_pairs={{0,1},{1,0},{2,3},{3,2},{4,5},{5,4},{6,7},{7,6},{8,9},{9,8},{10,11... | collective-permute-start | bytes 884744 | tf_op jit(solution)/shard_map/ppermute | solution.py:26
  24.2 5.8 %all-to-all-start.1 = ((bf16[16,64,128]{2,1,0:T(8,128)(2,1)}), bf16[16,64,128]{2,1,0:T(8,128)(2,1)}, u32[]{:S(2)}, u32[]{:S(2)}) async-start(bf16[16,64,128]{2,1,0:T(8,128)(2,1)} %copy-done.10), calls=%async_computation.1 | async-start | bytes 524288 | tf_op jit(solution)/shard_map/all_to_all | solution.py:30
  35.7 2.0 %all-to-all-done.1.own_ref = bf16[16,64,128]{2,1,0:T(8,128)(2,1)} async-done(((bf16[16,64,128]{2,1,0:T(8,128)(2,1)}), bf16[16,64,128]{2,1,0:T(8,128)(2,1)}, u32[]{:S(2)}, u32[]{:S(2)}) %all-to-all-start.1) | async-done | bytes 262176 | tf_op jit(solution)/shard_map/all_to_all | solution.py:30
  37.6 1.9 collective-permute-start.2
  39.6 11.1 %shard_map.138.own_ref = bf16[16384,128]{1,0:T(8,128)(2,1)} custom-call(s32[4096]{0:T(1024)} %bitcast.37, s32[32]{0:T(128)} %slice_reduce_fusion.repeats_ref, bf16[1,2,1,64,4096]{4,3,2,1,0:T(8,128)(2,1)} %coupling_ref.1), custom_call_target="tpu_custom_call" | custom-call | bytes 31457280 | tf_op jit(solution)/shard_map/pallas_call | solution.py:50
  53.2 2.4 %shard_map.135 = bf16[512,128]{1,0:T(8,128)(2,1)} custom-call(s32[1]{0:T(128)} %bitcast.core_ref, bf16[16,64,128]{2,1,0:T(8,128)(2,1)} %all-to-all-done.1.own_ref, bf16[16,64,128]{2,1,0:T(8,128)(2,1)S(1)} %collective-permute-done.2.other_ref, bf16[1,128,4096]{2,1,0:T(8,128)(2,1)S(1)} %copy-done.1, f32[128,128]{1,0:T(8,128)S(1)} %get-tuple-element.83.part_ref, ...), custom_call_target="tpu_custom_call" | custom-call | bytes 1048576 | tf_op jit(solution)/shard_map/pallas_call | solution.py:50
  55.6 6.1 %all-to-all-start.2 = ((bf16[128,4,128]{2,1,0:T(4,128)(2,1)}), bf16[128,4,128]{2,1,0:T(4,128)(2,1)S(1)}, u32[]{:S(2)}, u32[]{:S(2)}) async-start(bf16[128,4,128]{2,1,0:T(4,128)(2,1)} %bitcast.7), calls=%async_computation.2 | async-start | bytes 262144 | tf_op jit(solution)/shard_map/all_to_all | solution.py:30
  64.0 7.5 %all-to-all-done.2 = bf16[128,4,128]{2,1,0:T(4,128)(2,1)S(1)} async-done(((bf16[128,4,128]{2,1,0:T(4,128)(2,1)}), bf16[128,4,128]{2,1,0:T(4,128)(2,1)S(1)}, u32[]{:S(2)}, u32[]{:S(2)}) %all-to-all-start.2) | async-done | bytes 131104 | tf_op jit(solution)/shard_map/all_to_all | solution.py:30
  72.0 22.1 %all_to_all.40.blocks_ref.r0_ref = bf16[64,64,128]{2,1,0:T(8,128)(2,1)S(1)} all-to-all(bf16[64,64,128]{2,1,0:T(8,128)(2,1)S(1)} %get-tuple-element.91), channel_id=1, replica_groups=mesh['y'=4,'x'=4,'z'=4,'c'=2] {'y','x','z'}, dimensions={0} | all-to-all | bytes 2097152 | tf_op jit(solution)/shard_map/all_to_all | solution.py:30
  94.2 3.0 %shard_map.139 = bf16[64,64,128]{2,1,0:T(8,128)(2,1)S(1)} custom-call(s32[1]{0:T(128)} %bitcast.core_ref, bf16[64,64,128]{2,1,0:T(8,128)(2,1)S(1)} %all_to_all.40.blocks_ref.r0_ref, bf16[64,8192]{1,0:T(8,128)(2,1)S(1)} %slice_bitcast_fusion.3.lower_ref, bf16[64,8192]{1,0:T(8,128)(2,1)} %collective-permute-done.3.other_ref, ...), custom_call_target="tpu_custom_call" | custom-call | bytes 4194304 | tf_op jit(solution)/shard_map/pallas_call | solution.py:50
  97.2 21.3 %all_to_all.41.blocks_ref = bf16[64,64,128]{2,1,0:T(8,128)(2,1)S(1)} all-to-all(bf16[64,64,128]{2,1,0:T(8,128)(2,1)S(1)} %shard_map.139), channel_id=1, replica_groups=mesh['y'=4,'x'=4,'z'=4,'c'=2] {'y','x','z'}, dimensions={0} | all-to-all | bytes 2097152 | tf_op jit(solution)/shard_map/all_to_all | solution.py:30
  118.5 2.2 %shard_map.140 = bf16[64,64,128]{2,1,0:T(8,128)(2,1)S(1)} custom-call(s32[1]{0:T(128)} %bitcast.core_ref, bf16[64,64,128]{2,1,0:T(8,128)(2,1)S(1)} %all_to_all.41.blocks_ref, bf16[64,8192]{1,0:T(8,128)(2,1)S(1)} %get-tuple-element.86.own_ref, bf16[64,8192]{1,0:T(8,128)(2,1)} %collective-permute-done.5.other_ref), custom_call_target="tpu_custom_call" | custom-call | flops 134217728 | bytes 4194304 | tf_op jit(solution)/shard_map/pallas_call | solution.py:50
  120.8 21.8 %all_to_all.42.x1_ref = bf16[64,64,128]{2,1,0:T(8,128)(2,1)S(1)} all-to-all(bf16[64,64,128]{2,1,0:T(8,128)(2,1)S(1)} %shard_map.140), channel_id=1, replica_groups=mesh['y'=4,'x'=4,'z'=4,'c'=2] {'y','x','z'}, dimensions={0} | all-to-all | bytes 2097152 | tf_op jit(solution)/shard_map/all_to_all | solution.py:30
  142.6 3.4 %shard_map.141 = bf16[64,64,128]{2,1,0:T(8,128)(2,1)S(1)} custom-call(s32[1]{0:T(128)} %bitcast.core_ref, bf16[64,64,128]{2,1,0:T(8,128)(2,1)S(1)} %all_to_all.40.blocks_ref.r0_ref, bf16[64,8192]{1,0:T(8,128)(2,1)S(1)} %copy-done.2, bf16[64,8192]{1,0:T(8,128)(2,1)} %collective-permute-done.4.low_other_ref, bf16[64,64,128]{2,1,0:T(8,128)(2,1)S(1)} %all_to_all.42.x1_ref, ...), custom_call_target="tpu_custom_call" | custom-call | flops 268435456 | bytes 7340032 | tf_op jit(solution)/shard_map/pallas_call | solution.py:50
  146.0 21.9 %all_to_all.43.x0_ref = bf16[64,64,128]{2,1,0:T(8,128)(2,1)S(1)} all-to-all(bf16[64,64,128]{2,1,0:T(8,128)(2,1)S(1)} %shard_map.141), channel_id=1, replica_groups=mesh['y'=4,'x'=4,'z'=4,'c'=2] {'y','x','z'}, dimensions={0} | all-to-all | bytes 2097152 | tf_op jit(solution)/shard_map/all_to_all | solution.py:30
  168.0 3.8 %shard_map.142 = (f32[64,128]{1,0:T(8,128)S(1)}, f32[64,128]{1,0:T(8,128)S(1)}) custom-call(bf16[64,64,128]{2,1,0:T(8,128)(2,1)S(1)} %all_to_all.43.x0_ref, bf16[64,64,128]{2,1,0:T(8,128)(2,1)S(1)} %all_to_all.42.x1_ref, bf16[16384,128]{1,0:T(8,128)(2,1)S(1)} %copy-done, bf16[16384,128]{1,0:T(8,128)(2,1)} %collective-permute-done.7.other_ref), custom_call_target="tpu_custom_call" | custom-call | flops 536870912 | bytes 10485760 | tf_op jit(solution)/shard_map/pallas_call | solution.py:50
  171.8 3.4 %collective-permute-start.8 = (f32[64,128]{1,0:T(8,128)S(1)}, f32[64,128]{1,0:T(8,128)S(1)}, u32[]{:S(2)}, u32[]{:S(2)}) collective-permute-start(f32[64,128]{1,0:T(8,128)S(1)} %get-tuple-element.105), channel_id=1, source_target_pairs={{0,1},{1,0},{2,3},{3,2},{4,5},{5,4},{6,7},{7,6},{8,9},{9,8},{10,11... | collective-permute-start | bytes 98312 | tf_op jit(solution)/shard_map/ppermute | solution.py:26
  177.4 3.5 %all-to-all-start.7 = ((bf16[16,64,128]{2,1,0:T(8,128)(2,1)}), bf16[16,64,128]{2,1,0:T(8,128)(2,1)S(1)}, u32[]{:S(2)}, u32[]{:S(2)}) async-start(bf16[16,64,128]{2,1,0:T(8,128)(2,1)} %get-tuple-element.111.copies_ref), calls=%async_computation.7 | async-start | bytes 524288 | tf_op jit(solution)/shard_map/all_to_all | solution.py:30
  183.0 5.9 %all-to-all-done.7.own_ref = bf16[16,64,128]{2,1,0:T(8,128)(2,1)S(1)} async-done(((bf16[16,64,128]{2,1,0:T(8,128)(2,1)}), bf16[16,64,128]{2,1,0:T(8,128)(2,1)S(1)}, u32[]{:S(2)}, u32[]{:S(2)}) %all-to-all-start.7) | async-done | bytes 262176 | tf_op jit(solution)/shard_map/all_to_all | solution.py:30
  188.8 1.5 collective-permute-start.11
  191.5 1.8 shard_map.144
  (80 shorter events, 24.1 us)
Async XLA Ops:
  2.2 16.1 %all-to-all-start = ((bf16[16,72,128]{2,1,0:T(8,128)(2,1)}), bf16[16,72,128]{2,1,0:T(8,128)(2,1)S(1)}, u32[]{:S(2)}, u32[]{:S(2)}) async-start(bf16[16,72,128]{2,1,0:T(8,128)(2,1)} %shard_map.131), calls=%async_computation | async-start | bytes 589824 | tf_op jit(solution)/shard_map/all_to_all | solution.py:30
  10.6 4.9 %copy-start.14 = (bf16[2,1,64,128]{3,2,1,0:T(8,128)(2,1)S(1)}, bf16[2,1,64,128]{3,2,1,0:T(8,128)(2,1)}, u32[]{:S(2)}) copy-start(bf16[2,1,64,128]{3,2,1,0:T(8,128)(2,1)} %rhs_ref.3) | copy-start | bytes 98308
  10.6 11.0 %copy-start.13 = (bf16[1,2,1,64,128]{4,3,2,1,0:T(8,128)(2,1)S(1)}, bf16[1,2,1,64,128]{4,3,2,1,0:T(8,128)(2,1)}, u32[]{:S(2)}) copy-start(bf16[1,2,1,64,128]{4,3,2,1,0:T(8,128)(2,1)} %rhs_ref.4) | copy-start | bytes 98308
  10.6 20.2 %copy-start.1 = (bf16[1,128,4096]{2,1,0:T(8,128)(2,1)S(1)}, bf16[1,128,4096]{2,1,0:T(8,128)(2,1)}, u32[]{:S(2)}) copy-start(bf16[1,128,4096]{2,1,0:T(8,128)(2,1)} %update_ref.3) | copy-start | bytes 3145732
  18.3 3.3 %collective-permute-start = (bf16[16,72,128]{2,1,0:T(8,128)(2,1)S(1)}, bf16[16,72,128]{2,1,0:T(8,128)(2,1)S(1)}, u32[]{:S(2)}, u32[]{:S(2)}) collective-permute-start(bf16[16,72,128]{2,1,0:T(8,128)(2,1)S(1)} %all-to-all-done.own_ref), channel_id=1, source_target_pairs={{0,1},{1,0},{2,3},{3,2},{4,5},{5,4},{6,7},{7,6},{8,9},{9,8},{10,11... | collective-permute-start | bytes 884744 | tf_op jit(solution)/shard_map/ppermute | solution.py:26
  24.2 13.4 %all-to-all-start.1 = ((bf16[16,64,128]{2,1,0:T(8,128)(2,1)}), bf16[16,64,128]{2,1,0:T(8,128)(2,1)}, u32[]{:S(2)}, u32[]{:S(2)}) async-start(bf16[16,64,128]{2,1,0:T(8,128)(2,1)} %copy-done.10), calls=%async_computation.1 | async-start | bytes 524288 | tf_op jit(solution)/shard_map/all_to_all | solution.py:30
  30.0 5.0 %collective-permute-start.1 = (bf16[64,128]{1,0:T(8,128)(2,1)}, bf16[64,128]{1,0:T(8,128)(2,1)S(1)}, u32[]{:S(2)}, u32[]{:S(2)}) collective-permute-start(bf16[64,128]{1,0:T(8,128)(2,1)} %get-tuple-element.81), channel_id=1, source_target_pairs={{0,1},{1,0},{2,3},{3,2},{4,5},{5,4},{6,7},{7,6},{8,9},{9,8},{10,11... | collective-permute-start | bytes 49160 | tf_op jit(solution)/shard_map/ppermute | solution.py:26
  37.6 33.9 %copy-start.17 = (bf16[64,128]{1,0:T(8,128)(2,1)S(1)}, bf16[64,128]{1,0:T(8,128)(2,1)}, u32[]{:S(2)}) copy-start(bf16[64,128]{1,0:T(8,128)(2,1)} %copy-done.16) | copy-start | bytes 49156
  37.6 14.1 %collective-permute-start.2 = (bf16[16,64,128]{2,1,0:T(8,128)(2,1)}, bf16[16,64,128]{2,1,0:T(8,128)(2,1)S(1)}, u32[]{:S(2)}, u32[]{:S(2)}) collective-permute-start(bf16[16,64,128]{2,1,0:T(8,128)(2,1)} %all-to-all-done.1.own_ref), channel_id=1, source_target_pairs={{0,1},{1,0},{2,3},{3,2},{4,5},{5,4},{6,7},{7,6},{8,9},{9,8},{10,11... | collective-permute-start | bytes 786440 | tf_op jit(solution)/shard_map/ppermute | solution.py:26
  50.6 92.0 %collective-permute-start.7 = (bf16[16384,128]{1,0:T(8,128)(2,1)}, bf16[16384,128]{1,0:T(8,128)(2,1)}, u32[]{:S(2)}, u32[]{:S(2)}) collective-permute-start(bf16[16384,128]{1,0:T(8,128)(2,1)} %shard_map.138.own_ref), channel_id=1, source_target_pairs={{0,1},{1,0},{2,3},{3,2},{4,5},{5,4},{6,7},{7,6},{8,9},{9,8},{10,11... | collective-permute-start | bytes 12582920 | tf_op jit(solution)/shard_map/ppermute | solution.py:26
  50.8 20.6 %collective-permute-start.3 = (bf16[64,8192]{1,0:T(8,128)(2,1)S(1)}, bf16[64,8192]{1,0:T(8,128)(2,1)}, u32[]{:S(2)}, u32[]{:S(2)}) collective-permute-start(bf16[64,8192]{1,0:T(8,128)(2,1)S(1)} %slice_bitcast_fusion.3.lower_ref), channel_id=1, source_target_pairs={{0,1},{1,0},{2,3},{3,2},{4,5},{5,4},{6,7},{7,6},{8,9},{9,8},{10,11... | collective-permute-start | bytes 3145736 | tf_op jit(solution)/shard_map/ppermute | solution.py:26
  51.2 20.3 %collective-permute-start.4 = (bf16[64,8192]{1,0:T(8,128)(2,1)}, bf16[64,8192]{1,0:T(8,128)(2,1)}, u32[]{:S(2)}, u32[]{:S(2)}) collective-permute-start(bf16[64,8192]{1,0:T(8,128)(2,1)} %get-tuple-element.85.low_own_ref), channel_id=1, source_target_pairs={{0,1},{1,0},{2,3},{3,2},{4,5},{5,4},{6,7},{7,6},{8,9},{9,8},{10,11... | collective-permute-start | bytes 3145736 | tf_op jit(solution)/shard_map/ppermute | solution.py:26
  51.4 20.1 %collective-permute-start.5 = (bf16[64,8192]{1,0:T(8,128)(2,1)S(1)}, bf16[64,8192]{1,0:T(8,128)(2,1)}, u32[]{:S(2)}, u32[]{:S(2)}) collective-permute-start(bf16[64,8192]{1,0:T(8,128)(2,1)S(1)} %get-tuple-element.86.own_ref), channel_id=1, source_target_pairs={{0,1},{1,0},{2,3},{3,2},{4,5},{5,4},{6,7},{7,6},{8,9},{9,8},{10,11... | collective-permute-start | bytes 3145736 | tf_op jit(solution)/shard_map/ppermute | solution.py:26
  51.7 19.8 %collective-permute-start.6 = (bf16[64,8192]{1,0:T(8,128)(2,1)}, bf16[64,8192]{1,0:T(8,128)(2,1)}, u32[]{:S(2)}, u32[]{:S(2)}) collective-permute-start(bf16[64,8192]{1,0:T(8,128)(2,1)} %get-tuple-element.87.top_own_ref), channel_id=1, source_target_pairs={{0,1},{1,0},{2,3},{3,2},{4,5},{5,4},{6,7},{7,6},{8,9},{9,8},{10,11... | collective-permute-start | bytes 3145736 | tf_op jit(solution)/shard_map/ppermute | solution.py:26
  55.6 15.9 %all-to-all-start.2 = ((bf16[128,4,128]{2,1,0:T(4,128)(2,1)}), bf16[128,4,128]{2,1,0:T(4,128)(2,1)S(1)}, u32[]{:S(2)}, u32[]{:S(2)}) async-start(bf16[128,4,128]{2,1,0:T(4,128)(2,1)} %bitcast.7), calls=%async_computation.2 | async-start | bytes 262144 | tf_op jit(solution)/shard_map/all_to_all | solution.py:30
  97.2 45.4 %copy-start.2 = (bf16[64,8192]{1,0:T(8,128)(2,1)S(1)}, bf16[64,8192]{1,0:T(8,128)(2,1)}, u32[]{:S(2)}) copy-start(bf16[64,8192]{1,0:T(8,128)(2,1)} %get-tuple-element.85.low_own_ref) | copy-start | bytes 3145732
  97.2 45.4 %copy-start.3 = (bf16[64,8192]{1,0:T(8,128)(2,1)S(1)}, bf16[64,8192]{1,0:T(8,128)(2,1)}, u32[]{:S(2)}) copy-start(bf16[64,8192]{1,0:T(8,128)(2,1)} %get-tuple-element.87.top_own_ref) | copy-start | bytes 3145732
  142.6 25.4 %copy-start = (bf16[16384,128]{1,0:T(8,128)(2,1)S(1)}, bf16[16384,128]{1,0:T(8,128)(2,1)}, u32[]{:S(2)}) copy-start(bf16[16384,128]{1,0:T(8,128)(2,1)} %shard_map.138.own_ref) | copy-start | bytes 12582916
  168.0 8.1 %copy-start.9 = (bf16[1,2,1,64,4096]{4,3,2,1,0:T(8,128)(2,1)S(1)}, bf16[1,2,1,64,4096]{4,3,2,1,0:T(8,128)(2,1)}, u32[]{:S(2)}) copy-start(bf16[1,2,1,64,4096]{4,3,2,1,0:T(8,128)(2,1)} %upper_ref.1) | copy-start | bytes 3145732
  171.8 4.3 %collective-permute-start.8 = (f32[64,128]{1,0:T(8,128)S(1)}, f32[64,128]{1,0:T(8,128)S(1)}, u32[]{:S(2)}, u32[]{:S(2)}) collective-permute-start(f32[64,128]{1,0:T(8,128)S(1)} %get-tuple-element.105), channel_id=1, source_target_pairs={{0,1},{1,0},{2,3},{3,2},{4,5},{5,4},{6,7},{7,6},{8,9},{9,8},{10,11... | collective-permute-start | bytes 98312 | tf_op jit(solution)/shard_map/ppermute | solution.py:26
  177.0 4.2 %collective-permute-start.10 = (bf16[64,128]{1,0:T(8,128)(2,1)S(1)}, bf16[64,128]{1,0:T(8,128)(2,1)S(1)}, u32[]{:S(2)}, u32[]{:S(2)}) collective-permute-start(bf16[64,128]{1,0:T(8,128)(2,1)S(1)} %slice_bitcast_fusion.4), channel_id=1, source_target_pairs={{0,1},{1,0},{2,3},{3,2},{4,5},{5,4},{6,7},{7,6},{8,9},{9,8},{10,11... | collective-permute-start | bytes 49160 | tf_op jit(solution)/shard_map/ppermute | solution.py:26
  177.4 11.4 %all-to-all-start.7 = ((bf16[16,64,128]{2,1,0:T(8,128)(2,1)}), bf16[16,64,128]{2,1,0:T(8,128)(2,1)S(1)}, u32[]{:S(2)}, u32[]{:S(2)}) async-start(bf16[16,64,128]{2,1,0:T(8,128)(2,1)} %get-tuple-element.111.copies_ref), calls=%async_computation.7 | async-start | bytes 524288 | tf_op jit(solution)/shard_map/all_to_all | solution.py:30
  180.9 1.3 collective-permute-start.9
  188.8 2.7 %collective-permute-start.11 = (bf16[16,64,128]{2,1,0:T(8,128)(2,1)S(1)}, bf16[16,64,128]{2,1,0:T(8,128)(2,1)S(1)}, u32[]{:S(2)}, u32[]{:S(2)}) collective-permute-start(bf16[16,64,128]{2,1,0:T(8,128)(2,1)S(1)} %all-to-all-done.7.own_ref), channel_id=1, source_target_pairs={{0,1},{1,0},{2,3},{3,2},{4,5},{5,4},{6,7},{7,6},{8,9},{9,8},{10,11... | collective-permute-start | bytes 786440 | tf_op jit(solution)/shard_map/ppermute | solution.py:26
  (12 other events, 9.9 us)

commit v6 on v5

--- a/solution.py
+++ b/solution.py
@@ -99,11 +99,7 @@
         out_ref[j, rows : rows + 8] = marks
 
 
-def turn_kernel(core_ref, rhs_ref, lower_ref, kept_ref, given_ref, low_ref, sem):
-    copy = pltpu.make_async_copy(
-        lower_ref.at[0, 1, 0, :, pl.ds(0, low_ref.shape[1])], low_ref, sem
-    )
-    copy.start()
+def turn_kernel(core_ref, rhs_ref, kept_ref, given_ref):
     both = jnp.concatenate(
         [rhs_ref[0, 0].astype(F32).T, rhs_ref[1, 0].astype(F32).T], axis=1
     ).astype(BF16)
@@ -119,7 +115,19 @@
         kept_ref[...] = both[half:]
         given_ref[...] = both[:half]
 
-    copy.wait()
+
+def extract_kernel(lower_ref, inverse_ref, upper_ref, out_ref, sems):
+    kr = out_ref.shape[2]
+    copies = [
+        pltpu.make_async_copy(lower_ref.at[1, 0, :, pl.ds(0, kr)], out_ref.at[0], sems.at[0]),
+        pltpu.make_async_copy(inverse_ref.at[1, 0], out_ref.at[1], sems.at[1]),
+        pltpu.make_async_copy(inverse_ref.at[0, 0], out_ref.at[2], sems.at[2]),
+        pltpu.make_async_copy(upper_ref.at[0, 0, :, pl.ds(kr, kr)], out_ref.at[3], sems.at[3]),
+    ]
+    for copy in copies:
+        copy.start()
+    for copy in copies:
+        copy.wait()
 
 
 def advance_kernel(core_ref, own_ref, other_ref, low_ref, rhs_ref, out_ref):
@@ -135,8 +143,8 @@
 
 
 def aside_kernel(
-    rows, kr, core_ref, own_ref, other_ref, update_ref, inverse_ref,
-    part_ref, z0_ref, index_ref, repeats_ref, low_ref, diag_ref, sems
+    rows, kr, core_ref, own_ref, other_ref, update_ref, inverse_ref, owner_ref, slot_ref,
+    part_ref, z0_ref, index_ref, repeats_ref, select_ref, targets_ref, low_ref, diag_ref, sems
 ):
     kc = low_ref.shape[1]
     copies = [
@@ -145,6 +153,22 @@
     ]
     for copy in copies:
         copy.start()
+
+    held = owner_ref.shape[1]
+    owner = owner_ref[...].astype(F32)
+    owners = jnp.broadcast_to(owner, (held, held))
+    above = lax.broadcasted_iota(jnp.int32, (held, held), 0) < lax.broadcasted_iota(
+        jnp.int32, (held, held), 1
+    )
+    same = jnp.where((owners == owners.T) & above, 1.0, 0.0)
+    place = owner * 2.0 + jnp.sum(same, axis=0, keepdims=True)
+    row = lax.broadcasted_iota(jnp.int32, (select_ref.shape[0], held), 0)
+    wanted = (row // 8 * 4 + row % 4).astype(F32)
+    select_ref[...] = jnp.where(wanted == place, 1.0, 0.0).astype(BF16)
+    slot = slot_ref[...]
+    target = slot // rows * (2 * rows) + owner_ref[...] % 2 * rows + slot % rows + 1
+    targets_ref[...] = jnp.broadcast_to(target.astype(F32), (held, held)).T.astype(BF16)
+
 
     def work(first, second):
         for j in range(own_ref.shape[0]):
@@ -172,52 +196,31 @@
 
 
 def contribute_kernel(
-    core_ref, own_ref, other_ref, update_ref, part_ref, owner_ref, slot_ref, out_ref, high_ref, sem
+    core_ref, own_ref, other_ref, update_ref, inverse_ref, part_ref, select_ref, targets_ref,
+    out_ref, z1_ref, high_ref, diag_ref, sems
 ):
     kc = high_ref.shape[1]
-    copy = pltpu.make_async_copy(update_ref.at[0, :, pl.ds(kc, kc)], high_ref, sem)
-    copy.start()
+    load = pltpu.make_async_copy(update_ref.at[0, :, pl.ds(kc, kc)], high_ref, sems.at[0])
+    later = pltpu.make_async_copy(inverse_ref.at[0, 1, 0], diag_ref, sems.at[1])
+    load.start()
+    later.start()
     rows = own_ref.shape[1]
-    held = owner_ref.shape[1]
-    owner = owner_ref[...].astype(F32)
-    owners = jnp.broadcast_to(owner, (held, held))
-    above = lax.broadcasted_iota(jnp.int32, (held, held), 0) < lax.broadcasted_iota(
-        jnp.int32, (held, held), 1
-    )
-    same = jnp.where((owners == owners.T) & above, 1.0, 0.0)
-    place = owner * 2.0 + jnp.sum(same, axis=0, keepdims=True)
-    row = lax.broadcasted_iota(jnp.int32, (out_ref.shape[0], held), 0)
-    wanted = (row // 8 * 4 + row % 4).astype(F32)
-    select = jnp.where(wanted == place, 1.0, 0.0).astype(BF16)
-    slot = slot_ref[...]
-    target = slot // rows * (2 * rows) + owner_ref[...] % 2 * rows + slot % rows + 1
-    targets = jnp.broadcast_to(target.astype(F32), (held, held)).T[:, :rows].astype(BF16)
-
-    copy.wait()
+    load.wait()
 
     def work(first, second):
         contribution = -(part_ref[...] + plane_dot(high_ref, first, second, rows))
         contribution = contribution.astype(BF16)
         half = contribution.shape[1] // 2
+        targets = targets_ref[:, :half]
         source = jnp.concatenate(
             [contribution[:, :half], targets, contribution[:, half:], targets], axis=1
         )
-        both = jnp.dot(select, source, preferred_element_type=F32)
+        both = jnp.dot(select_ref[...], source, preferred_element_type=F32)
         lanes = 2 * half
         upper = lax.broadcasted_iota(jnp.int32, (both.shape[0], lanes), 0) % 8 >= 4
         out_ref[...] = jnp.where(upper, both[:, lanes:], both[:, :lanes]).astype(BF16)
-
-    by_core(core_ref, own_ref, other_ref, work)
-
-
-def diagonal_kernel(core_ref, own_ref, other_ref, inverse_ref, z1_ref, diag_ref, sem):
-    copy = pltpu.make_async_copy(inverse_ref.at[0, 1, 0], diag_ref, sem)
-    copy.start()
-    copy.wait()
-
-    def work(first, second):
-        total = plane_dot(diag_ref, first, second, own_ref.shape[1])
-        z1_ref[...] = total.astype(BF16).astype(F32)
+        later.wait()
+        z1_ref[...] = plane_dot(diag_ref, first, second, rows).astype(BF16).astype(F32)
 
     by_core(core_ref, own_ref, other_ref, work)
 
@@ -362,49 +365,20 @@
         copies_ref[j] = value
 
 
-def first_product_kernel(
-    core_ref, blocks_ref, lower_ref, other_ref, base_ref, copies_ref, held_ref, sems
-):
-    kr = held_ref.shape[2]
-    chips = blocks_ref.shape[0]
-    steps = sems.shape[0]
-    width, span = kr // steps, chips // steps
-    copies = []
-    for i in range(steps):
-        columns = pl.ds(i * width, width)
-        pairs = [
-            (lower_ref.at[:, columns], held_ref.at[0, :, columns]),
-            (other_ref.at[:, columns], held_ref.at[1, :, columns]),
-        ]
-        copies.append(
-            [pltpu.make_async_copy(a, b, sems.at[i, n]) for n, (a, b) in enumerate(pairs)]
-        )
-    for group in copies:
-        for copy in group:
-            copy.start()
-    total = base_ref[...]
-    for i, group in enumerate(copies):
-        for copy in group:
-            copy.wait()
-        term = pair_dot(
-            blocks_ref, i * span, (i + 1) * span, against(held_ref.at[0], held_ref.at[1])
-        )
-        total = total - ordered(core_ref, term)
+def product_kernel(which, subtract, core_ref, blocks_ref, own_ref, other_ref, *refs):
+    copies_ref = refs[-1]
+    rights = against(own_ref.at[which], other_ref.at[which])
+    total = ordered(core_ref, pair_dot(blocks_ref, 0, blocks_ref.shape[0], rights))
+    if subtract:
+        total = refs[0][...] - total
     write_copies(copies_ref, total.astype(BF16))
 
 
-def product_kernel(core_ref, blocks_ref, own_ref, other_ref, copies_ref):
-    total = pair_dot(blocks_ref, 0, blocks_ref.shape[0], against(own_ref, other_ref))
-    write_copies(copies_ref, ordered(core_ref, total).astype(BF16))
-
-
-def last_product_kernel(
-    core_ref, r0_ref, low_own_ref, low_other_ref, x1_ref, top_own_ref, top_other_ref, copies_ref
-):
+def last_product_kernel(core_ref, r0_ref, x1_ref, own_ref, other_ref, copies_ref):
     chips = x1_ref.shape[0]
-    diagonal = pair_dot(r0_ref, 0, chips, against(low_own_ref, low_other_ref))
+    diagonal = pair_dot(r0_ref, 0, chips, against(own_ref.at[2], other_ref.at[2]))
     diagonal = diagonal.astype(BF16).astype(F32)
-    total = diagonal - pair_dot(x1_ref, 0, chips, against(top_own_ref, top_other_ref))
+    total = diagonal - pair_dot(x1_ref, 0, chips, against(own_ref.at[3], other_ref.at[3]))
     write_copies(copies_ref, ordered(core_ref, total).astype(BF16))
 
 
@@ -428,11 +402,7 @@
     theirs_ref[...] = total[:, width:]
 
 
-def settle_kernel(core_ref, mine_ref, got_ref, z0_ref, z1_ref, upper_ref,
-                  copies_ref, rest_ref, top_ref, sem):
-    width = top_ref.shape[1]
-    copy = pltpu.make_async_copy(upper_ref.at[0, 0, 0, :, pl.ds(width, width)], top_ref, sem)
-    copy.start()
+def settle_kernel(core_ref, mine_ref, got_ref, z0_ref, z1_ref, copies_ref, rest_ref):
     stripe = z0_ref.shape[0]
 
     def work(first, second):
@@ -441,7 +411,6 @@
         write_copies(copies_ref, (z1_ref[...] - both[stripe:]).astype(BF16))
 
     by_core(core_ref, mine_ref, got_ref, work)
-    copy.wait()
 
 
 def closing_kernel(core_ref, own_ref, other_ref, top_ref, rest_ref, copies_ref, out_ref):
@@ -475,6 +444,7 @@
     half = rhs // 2
     kc = child_inverse.shape[-1]
     kr = root_inverse.shape[-1]
+    nc = child_lower.shape[-1]
     held = update_slot.shape[1]
     owner = update_owner.reshape(1, held)
     slot = update_slot
@@ -486,22 +456,21 @@
         opening_kernel, (child_rhs, owner, slot), [VMEM] * 3,
         like((planes, stripe + 8, rhs)), VMEM,
     )
-    opened, root_rhs, child_lower, root_lower, root_inverse, root_upper = tie(
-        (opened, root_rhs, child_lower, root_lower, root_inverse, root_upper)
+    opened, root_rhs, root_lower, root_inverse, root_upper, child_lower, child_upper = tie(
+        (opened, root_rhs, root_lower, root_inverse, root_upper, child_lower, child_upper)
     )
     own_first = spread(opened, PLANE)
-    kept, given, low = kernel_call(
-        turn_kernel, (core, root_rhs, child_lower), [SMEM, VMEM, HBM],
-        [like((half, rhs)), like((half, rhs)), pltpu.VMEM((stripe, kc), BF16)], [VMEM] * 3,
-        scratch=[DMA], limit=2, moved=MIB,
-    )
-    own = [
-        rows_of(root_lower, 1, 0, kr),
-        rows_of(root_inverse, 0, 0, kr),
-        rows_of(root_inverse, 1, 0, kr),
-        rows_of(root_upper, 0, kr, 2 * kr),
-    ]
-    own_first, own, kept, given, low = tie((own_first, own, kept, given, low))
+    kept, given = kernel_call(
+        turn_kernel, (core, root_rhs), [SMEM, VMEM], [like((half, rhs))] * 2, [VMEM] * 2,
+        limit=2, moved=MIB,
+    )
+    low = rows_of(child_lower, 1, 0, kc)
+    top = rows_of(child_upper, 0, kc, nc)
+    own = kernel_call(
+        extract_kernel, (root_lower, root_inverse, root_upper), [HBM] * 3,
+        like((4, stripe, kr)), HBM, scratch=[DMA((4,))], limit=62, moved=8 * MIB,
+    )
+    own_first, own, kept, given, low, top = tie((own_first, own, kept, given, low, top))
     other_first = swap(own_first)
     y1_copies = kernel_call(
         advance_kernel, (core, own_first, other_first, low, child_rhs), [SMEM] + [VMEM] * 4,
@@ -510,68 +479,66 @@
     y1_copies, own, given = tie((y1_copies, own, given))
     own_second = spread(y1_copies, PLANE)
 
-    lower_other, low_other, high_other, upper_other = [swap(m) for m in own]
-    got = swap(given)
-    part, z0c, index, repeats = kernel_call(
+    part, z0c, index, repeats, select, targets = kernel_call(
         functools.partial(aside_kernel, stripe, kr),
-        (core, own_first, other_first, child_update, child_inverse),
-        [SMEM, VMEM, VMEM, HBM, HBM],
+        (core, own_first, other_first, child_update, child_inverse, owner, slot),
+        [SMEM, VMEM, VMEM, HBM, HBM, VMEM, VMEM],
         [
             like((held, rhs), F32),
             like((stripe, rhs), F32),
             like((2 * planes, held), jnp.int32),
             like((2 * planes, held), jnp.int32),
+            like((devices * 4, held)),
+            like((held, held)),
         ],
-        [VMEM] * 4,
+        [VMEM] * 6,
         scratch=[pltpu.VMEM((held, kc), BF16), pltpu.VMEM((stripe, kc), BF16), DMA((2,))],
         limit=4, moved=2 * MIB,
     )
     index, repeats = index.reshape(-1), repeats[:, 0]
-    own_second, part, z0c, index, repeats, got = tie(
-        (own_second, part, z0c, index, repeats, got)
+    got = swap(given)
+    own_second, part, z0c, index, repeats, select, targets, got = tie(
+        (own_second, part, z0c, index, repeats, select, targets, got)
     )
     other_second = swap(own_second)
 
-    packed = kernel_call(
-        contribute_kernel, (core, own_second, other_second, child_update, part, owner, slot),
-        [SMEM, VMEM, VMEM, HBM] + [VMEM] * 3, like((devices * 4, rhs)), VMEM,
-        scratch=[pltpu.VMEM((held, kc), BF16), DMA], limit=4, moved=MIB,
-    )
+    packed, z1c = kernel_call(
+        contribute_kernel,
+        (core, own_second, other_second, child_update, child_inverse, part, select, targets),
+        [SMEM, VMEM, VMEM, HBM, HBM] + [VMEM] * 3,
+        [like((devices * 4, rhs)), like((stripe, rhs), F32)], [VMEM] * 2,
+        scratch=[pltpu.VMEM((held, kc), BF16), pltpu.VMEM((stripe, kc), BF16), DMA((2,))],
+        limit=4, moved=MIB,
+    )
+    packed, z1c, index, repeats = tie((packed, z1c, index, repeats))
     arrived = spread(packed.reshape(devices, 4, rhs), ALL)
-    z1c = kernel_call(
-        diagonal_kernel, (core, own_second, other_second, child_inverse),
-        [SMEM, VMEM, VMEM, HBM], like((stripe, rhs), F32), VMEM,
-        scratch=[pltpu.VMEM((stripe, kc), BF16), DMA], limit=2, moved=MIB,
-    )
-    arrived, z1c, lower_other, low_other, high_other, upper_other = tie(
-        (arrived, z1c, lower_other, low_other, high_other, upper_other)
-    )
+    summed = build_coupling(index, repeats, child_coupling, 2 * kr)
+    arrived, summed, own = tie((arrived, summed, own))
 
     r0_copies, right = kernel_call(
         unpack_kernel, (core, arrived.reshape(devices * 4, rhs), kept, got), [SMEM] + [VMEM] * 3,
         [like((cubes, half, rhs)), like((half, rhs), F32)], [VMEM] * 2, limit=4, moved=MIB,
     )
-    r0 = spread(r0_copies, CUBE)
-    summed = build_coupling(index, repeats, child_coupling, 2 * kr)
+    other = swap(own)
+    whole = (cubes, half, rhs)
+    work = dict(limit=4, flops=2 * cubes * half * rhs * rhs, moved=4 * MIB)
+    r0, other = tie((spread(r0_copies, CUBE), other))
+    r1_copies = kernel_call(
+        functools.partial(product_kernel, 0, True), (core, r0, own, other, right),
+        [SMEM] + [VMEM] * 4, like(whole), VMEM, **work,
+    )
+    r1_copies, summed = tie((r1_copies, summed))
     summed_other = swap(summed)
-    r0, summed = tie((r0, summed))
-    whole = (cubes, half, rhs)
-    r1_copies = kernel_call(
-        first_product_kernel, (core, r0, own[0], lower_other, right),
-        [SMEM, VMEM, HBM, HBM, VMEM], like(whole), VMEM,
-        scratch=[pltpu.VMEM((2, stripe, kr), BF16), DMA((4, 2))], limit=50, moved=4 * MIB,
-    )
     r1 = spread(r1_copies, CUBE)
     x1_copies = kernel_call(
-        product_kernel, (core, r1, own[2], high_other), [SMEM] + [VMEM] * 3, like(whole), VMEM,
-        limit=4, flops=2 * cubes * half * rhs * rhs, moved=4 * MIB,
+        functools.partial(product_kernel, 1, False), (core, r1, own, other),
+        [SMEM] + [VMEM] * 3, like(whole), VMEM, **work,
     )
     x1 = spread(x1_copies, CUBE)
     x1, summed_other = tie((x1, summed_other))
     x0_copies = kernel_call(
-        last_product_kernel, (core, r0, own[1], low_other, x1, own[3], upper_other),
-        [SMEM] + [VMEM] * 6, like(whole), VMEM,
-        limit=4, flops=4 * cubes * half * rhs * rhs, moved=7 * MIB,
+        last_product_kernel, (core, r0, x1, own, other), [SMEM] + [VMEM] * 4,
+        like(whole), VMEM, **work,
     )
     x0, x0_copies, x1_copies = tie((spread(x0_copies, CUBE), x0_copies, x1_copies))
 
@@ -580,11 +547,9 @@
         [like((half, 2 * stripe), F32)] * 2, [VMEM] * 2,
         limit=4, flops=8 * cubes * half * rhs * rhs, moved=10 * MIB,
     )
-    c1_copies, rest, top_child = kernel_call(
-        settle_kernel, (core, mine, swap(given), z0c, z1c, child_upper),
-        [SMEM] + [VMEM] * 4 + [HBM],
-        [like(piece), like((stripe, rhs), F32), pltpu.VMEM((stripe, kc), BF16)], [VMEM] * 3,
-        scratch=[DMA], limit=2, moved=MIB,
+    c1_copies, rest = kernel_call(
+        settle_kernel, (core, mine, swap(given), z0c, z1c), [SMEM] + [VMEM] * 4,
+        [like(piece), like((stripe, rhs), F32)], [VMEM] * 2, limit=2, moved=MIB,
     )
     c1_copies, x0_own, x1_own = tie((c1_copies, x0_copies[0], x1_copies[0]))
     own_c1 = spread(c1_copies, PLANE)
@@ -597,7 +562,7 @@
     root_solution = jnp.stack([own_rows(x0_own), own_rows(x1_own)])[:, None]
     own_c1, root_solution = tie((own_c1, root_solution))
     child_solution = kernel_call(
-        closing_kernel, (core, own_c1, swap(own_c1), top_child, rest, c1_copies),
+        closing_kernel, (core, own_c1, swap(own_c1), top, rest, c1_copies),
         [SMEM] + [VMEM] * 5, like(child_rhs.shape), VMEM, limit=2, moved=MIB,
     )
     return child_solution, root_solution

time: 194 us -> 308 us (1.59)
  Pallas kernels: 33.8 us -> 153 us
  local copies, waits for them, and re-layouts: 15.7 us -> 6.08 us
  blocking collectives: 87.2 us -> 92.7 us
  waiting for transfers between devices: 19.5 us -> 16.1 us
    pallas_call x14, Pallas kernels: 33.8 us -> 153 us  [kernel_call(): pl.pallas_call(body, out_shape=shapes, in_specs=specs, out_specs=out_spec...]
    unnamed x40 -> x18, local copies, waits for them, and re-layouts: 9.9 us -> 4.16 us
    all_to_all x4, blocking collectives: 87.2 us -> 92.7 us  [spread(): return lax.all_to_all(copies, axes, 0, 0)]
    reshape x2 -> x1, local copies, waits for them, and re-layouts: 4.84 us -> 1.07 us  [rows_of(): return lax.slice(array, start, stop).reshape(array.shape[-2], last - first)]
    all_to_all x4, waiting for transfers between devices: 15.4 us -> 11.7 us  [spread(): return lax.all_to_all(copies, axes, 0, 0)]
    ppermute x12 -> x9, starting transfers between devices: 11.6 us -> 12.4 us  [swap(): return lax.ppermute(array, 'c', [(0, 1), (1, 0)])]
  transfers between devices with their start and end apart: 16 -> 13, of which waited for: 7 -> 6; matrix products, arithmetic and copies ran while one was open for 3% -> 1% of each run, Pallas kernels for 11% -> 46%
where the time goes in v6:
time: 308 us; the launch traced here: 307 us
  Pallas kernels  153 us (50%)
  blocking collectives  92.7 us (30%)
  starting transfers between devices  37.4 us (12%)
  waiting for transfers between devices  16.1 us (5%)
  local copies, waits for them, and re-layouts  6.08 us (2%)
    pallas_call x14, Pallas kernels, kernel_call(): pl.pallas_call(body, out_shape=shapes, in_specs=specs, out_specs=out_spec...  153 us
    all_to_all x4, blocking collectives, spread(): return lax.all_to_all(copies, axes, 0, 0)  92.7 us
    all_to_all x4, starting transfers between devices, spread(): return lax.all_to_all(copies, axes, 0, 0)  25 us
    ppermute x9, starting transfers between devices, swap(): return lax.ppermute(array, 'c', [(0, 1), (1, 0)])  12.4 us
    all_to_all x4, waiting for transfers between devices, spread(): return lax.all_to_all(copies, axes, 0, 0)  11.7 us
  transfers between devices with their start and end apart: 13, of which 6 were waited for; matrix products, arithmetic and copies ran while one was open for 1% of the time, Pallas kernels for 46%

profile of v6, /device:TPU:1, one launch (start us, length us, event | category | flops | bytes accessed | tf_op | source)
XLA Modules:
  0.0 307.1 jit_solution(10784129760724384293)
XLA Ops:
  0.6 1.5 shard_map.131
  2.2 8.4 %all-to-all-start = ((bf16[16,72,128]{2,1,0:T(8,128)(2,1)}), bf16[16,72,128]{2,1,0:T(8,128)(2,1)S(1)}, u32[]{:S(2)}, u32[]{:S(2)}) async-start(bf16[16,72,128]{2,1,0:T(8,128)(2,1)} %shard_map.131), calls=%async_computation | async-start | bytes 589824 | tf_op jit(solution)/shard_map/all_to_all | solution.py:30
  11.6 128.2 %shard_map.132.own_ref = bf16[4,64,8192]{2,1,0:T(8,128)(2,1)} custom-call(bf16[2,1,64,16384]{3,2,1,0:T(8,128)(2,1)} %lower_ref, bf16[2,1,64,8192]{3,2,1,0:T(8,128)(2,1)} %inverse_ref.2, bf16[2,1,64,16384]{3,2,1,0:T(8,128)(2,1)} %upper_ref), custom_call_target="tpu_custom_call" | custom-call | bytes 8388608 | tf_op jit(solution)/shard_map/pallas_call | solution.py:50
  141.9 1.2 collective-permute-done.other_ref
  144.1 6.9 %all-to-all-start.1 = ((bf16[16,64,128]{2,1,0:T(8,128)(2,1)}), bf16[16,64,128]{2,1,0:T(8,128)(2,1)S(1)}, u32[]{:S(2)}, u32[]{:S(2)}) async-start(bf16[16,64,128]{2,1,0:T(8,128)(2,1)} %shard_map.134), calls=%async_computation.1 | async-start | bytes 524288 | tf_op jit(solution)/shard_map/all_to_all | solution.py:30
  153.6 5.0 %all-to-all-done.1.own_ref = bf16[16,64,128]{2,1,0:T(8,128)(2,1)S(1)} async-done(((bf16[16,64,128]{2,1,0:T(8,128)(2,1)}), bf16[16,64,128]{2,1,0:T(8,128)(2,1)S(1)}, u32[]{:S(2)}, u32[]{:S(2)}) %all-to-all-start.1) | async-done | bytes 262176 | tf_op jit(solution)/shard_map/all_to_all | solution.py:30
  158.6 1.9 collective-permute-start.2
  161.6 1.6 shard_map.136
  163.3 6.1 %all-to-all-start.2 = ((bf16[128,4,128]{2,1,0:T(4,128)(2,1)}), bf16[128,4,128]{2,1,0:T(4,128)(2,1)S(1)}, u32[]{:S(2)}, u32[]{:S(2)}) async-start(bf16[128,4,128]{2,1,0:T(4,128)(2,1)} %bitcast.5), calls=%async_computation.2 | async-start | bytes 262144 | tf_op jit(solution)/shard_map/all_to_all | solution.py:30
  169.4 11.1 %shard_map.137.own_ref = bf16[16384,128]{1,0:T(8,128)(2,1)} custom-call(s32[4096]{0:T(1024)} %bitcast.33, s32[32]{0:T(128)} %slice_reduce_fusion.repeats_ref, bf16[1,2,1,64,4096]{4,3,2,1,0:T(8,128)(2,1)} %coupling_ref.1), custom_call_target="tpu_custom_call" | custom-call | bytes 31457280 | tf_op jit(solution)/shard_map/pallas_call | solution.py:50
  182.1 27.4 %all_to_all.40.blocks_ref.r0_ref = bf16[64,64,128]{2,1,0:T(8,128)(2,1)S(1)} all-to-all(bf16[64,64,128]{2,1,0:T(8,128)(2,1)S(1)} %get-tuple-element.99), channel_id=1, replica_groups=mesh['y'=4,'x'=4,'z'=4,'c'=2] {'y','x','z'}, dimensions={0} | all-to-all | bytes 2097152 | tf_op jit(solution)/shard_map/all_to_all | solution.py:30
  209.6 2.2 copy-done
  212.8 1.2 copy-done.1
  214.0 1.9 collective-permute-start.4
  215.8 22.1 %all_to_all.41.blocks_ref = bf16[64,64,128]{2,1,0:T(8,128)(2,1)S(1)} all-to-all(bf16[64,64,128]{2,1,0:T(8,128)(2,1)S(1)} %shard_map.139), channel_id=1, replica_groups=mesh['y'=4,'x'=4,'z'=4,'c'=2] {'y','x','z'}, dimensions={0} | all-to-all | bytes 2097152 | tf_op jit(solution)/shard_map/all_to_all | solution.py:30
  239.0 21.3 %all_to_all.42.x1_ref = bf16[64,64,128]{2,1,0:T(8,128)(2,1)S(1)} all-to-all(bf16[64,64,128]{2,1,0:T(8,128)(2,1)S(1)} %shard_map.140), channel_id=1, replica_groups=mesh['y'=4,'x'=4,'z'=4,'c'=2] {'y','x','z'}, dimensions={0} | all-to-all | bytes 2097152 | tf_op jit(solution)/shard_map/all_to_all | solution.py:30
  260.3 1.7 shard_map.141
  262.1 21.8 %all_to_all.43.x0_ref = bf16[64,64,128]{2,1,0:T(8,128)(2,1)S(1)} all-to-all(bf16[64,64,128]{2,1,0:T(8,128)(2,1)S(1)} %shard_map.141), channel_id=1, replica_groups=mesh['y'=4,'x'=4,'z'=4,'c'=2] {'y','x','z'}, dimensions={0} | all-to-all | bytes 2097152 | tf_op jit(solution)/shard_map/all_to_all | solution.py:30
  283.9 1.6 shard_map.142
  285.5 3.4 %collective-permute-start.5 = (f32[64,128]{1,0:T(8,128)S(1)}, f32[64,128]{1,0:T(8,128)S(1)}, u32[]{:S(2)}, u32[]{:S(2)}) collective-permute-start(f32[64,128]{1,0:T(8,128)S(1)} %get-tuple-element.111), channel_id=1, source_target_pairs={{0,1},{1,0},{2,3},{3,2},{4,5},{5,4},{6,7},{7,6},{8,9},{9,8},{10,11... | collective-permute-start | bytes 98312 | tf_op jit(solution)/shard_map/ppermute | solution.py:26
  291.2 3.5 %all-to-all-start.7 = ((bf16[16,64,128]{2,1,0:T(8,128)(2,1)}), bf16[16,64,128]{2,1,0:T(8,128)(2,1)S(1)}, u32[]{:S(2)}, u32[]{:S(2)}) async-start(bf16[16,64,128]{2,1,0:T(8,128)(2,1)} %get-tuple-element.117.copies_ref), calls=%async_computation.7 | async-start | bytes 524288 | tf_op jit(solution)/shard_map/all_to_all | solution.py:30
  295.7 6.7 %all-to-all-done.7.own_ref = bf16[16,64,128]{2,1,0:T(8,128)(2,1)S(1)} async-done(((bf16[16,64,128]{2,1,0:T(8,128)(2,1)}), bf16[16,64,128]{2,1,0:T(8,128)(2,1)S(1)}, u32[]{:S(2)}, u32[]{:S(2)}) %all-to-all-start.7) | async-done | bytes 262176 | tf_op jit(solution)/shard_map/all_to_all | solution.py:30
  302.4 1.7 collective-permute-start.8
  305.3 1.8 shard_map.144
  (51 shorter events, 15.6 us)
Async XLA Ops:
  2.2 138.7 %all-to-all-start = ((bf16[16,72,128]{2,1,0:T(8,128)(2,1)}), bf16[16,72,128]{2,1,0:T(8,128)(2,1)S(1)}, u32[]{:S(2)}, u32[]{:S(2)}) async-start(bf16[16,72,128]{2,1,0:T(8,128)(2,1)} %shard_map.131), calls=%async_computation | async-start | bytes 589824 | tf_op jit(solution)/shard_map/all_to_all | solution.py:30
  10.6 0.8 copy-start.5
  11.5 131.6 %copy-start.4 = (bf16[1,2,1,64,128]{4,3,2,1,0:T(8,128)(2,1)S(1)}, bf16[1,2,1,64,128]{4,3,2,1,0:T(8,128)(2,1)}, u32[]{:S(2)}) copy-start(bf16[1,2,1,64,128]{4,3,2,1,0:T(8,128)(2,1)} %rhs_ref.4) | copy-start | bytes 98308
  11.5 140.2 %copy-start.2 = (bf16[1,128,4096]{2,1,0:T(8,128)(2,1)S(1)}, bf16[1,128,4096]{2,1,0:T(8,128)(2,1)}, u32[]{:S(2)}) copy-start(bf16[1,128,4096]{2,1,0:T(8,128)(2,1)} %update_ref.3) | copy-start | bytes 3145732
  11.5 140.2 %copy-start.3 = (bf16[1,2,1,64,2048]{4,3,2,1,0:T(8,128)(2,1)S(1)}, bf16[1,2,1,64,2048]{4,3,2,1,0:T(8,128)(2,1)}, u32[]{:S(2)}) copy-start(bf16[1,2,1,64,2048]{4,3,2,1,0:T(8,128)(2,1)} %inverse_ref.4) | copy-start | bytes 1572868
  11.6 140.2 %copy-start.7 = (s32[1,128,1]{1,2,0:T(1,128)S(1)}, s32[1,128,1]{1,2,0:T(1,128)}, u32[]{:S(2)}) copy-start(s32[1,128,1]{1,2,0:T(1,128)} %param.18) | copy-start | bytes 1540
  11.6 140.2 %copy-start.8 = (s32[1,128]{1,0:T(1,128)S(1)}, s32[1,128]{1,0:T(1,128)}, u32[]{:S(2)}) copy-start(s32[1,128]{1,0:T(1,128)} %slot_ref.3) | copy-start | bytes 1540
  140.9 2.3 collective-permute-start
  144.1 14.5 %all-to-all-start.1 = ((bf16[16,64,128]{2,1,0:T(8,128)(2,1)}), bf16[16,64,128]{2,1,0:T(8,128)(2,1)S(1)}, u32[]{:S(2)}, u32[]{:S(2)}) async-start(bf16[16,64,128]{2,1,0:T(8,128)(2,1)} %shard_map.134), calls=%async_computation.1 | async-start | bytes 524288 | tf_op jit(solution)/shard_map/all_to_all | solution.py:30
  151.0 2.6 collective-permute-start.1
  152.9 16.5 %copy-start.6 = (s32[32,128]{1,0:T(8,128)}, s32[32,128]{1,0:T(8,128)S(1)}, u32[]{:S(2)}) copy-start(s32[32,128]{1,0:T(8,128)S(1)} %get-tuple-element.79) | copy-start | bytes 49156
  158.6 3.1 %collective-permute-start.2 = (bf16[16,64,128]{2,1,0:T(8,128)(2,1)S(1)}, bf16[16,64,128]{2,1,0:T(8,128)(2,1)S(1)}, u32[]{:S(2)}, u32[]{:S(2)}) collective-permute-start(bf16[16,64,128]{2,1,0:T(8,128)(2,1)S(1)} %all-to-all-done.1.own_ref), channel_id=1, source_target_pairs={{0,1},{1,0},{2,3},{3,2},{4,5},{5,4},{6,7},{7,6},{8,9},{9,8},{10,11... | collective-permute-start | bytes 786440 | tf_op jit(solution)/shard_map/ppermute | solution.py:26
  163.3 17.3 %all-to-all-start.2 = ((bf16[128,4,128]{2,1,0:T(4,128)(2,1)}), bf16[128,4,128]{2,1,0:T(4,128)(2,1)S(1)}, u32[]{:S(2)}, u32[]{:S(2)}) async-start(bf16[128,4,128]{2,1,0:T(4,128)(2,1)} %bitcast.5), calls=%async_computation.2 | async-start | bytes 262144 | tf_op jit(solution)/shard_map/all_to_all | solution.py:30
  180.5 29.1 %collective-permute-start.3 = (bf16[4,64,8192]{2,1,0:T(8,128)(2,1)}, bf16[4,64,8192]{2,1,0:T(8,128)(2,1)S(1)}, u32[]{:S(2)}, u32[]{:S(2)}) collective-permute-start(bf16[4,64,8192]{2,1,0:T(8,128)(2,1)} %shard_map.132.own_ref), channel_id=1, source_target_pairs={{0,1},{1,0},{2,3},{3,2},{4,5},{5,4},{6,7},{7,6},{8,9},{9,8},{10,11... | collective-permute-start | bytes 12582920 | tf_op jit(solution)/shard_map/ppermute | solution.py:26
  209.6 2.2 copy-start
  211.8 2.2 copy-start.1
  214.0 46.4 %collective-permute-start.4 = (bf16[16384,128]{1,0:T(8,128)(2,1)S(1)}, bf16[16384,128]{1,0:T(8,128)(2,1)S(1)}, u32[]{:S(2)}, u32[]{:S(2)}) collective-permute-start(bf16[16384,128]{1,0:T(8,128)(2,1)S(1)} %copy-done.1), channel_id=1, source_target_pairs={{0,1},{1,0},{2,3},{3,2},{4,5},{5,4},{6,7},{7,6},{8,9},{9,8},{10,11... | collective-permute-start | bytes 12582920 | tf_op jit(solution)/shard_map/ppermute | solution.py:26
  285.5 4.3 %collective-permute-start.5 = (f32[64,128]{1,0:T(8,128)S(1)}, f32[64,128]{1,0:T(8,128)S(1)}, u32[]{:S(2)}, u32[]{:S(2)}) collective-permute-start(f32[64,128]{1,0:T(8,128)S(1)} %get-tuple-element.111), channel_id=1, source_target_pairs={{0,1},{1,0},{2,3},{3,2},{4,5},{5,4},{6,7},{7,6},{8,9},{9,8},{10,11... | collective-permute-start | bytes 98312 | tf_op jit(solution)/shard_map/ppermute | solution.py:26
  290.6 4.1 %collective-permute-start.6 = (bf16[64,128]{1,0:T(8,128)(2,1)S(1)}, bf16[64,128]{1,0:T(8,128)(2,1)S(1)}, u32[]{:S(2)}, u32[]{:S(2)}) collective-permute-start(bf16[64,128]{1,0:T(8,128)(2,1)S(1)} %slice_bitcast_fusion.3), channel_id=1, source_target_pairs={{0,1},{1,0},{2,3},{3,2},{4,5},{5,4},{6,7},{7,6},{8,9},{9,8},{10,11... | collective-permute-start | bytes 49160 | tf_op jit(solution)/shard_map/ppermute | solution.py:26
  291.0 3.9 %collective-permute-start.7 = (bf16[64,128]{1,0:T(8,128)(2,1)S(1)}, bf16[64,128]{1,0:T(8,128)(2,1)S(1)}, u32[]{:S(2)}, u32[]{:S(2)}) collective-permute-start(bf16[64,128]{1,0:T(8,128)(2,1)S(1)} %slice_bitcast_fusion.2), channel_id=1, source_target_pairs={{0,1},{1,0},{2,3},{3,2},{4,5},{5,4},{6,7},{7,6},{8,9},{9,8},{10,11... | collective-permute-start | bytes 49160 | tf_op jit(solution)/shard_map/ppermute | solution.py:26
  291.2 11.2 %all-to-all-start.7 = ((bf16[16,64,128]{2,1,0:T(8,128)(2,1)}), bf16[16,64,128]{2,1,0:T(8,128)(2,1)S(1)}, u32[]{:S(2)}, u32[]{:S(2)}) async-start(bf16[16,64,128]{2,1,0:T(8,128)(2,1)} %get-tuple-element.117.copies_ref), calls=%async_computation.7 | async-start | bytes 524288 | tf_op jit(solution)/shard_map/all_to_all | solution.py:30
  302.4 2.9 collective-permute-start.8

commit v7 on v6

--- a/solution.py
+++ b/solution.py
@@ -18,6 +18,7 @@
 HBM = pl.BlockSpec(memory_space=pltpu.HBM)
 DMA = pltpu.SemaphoreType.DMA
 MIB = 1 << 20
+FIRST = 50
 BATCH = 8
 tie = lax.optimization_barrier
 
@@ -114,20 +115,6 @@
     def _():
         kept_ref[...] = both[half:]
         given_ref[...] = both[:half]
-
-
-def extract_kernel(lower_ref, inverse_ref, upper_ref, out_ref, sems):
-    kr = out_ref.shape[2]
-    copies = [
-        pltpu.make_async_copy(lower_ref.at[1, 0, :, pl.ds(0, kr)], out_ref.at[0], sems.at[0]),
-        pltpu.make_async_copy(inverse_ref.at[1, 0], out_ref.at[1], sems.at[1]),
-        pltpu.make_async_copy(inverse_ref.at[0, 0], out_ref.at[2], sems.at[2]),
-        pltpu.make_async_copy(upper_ref.at[0, 0, :, pl.ds(kr, kr)], out_ref.at[3], sems.at[3]),
-    ]
-    for copy in copies:
-        copy.start()
-    for copy in copies:
-        copy.wait()
 
 
 def advance_kernel(core_ref, own_ref, other_ref, low_ref, rhs_ref, out_ref):
@@ -365,20 +352,50 @@
         copies_ref[j] = value
 
 
-def product_kernel(which, subtract, core_ref, blocks_ref, own_ref, other_ref, *refs):
-    copies_ref = refs[-1]
-    rights = against(own_ref.at[which], other_ref.at[which])
-    total = ordered(core_ref, pair_dot(blocks_ref, 0, blocks_ref.shape[0], rights))
-    if subtract:
-        total = refs[0][...] - total
-    write_copies(copies_ref, total.astype(BF16))
-
-
-def last_product_kernel(core_ref, r0_ref, x1_ref, own_ref, other_ref, copies_ref):
+def first_product_kernel(
+    core_ref, blocks_ref, lower_ref, other_ref, base_ref, copies_ref, held_ref, sems
+):
+    kr = held_ref.shape[2]
+    chips = blocks_ref.shape[0]
+    steps = sems.shape[0]
+    width, span = kr // steps, chips // steps
+    loads = []
+    for i in range(steps):
+        columns = pl.ds(i * width, width)
+        pairs = [
+            (lower_ref.at[1, 0, :, columns], held_ref.at[0, :, columns]),
+            (other_ref.at[:, columns], held_ref.at[1, :, columns]),
+        ]
+        loads.append(
+            [pltpu.make_async_copy(a, b, sems.at[i, n]) for n, (a, b) in enumerate(pairs)]
+        )
+    for group in loads:
+        for load in group:
+            load.start()
+    total = None
+    for i, group in enumerate(loads):
+        for load in group:
+            load.wait()
+        term = pair_dot(
+            blocks_ref, i * span, (i + 1) * span, against(held_ref.at[0], held_ref.at[1])
+        )
+        total = term if total is None else total + term
+    write_copies(copies_ref, (base_ref[...] - ordered(core_ref, total)).astype(BF16))
+
+
+def product_kernel(core_ref, blocks_ref, own_ref, other_ref, copies_ref):
+    rights = against(own_ref.at[1, 0], other_ref.at[1, 0])
+    total = pair_dot(blocks_ref, 0, blocks_ref.shape[0], rights)
+    write_copies(copies_ref, ordered(core_ref, total).astype(BF16))
+
+
+def last_product_kernel(
+    core_ref, r0_ref, x1_ref, own_ref, other_ref, upper_own_ref, upper_other_ref, copies_ref
+):
     chips = x1_ref.shape[0]
-    diagonal = pair_dot(r0_ref, 0, chips, against(own_ref.at[2], other_ref.at[2]))
+    diagonal = pair_dot(r0_ref, 0, chips, against(own_ref.at[0, 0], other_ref.at[0, 0]))
     diagonal = diagonal.astype(BF16).astype(F32)
-    total = diagonal - pair_dot(x1_ref, 0, chips, against(own_ref.at[3], other_ref.at[3]))
+    total = diagonal - pair_dot(x1_ref, 0, chips, against(upper_own_ref, upper_other_ref))
     write_copies(copies_ref, ordered(core_ref, total).astype(BF16))
 
 
@@ -466,17 +483,17 @@
     )
     low = rows_of(child_lower, 1, 0, kc)
     top = rows_of(child_upper, 0, kc, nc)
-    own = kernel_call(
-        extract_kernel, (root_lower, root_inverse, root_upper), [HBM] * 3,
-        like((4, stripe, kr)), HBM, scratch=[DMA((4,))], limit=62, moved=8 * MIB,
-    )
-    own_first, own, kept, given, low, top = tie((own_first, own, kept, given, low, top))
+    lower_own = rows_of(root_lower, 1, 0, kr)
+    upper_own = rows_of(root_upper, 0, kr, 2 * kr)
+    own_first, lower_own, upper_own, kept, given, low, top = tie(
+        (own_first, lower_own, upper_own, kept, given, low, top)
+    )
     other_first = swap(own_first)
     y1_copies = kernel_call(
         advance_kernel, (core, own_first, other_first, low, child_rhs), [SMEM] + [VMEM] * 4,
         like(piece), VMEM, limit=2, moved=MIB,
     )
-    y1_copies, own, given = tie((y1_copies, own, given))
+    y1_copies, given = tie((y1_copies, given))
     own_second = spread(y1_copies, PLANE)
 
     part, z0c, index, repeats, select, targets = kernel_call(
@@ -510,35 +527,37 @@
         scratch=[pltpu.VMEM((held, kc), BF16), pltpu.VMEM((stripe, kc), BF16), DMA((2,))],
         limit=4, moved=MIB,
     )
-    packed, z1c, index, repeats = tie((packed, z1c, index, repeats))
+    packed, z1c, lower_own = tie((packed, z1c, lower_own))
     arrived = spread(packed.reshape(devices, 4, rhs), ALL)
-    summed = build_coupling(index, repeats, child_coupling, 2 * kr)
-    arrived, summed, own = tie((arrived, summed, own))
+    lower_other = swap(lower_own)
 
     r0_copies, right = kernel_call(
         unpack_kernel, (core, arrived.reshape(devices * 4, rhs), kept, got), [SMEM] + [VMEM] * 3,
         [like((cubes, half, rhs)), like((half, rhs), F32)], [VMEM] * 2, limit=4, moved=MIB,
     )
-    other = swap(own)
+    r0_copies, index, repeats = tie((r0_copies, index, repeats))
+    summed = build_coupling(index, repeats, child_coupling, 2 * kr)
     whole = (cubes, half, rhs)
-    work = dict(limit=4, flops=2 * cubes * half * rhs * rhs, moved=4 * MIB)
-    r0, other = tie((spread(r0_copies, CUBE), other))
+    work = dict(flops=2 * cubes * half * rhs * rhs, moved=4 * MIB)
+    r0, summed, lower_other = tie((spread(r0_copies, CUBE), summed, lower_other))
     r1_copies = kernel_call(
-        functools.partial(product_kernel, 0, True), (core, r0, own, other, right),
-        [SMEM] + [VMEM] * 4, like(whole), VMEM, **work,
-    )
-    r1_copies, summed = tie((r1_copies, summed))
+        first_product_kernel, (core, r0, root_lower, lower_other, right),
+        [SMEM, VMEM, HBM, HBM, VMEM], like(whole), VMEM,
+        scratch=[pltpu.VMEM((2, stripe, kr), BF16), DMA((4, 2))], limit=FIRST, **work,
+    )
+    r1_copies, inverse, upper_own = tie((r1_copies, root_inverse, upper_own))
+    inverse_other, upper_other = swap(inverse), swap(upper_own)
+    r1, inverse_other, upper_other = tie((spread(r1_copies, CUBE), inverse_other, upper_other))
+    x1_copies = kernel_call(
+        product_kernel, (core, r1, root_inverse, inverse_other), [SMEM] + [VMEM] * 3,
+        like(whole), VMEM, limit=4, **work,
+    )
+    x1_copies, summed = tie((x1_copies, summed))
     summed_other = swap(summed)
-    r1 = spread(r1_copies, CUBE)
-    x1_copies = kernel_call(
-        functools.partial(product_kernel, 1, False), (core, r1, own, other),
-        [SMEM] + [VMEM] * 3, like(whole), VMEM, **work,
-    )
-    x1 = spread(x1_copies, CUBE)
-    x1, summed_other = tie((x1, summed_other))
+    x1, summed_other = tie((spread(x1_copies, CUBE), summed_other))
     x0_copies = kernel_call(
-        last_product_kernel, (core, r0, x1, own, other), [SMEM] + [VMEM] * 4,
-        like(whole), VMEM, **work,
+        last_product_kernel, (core, r0, x1, root_inverse, inverse_other, upper_own, upper_other),
+        [SMEM] + [VMEM] * 6, like(whole), VMEM, limit=4, **work,
     )
     x0, x0_copies, x1_copies = tie((spread(x0_copies, CUBE), x0_copies, x1_copies))
 

time: 308 us -> 177 us (0.57)
  Pallas kernels: 153 us -> 27.9 us
  blocking collectives: 92.7 us -> 65.1 us
  waiting for transfers between devices: 16.1 us -> 33.7 us
  starting transfers between devices: 37.4 us -> 42.5 us
    pallas_call x14 -> x13, Pallas kernels: 153 us -> 27.9 us  [kernel_call(): pl.pallas_call(body, out_shape=shapes, in_specs=specs, out_specs=out_spec...]
    all_to_all x4 -> x3, blocking collectives: 92.7 us -> 65.1 us  [spread(): return lax.all_to_all(copies, axes, 0, 0)]
    all_to_all x4 -> x5, waiting for transfers between devices: 11.7 us -> 29.3 us  [spread(): return lax.all_to_all(copies, axes, 0, 0)]
    ppermute x9 -> x11, starting transfers between devices: 12.4 us -> 16 us  [swap(): return lax.ppermute(array, 'c', [(0, 1), (1, 0)])]
    unnamed x18 -> x20, local copies, waits for them, and re-layouts: 4.16 us -> 0.79 us
    reshape x1 -> x2, local copies, waits for them, and re-layouts: 1.07 us -> 4.17 us  [rows_of(): return lax.slice(array, start, stop).reshape(array.shape[-2], last - first)]
    all_to_all x4 -> x5, starting transfers between devices: 25 us -> 26.6 us  [spread(): return lax.all_to_all(copies, axes, 0, 0)]
  transfers between devices with their start and end apart: 13 -> 16, of which waited for: 6 -> 9; matrix products, arithmetic and copies ran while one was open for 1% -> 3% of each run, Pallas kernels for 46% -> 8%
where the time goes in v7:
time: 177 us
  blocking collectives  65.1 us (37%)
  starting transfers between devices  42.5 us (24%)
  waiting for transfers between devices  33.7 us (19%)
  Pallas kernels  27.9 us (16%)
  local copies, waits for them, and re-layouts  5.81 us (3%)
    all_to_all x3, blocking collectives, spread(): return lax.all_to_all(copies, axes, 0, 0)  65.1 us
    all_to_all x5, waiting for transfers between devices, spread(): return lax.all_to_all(copies, axes, 0, 0)  29.3 us
    pallas_call x13, Pallas kernels, kernel_call(): pl.pallas_call(body, out_shape=shapes, in_specs=specs, out_specs=out_spec...  27.9 us
    all_to_all x5, starting transfers between devices, spread(): return lax.all_to_all(copies, axes, 0, 0)  26.6 us
    ppermute x11, starting transfers between devices, swap(): return lax.ppermute(array, 'c', [(0, 1), (1, 0)])  16 us
    ppermute x11, waiting for transfers between devices, swap(): return lax.ppermute(array, 'c', [(0, 1), (1, 0)])  4.41 us
    reshape x2, local copies, waits for them, and re-layouts, rows_of(): return lax.slice(array, start, stop).reshape(array.shape[-2], last - first)  4.17 us
  transfers between devices with their start and end apart: 16, of which 9 were waited for; matrix products, arithmetic and copies ran while one was open for 3% of the time, Pallas kernels for 8%

profile of v7, /device:TPU:1, one launch (start us, length us, event | category | flops | bytes accessed | tf_op | source)
XLA Modules:
  0.0 176.6 jit_solution(18207900010535278536)
XLA Ops:
  2.3 8.4 %all-to-all-start = ((bf16[16,72,128]{2,1,0:T(8,128)(2,1)}), bf16[16,72,128]{2,1,0:T(8,128)(2,1)S(1)}, u32[]{:S(2)}, u32[]{:S(2)}) async-start(bf16[16,72,128]{2,1,0:T(8,128)(2,1)} %shard_map.131), calls=%async_computation | async-start | bytes 589824 | tf_op jit(solution)/shard_map/all_to_all | solution.py:31
  11.7 3.1 %slice_bitcast_fusion = (bf16[64,8192]{1,0:T(8,128)(2,1)}, bf16[64,8192]{1,0:T(8,128)(2,1)}) fusion(bf16[2,1,64,16384]{3,2,1,0:T(8,128)(2,1)} %param.23, bf16[2,1,64,16384]{3,2,1,0:T(8,128)(2,1)} %lower_ref), kind=kLoop, calls=%fused_computation | loop fusion | bytes 4194304 | tf_op jit(solution)/shard_map/reshape | solution.py:43
  15.9 2.4 %all-to-all-done.own_ref = bf16[16,72,128]{2,1,0:T(8,128)(2,1)S(1)} async-done(((bf16[16,72,128]{2,1,0:T(8,128)(2,1)}), bf16[16,72,128]{2,1,0:T(8,128)(2,1)S(1)}, u32[]{:S(2)}, u32[]{:S(2)}) %all-to-all-start) | async-done | bytes 294944 | tf_op jit(solution)/shard_map/all_to_all | solution.py:31
  18.3 2.2 %collective-permute-start = (bf16[16,72,128]{2,1,0:T(8,128)(2,1)S(1)}, bf16[16,72,128]{2,1,0:T(8,128)(2,1)S(1)}, u32[]{:S(2)}, u32[]{:S(2)}) collective-permute-start(bf16[16,72,128]{2,1,0:T(8,128)(2,1)S(1)} %all-to-all-done.own_ref), channel_id=1, source_target_pairs={{0,1},{1,0},{2,3},{3,2},{4,5},{5,4},{6,7},{7,6},{8,9},{9,8},{10,11... | collective-permute-start | bytes 884744 | tf_op jit(solution)/shard_map/ppermute | solution.py:27
  22.7 3.5 %all-to-all-start.1 = ((bf16[16,64,128]{2,1,0:T(8,128)(2,1)}), bf16[16,64,128]{2,1,0:T(8,128)(2,1)S(1)}, u32[]{:S(2)}, u32[]{:S(2)}) async-start(bf16[16,64,128]{2,1,0:T(8,128)(2,1)} %shard_map.133), calls=%async_computation.1 | async-start | bytes 524288 | tf_op jit(solution)/shard_map/all_to_all | solution.py:31
  28.6 5.2 %all-to-all-done.1.own_ref = bf16[16,64,128]{2,1,0:T(8,128)(2,1)S(1)} async-done(((bf16[16,64,128]{2,1,0:T(8,128)(2,1)}), bf16[16,64,128]{2,1,0:T(8,128)(2,1)S(1)}, u32[]{:S(2)}, u32[]{:S(2)}) %all-to-all-start.1) | async-done | bytes 262176 | tf_op jit(solution)/shard_map/all_to_all | solution.py:31
  33.8 1.8 %collective-permute-start.2 = (bf16[16,64,128]{2,1,0:T(8,128)(2,1)S(1)}, bf16[16,64,128]{2,1,0:T(8,128)(2,1)S(1)}, u32[]{:S(2)}, u32[]{:S(2)}) collective-permute-start(bf16[16,64,128]{2,1,0:T(8,128)(2,1)S(1)} %all-to-all-done.1.own_ref), channel_id=1, source_target_pairs={{0,1},{1,0},{2,3},{3,2},{4,5},{5,4},{6,7},{7,6},{8,9},{9,8},{10,11... | collective-permute-start | bytes 786440 | tf_op jit(solution)/shard_map/ppermute | solution.py:27
  38.4 6.1 %all-to-all-start.2 = ((bf16[128,4,128]{2,1,0:T(4,128)(2,1)}), bf16[128,4,128]{2,1,0:T(4,128)(2,1)S(1)}, u32[]{:S(2)}, u32[]{:S(2)}) async-start(bf16[128,4,128]{2,1,0:T(4,128)(2,1)} %bitcast.7), calls=%async_computation.2 | async-start | bytes 262144 | tf_op jit(solution)/shard_map/all_to_all | solution.py:31
  45.7 8.7 %all-to-all-done.2 = bf16[128,4,128]{2,1,0:T(4,128)(2,1)S(1)} async-done(((bf16[128,4,128]{2,1,0:T(4,128)(2,1)}), bf16[128,4,128]{2,1,0:T(4,128)(2,1)S(1)}, u32[]{:S(2)}, u32[]{:S(2)}) %all-to-all-start.2) | async-done | bytes 131104 | tf_op jit(solution)/shard_map/all_to_all | solution.py:31
  55.9 4.9 %all-to-all-start.3 = ((bf16[64,64,128]{2,1,0:T(8,128)(2,1)}), bf16[64,64,128]{2,1,0:T(8,128)(2,1)S(1)}, u32[]{:S(2)}, u32[]{:S(2)}) async-start(bf16[64,64,128]{2,1,0:T(8,128)(2,1)} %get-tuple-element.101), calls=%async_computation.3 | async-start | bytes 2097152 | tf_op jit(solution)/shard_map/all_to_all | solution.py:31
  60.9 11.1 %shard_map.137.own_ref = bf16[16384,128]{1,0:T(8,128)(2,1)} custom-call(s32[4096]{0:T(1024)} %bitcast.37, s32[32]{0:T(128)} %slice_reduce_fusion.repeats_ref, bf16[1,2,1,64,4096]{4,3,2,1,0:T(8,128)(2,1)} %coupling_ref.1), custom_call_target="tpu_custom_call" | custom-call | bytes 31457280 | tf_op jit(solution)/shard_map/pallas_call | solution.py:51
  72.0 6.3 %all-to-all-done.3.blocks_ref.r0_ref = bf16[64,64,128]{2,1,0:T(8,128)(2,1)S(1)} async-done(((bf16[64,64,128]{2,1,0:T(8,128)(2,1)}), bf16[64,64,128]{2,1,0:T(8,128)(2,1)S(1)}, u32[]{:S(2)}, u32[]{:S(2)}) %all-to-all-start.3) | async-done | bytes 1048608 | tf_op jit(solution)/shard_map/all_to_all | solution.py:31
  78.3 2.8 %shard_map.138 = bf16[64,64,128]{2,1,0:T(8,128)(2,1)S(1)} custom-call(s32[1]{0:T(128)} %bitcast.core_ref, bf16[64,64,128]{2,1,0:T(8,128)(2,1)S(1)} %all-to-all-done.3.blocks_ref.r0_ref, bf16[2,1,64,16384]{3,2,1,0:T(8,128)(2,1)} %lower_ref, bf16[64,8192]{1,0:T(8,128)(2,1)} %collective-permute-done.3.other_ref, f32[64,128]{1,0:T(8,128)S(1)} %get-tuple-element.107.base_ref), custom_call_target="tpu_custom_call" | custom-call | flops 134217728 | bytes 4194304 | tf_op jit(solution)/shard_map/pallas_call | solution.py:51
  81.1 2.3 %collective-permute-start.4 = (bf16[2,1,64,8192]{3,2,1,0:T(8,128)(2,1)S(1)}, bf16[2,1,64,8192]{3,2,1,0:T(8,128)(2,1)S(1)}, u32[]{:S(2)}, u32[]{:S(2)}) collective-permute-start(bf16[2,1,64,8192]{3,2,1,0:T(8,128)(2,1)S(1)} %copy-done.1), channel_id=1, source_target_pairs={{0,1},{1,0},{2,3},{3,2},{4,5},{5,4},{6,7},{7,6},{8,9},{9,8},{10,11... | collective-permute-start | bytes 6291464 | tf_op jit(solution)/shard_map/ppermute | solution.py:27
  83.5 21.5 %all_to_all.40.blocks_ref = bf16[64,64,128]{2,1,0:T(8,128)(2,1)S(1)} all-to-all(bf16[64,64,128]{2,1,0:T(8,128)(2,1)S(1)} %shard_map.138), channel_id=1, replica_groups=mesh['y'=4,'x'=4,'z'=4,'c'=2] {'y','x','z'}, dimensions={0} | all-to-all | bytes 2097152 | tf_op jit(solution)/shard_map/all_to_all | solution.py:31
  106.1 2.4 %collective-permute-start.6 = (bf16[16384,128]{1,0:T(8,128)(2,1)S(1)}, bf16[16384,128]{1,0:T(8,128)(2,1)S(1)}, u32[]{:S(2)}, u32[]{:S(2)}) collective-permute-start(bf16[16384,128]{1,0:T(8,128)(2,1)S(1)} %copy-done), channel_id=1, source_target_pairs={{0,1},{1,0},{2,3},{3,2},{4,5},{5,4},{6,7},{7,6},{8,9},{9,8},{10,11... | collective-permute-start | bytes 12582920 | tf_op jit(solution)/shard_map/ppermute | solution.py:27
  108.5 22.1 %all_to_all.41.x1_ref = bf16[64,64,128]{2,1,0:T(8,128)(2,1)S(1)} all-to-all(bf16[64,64,128]{2,1,0:T(8,128)(2,1)S(1)} %shard_map.139), channel_id=1, replica_groups=mesh['y'=4,'x'=4,'z'=4,'c'=2] {'y','x','z'}, dimensions={0} | all-to-all | bytes 2097152 | tf_op jit(solution)/shard_map/all_to_all | solution.py:31
  130.6 1.7 shard_map.140
  132.4 21.5 %all_to_all.42.x0_ref = bf16[64,64,128]{2,1,0:T(8,128)(2,1)S(1)} all-to-all(bf16[64,64,128]{2,1,0:T(8,128)(2,1)S(1)} %shard_map.140), channel_id=1, replica_groups=mesh['y'=4,'x'=4,'z'=4,'c'=2] {'y','x','z'}, dimensions={0} | all-to-all | bytes 2097152 | tf_op jit(solution)/shard_map/all_to_all | solution.py:31
  155.4 3.1 %collective-permute-start.7 = (f32[64,128]{1,0:T(8,128)S(1)}, f32[64,128]{1,0:T(8,128)S(1)}, u32[]{:S(2)}, u32[]{:S(2)}) collective-permute-start(f32[64,128]{1,0:T(8,128)S(1)} %get-tuple-element.123), channel_id=1, source_target_pairs={{0,1},{1,0},{2,3},{3,2},{4,5},{5,4},{6,7},{7,6},{8,9},{9,8},{10,11... | collective-permute-start | bytes 98312 | tf_op jit(solution)/shard_map/ppermute | solution.py:27
  160.7 3.5 %all-to-all-start.7 = ((bf16[16,64,128]{2,1,0:T(8,128)(2,1)}), bf16[16,64,128]{2,1,0:T(8,128)(2,1)S(1)}, u32[]{:S(2)}, u32[]{:S(2)}) async-start(bf16[16,64,128]{2,1,0:T(8,128)(2,1)} %get-tuple-element.129.copies_ref), calls=%async_computation.7 | async-start | bytes 524288 | tf_op jit(solution)/shard_map/all_to_all | solution.py:31
  165.2 6.7 %all-to-all-done.7.own_ref = bf16[16,64,128]{2,1,0:T(8,128)(2,1)S(1)} async-done(((bf16[16,64,128]{2,1,0:T(8,128)(2,1)}), bf16[16,64,128]{2,1,0:T(8,128)(2,1)S(1)}, u32[]{:S(2)}, u32[]{:S(2)}) %all-to-all-start.7) | async-done | bytes 262176 | tf_op jit(solution)/shard_map/all_to_all | solution.py:31
  171.9 1.7 collective-permute-start.10
  174.8 1.8 %shard_map.143 = bf16[1,2,1,64,128]{4,3,2,1,0:T(8,128)(2,1)} custom-call(s32[1]{0:T(128)} %bitcast.core_ref, bf16[16,64,128]{2,1,0:T(8,128)(2,1)S(1)} %all-to-all-done.7.own_ref, bf16[16,64,128]{2,1,0:T(8,128)(2,1)S(1)} %collective-permute-done.10.other_ref, bf16[64,2048]{1,0:T(8,128)(2,1)S(1)} %get-tuple-element.133.top_ref, ...), custom_call_target="tpu_custom_call" | custom-call | bytes 1048576 | tf_op jit(solution)/shard_map/pallas_call | solution.py:51
  (58 shorter events, 20.6 us)
Async XLA Ops:
  0.6 21.1 %copy-start.5 = (bf16[1,2,1,64,128]{4,3,2,1,0:T(8,128)(2,1)S(1)}, bf16[1,2,1,64,128]{4,3,2,1,0:T(8,128)(2,1)}, u32[]{:S(2)}) copy-start(bf16[1,2,1,64,128]{4,3,2,1,0:T(8,128)(2,1)} %rhs_ref.4) | copy-start | bytes 98308
  0.6 26.2 %copy-start.4 = (bf16[1,2,1,64,2048]{4,3,2,1,0:T(8,128)(2,1)S(1)}, bf16[1,2,1,64,2048]{4,3,2,1,0:T(8,128)(2,1)}, u32[]{:S(2)}) copy-start(bf16[1,2,1,64,2048]{4,3,2,1,0:T(8,128)(2,1)} %inverse_ref.3) | copy-start | bytes 1572868
  0.7 26.1 %copy-start.2 = (bf16[1,128,4096]{2,1,0:T(8,128)(2,1)S(1)}, bf16[1,128,4096]{2,1,0:T(8,128)(2,1)}, u32[]{:S(2)}) copy-start(bf16[1,128,4096]{2,1,0:T(8,128)(2,1)} %update_ref.3) | copy-start | bytes 3145732
  2.3 16.0 %all-to-all-start = ((bf16[16,72,128]{2,1,0:T(8,128)(2,1)}), bf16[16,72,128]{2,1,0:T(8,128)(2,1)S(1)}, u32[]{:S(2)}, u32[]{:S(2)}) async-start(bf16[16,72,128]{2,1,0:T(8,128)(2,1)} %shard_map.131), calls=%async_computation | async-start | bytes 589824 | tf_op jit(solution)/shard_map/all_to_all | solution.py:31
  11.5 15.3 %copy-start.8 = (s32[1,128,1]{1,2,0:T(1,128)S(1)}, s32[1,128,1]{1,2,0:T(1,128)}, u32[]{:S(2)}) copy-start(s32[1,128,1]{1,2,0:T(1,128)} %param.18) | copy-start | bytes 1540
  11.5 15.3 %copy-start.9 = (s32[1,128]{1,0:T(1,128)S(1)}, s32[1,128]{1,0:T(1,128)}, u32[]{:S(2)}) copy-start(s32[1,128]{1,0:T(1,128)} %slot_ref.3) | copy-start | bytes 1540
  18.3 3.4 %collective-permute-start = (bf16[16,72,128]{2,1,0:T(8,128)(2,1)S(1)}, bf16[16,72,128]{2,1,0:T(8,128)(2,1)S(1)}, u32[]{:S(2)}, u32[]{:S(2)}) collective-permute-start(bf16[16,72,128]{2,1,0:T(8,128)(2,1)S(1)} %all-to-all-done.own_ref), channel_id=1, source_target_pairs={{0,1},{1,0},{2,3},{3,2},{4,5},{5,4},{6,7},{7,6},{8,9},{9,8},{10,11... | collective-permute-start | bytes 884744 | tf_op jit(solution)/shard_map/ppermute | solution.py:27
  22.7 11.1 %all-to-all-start.1 = ((bf16[16,64,128]{2,1,0:T(8,128)(2,1)}), bf16[16,64,128]{2,1,0:T(8,128)(2,1)S(1)}, u32[]{:S(2)}, u32[]{:S(2)}) async-start(bf16[16,64,128]{2,1,0:T(8,128)(2,1)} %shard_map.133), calls=%async_computation.1 | async-start | bytes 524288 | tf_op jit(solution)/shard_map/all_to_all | solution.py:31
  26.2 2.4 %collective-permute-start.1 = (bf16[64,128]{1,0:T(8,128)(2,1)S(1)}, bf16[64,128]{1,0:T(8,128)(2,1)S(1)}, u32[]{:S(2)}, u32[]{:S(2)}) collective-permute-start(bf16[64,128]{1,0:T(8,128)(2,1)S(1)} %get-tuple-element.87), channel_id=1, source_target_pairs={{0,1},{1,0},{2,3},{3,2},{4,5},{5,4},{6,7},{7,6},{8,9},{9,8},{10,11... | collective-permute-start | bytes 49160 | tf_op jit(solution)/shard_map/ppermute | solution.py:27
  28.0 26.4 %copy-start.7 = (s32[32,128]{1,0:T(8,128)}, s32[32,128]{1,0:T(8,128)S(1)}, u32[]{:S(2)}) copy-start(s32[32,128]{1,0:T(8,128)S(1)} %get-tuple-element.83) | copy-start | bytes 49156
  33.8 3.0 %collective-permute-start.2 = (bf16[16,64,128]{2,1,0:T(8,128)(2,1)S(1)}, bf16[16,64,128]{2,1,0:T(8,128)(2,1)S(1)}, u32[]{:S(2)}, u32[]{:S(2)}) collective-permute-start(bf16[16,64,128]{2,1,0:T(8,128)(2,1)S(1)} %all-to-all-done.1.own_ref), channel_id=1, source_target_pairs={{0,1},{1,0},{2,3},{3,2},{4,5},{5,4},{6,7},{7,6},{8,9},{9,8},{10,11... | collective-permute-start | bytes 786440 | tf_op jit(solution)/shard_map/ppermute | solution.py:27
  38.4 16.0 %all-to-all-start.2 = ((bf16[128,4,128]{2,1,0:T(4,128)(2,1)}), bf16[128,4,128]{2,1,0:T(4,128)(2,1)S(1)}, u32[]{:S(2)}, u32[]{:S(2)}) async-start(bf16[128,4,128]{2,1,0:T(4,128)(2,1)} %bitcast.7), calls=%async_computation.2 | async-start | bytes 262144 | tf_op jit(solution)/shard_map/all_to_all | solution.py:31
  44.6 27.4 %collective-permute-start.3 = (bf16[64,8192]{1,0:T(8,128)(2,1)}, bf16[64,8192]{1,0:T(8,128)(2,1)}, u32[]{:S(2)}, u32[]{:S(2)}) collective-permute-start(bf16[64,8192]{1,0:T(8,128)(2,1)} %get-tuple-element.104), channel_id=1, source_target_pairs={{0,1},{1,0},{2,3},{3,2},{4,5},{5,4},{6,7},{7,6},{8,9},{9,8},{10,11... | collective-permute-start | bytes 3145736 | tf_op jit(solution)/shard_map/ppermute | solution.py:27
  55.9 22.4 %all-to-all-start.3 = ((bf16[64,64,128]{2,1,0:T(8,128)(2,1)}), bf16[64,64,128]{2,1,0:T(8,128)(2,1)S(1)}, u32[]{:S(2)}, u32[]{:S(2)}) async-start(bf16[64,64,128]{2,1,0:T(8,128)(2,1)} %get-tuple-element.101), calls=%async_computation.3 | async-start | bytes 2097152 | tf_op jit(solution)/shard_map/all_to_all | solution.py:31
  72.0 9.1 %copy-start.1 = (bf16[2,1,64,8192]{3,2,1,0:T(8,128)(2,1)S(1)}, bf16[2,1,64,8192]{3,2,1,0:T(8,128)(2,1)}, u32[]{:S(2)}) copy-start(bf16[2,1,64,8192]{3,2,1,0:T(8,128)(2,1)} %own_ref.1) | copy-start | bytes 6291460
  81.1 25.0 %copy-start = (bf16[16384,128]{1,0:T(8,128)(2,1)S(1)}, bf16[16384,128]{1,0:T(8,128)(2,1)}, u32[]{:S(2)}) copy-start(bf16[16384,128]{1,0:T(8,128)(2,1)} %shard_map.137.own_ref) | copy-start | bytes 12582916
  81.1 24.0 %collective-permute-start.4 = (bf16[2,1,64,8192]{3,2,1,0:T(8,128)(2,1)S(1)}, bf16[2,1,64,8192]{3,2,1,0:T(8,128)(2,1)S(1)}, u32[]{:S(2)}, u32[]{:S(2)}) collective-permute-start(bf16[2,1,64,8192]{3,2,1,0:T(8,128)(2,1)S(1)} %copy-done.1), channel_id=1, source_target_pairs={{0,1},{1,0},{2,3},{3,2},{4,5},{5,4},{6,7},{7,6},{8,9},{9,8},{10,11... | collective-permute-start | bytes 6291464 | tf_op jit(solution)/shard_map/ppermute | solution.py:27
  83.4 21.6 %collective-permute-start.5 = (bf16[64,8192]{1,0:T(8,128)(2,1)S(1)}, bf16[64,8192]{1,0:T(8,128)(2,1)S(1)}, u32[]{:S(2)}, u32[]{:S(2)}) collective-permute-start(bf16[64,8192]{1,0:T(8,128)(2,1)S(1)} %copy-done.3), channel_id=1, source_target_pairs={{0,1},{1,0},{2,3},{3,2},{4,5},{5,4},{6,7},{7,6},{8,9},{9,8},{10,11... | collective-permute-start | bytes 3145736 | tf_op jit(solution)/shard_map/ppermute | solution.py:27
  106.1 24.5 %collective-permute-start.6 = (bf16[16384,128]{1,0:T(8,128)(2,1)S(1)}, bf16[16384,128]{1,0:T(8,128)(2,1)S(1)}, u32[]{:S(2)}, u32[]{:S(2)}) collective-permute-start(bf16[16384,128]{1,0:T(8,128)(2,1)S(1)} %copy-done), channel_id=1, source_target_pairs={{0,1},{1,0},{2,3},{3,2},{4,5},{5,4},{6,7},{7,6},{8,9},{9,8},{10,11... | collective-permute-start | bytes 12582920 | tf_op jit(solution)/shard_map/ppermute | solution.py:27
  155.4 4.0 %collective-permute-start.7 = (f32[64,128]{1,0:T(8,128)S(1)}, f32[64,128]{1,0:T(8,128)S(1)}, u32[]{:S(2)}, u32[]{:S(2)}) collective-permute-start(f32[64,128]{1,0:T(8,128)S(1)} %get-tuple-element.123), channel_id=1, source_target_pairs={{0,1},{1,0},{2,3},{3,2},{4,5},{5,4},{6,7},{7,6},{8,9},{9,8},{10,11... | collective-permute-start | bytes 98312 | tf_op jit(solution)/shard_map/ppermute | solution.py:27
  160.2 4.1 %collective-permute-start.8 = (bf16[64,128]{1,0:T(8,128)(2,1)S(1)}, bf16[64,128]{1,0:T(8,128)(2,1)S(1)}, u32[]{:S(2)}, u32[]{:S(2)}) collective-permute-start(bf16[64,128]{1,0:T(8,128)(2,1)S(1)} %slice_bitcast_fusion.5), channel_id=1, source_target_pairs={{0,1},{1,0},{2,3},{3,2},{4,5},{5,4},{6,7},{7,6},{8,9},{9,8},{10,11... | collective-permute-start | bytes 49160 | tf_op jit(solution)/shard_map/ppermute | solution.py:27
  160.5 3.9 %collective-permute-start.9 = (bf16[64,128]{1,0:T(8,128)(2,1)S(1)}, bf16[64,128]{1,0:T(8,128)(2,1)S(1)}, u32[]{:S(2)}, u32[]{:S(2)}) collective-permute-start(bf16[64,128]{1,0:T(8,128)(2,1)S(1)} %slice_bitcast_fusion.4), channel_id=1, source_target_pairs={{0,1},{1,0},{2,3},{3,2},{4,5},{5,4},{6,7},{7,6},{8,9},{9,8},{10,11... | collective-permute-start | bytes 49160 | tf_op jit(solution)/shard_map/ppermute | solution.py:27
  160.7 11.2 %all-to-all-start.7 = ((bf16[16,64,128]{2,1,0:T(8,128)(2,1)}), bf16[16,64,128]{2,1,0:T(8,128)(2,1)S(1)}, u32[]{:S(2)}, u32[]{:S(2)}) async-start(bf16[16,64,128]{2,1,0:T(8,128)(2,1)} %get-tuple-element.129.copies_ref), calls=%async_computation.7 | async-start | bytes 524288 | tf_op jit(solution)/shard_map/all_to_all | solution.py:31
  171.9 2.9 %collective-permute-start.10 = (bf16[16,64,128]{2,1,0:T(8,128)(2,1)S(1)}, bf16[16,64,128]{2,1,0:T(8,128)(2,1)S(1)}, u32[]{:S(2)}, u32[]{:S(2)}) collective-permute-start(bf16[16,64,128]{2,1,0:T(8,128)(2,1)S(1)} %all-to-all-done.7.own_ref), channel_id=1, source_target_pairs={{0,1},{1,0},{2,3},{3,2},{4,5},{5,4},{6,7},{7,6},{8,9},{9,8},{10,11... | collective-permute-start | bytes 786440 | tf_op jit(solution)/shard_map/ppermute | solution.py:27
  (2 other events, 5.9 us)

commit v8 on v7

--- a/solution.py
+++ b/solution.py
@@ -18,7 +18,6 @@
 HBM = pl.BlockSpec(memory_space=pltpu.HBM)
 DMA = pltpu.SemaphoreType.DMA
 MIB = 1 << 20
-FIRST = 50
 BATCH = 8
 tie = lax.optimization_barrier
 
@@ -352,35 +351,22 @@
         copies_ref[j] = value
 
 
-def first_product_kernel(
-    core_ref, blocks_ref, lower_ref, other_ref, base_ref, copies_ref, held_ref, sems
-):
-    kr = held_ref.shape[2]
-    chips = blocks_ref.shape[0]
-    steps = sems.shape[0]
-    width, span = kr // steps, chips // steps
-    loads = []
-    for i in range(steps):
-        columns = pl.ds(i * width, width)
-        pairs = [
-            (lower_ref.at[1, 0, :, columns], held_ref.at[0, :, columns]),
-            (other_ref.at[:, columns], held_ref.at[1, :, columns]),
-        ]
-        loads.append(
-            [pltpu.make_async_copy(a, b, sems.at[i, n]) for n, (a, b) in enumerate(pairs)]
-        )
-    for group in loads:
-        for load in group:
-            load.start()
-    total = None
-    for i, group in enumerate(loads):
-        for load in group:
-            load.wait()
-        term = pair_dot(
-            blocks_ref, i * span, (i + 1) * span, against(held_ref.at[0], held_ref.at[1])
-        )
-        total = term if total is None else total + term
-    write_copies(copies_ref, (base_ref[...] - ordered(core_ref, total)).astype(BF16))
+def fetch_kernel(lower_ref, other_ref, out_ref, sems):
+    kr = out_ref.shape[2]
+    loads = [
+        pltpu.make_async_copy(lower_ref.at[1, 0, :, pl.ds(0, kr)], out_ref.at[0], sems.at[0]),
+        pltpu.make_async_copy(other_ref, out_ref.at[1], sems.at[1]),
+    ]
+    for load in loads:
+        load.start()
+    for load in loads:
+        load.wait()
+
+
+def first_product_kernel(core_ref, blocks_ref, pair_ref, base_ref, copies_ref):
+    rights = against(pair_ref.at[0], pair_ref.at[1])
+    total = ordered(core_ref, pair_dot(blocks_ref, 0, blocks_ref.shape[0], rights))
+    write_copies(copies_ref, (base_ref[...] - total).astype(BF16))
 
 
 def product_kernel(core_ref, blocks_ref, own_ref, other_ref, copies_ref):
@@ -399,39 +385,35 @@
     write_copies(copies_ref, ordered(core_ref, total).astype(BF16))
 
 
-def couple_kernel(x0_ref, x1_ref, own_ref, other_ref, mine_ref, theirs_ref):
+def couple_kernel(x0_ref, x1_ref, matrix_ref, out_ref):
     count, half, lanes = x0_ref.shape
     total = None
     for start, blocks_ref in ((0, x0_ref), (count * lanes, x1_ref)):
 
         def rights(left, columns):
             rows = slice(start + columns.start, start + columns.stop)
-            return jnp.dot(
-                left,
-                jnp.concatenate([own_ref[rows, :], other_ref[rows, :]], axis=1),
-                preferred_element_type=F32,
-            )
+            return jnp.dot(left, matrix_ref[rows, :], preferred_element_type=F32)
 
         term = pair_dot(blocks_ref, 0, count, rights)
         total = term if total is None else total + term
-    width = mine_ref.shape[1]
-    mine_ref[...] = total[:, :width]
-    theirs_ref[...] = total[:, width:]
-
-
-def settle_kernel(core_ref, mine_ref, got_ref, z0_ref, z1_ref, copies_ref, rest_ref):
+    out_ref[...] = total
+
+
+def settle_kernel(core_ref, mine_ref, got_ref, z0_ref, z1_ref, copies_ref, c1_ref, rest_ref):
     stripe = z0_ref.shape[0]
 
     def work(first, second):
         both = jnp.concatenate([first[...], second[...]], axis=0).T
         rest_ref[...] = z0_ref[...] - both[:stripe]
-        write_copies(copies_ref, (z1_ref[...] - both[stripe:]).astype(BF16))
+        value = (z1_ref[...] - both[stripe:]).astype(BF16)
+        write_copies(copies_ref, value)
+        c1_ref[...] = value
 
     by_core(core_ref, mine_ref, got_ref, work)
 
 
-def closing_kernel(core_ref, own_ref, other_ref, top_ref, rest_ref, copies_ref, out_ref):
-    out_ref[0, 1, 0] = copies_ref[0]
+def closing_kernel(core_ref, own_ref, other_ref, top_ref, rest_ref, c1_ref, out_ref):
+    out_ref[0, 1, 0] = c1_ref[...]
 
     def work(first, second):
         total = rest_ref[...] - plane_dot(top_ref, first, second, own_ref.shape[1])
@@ -539,11 +521,15 @@
     summed = build_coupling(index, repeats, child_coupling, 2 * kr)
     whole = (cubes, half, rhs)
     work = dict(flops=2 * cubes * half * rhs * rhs, moved=4 * MIB)
-    r0, summed, lower_other = tie((spread(r0_copies, CUBE), summed, lower_other))
+    summed, lower_other = tie((summed, lower_other))
+    pair = kernel_call(
+        fetch_kernel, (root_lower, lower_other), [HBM, HBM], pltpu.VMEM((2, stripe, kr), BF16),
+        VMEM, scratch=[DMA((2,))], limit=60, moved=4 * MIB,
+    )
+    r0, summed, pair = tie((spread(r0_copies, CUBE), summed, pair))
     r1_copies = kernel_call(
-        first_product_kernel, (core, r0, root_lower, lower_other, right),
-        [SMEM, VMEM, HBM, HBM, VMEM], like(whole), VMEM,
-        scratch=[pltpu.VMEM((2, stripe, kr), BF16), DMA((4, 2))], limit=FIRST, **work,
+        first_product_kernel, (core, r0, pair, right), [SMEM] + [VMEM] * 3, like(whole), VMEM,
+        limit=4, **work,
     )
     r1_copies, inverse, upper_own = tie((r1_copies, root_inverse, upper_own))
     inverse_other, upper_other = swap(inverse), swap(upper_own)
@@ -561,14 +547,18 @@
     )
     x0, x0_copies, x1_copies = tie((spread(x0_copies, CUBE), x0_copies, x1_copies))
 
-    mine, given = kernel_call(
-        couple_kernel, (x0, x1, summed, summed_other), [VMEM] * 4,
-        [like((half, 2 * stripe), F32)] * 2, [VMEM] * 2,
-        limit=4, flops=8 * cubes * half * rhs * rhs, moved=10 * MIB,
-    )
-    c1_copies, rest = kernel_call(
-        settle_kernel, (core, mine, swap(given), z0c, z1c), [SMEM] + [VMEM] * 4,
-        [like(piece), like((stripe, rhs), F32)], [VMEM] * 2, limit=2, moved=MIB,
+    def couple(x0, matrix):
+        return kernel_call(
+            couple_kernel, (x0, x1, matrix), [VMEM] * 3, like((half, 2 * stripe), F32), VMEM,
+            limit=4, flops=4 * cubes * half * rhs * rhs, moved=6 * MIB,
+        )
+
+    given, x0 = tie((couple(x0, summed_other), x0))
+    theirs, mine = swap(given), couple(x0, summed)
+    c1_copies, c1, rest = kernel_call(
+        settle_kernel, (core, mine, theirs, z0c, z1c), [SMEM] + [VMEM] * 4,
+        [like(piece), like((stripe, rhs)), like((stripe, rhs), F32)], [VMEM] * 3,
+        limit=2, moved=MIB,
     )
     c1_copies, x0_own, x1_own = tie((c1_copies, x0_copies[0], x1_copies[0]))
     own_c1 = spread(c1_copies, PLANE)
@@ -581,7 +571,7 @@
     root_solution = jnp.stack([own_rows(x0_own), own_rows(x1_own)])[:, None]
     own_c1, root_solution = tie((own_c1, root_solution))
     child_solution = kernel_call(
-        closing_kernel, (core, own_c1, swap(own_c1), top, rest, c1_copies),
+        closing_kernel, (core, own_c1, swap(own_c1), top, rest, c1),
         [SMEM] + [VMEM] * 5, like(child_rhs.shape), VMEM, limit=2, moved=MIB,
     )
     return child_solution, root_solution

time: 177 us -> 177 us (level)
  waiting for transfers between devices: 33.7 us -> 30.1 us
  local copies, waits for them, and re-layouts: 5.81 us -> 8.91 us
    unnamed x20 -> x24, local copies, waits for them, and re-layouts: 0.79 us -> 3.91 us
    all_to_all x5, waiting for transfers between devices: 29.3 us -> 26.5 us  [spread(): return lax.all_to_all(copies, axes, 0, 0)]
    pallas_call x13 -> x15, Pallas kernels: 27.9 us -> 27 us  [kernel_call(): pl.pallas_call(body, out_shape=shapes, in_specs=specs, out_specs=out_spec...]
  transfers between devices with their start and end apart: 16 -> 16, of which waited for: 9 -> 8; matrix products, arithmetic and copies ran while one was open for 3% -> 3% of each run, Pallas kernels for 8% -> 9%
where the time goes in v8:
time: 177 us; the launch traced here: 176 us
  blocking collectives  66 us (37%)
  starting transfers between devices  42.4 us (24%)
  waiting for transfers between devices  30.1 us (17%)
  Pallas kernels  27 us (15%)
  local copies, waits for them, and re-layouts  8.91 us (5%)
    all_to_all x3, blocking collectives, spread(): return lax.all_to_all(copies, axes, 0, 0)  66 us
    pallas_call x15, Pallas kernels, kernel_call(): pl.pallas_call(body, out_shape=shapes, in_specs=specs, out_specs=out_spec...  27 us
    all_to_all x5, starting transfers between devices, spread(): return lax.all_to_all(copies, axes, 0, 0)  26.6 us
    all_to_all x5, waiting for transfers between devices, spread(): return lax.all_to_all(copies, axes, 0, 0)  26.5 us
    ppermute x11, starting transfers between devices, swap(): return lax.ppermute(array, 'c', [(0, 1), (1, 0)])  15.8 us
    reshape x2, local copies, waits for them, and re-layouts, rows_of(): return lax.slice(array, start, stop).reshape(array.shape[-2], last - first)  4.15 us
    unnamed x24, local copies, waits for them, and re-layouts  3.91 us
    ppermute x11, waiting for transfers between devices, swap(): return lax.ppermute(array, 'c', [(0, 1), (1, 0)])  3.55 us
  transfers between devices with their start and end apart: 16, of which 8 were waited for; matrix products, arithmetic and copies ran while one was open for 3% of the time, Pallas kernels for 9%

profile of v8, /device:TPU:1, one launch (start us, length us, event | category | flops | bytes accessed | tf_op | source)
XLA Modules:
  0.0 176.0 jit_solution(15531486192781560817)
XLA Ops:
  0.7 1.6 shard_map.131
  2.3 8.4 %all-to-all-start = ((bf16[16,72,128]{2,1,0:T(8,128)(2,1)}), bf16[16,72,128]{2,1,0:T(8,128)(2,1)S(1)}, u32[]{:S(2)}, u32[]{:S(2)}) async-start(bf16[16,72,128]{2,1,0:T(8,128)(2,1)} %shard_map.131), calls=%async_computation | async-start | bytes 589824 | tf_op jit(solution)/shard_map/all_to_all | solution.py:30
  11.7 3.1 %slice_bitcast_fusion = (bf16[64,8192]{1,0:T(8,128)(2,1)}, bf16[64,8192]{1,0:T(8,128)(2,1)}) fusion(bf16[2,1,64,16384]{3,2,1,0:T(8,128)(2,1)} %param.23, bf16[2,1,64,16384]{3,2,1,0:T(8,128)(2,1)} %lower_ref), kind=kLoop, calls=%fused_computation | loop fusion | bytes 4194304 | tf_op jit(solution)/shard_map/reshape | solution.py:42
  15.8 2.5 %all-to-all-done.own_ref = bf16[16,72,128]{2,1,0:T(8,128)(2,1)S(1)} async-done(((bf16[16,72,128]{2,1,0:T(8,128)(2,1)}), bf16[16,72,128]{2,1,0:T(8,128)(2,1)S(1)}, u32[]{:S(2)}, u32[]{:S(2)}) %all-to-all-start) | async-done | bytes 294944 | tf_op jit(solution)/shard_map/all_to_all | solution.py:30
  18.3 2.2 %collective-permute-start = (bf16[16,72,128]{2,1,0:T(8,128)(2,1)S(1)}, bf16[16,72,128]{2,1,0:T(8,128)(2,1)S(1)}, u32[]{:S(2)}, u32[]{:S(2)}) collective-permute-start(bf16[16,72,128]{2,1,0:T(8,128)(2,1)S(1)} %all-to-all-done.own_ref), channel_id=1, source_target_pairs={{0,1},{1,0},{2,3},{3,2},{4,5},{5,4},{6,7},{7,6},{8,9},{9,8},{10,11... | collective-permute-start | bytes 884744 | tf_op jit(solution)/shard_map/ppermute | solution.py:26
  22.7 3.5 %all-to-all-start.1 = ((bf16[16,64,128]{2,1,0:T(8,128)(2,1)}), bf16[16,64,128]{2,1,0:T(8,128)(2,1)S(1)}, u32[]{:S(2)}, u32[]{:S(2)}) async-start(bf16[16,64,128]{2,1,0:T(8,128)(2,1)} %shard_map.133), calls=%async_computation.1 | async-start | bytes 524288 | tf_op jit(solution)/shard_map/all_to_all | solution.py:30
  28.6 5.2 %all-to-all-done.1.own_ref = bf16[16,64,128]{2,1,0:T(8,128)(2,1)S(1)} async-done(((bf16[16,64,128]{2,1,0:T(8,128)(2,1)}), bf16[16,64,128]{2,1,0:T(8,128)(2,1)S(1)}, u32[]{:S(2)}, u32[]{:S(2)}) %all-to-all-start.1) | async-done | bytes 262176 | tf_op jit(solution)/shard_map/all_to_all | solution.py:30
  33.8 1.8 %collective-permute-start.2 = (bf16[16,64,128]{2,1,0:T(8,128)(2,1)S(1)}, bf16[16,64,128]{2,1,0:T(8,128)(2,1)S(1)}, u32[]{:S(2)}, u32[]{:S(2)}) collective-permute-start(bf16[16,64,128]{2,1,0:T(8,128)(2,1)S(1)} %all-to-all-done.1.own_ref), channel_id=1, source_target_pairs={{0,1},{1,0},{2,3},{3,2},{4,5},{5,4},{6,7},{7,6},{8,9},{9,8},{10,11... | collective-permute-start | bytes 786440 | tf_op jit(solution)/shard_map/ppermute | solution.py:26
  36.8 1.6 shard_map.135
  38.4 6.1 %all-to-all-start.2 = ((bf16[128,4,128]{2,1,0:T(4,128)(2,1)}), bf16[128,4,128]{2,1,0:T(4,128)(2,1)S(1)}, u32[]{:S(2)}, u32[]{:S(2)}) async-start(bf16[128,4,128]{2,1,0:T(4,128)(2,1)} %bitcast.7), calls=%async_computation.2 | async-start | bytes 262144 | tf_op jit(solution)/shard_map/all_to_all | solution.py:30
  45.7 8.7 %all-to-all-done.2 = bf16[128,4,128]{2,1,0:T(4,128)(2,1)S(1)} async-done(((bf16[128,4,128]{2,1,0:T(4,128)(2,1)}), bf16[128,4,128]{2,1,0:T(4,128)(2,1)S(1)}, u32[]{:S(2)}, u32[]{:S(2)}) %all-to-all-start.2) | async-done | bytes 131104 | tf_op jit(solution)/shard_map/all_to_all | solution.py:30
  55.9 4.9 %all-to-all-start.3 = ((bf16[64,64,128]{2,1,0:T(8,128)(2,1)}), bf16[64,64,128]{2,1,0:T(8,128)(2,1)S(1)}, u32[]{:S(2)}, u32[]{:S(2)}) async-start(bf16[64,64,128]{2,1,0:T(8,128)(2,1)} %get-tuple-element.104), calls=%async_computation.3 | async-start | bytes 2097152 | tf_op jit(solution)/shard_map/all_to_all | solution.py:30
  60.9 11.1 %shard_map.137.matrix_ref = bf16[16384,128]{1,0:T(8,128)(2,1)} custom-call(s32[4096]{0:T(1024)} %bitcast.37, s32[32]{0:T(128)} %slice_reduce_fusion.repeats_ref, bf16[1,2,1,64,4096]{4,3,2,1,0:T(8,128)(2,1)} %coupling_ref.1), custom_call_target="tpu_custom_call" | custom-call | bytes 31457280 | tf_op jit(solution)/shard_map/pallas_call | solution.py:50
  74.9 3.3 %all-to-all-done.3.blocks_ref.r0_ref = bf16[64,64,128]{2,1,0:T(8,128)(2,1)S(1)} async-done(((bf16[64,64,128]{2,1,0:T(8,128)(2,1)}), bf16[64,64,128]{2,1,0:T(8,128)(2,1)S(1)}, u32[]{:S(2)}, u32[]{:S(2)}) %all-to-all-start.3) | async-done | bytes 1048608 | tf_op jit(solution)/shard_map/all_to_all | solution.py:30
  78.3 1.7 copy-done.3
  81.0 2.3 %collective-permute-start.4 = (bf16[2,1,64,8192]{3,2,1,0:T(8,128)(2,1)S(1)}, bf16[2,1,64,8192]{3,2,1,0:T(8,128)(2,1)S(1)}, u32[]{:S(2)}, u32[]{:S(2)}) collective-permute-start(bf16[2,1,64,8192]{3,2,1,0:T(8,128)(2,1)S(1)} %copy-done.1), channel_id=1, source_target_pairs={{0,1},{1,0},{2,3},{3,2},{4,5},{5,4},{6,7},{7,6},{8,9},{9,8},{10,11... | collective-permute-start | bytes 6291464 | tf_op jit(solution)/shard_map/ppermute | solution.py:26
  83.6 22.4 %all_to_all.40.blocks_ref = bf16[64,64,128]{2,1,0:T(8,128)(2,1)S(1)} all-to-all(bf16[64,64,128]{2,1,0:T(8,128)(2,1)S(1)} %shard_map.139), channel_id=1, replica_groups=mesh['y'=4,'x'=4,'z'=4,'c'=2] {'y','x','z'}, dimensions={0} | all-to-all | bytes 2097152 | tf_op jit(solution)/shard_map/all_to_all | solution.py:30
  107.1 2.3 %collective-permute-start.6 = (bf16[16384,128]{1,0:T(8,128)(2,1)S(1)}, bf16[16384,128]{1,0:T(8,128)(2,1)S(1)}, u32[]{:S(2)}, u32[]{:S(2)}) collective-permute-start(bf16[16384,128]{1,0:T(8,128)(2,1)S(1)} %copy-done), channel_id=1, source_target_pairs={{0,1},{1,0},{2,3},{3,2},{4,5},{5,4},{6,7},{7,6},{8,9},{9,8},{10,11... | collective-permute-start | bytes 12582920 | tf_op jit(solution)/shard_map/ppermute | solution.py:26
  109.4 22.1 %all_to_all.41.x1_ref = bf16[64,64,128]{2,1,0:T(8,128)(2,1)S(1)} all-to-all(bf16[64,64,128]{2,1,0:T(8,128)(2,1)S(1)} %shard_map.140), channel_id=1, replica_groups=mesh['y'=4,'x'=4,'z'=4,'c'=2] {'y','x','z'}, dimensions={0} | all-to-all | bytes 2097152 | tf_op jit(solution)/shard_map/all_to_all | solution.py:30
  131.5 1.7 shard_map.141
  133.2 21.5 %all_to_all.42.x0_ref = bf16[64,64,128]{2,1,0:T(8,128)(2,1)S(1)} all-to-all(bf16[64,64,128]{2,1,0:T(8,128)(2,1)S(1)} %shard_map.141), channel_id=1, replica_groups=mesh['y'=4,'x'=4,'z'=4,'c'=2] {'y','x','z'}, dimensions={0} | all-to-all | bytes 2097152 | tf_op jit(solution)/shard_map/all_to_all | solution.py:30
  155.6 3.1 %collective-permute-start.7 = (f32[64,128]{1,0:T(8,128)S(1)}, f32[64,128]{1,0:T(8,128)S(1)}, u32[]{:S(2)}, u32[]{:S(2)}) collective-permute-start(f32[64,128]{1,0:T(8,128)S(1)} %shard_map.142), channel_id=1, source_target_pairs={{0,1},{1,0},{2,3},{3,2},{4,5},{5,4},{6,7},{7,6},{8,9},{9,8},{10,11... | collective-permute-start | bytes 98312 | tf_op jit(solution)/shard_map/ppermute | solution.py:26
  161.0 3.5 %all-to-all-start.7 = ((bf16[16,64,128]{2,1,0:T(8,128)(2,1)}), bf16[16,64,128]{2,1,0:T(8,128)(2,1)S(1)}, u32[]{:S(2)}, u32[]{:S(2)}) async-start(bf16[16,64,128]{2,1,0:T(8,128)(2,1)} %get-tuple-element.134), calls=%async_computation.7 | async-start | bytes 524288 | tf_op jit(solution)/shard_map/all_to_all | solution.py:30
  165.5 6.9 %all-to-all-done.7.own_ref = bf16[16,64,128]{2,1,0:T(8,128)(2,1)S(1)} async-done(((bf16[16,64,128]{2,1,0:T(8,128)(2,1)}), bf16[16,64,128]{2,1,0:T(8,128)(2,1)S(1)}, u32[]{:S(2)}, u32[]{:S(2)}) %all-to-all-start.7) | async-done | bytes 262176 | tf_op jit(solution)/shard_map/all_to_all | solution.py:30
  (64 shorter events, 23.3 us)
Async XLA Ops:
  0.6 21.1 %copy-start.7 = (bf16[1,2,1,64,128]{4,3,2,1,0:T(8,128)(2,1)S(1)}, bf16[1,2,1,64,128]{4,3,2,1,0:T(8,128)(2,1)}, u32[]{:S(2)}) copy-start(bf16[1,2,1,64,128]{4,3,2,1,0:T(8,128)(2,1)} %rhs_ref.4) | copy-start | bytes 98308
  0.6 26.1 %copy-start.6 = (bf16[1,2,1,64,2048]{4,3,2,1,0:T(8,128)(2,1)S(1)}, bf16[1,2,1,64,2048]{4,3,2,1,0:T(8,128)(2,1)}, u32[]{:S(2)}) copy-start(bf16[1,2,1,64,2048]{4,3,2,1,0:T(8,128)(2,1)} %inverse_ref.3) | copy-start | bytes 1572868
  0.7 26.1 %copy-start.4 = (bf16[1,128,4096]{2,1,0:T(8,128)(2,1)S(1)}, bf16[1,128,4096]{2,1,0:T(8,128)(2,1)}, u32[]{:S(2)}) copy-start(bf16[1,128,4096]{2,1,0:T(8,128)(2,1)} %update_ref.3) | copy-start | bytes 3145732
  2.3 16.0 %all-to-all-start = ((bf16[16,72,128]{2,1,0:T(8,128)(2,1)}), bf16[16,72,128]{2,1,0:T(8,128)(2,1)S(1)}, u32[]{:S(2)}, u32[]{:S(2)}) async-start(bf16[16,72,128]{2,1,0:T(8,128)(2,1)} %shard_map.131), calls=%async_computation | async-start | bytes 589824 | tf_op jit(solution)/shard_map/all_to_all | solution.py:30
  11.5 15.3 %copy-start.10 = (s32[1,128,1]{1,2,0:T(1,128)S(1)}, s32[1,128,1]{1,2,0:T(1,128)}, u32[]{:S(2)}) copy-start(s32[1,128,1]{1,2,0:T(1,128)} %param.18) | copy-start | bytes 1540
  11.5 15.3 %copy-start.11 = (s32[1,128]{1,0:T(1,128)S(1)}, s32[1,128]{1,0:T(1,128)}, u32[]{:S(2)}) copy-start(s32[1,128]{1,0:T(1,128)} %slot_ref.3) | copy-start | bytes 1540
  18.3 3.4 %collective-permute-start = (bf16[16,72,128]{2,1,0:T(8,128)(2,1)S(1)}, bf16[16,72,128]{2,1,0:T(8,128)(2,1)S(1)}, u32[]{:S(2)}, u32[]{:S(2)}) collective-permute-start(bf16[16,72,128]{2,1,0:T(8,128)(2,1)S(1)} %all-to-all-done.own_ref), channel_id=1, source_target_pairs={{0,1},{1,0},{2,3},{3,2},{4,5},{5,4},{6,7},{7,6},{8,9},{9,8},{10,11... | collective-permute-start | bytes 884744 | tf_op jit(solution)/shard_map/ppermute | solution.py:26
  22.7 11.1 %all-to-all-start.1 = ((bf16[16,64,128]{2,1,0:T(8,128)(2,1)}), bf16[16,64,128]{2,1,0:T(8,128)(2,1)S(1)}, u32[]{:S(2)}, u32[]{:S(2)}) async-start(bf16[16,64,128]{2,1,0:T(8,128)(2,1)} %shard_map.133), calls=%async_computation.1 | async-start | bytes 524288 | tf_op jit(solution)/shard_map/all_to_all | solution.py:30
  26.2 2.4 %collective-permute-start.1 = (bf16[64,128]{1,0:T(8,128)(2,1)S(1)}, bf16[64,128]{1,0:T(8,128)(2,1)S(1)}, u32[]{:S(2)}, u32[]{:S(2)}) collective-permute-start(bf16[64,128]{1,0:T(8,128)(2,1)S(1)} %get-tuple-element.90), channel_id=1, source_target_pairs={{0,1},{1,0},{2,3},{3,2},{4,5},{5,4},{6,7},{7,6},{8,9},{9,8},{10,11... | collective-permute-start | bytes 49160 | tf_op jit(solution)/shard_map/ppermute | solution.py:26
  28.0 27.9 %copy-start.9 = (s32[32,128]{1,0:T(8,128)}, s32[32,128]{1,0:T(8,128)S(1)}, u32[]{:S(2)}) copy-start(s32[32,128]{1,0:T(8,128)S(1)} %get-tuple-element.86) | copy-start | bytes 49156
  33.8 3.0 %collective-permute-start.2 = (bf16[16,64,128]{2,1,0:T(8,128)(2,1)S(1)}, bf16[16,64,128]{2,1,0:T(8,128)(2,1)S(1)}, u32[]{:S(2)}, u32[]{:S(2)}) collective-permute-start(bf16[16,64,128]{2,1,0:T(8,128)(2,1)S(1)} %all-to-all-done.1.own_ref), channel_id=1, source_target_pairs={{0,1},{1,0},{2,3},{3,2},{4,5},{5,4},{6,7},{7,6},{8,9},{9,8},{10,11... | collective-permute-start | bytes 786440 | tf_op jit(solution)/shard_map/ppermute | solution.py:26
  38.4 16.0 %all-to-all-start.2 = ((bf16[128,4,128]{2,1,0:T(4,128)(2,1)}), bf16[128,4,128]{2,1,0:T(4,128)(2,1)S(1)}, u32[]{:S(2)}, u32[]{:S(2)}) async-start(bf16[128,4,128]{2,1,0:T(4,128)(2,1)} %bitcast.7), calls=%async_computation.2 | async-start | bytes 262144 | tf_op jit(solution)/shard_map/all_to_all | solution.py:30
  44.5 27.4 %collective-permute-start.3 = (bf16[64,8192]{1,0:T(8,128)(2,1)}, bf16[64,8192]{1,0:T(8,128)(2,1)}, u32[]{:S(2)}, u32[]{:S(2)}) collective-permute-start(bf16[64,8192]{1,0:T(8,128)(2,1)} %get-tuple-element.107), channel_id=1, source_target_pairs={{0,1},{1,0},{2,3},{3,2},{4,5},{5,4},{6,7},{7,6},{8,9},{9,8},{10,11... | collective-permute-start | bytes 3145736 | tf_op jit(solution)/shard_map/ppermute | solution.py:26
  55.9 22.4 %all-to-all-start.3 = ((bf16[64,64,128]{2,1,0:T(8,128)(2,1)}), bf16[64,64,128]{2,1,0:T(8,128)(2,1)S(1)}, u32[]{:S(2)}, u32[]{:S(2)}) async-start(bf16[64,64,128]{2,1,0:T(8,128)(2,1)} %get-tuple-element.104), calls=%async_computation.3 | async-start | bytes 2097152 | tf_op jit(solution)/shard_map/all_to_all | solution.py:30
  80.0 3.4 %copy-start.5 = (bf16[64,8192]{1,0:T(8,128)(2,1)S(1)}, bf16[64,8192]{1,0:T(8,128)(2,1)}, u32[]{:S(2)}) copy-start(bf16[64,8192]{1,0:T(8,128)(2,1)} %get-tuple-element.117.upper_own_ref) | copy-start | bytes 3145732
  81.0 26.0 %copy-start = (bf16[16384,128]{1,0:T(8,128)(2,1)S(1)}, bf16[16384,128]{1,0:T(8,128)(2,1)}, u32[]{:S(2)}) copy-start(bf16[16384,128]{1,0:T(8,128)(2,1)} %shard_map.137.matrix_ref) | copy-start | bytes 12582916
  81.0 25.0 %collective-permute-start.4 = (bf16[2,1,64,8192]{3,2,1,0:T(8,128)(2,1)S(1)}, bf16[2,1,64,8192]{3,2,1,0:T(8,128)(2,1)S(1)}, u32[]{:S(2)}, u32[]{:S(2)}) collective-permute-start(bf16[2,1,64,8192]{3,2,1,0:T(8,128)(2,1)S(1)} %copy-done.1), channel_id=1, source_target_pairs={{0,1},{1,0},{2,3},{3,2},{4,5},{5,4},{6,7},{7,6},{8,9},{9,8},{10,11... | collective-permute-start | bytes 6291464 | tf_op jit(solution)/shard_map/ppermute | solution.py:26
  83.4 22.7 %collective-permute-start.5 = (bf16[64,8192]{1,0:T(8,128)(2,1)S(1)}, bf16[64,8192]{1,0:T(8,128)(2,1)S(1)}, u32[]{:S(2)}, u32[]{:S(2)}) collective-permute-start(bf16[64,8192]{1,0:T(8,128)(2,1)S(1)} %copy-done.5), channel_id=1, source_target_pairs={{0,1},{1,0},{2,3},{3,2},{4,5},{5,4},{6,7},{7,6},{8,9},{9,8},{10,11... | collective-permute-start | bytes 3145736 | tf_op jit(solution)/shard_map/ppermute | solution.py:26
  107.1 24.4 %collective-permute-start.6 = (bf16[16384,128]{1,0:T(8,128)(2,1)S(1)}, bf16[16384,128]{1,0:T(8,128)(2,1)S(1)}, u32[]{:S(2)}, u32[]{:S(2)}) collective-permute-start(bf16[16384,128]{1,0:T(8,128)(2,1)S(1)} %copy-done), channel_id=1, source_target_pairs={{0,1},{1,0},{2,3},{3,2},{4,5},{5,4},{6,7},{7,6},{8,9},{9,8},{10,11... | collective-permute-start | bytes 12582920 | tf_op jit(solution)/shard_map/ppermute | solution.py:26
  155.6 4.0 %collective-permute-start.7 = (f32[64,128]{1,0:T(8,128)S(1)}, f32[64,128]{1,0:T(8,128)S(1)}, u32[]{:S(2)}, u32[]{:S(2)}) collective-permute-start(f32[64,128]{1,0:T(8,128)S(1)} %shard_map.142), channel_id=1, source_target_pairs={{0,1},{1,0},{2,3},{3,2},{4,5},{5,4},{6,7},{7,6},{8,9},{9,8},{10,11... | collective-permute-start | bytes 98312 | tf_op jit(solution)/shard_map/ppermute | solution.py:26
  160.5 4.1 %collective-permute-start.8 = (bf16[64,128]{1,0:T(8,128)(2,1)S(1)}, bf16[64,128]{1,0:T(8,128)(2,1)S(1)}, u32[]{:S(2)}, u32[]{:S(2)}) collective-permute-start(bf16[64,128]{1,0:T(8,128)(2,1)S(1)} %slice_bitcast_fusion.5), channel_id=1, source_target_pairs={{0,1},{1,0},{2,3},{3,2},{4,5},{5,4},{6,7},{7,6},{8,9},{9,8},{10,11... | collective-permute-start | bytes 49160 | tf_op jit(solution)/shard_map/ppermute | solution.py:26
  160.7 4.0 %collective-permute-start.9 = (bf16[64,128]{1,0:T(8,128)(2,1)S(1)}, bf16[64,128]{1,0:T(8,128)(2,1)S(1)}, u32[]{:S(2)}, u32[]{:S(2)}) collective-permute-start(bf16[64,128]{1,0:T(8,128)(2,1)S(1)} %slice_bitcast_fusion.4), channel_id=1, source_target_pairs={{0,1},{1,0},{2,3},{3,2},{4,5},{5,4},{6,7},{7,6},{8,9},{9,8},{10,11... | collective-permute-start | bytes 49160 | tf_op jit(solution)/shard_map/ppermute | solution.py:26
  161.0 11.4 %all-to-all-start.7 = ((bf16[16,64,128]{2,1,0:T(8,128)(2,1)}), bf16[16,64,128]{2,1,0:T(8,128)(2,1)S(1)}, u32[]{:S(2)}, u32[]{:S(2)}) async-start(bf16[16,64,128]{2,1,0:T(8,128)(2,1)} %get-tuple-element.134), calls=%async_computation.7 | async-start | bytes 524288 | tf_op jit(solution)/shard_map/all_to_all | solution.py:30
  172.4 2.7 %collective-permute-start.10 = (bf16[16,64,128]{2,1,0:T(8,128)(2,1)S(1)}, bf16[16,64,128]{2,1,0:T(8,128)(2,1)S(1)}, u32[]{:S(2)}, u32[]{:S(2)}) collective-permute-start(bf16[16,64,128]{2,1,0:T(8,128)(2,1)S(1)} %all-to-all-done.7.own_ref), channel_id=1, source_target_pairs={{0,1},{1,0},{2,3},{3,2},{4,5},{5,4},{6,7},{7,6},{8,9},{9,8},{10,11... | collective-permute-start | bytes 786440 | tf_op jit(solution)/shard_map/ppermute | solution.py:26
  (4 other events, 6.7 us)

commit v9 on v8

--- a/solution.py
+++ b/solution.py
@@ -89,7 +89,8 @@
     return total
 
 
-def opening_kernel(rhs_ref, owner_ref, slot_ref, out_ref):
+def opening_kernel(rhs_ref, owner_ref, slot_ref, out_ref, second_ref):
+    second_ref[...] = rhs_ref[0, 1, 0].astype(F32)
     row = lax.broadcasted_iota(jnp.int32, (8, 128), 0)
     marks = jnp.where(row == 0, owner_ref[...], jnp.where(row == 1, slot_ref[...], 0))
     marks = marks.astype(F32).astype(BF16)
@@ -120,7 +121,7 @@
     rows = out_ref.shape[1]
 
     def work(first, second):
-        total = rhs_ref[0, 1, 0].astype(F32) - plane_dot(low_ref, first, second, rows)
+        total = rhs_ref[...] - plane_dot(low_ref, first, second, rows)
         value = total.astype(BF16)
         for j in range(out_ref.shape[0]):
             out_ref[j] = value
@@ -183,15 +184,12 @@
 
 def contribute_kernel(
     core_ref, own_ref, other_ref, update_ref, inverse_ref, part_ref, select_ref, targets_ref,
-    out_ref, z1_ref, high_ref, diag_ref, sems
+    out_ref, z1_ref, diag_ref, sem
 ):
-    kc = high_ref.shape[1]
-    load = pltpu.make_async_copy(update_ref.at[0, :, pl.ds(kc, kc)], high_ref, sems.at[0])
-    later = pltpu.make_async_copy(inverse_ref.at[0, 1, 0], diag_ref, sems.at[1])
-    load.start()
+    later = pltpu.make_async_copy(inverse_ref.at[0, 1, 0], diag_ref, sem)
     later.start()
     rows = own_ref.shape[1]
-    load.wait()
+    high_ref = update_ref.at[0, :, pl.ds(diag_ref.shape[1], diag_ref.shape[1])]
 
     def work(first, second):
         contribution = -(part_ref[...] + plane_dot(high_ref, first, second, rows))
@@ -351,22 +349,9 @@
         copies_ref[j] = value
 
 
-def fetch_kernel(lower_ref, other_ref, out_ref, sems):
-    kr = out_ref.shape[2]
-    loads = [
-        pltpu.make_async_copy(lower_ref.at[1, 0, :, pl.ds(0, kr)], out_ref.at[0], sems.at[0]),
-        pltpu.make_async_copy(other_ref, out_ref.at[1], sems.at[1]),
-    ]
-    for load in loads:
-        load.start()
-    for load in loads:
-        load.wait()
-
-
-def first_product_kernel(core_ref, blocks_ref, pair_ref, base_ref, copies_ref):
-    rights = against(pair_ref.at[0], pair_ref.at[1])
-    total = ordered(core_ref, pair_dot(blocks_ref, 0, blocks_ref.shape[0], rights))
-    write_copies(copies_ref, (base_ref[...] - total).astype(BF16))
+def first_product_kernel(core_ref, blocks_ref, own_ref, other_ref, base_ref, copies_ref):
+    total = pair_dot(blocks_ref, 0, blocks_ref.shape[0], against(own_ref, other_ref))
+    write_copies(copies_ref, (base_ref[...] - ordered(core_ref, total)).astype(BF16))
 
 
 def product_kernel(core_ref, blocks_ref, own_ref, other_ref, copies_ref):
@@ -451,31 +436,20 @@
     core = me.astype(jnp.int32).reshape(1)
     piece = (planes, stripe, rhs)
 
-    opened = kernel_call(
+    opened, second = kernel_call(
         opening_kernel, (child_rhs, owner, slot), [VMEM] * 3,
-        like((planes, stripe + 8, rhs)), VMEM,
-    )
-    opened, root_rhs, root_lower, root_inverse, root_upper, child_lower, child_upper = tie(
-        (opened, root_rhs, root_lower, root_inverse, root_upper, child_lower, child_upper)
-    )
+        [like((planes, stripe + 8, rhs)), like((stripe, rhs), F32)], [VMEM] * 2,
+    )
+    opened, child_lower = tie((opened, child_lower))
     own_first = spread(opened, PLANE)
-    kept, given = kernel_call(
-        turn_kernel, (core, root_rhs), [SMEM, VMEM], [like((half, rhs))] * 2, [VMEM] * 2,
-        limit=2, moved=MIB,
-    )
     low = rows_of(child_lower, 1, 0, kc)
-    top = rows_of(child_upper, 0, kc, nc)
-    lower_own = rows_of(root_lower, 1, 0, kr)
-    upper_own = rows_of(root_upper, 0, kr, 2 * kr)
-    own_first, lower_own, upper_own, kept, given, low, top = tie(
-        (own_first, lower_own, upper_own, kept, given, low, top)
-    )
+    own_first, low = tie((own_first, low))
     other_first = swap(own_first)
     y1_copies = kernel_call(
-        advance_kernel, (core, own_first, other_first, low, child_rhs), [SMEM] + [VMEM] * 4,
+        advance_kernel, (core, own_first, other_first, low, second), [SMEM] + [VMEM] * 4,
         like(piece), VMEM, limit=2, moved=MIB,
     )
-    y1_copies, given = tie((y1_copies, given))
+    y1_copies, root_rhs, child_upper = tie((y1_copies, root_rhs, child_upper))
     own_second = spread(y1_copies, PLANE)
 
     part, z0c, index, repeats, select, targets = kernel_call(
@@ -495,41 +469,46 @@
         limit=4, moved=2 * MIB,
     )
     index, repeats = index.reshape(-1), repeats[:, 0]
-    got = swap(given)
-    own_second, part, z0c, index, repeats, select, targets, got = tie(
-        (own_second, part, z0c, index, repeats, select, targets, got)
+    kept, given = kernel_call(
+        turn_kernel, (core, root_rhs), [SMEM, VMEM], [like((half, rhs))] * 2, [VMEM] * 2,
+        limit=2, moved=MIB,
+    )
+    top = rows_of(child_upper, 0, kc, nc)
+    own_second, part, z0c, index, repeats, select, targets, kept, given, top = tie(
+        (own_second, part, z0c, index, repeats, select, targets, kept, given, top)
     )
     other_second = swap(own_second)
 
     packed, z1c = kernel_call(
         contribute_kernel,
         (core, own_second, other_second, child_update, child_inverse, part, select, targets),
-        [SMEM, VMEM, VMEM, HBM, HBM] + [VMEM] * 3,
+        [SMEM, VMEM, VMEM, VMEM, HBM] + [VMEM] * 3,
         [like((devices * 4, rhs)), like((stripe, rhs), F32)], [VMEM] * 2,
-        scratch=[pltpu.VMEM((held, kc), BF16), pltpu.VMEM((stripe, kc), BF16), DMA((2,))],
+        scratch=[pltpu.VMEM((stripe, kc), BF16), DMA],
         limit=4, moved=MIB,
     )
-    packed, z1c, lower_own = tie((packed, z1c, lower_own))
+    packed, z1c, root_lower, root_upper, given = tie(
+        (packed, z1c, root_lower, root_upper, given)
+    )
     arrived = spread(packed.reshape(devices, 4, rhs), ALL)
-    lower_other = swap(lower_own)
+    got = swap(given)
+    lower_own = rows_of(root_lower, 1, 0, kr)
+    upper_own = rows_of(root_upper, 0, kr, 2 * kr)
+    arrived, lower_own, upper_own, got = tie((arrived, lower_own, upper_own, got))
 
     r0_copies, right = kernel_call(
         unpack_kernel, (core, arrived.reshape(devices * 4, rhs), kept, got), [SMEM] + [VMEM] * 3,
         [like((cubes, half, rhs)), like((half, rhs), F32)], [VMEM] * 2, limit=4, moved=MIB,
     )
-    r0_copies, index, repeats = tie((r0_copies, index, repeats))
+    r0_copies, index, repeats, lower_own = tie((r0_copies, index, repeats, lower_own))
+    lower_other = swap(lower_own)
     summed = build_coupling(index, repeats, child_coupling, 2 * kr)
     whole = (cubes, half, rhs)
     work = dict(flops=2 * cubes * half * rhs * rhs, moved=4 * MIB)
-    summed, lower_other = tie((summed, lower_other))
-    pair = kernel_call(
-        fetch_kernel, (root_lower, lower_other), [HBM, HBM], pltpu.VMEM((2, stripe, kr), BF16),
-        VMEM, scratch=[DMA((2,))], limit=60, moved=4 * MIB,
-    )
-    r0, summed, pair = tie((spread(r0_copies, CUBE), summed, pair))
+    r0, summed, lower_other = tie((spread(r0_copies, CUBE), summed, lower_other))
     r1_copies = kernel_call(
-        first_product_kernel, (core, r0, pair, right), [SMEM] + [VMEM] * 3, like(whole), VMEM,
-        limit=4, **work,
+        first_product_kernel, (core, r0, lower_own, lower_other, right),
+        [SMEM] + [VMEM] * 4, like(whole), VMEM, limit=4, **work,
     )
     r1_copies, inverse, upper_own = tie((r1_copies, root_inverse, upper_own))
     inverse_other, upper_other = swap(inverse), swap(upper_own)

time: 177 us -> 179 us (1.011)
  local copies, waits for them, and re-layouts: 8.91 us -> 11 us
    reshape x2 -> x3, local copies, waits for them, and re-layouts: 4.15 us -> 5.06 us  [rows_of(): return lax.slice(array, start, stop).reshape(array.shape[-2], last - first)]
    pallas_call x15 -> x14, Pallas kernels: 27 us -> 27.1 us  [kernel_call(): pl.pallas_call(body, out_shape=shapes, in_specs=specs, out_specs=out_spec...]
  transfers between devices with their start and end apart: 16 -> 16, of which waited for: 8 -> 8; matrix products, arithmetic and copies ran while one was open for 3% -> 4% of each run, Pallas kernels for 9% -> 8%
where the time goes in v9:
time: 179 us; the launch traced here: 178 us
  blocking collectives  65.2 us (36%)
  starting transfers between devices  42.9 us (24%)
  waiting for transfers between devices  30.7 us (17%)
  Pallas kernels  27.1 us (15%)
  local copies, waits for them, and re-layouts  11 us (6%)
    all_to_all x3, blocking collectives, spread(): return lax.all_to_all(copies, axes, 0, 0)  65.2 us
    all_to_all x5, starting transfers between devices, spread(): return lax.all_to_all(copies, axes, 0, 0)  28 us
    all_to_all x5, waiting for transfers between devices, spread(): return lax.all_to_all(copies, axes, 0, 0)  27.2 us
    pallas_call x14, Pallas kernels, kernel_call(): pl.pallas_call(body, out_shape=shapes, in_specs=specs, out_specs=out_spec...  27.1 us
    ppermute x11, starting transfers between devices, swap(): return lax.ppermute(array, 'c', [(0, 1), (1, 0)])  14.9 us
    unnamed x24, local copies, waits for them, and re-layouts  5.12 us
    reshape x3, local copies, waits for them, and re-layouts, rows_of(): return lax.slice(array, start, stop).reshape(array.shape[-2], last - first)  5.06 us
  transfers between devices with their start and end apart: 16, of which 8 were waited for; matrix products, arithmetic and copies ran while one was open for 4% of the time, Pallas kernels for 8%

profile of v9, /device:TPU:1, one launch (start us, length us, event | category | flops | bytes accessed | tf_op | source)
XLA Modules:
  0.0 178.5 jit_solution(12044306928758441780)
XLA Ops:
  0.7 1.6 shard_map.131
  2.3 8.4 %all-to-all-start = ((bf16[16,72,128]{2,1,0:T(8,128)(2,1)}), bf16[16,72,128]{2,1,0:T(8,128)(2,1)S(1)}, u32[]{:S(2)}, u32[]{:S(2)}) async-start(bf16[16,72,128]{2,1,0:T(8,128)(2,1)} %get-tuple-element.73), calls=%async_computation | async-start | bytes 589824 | tf_op jit(solution)/shard_map/all_to_all | solution.py:30
  11.7 6.6 %all-to-all-done.own_ref = bf16[16,72,128]{2,1,0:T(8,128)(2,1)S(1)} async-done(((bf16[16,72,128]{2,1,0:T(8,128)(2,1)}), bf16[16,72,128]{2,1,0:T(8,128)(2,1)S(1)}, u32[]{:S(2)}, u32[]{:S(2)}) %all-to-all-start) | async-done | bytes 294944 | tf_op jit(solution)/shard_map/all_to_all | solution.py:30
  18.3 2.2 %collective-permute-start = (bf16[16,72,128]{2,1,0:T(8,128)(2,1)S(1)}, bf16[16,72,128]{2,1,0:T(8,128)(2,1)S(1)}, u32[]{:S(2)}, u32[]{:S(2)}) collective-permute-start(bf16[16,72,128]{2,1,0:T(8,128)(2,1)S(1)} %all-to-all-done.own_ref), channel_id=1, source_target_pairs={{0,1},{1,0},{2,3},{3,2},{4,5},{5,4},{6,7},{7,6},{8,9},{9,8},{10,11... | collective-permute-start | bytes 884744 | tf_op jit(solution)/shard_map/ppermute | solution.py:26
  23.4 3.5 %all-to-all-start.1 = ((bf16[16,64,128]{2,1,0:T(8,128)(2,1)}), bf16[16,64,128]{2,1,0:T(8,128)(2,1)S(1)}, u32[]{:S(2)}, u32[]{:S(2)}) async-start(bf16[16,64,128]{2,1,0:T(8,128)(2,1)} %shard_map.132), calls=%async_computation.1 | async-start | bytes 524288 | tf_op jit(solution)/shard_map/all_to_all | solution.py:30
  34.5 1.8 %collective-permute-start.1 = (bf16[16,64,128]{2,1,0:T(8,128)(2,1)S(1)}, bf16[16,64,128]{2,1,0:T(8,128)(2,1)S(1)}, u32[]{:S(2)}, u32[]{:S(2)}) collective-permute-start(bf16[16,64,128]{2,1,0:T(8,128)(2,1)S(1)} %all-to-all-done.1.own_ref), channel_id=1, source_target_pairs={{0,1},{1,0},{2,3},{3,2},{4,5},{5,4},{6,7},{7,6},{8,9},{9,8},{10,11... | collective-permute-start | bytes 786440 | tf_op jit(solution)/shard_map/ppermute | solution.py:26
  39.5 7.9 %all-to-all-start.2 = ((bf16[128,4,128]{2,1,0:T(4,128)(2,1)}), bf16[128,4,128]{2,1,0:T(4,128)(2,1)S(1)}, u32[]{:S(2)}, u32[]{:S(2)}) async-start(bf16[128,4,128]{2,1,0:T(4,128)(2,1)} %bitcast.5), calls=%async_computation.2 | async-start | bytes 262144 | tf_op jit(solution)/shard_map/all_to_all | solution.py:30
  47.4 3.1 %slice_bitcast_fusion = (bf16[64,8192]{1,0:T(8,128)(2,1)}, bf16[64,8192]{1,0:T(8,128)(2,1)}) fusion(bf16[2,1,64,16384]{3,2,1,0:T(8,128)(2,1)} %param.23, bf16[2,1,64,16384]{3,2,1,0:T(8,128)(2,1)} %param.21), kind=kLoop, calls=%fused_computation | loop fusion | bytes 4194304 | tf_op jit(solution)/shard_map/reshape | solution.py:42
  50.5 6.7 %all-to-all-done.2 = bf16[128,4,128]{2,1,0:T(4,128)(2,1)S(1)} async-done(((bf16[128,4,128]{2,1,0:T(4,128)(2,1)}), bf16[128,4,128]{2,1,0:T(4,128)(2,1)S(1)}, u32[]{:S(2)}, u32[]{:S(2)}) %all-to-all-start.2) | async-done | bytes 131104 | tf_op jit(solution)/shard_map/all_to_all | solution.py:30
  57.2 1.6 shard_map.136
  59.7 4.7 %all-to-all-start.3 = ((bf16[64,64,128]{2,1,0:T(8,128)(2,1)}), bf16[64,64,128]{2,1,0:T(8,128)(2,1)S(1)}, u32[]{:S(2)}, u32[]{:S(2)}) async-start(bf16[64,64,128]{2,1,0:T(8,128)(2,1)} %get-tuple-element.107), calls=%async_computation.3 | async-start | bytes 2097152 | tf_op jit(solution)/shard_map/all_to_all | solution.py:30
  64.3 11.2 %shard_map.137.matrix_ref = bf16[16384,128]{1,0:T(8,128)(2,1)} custom-call(s32[4096]{0:T(1024)} %bitcast.37, s32[32]{0:T(128)} %slice_reduce_fusion.repeats_ref, bf16[1,2,1,64,4096]{4,3,2,1,0:T(8,128)(2,1)} %coupling_ref.1), custom_call_target="tpu_custom_call" | custom-call | bytes 31457280 | tf_op jit(solution)/shard_map/pallas_call | solution.py:50
  75.6 6.7 %all-to-all-done.3.blocks_ref.r0_ref = bf16[64,64,128]{2,1,0:T(8,128)(2,1)S(1)} async-done(((bf16[64,64,128]{2,1,0:T(8,128)(2,1)}), bf16[64,64,128]{2,1,0:T(8,128)(2,1)S(1)}, u32[]{:S(2)}, u32[]{:S(2)}) %all-to-all-start.3) | async-done | bytes 1048608 | tf_op jit(solution)/shard_map/all_to_all | solution.py:30
  82.3 2.6 %shard_map.138 = bf16[64,64,128]{2,1,0:T(8,128)(2,1)S(1)} custom-call(s32[1]{0:T(128)} %bitcast.core_ref, bf16[64,64,128]{2,1,0:T(8,128)(2,1)S(1)} %all-to-all-done.3.blocks_ref.r0_ref, bf16[64,8192]{1,0:T(8,128)(2,1)} %get-tuple-element.110.own_ref, bf16[64,8192]{1,0:T(8,128)(2,1)} %collective-permute-done.3.other_ref, ...), custom_call_target="tpu_custom_call" | custom-call | flops 134217728 | bytes 4194304 | tf_op jit(solution)/shard_map/pallas_call | solution.py:50
  85.0 1.8 collective-permute-start.4
  86.8 21.6 %all_to_all.40.blocks_ref = bf16[64,64,128]{2,1,0:T(8,128)(2,1)S(1)} all-to-all(bf16[64,64,128]{2,1,0:T(8,128)(2,1)S(1)} %shard_map.138), channel_id=1, replica_groups=mesh['y'=4,'x'=4,'z'=4,'c'=2] {'y','x','z'}, dimensions={0} | all-to-all | bytes 2097152 | tf_op jit(solution)/shard_map/all_to_all | solution.py:30
  109.5 2.4 %collective-permute-start.6 = (bf16[16384,128]{1,0:T(8,128)(2,1)S(1)}, bf16[16384,128]{1,0:T(8,128)(2,1)S(1)}, u32[]{:S(2)}, u32[]{:S(2)}) collective-permute-start(bf16[16384,128]{1,0:T(8,128)(2,1)S(1)} %copy-done), channel_id=1, source_target_pairs={{0,1},{1,0},{2,3},{3,2},{4,5},{5,4},{6,7},{7,6},{8,9},{9,8},{10,11... | collective-permute-start | bytes 12582920 | tf_op jit(solution)/shard_map/ppermute | solution.py:26
  111.9 22.1 %all_to_all.41.x1_ref = bf16[64,64,128]{2,1,0:T(8,128)(2,1)S(1)} all-to-all(bf16[64,64,128]{2,1,0:T(8,128)(2,1)S(1)} %shard_map.139), channel_id=1, replica_groups=mesh['y'=4,'x'=4,'z'=4,'c'=2] {'y','x','z'}, dimensions={0} | all-to-all | bytes 2097152 | tf_op jit(solution)/shard_map/all_to_all | solution.py:30
  134.0 1.7 shard_map.140
  135.8 21.5 %all_to_all.42.x0_ref = bf16[64,64,128]{2,1,0:T(8,128)(2,1)S(1)} all-to-all(bf16[64,64,128]{2,1,0:T(8,128)(2,1)S(1)} %shard_map.140), channel_id=1, replica_groups=mesh['y'=4,'x'=4,'z'=4,'c'=2] {'y','x','z'}, dimensions={0} | all-to-all | bytes 2097152 | tf_op jit(solution)/shard_map/all_to_all | solution.py:30
  158.2 3.1 %collective-permute-start.7 = (f32[64,128]{1,0:T(8,128)S(1)}, f32[64,128]{1,0:T(8,128)S(1)}, u32[]{:S(2)}, u32[]{:S(2)}) collective-permute-start(f32[64,128]{1,0:T(8,128)S(1)} %shard_map.141), channel_id=1, source_target_pairs={{0,1},{1,0},{2,3},{3,2},{4,5},{5,4},{6,7},{7,6},{8,9},{9,8},{10,11... | collective-permute-start | bytes 98312 | tf_op jit(solution)/shard_map/ppermute | solution.py:26
  163.5 3.5 %all-to-all-start.7 = ((bf16[16,64,128]{2,1,0:T(8,128)(2,1)}), bf16[16,64,128]{2,1,0:T(8,128)(2,1)S(1)}, u32[]{:S(2)}, u32[]{:S(2)}) async-start(bf16[16,64,128]{2,1,0:T(8,128)(2,1)} %get-tuple-element.134), calls=%async_computation.7 | async-start | bytes 524288 | tf_op jit(solution)/shard_map/all_to_all | solution.py:30
  168.1 6.8 %all-to-all-done.7.own_ref = bf16[16,64,128]{2,1,0:T(8,128)(2,1)S(1)} async-done(((bf16[16,64,128]{2,1,0:T(8,128)(2,1)}), bf16[16,64,128]{2,1,0:T(8,128)(2,1)S(1)}, u32[]{:S(2)}, u32[]{:S(2)}) %all-to-all-start.7) | async-done | bytes 262176 | tf_op jit(solution)/shard_map/all_to_all | solution.py:30
  174.9 1.6 collective-permute-start.10
  (64 shorter events, 22.7 us)
Async XLA Ops:
  0.6 36.9 %copy-start.6 = (bf16[1,2,1,64,2048]{4,3,2,1,0:T(8,128)(2,1)S(1)}, bf16[1,2,1,64,2048]{4,3,2,1,0:T(8,128)(2,1)}, u32[]{:S(2)}) copy-start(bf16[1,2,1,64,2048]{4,3,2,1,0:T(8,128)(2,1)} %inverse_ref.3) | copy-start | bytes 1572868
  0.6 36.9 %copy-start.3 = (bf16[1,128,4096]{2,1,0:T(8,128)(2,1)S(1)}, bf16[1,128,4096]{2,1,0:T(8,128)(2,1)}, u32[]{:S(2)}) copy-start(bf16[1,128,4096]{2,1,0:T(8,128)(2,1)} %update_ref.3) | copy-start | bytes 3145732
  2.3 16.0 %all-to-all-start = ((bf16[16,72,128]{2,1,0:T(8,128)(2,1)}), bf16[16,72,128]{2,1,0:T(8,128)(2,1)S(1)}, u32[]{:S(2)}, u32[]{:S(2)}) async-start(bf16[16,72,128]{2,1,0:T(8,128)(2,1)} %get-tuple-element.73), calls=%async_computation | async-start | bytes 589824 | tf_op jit(solution)/shard_map/all_to_all | solution.py:30
  18.3 3.4 %collective-permute-start = (bf16[16,72,128]{2,1,0:T(8,128)(2,1)S(1)}, bf16[16,72,128]{2,1,0:T(8,128)(2,1)S(1)}, u32[]{:S(2)}, u32[]{:S(2)}) collective-permute-start(bf16[16,72,128]{2,1,0:T(8,128)(2,1)S(1)} %all-to-all-done.own_ref), channel_id=1, source_target_pairs={{0,1},{1,0},{2,3},{3,2},{4,5},{5,4},{6,7},{7,6},{8,9},{9,8},{10,11... | collective-permute-start | bytes 884744 | tf_op jit(solution)/shard_map/ppermute | solution.py:26
  23.4 11.1 %all-to-all-start.1 = ((bf16[16,64,128]{2,1,0:T(8,128)(2,1)}), bf16[16,64,128]{2,1,0:T(8,128)(2,1)S(1)}, u32[]{:S(2)}, u32[]{:S(2)}) async-start(bf16[16,64,128]{2,1,0:T(8,128)(2,1)} %shard_map.132), calls=%async_computation.1 | async-start | bytes 524288 | tf_op jit(solution)/shard_map/all_to_all | solution.py:30
  28.9 1.2 copy-start.2
  30.1 1.0 copy-start.5
  33.6 23.6 %copy-start.9 = (s32[32,128]{1,0:T(8,128)}, s32[32,128]{1,0:T(8,128)S(1)}, u32[]{:S(2)}) copy-start(s32[32,128]{1,0:T(8,128)S(1)} %get-tuple-element.81) | copy-start | bytes 49156
  34.5 3.0 %collective-permute-start.1 = (bf16[16,64,128]{2,1,0:T(8,128)(2,1)S(1)}, bf16[16,64,128]{2,1,0:T(8,128)(2,1)S(1)}, u32[]{:S(2)}, u32[]{:S(2)}) collective-permute-start(bf16[16,64,128]{2,1,0:T(8,128)(2,1)S(1)} %all-to-all-done.1.own_ref), channel_id=1, source_target_pairs={{0,1},{1,0},{2,3},{3,2},{4,5},{5,4},{6,7},{7,6},{8,9},{9,8},{10,11... | collective-permute-start | bytes 786440 | tf_op jit(solution)/shard_map/ppermute | solution.py:26
  39.1 11.4 %collective-permute-start.2 = (bf16[64,128]{1,0:T(8,128)(2,1)S(1)}, bf16[64,128]{1,0:T(8,128)(2,1)S(1)}, u32[]{:S(2)}, u32[]{:S(2)}) collective-permute-start(bf16[64,128]{1,0:T(8,128)(2,1)S(1)} %get-tuple-element.99), channel_id=1, source_target_pairs={{0,1},{1,0},{2,3},{3,2},{4,5},{5,4},{6,7},{7,6},{8,9},{9,8},{10,11... | collective-permute-start | bytes 49160 | tf_op jit(solution)/shard_map/ppermute | solution.py:26
  39.5 17.7 %all-to-all-start.2 = ((bf16[128,4,128]{2,1,0:T(4,128)(2,1)}), bf16[128,4,128]{2,1,0:T(4,128)(2,1)S(1)}, u32[]{:S(2)}, u32[]{:S(2)}) async-start(bf16[128,4,128]{2,1,0:T(4,128)(2,1)} %bitcast.5), calls=%async_computation.2 | async-start | bytes 262144 | tf_op jit(solution)/shard_map/all_to_all | solution.py:30
  58.8 23.5 %collective-permute-start.3 = (bf16[64,8192]{1,0:T(8,128)(2,1)}, bf16[64,8192]{1,0:T(8,128)(2,1)}, u32[]{:S(2)}, u32[]{:S(2)}) collective-permute-start(bf16[64,8192]{1,0:T(8,128)(2,1)} %get-tuple-element.110.own_ref), channel_id=1, source_target_pairs={{0,1},{1,0},{2,3},{3,2},{4,5},{5,4},{6,7},{7,6},{8,9},{9,8},{10,11... | collective-permute-start | bytes 3145736 | tf_op jit(solution)/shard_map/ppermute | solution.py:26
  59.7 22.6 %all-to-all-start.3 = ((bf16[64,64,128]{2,1,0:T(8,128)(2,1)}), bf16[64,64,128]{2,1,0:T(8,128)(2,1)S(1)}, u32[]{:S(2)}, u32[]{:S(2)}) async-start(bf16[64,64,128]{2,1,0:T(8,128)(2,1)} %get-tuple-element.107), calls=%async_computation.3 | async-start | bytes 2097152 | tf_op jit(solution)/shard_map/all_to_all | solution.py:30
  64.3 20.6 %copy-start.1 = (bf16[2,1,64,8192]{3,2,1,0:T(8,128)(2,1)S(1)}, bf16[2,1,64,8192]{3,2,1,0:T(8,128)(2,1)}, u32[]{:S(2)}) copy-start(bf16[2,1,64,8192]{3,2,1,0:T(8,128)(2,1)} %own_ref.3) | copy-start | bytes 6291460
  82.3 4.4 %copy-start.4 = (bf16[64,8192]{1,0:T(8,128)(2,1)S(1)}, bf16[64,8192]{1,0:T(8,128)(2,1)}, u32[]{:S(2)}) copy-start(bf16[64,8192]{1,0:T(8,128)(2,1)} %get-tuple-element.117.upper_own_ref) | copy-start | bytes 3145732
  85.0 24.5 %copy-start = (bf16[16384,128]{1,0:T(8,128)(2,1)S(1)}, bf16[16384,128]{1,0:T(8,128)(2,1)}, u32[]{:S(2)}) copy-start(bf16[16384,128]{1,0:T(8,128)(2,1)} %shard_map.137.matrix_ref) | copy-start | bytes 12582916
  85.0 23.5 %collective-permute-start.4 = (bf16[2,1,64,8192]{3,2,1,0:T(8,128)(2,1)S(1)}, bf16[2,1,64,8192]{3,2,1,0:T(8,128)(2,1)S(1)}, u32[]{:S(2)}, u32[]{:S(2)}) collective-permute-start(bf16[2,1,64,8192]{3,2,1,0:T(8,128)(2,1)S(1)} %copy-done.1), channel_id=1, source_target_pairs={{0,1},{1,0},{2,3},{3,2},{4,5},{5,4},{6,7},{7,6},{8,9},{9,8},{10,11... | collective-permute-start | bytes 6291464 | tf_op jit(solution)/shard_map/ppermute | solution.py:26
  86.7 21.7 %collective-permute-start.5 = (bf16[64,8192]{1,0:T(8,128)(2,1)S(1)}, bf16[64,8192]{1,0:T(8,128)(2,1)S(1)}, u32[]{:S(2)}, u32[]{:S(2)}) collective-permute-start(bf16[64,8192]{1,0:T(8,128)(2,1)S(1)} %copy-done.4), channel_id=1, source_target_pairs={{0,1},{1,0},{2,3},{3,2},{4,5},{5,4},{6,7},{7,6},{8,9},{9,8},{10,11... | collective-permute-start | bytes 3145736 | tf_op jit(solution)/shard_map/ppermute | solution.py:26
  109.5 24.5 %collective-permute-start.6 = (bf16[16384,128]{1,0:T(8,128)(2,1)S(1)}, bf16[16384,128]{1,0:T(8,128)(2,1)S(1)}, u32[]{:S(2)}, u32[]{:S(2)}) collective-permute-start(bf16[16384,128]{1,0:T(8,128)(2,1)S(1)} %copy-done), channel_id=1, source_target_pairs={{0,1},{1,0},{2,3},{3,2},{4,5},{5,4},{6,7},{7,6},{8,9},{9,8},{10,11... | collective-permute-start | bytes 12582920 | tf_op jit(solution)/shard_map/ppermute | solution.py:26
  158.2 4.0 %collective-permute-start.7 = (f32[64,128]{1,0:T(8,128)S(1)}, f32[64,128]{1,0:T(8,128)S(1)}, u32[]{:S(2)}, u32[]{:S(2)}) collective-permute-start(f32[64,128]{1,0:T(8,128)S(1)} %shard_map.141), channel_id=1, source_target_pairs={{0,1},{1,0},{2,3},{3,2},{4,5},{5,4},{6,7},{7,6},{8,9},{9,8},{10,11... | collective-permute-start | bytes 98312 | tf_op jit(solution)/shard_map/ppermute | solution.py:26
  163.0 4.1 %collective-permute-start.8 = (bf16[64,128]{1,0:T(8,128)(2,1)S(1)}, bf16[64,128]{1,0:T(8,128)(2,1)S(1)}, u32[]{:S(2)}, u32[]{:S(2)}) collective-permute-start(bf16[64,128]{1,0:T(8,128)(2,1)S(1)} %slice_bitcast_fusion.5), channel_id=1, source_target_pairs={{0,1},{1,0},{2,3},{3,2},{4,5},{5,4},{6,7},{7,6},{8,9},{9,8},{10,11... | collective-permute-start | bytes 49160 | tf_op jit(solution)/shard_map/ppermute | solution.py:26
  163.3 4.0 %collective-permute-start.9 = (bf16[64,128]{1,0:T(8,128)(2,1)S(1)}, bf16[64,128]{1,0:T(8,128)(2,1)S(1)}, u32[]{:S(2)}, u32[]{:S(2)}) collective-permute-start(bf16[64,128]{1,0:T(8,128)(2,1)S(1)} %slice_bitcast_fusion.4), channel_id=1, source_target_pairs={{0,1},{1,0},{2,3},{3,2},{4,5},{5,4},{6,7},{7,6},{8,9},{9,8},{10,11... | collective-permute-start | bytes 49160 | tf_op jit(solution)/shard_map/ppermute | solution.py:26
  163.5 11.4 %all-to-all-start.7 = ((bf16[16,64,128]{2,1,0:T(8,128)(2,1)}), bf16[16,64,128]{2,1,0:T(8,128)(2,1)S(1)}, u32[]{:S(2)}, u32[]{:S(2)}) async-start(bf16[16,64,128]{2,1,0:T(8,128)(2,1)} %get-tuple-element.134), calls=%async_computation.7 | async-start | bytes 524288 | tf_op jit(solution)/shard_map/all_to_all | solution.py:30
  174.9 2.7 %collective-permute-start.10 = (bf16[16,64,128]{2,1,0:T(8,128)(2,1)S(1)}, bf16[16,64,128]{2,1,0:T(8,128)(2,1)S(1)}, u32[]{:S(2)}, u32[]{:S(2)}) collective-permute-start(bf16[16,64,128]{2,1,0:T(8,128)(2,1)S(1)} %all-to-all-done.7.own_ref), channel_id=1, source_target_pairs={{0,1},{1,0},{2,3},{3,2},{4,5},{5,4},{6,7},{7,6},{8,9},{9,8},{10,11... | collective-permute-start | bytes 786440 | tf_op jit(solution)/shard_map/ppermute | solution.py:26
  (4 other events, 2.8 us)

commit v10 on v8

--- a/solution.py
+++ b/solution.py
@@ -182,14 +182,12 @@
 
 
 def contribute_kernel(
-    core_ref, own_ref, other_ref, update_ref, inverse_ref, part_ref, select_ref, targets_ref,
-    out_ref, z1_ref, high_ref, diag_ref, sems
+    core_ref, own_ref, other_ref, update_ref, part_ref, select_ref, targets_ref,
+    out_ref, high_ref, sem
 ):
     kc = high_ref.shape[1]
-    load = pltpu.make_async_copy(update_ref.at[0, :, pl.ds(kc, kc)], high_ref, sems.at[0])
-    later = pltpu.make_async_copy(inverse_ref.at[0, 1, 0], diag_ref, sems.at[1])
+    load = pltpu.make_async_copy(update_ref.at[0, :, pl.ds(kc, kc)], high_ref, sem)
     load.start()
-    later.start()
     rows = own_ref.shape[1]
     load.wait()
 
@@ -205,8 +203,18 @@
         lanes = 2 * half
         upper = lax.broadcasted_iota(jnp.int32, (both.shape[0], lanes), 0) % 8 >= 4
         out_ref[...] = jnp.where(upper, both[:, lanes:], both[:, :lanes]).astype(BF16)
-        later.wait()
-        z1_ref[...] = plane_dot(diag_ref, first, second, rows).astype(BF16).astype(F32)
+
+    by_core(core_ref, own_ref, other_ref, work)
+
+
+def diagonal_kernel(core_ref, own_ref, other_ref, inverse_ref, z1_ref, diag_ref, sem):
+    load = pltpu.make_async_copy(inverse_ref.at[0, 1, 0], diag_ref, sem)
+    load.start()
+    load.wait()
+
+    def work(first, second):
+        total = plane_dot(diag_ref, first, second, own_ref.shape[1])
+        z1_ref[...] = total.astype(BF16).astype(F32)
 
     by_core(core_ref, own_ref, other_ref, work)
 
@@ -351,22 +359,9 @@
         copies_ref[j] = value
 
 
-def fetch_kernel(lower_ref, other_ref, out_ref, sems):
-    kr = out_ref.shape[2]
-    loads = [
-        pltpu.make_async_copy(lower_ref.at[1, 0, :, pl.ds(0, kr)], out_ref.at[0], sems.at[0]),
-        pltpu.make_async_copy(other_ref, out_ref.at[1], sems.at[1]),
-    ]
-    for load in loads:
-        load.start()
-    for load in loads:
-        load.wait()
-
-
-def first_product_kernel(core_ref, blocks_ref, pair_ref, base_ref, copies_ref):
-    rights = against(pair_ref.at[0], pair_ref.at[1])
-    total = ordered(core_ref, pair_dot(blocks_ref, 0, blocks_ref.shape[0], rights))
-    write_copies(copies_ref, (base_ref[...] - total).astype(BF16))
+def first_product_kernel(core_ref, blocks_ref, own_ref, other_ref, base_ref, copies_ref):
+    total = pair_dot(blocks_ref, 0, blocks_ref.shape[0], against(own_ref, other_ref))
+    write_copies(copies_ref, (base_ref[...] - ordered(core_ref, total)).astype(BF16))
 
 
 def product_kernel(core_ref, blocks_ref, own_ref, other_ref, copies_ref):
@@ -501,16 +496,21 @@
     )
     other_second = swap(own_second)
 
-    packed, z1c = kernel_call(
-        contribute_kernel,
-        (core, own_second, other_second, child_update, child_inverse, part, select, targets),
-        [SMEM, VMEM, VMEM, HBM, HBM] + [VMEM] * 3,
-        [like((devices * 4, rhs)), like((stripe, rhs), F32)], [VMEM] * 2,
-        scratch=[pltpu.VMEM((held, kc), BF16), pltpu.VMEM((stripe, kc), BF16), DMA((2,))],
-        limit=4, moved=MIB,
-    )
-    packed, z1c, lower_own = tie((packed, z1c, lower_own))
+    packed = kernel_call(
+        contribute_kernel, (core, own_second, other_second, child_update, part, select, targets),
+        [SMEM, VMEM, VMEM, HBM] + [VMEM] * 3, like((devices * 4, rhs)), VMEM,
+        scratch=[pltpu.VMEM((held, kc), BF16), DMA], limit=4, moved=MIB,
+    )
+    packed, lower_own, own_second, other_second = tie(
+        (packed, lower_own, own_second, other_second)
+    )
     arrived = spread(packed.reshape(devices, 4, rhs), ALL)
+    z1c = kernel_call(
+        diagonal_kernel, (core, own_second, other_second, child_inverse),
+        [SMEM, VMEM, VMEM, HBM], like((stripe, rhs), F32), VMEM,
+        scratch=[pltpu.VMEM((stripe, kc), BF16), DMA], limit=4, moved=MIB,
+    )
+    arrived, z1c = tie((arrived, z1c))
     lower_other = swap(lower_own)
 
     r0_copies, right = kernel_call(
@@ -521,15 +521,10 @@
     summed = build_coupling(index, repeats, child_coupling, 2 * kr)
     whole = (cubes, half, rhs)
     work = dict(flops=2 * cubes * half * rhs * rhs, moved=4 * MIB)
-    summed, lower_other = tie((summed, lower_other))
-    pair = kernel_call(
-        fetch_kernel, (root_lower, lower_other), [HBM, HBM], pltpu.VMEM((2, stripe, kr), BF16),
-        VMEM, scratch=[DMA((2,))], limit=60, moved=4 * MIB,
-    )
-    r0, summed, pair = tie((spread(r0_copies, CUBE), summed, pair))
+    r0, summed, lower_other = tie((spread(r0_copies, CUBE), summed, lower_other))
     r1_copies = kernel_call(
-        first_product_kernel, (core, r0, pair, right), [SMEM] + [VMEM] * 3, like(whole), VMEM,
-        limit=4, **work,
+        first_product_kernel, (core, r0, lower_own, lower_other, right),
+        [SMEM] + [VMEM] * 4, like(whole), VMEM, limit=4, **work,
     )
     r1_copies, inverse, upper_own = tie((r1_copies, root_inverse, upper_own))
     inverse_other, upper_other = swap(inverse), swap(upper_own)

time: 177 us -> 175 us (0.989)
  local copies, waits for them, and re-layouts: 8.91 us -> 5.82 us
  waiting for transfers between devices: 30.1 us -> 32.6 us
    unnamed x24 -> x20, local copies, waits for them, and re-layouts: 3.91 us -> 0.79 us
    all_to_all x5, waiting for transfers between devices: 26.5 us -> 29 us  [spread(): return lax.all_to_all(copies, axes, 0, 0)]
where the time goes in v10:
time: 175 us
  blocking collectives  65 us (37%)
  starting transfers between devices  42.4 us (24%)
  waiting for transfers between devices  32.6 us (19%)
  Pallas kernels  27.1 us (15%)
  local copies, waits for them, and re-layouts  5.82 us (3%)
    all_to_all x3, blocking collectives, spread(): return lax.all_to_all(copies, axes, 0, 0)  65 us
    all_to_all x5, waiting for transfers between devices, spread(): return lax.all_to_all(copies, axes, 0, 0)  29 us
    pallas_call x15, Pallas kernels, kernel_call(): pl.pallas_call(body, out_shape=shapes, in_specs=specs, out_specs=out_spec...  27.1 us
    all_to_all x5, starting transfers between devices, spread(): return lax.all_to_all(copies, axes, 0, 0)  26.6 us
    ppermute x11, starting transfers between devices, swap(): return lax.ppermute(array, 'c', [(0, 1), (1, 0)])  15.8 us
    reshape x2, local copies, waits for them, and re-layouts, rows_of(): return lax.slice(array, start, stop).reshape(array.shape[-2], last - first)  4.18 us
    ppermute x11, waiting for transfers between devices, swap(): return lax.ppermute(array, 'c', [(0, 1), (1, 0)])  3.55 us
  transfers between devices with their start and end apart: 16, of which 8 were waited for; matrix products, arithmetic and copies ran while one was open for 3% of the time, Pallas kernels for 9%

profile of v10, /device:TPU:1, one launch (start us, length us, event | category | flops | bytes accessed | tf_op | source)
XLA Modules:
  0.0 174.6 jit_solution(15705696299213591414)
XLA Ops:
  0.7 1.7 shard_map.131
  2.3 8.4 %all-to-all-start = ((bf16[16,72,128]{2,1,0:T(8,128)(2,1)}), bf16[16,72,128]{2,1,0:T(8,128)(2,1)S(1)}, u32[]{:S(2)}, u32[]{:S(2)}) async-start(bf16[16,72,128]{2,1,0:T(8,128)(2,1)} %shard_map.131), calls=%async_computation | async-start | bytes 589824 | tf_op jit(solution)/shard_map/all_to_all | solution.py:30
  11.7 3.1 %slice_bitcast_fusion = (bf16[64,8192]{1,0:T(8,128)(2,1)}, bf16[64,8192]{1,0:T(8,128)(2,1)}) fusion(bf16[2,1,64,16384]{3,2,1,0:T(8,128)(2,1)} %param.23, bf16[2,1,64,16384]{3,2,1,0:T(8,128)(2,1)} %param.21), kind=kLoop, calls=%fused_computation | loop fusion | bytes 4194304 | tf_op jit(solution)/shard_map/reshape | solution.py:42
  15.9 2.4 %all-to-all-done.own_ref = bf16[16,72,128]{2,1,0:T(8,128)(2,1)S(1)} async-done(((bf16[16,72,128]{2,1,0:T(8,128)(2,1)}), bf16[16,72,128]{2,1,0:T(8,128)(2,1)S(1)}, u32[]{:S(2)}, u32[]{:S(2)}) %all-to-all-start) | async-done | bytes 294944 | tf_op jit(solution)/shard_map/all_to_all | solution.py:30
  18.3 2.2 %collective-permute-start = (bf16[16,72,128]{2,1,0:T(8,128)(2,1)S(1)}, bf16[16,72,128]{2,1,0:T(8,128)(2,1)S(1)}, u32[]{:S(2)}, u32[]{:S(2)}) collective-permute-start(bf16[16,72,128]{2,1,0:T(8,128)(2,1)S(1)} %all-to-all-done.own_ref), channel_id=1, source_target_pairs={{0,1},{1,0},{2,3},{3,2},{4,5},{5,4},{6,7},{7,6},{8,9},{9,8},{10,11... | collective-permute-start | bytes 884744 | tf_op jit(solution)/shard_map/ppermute | solution.py:26
  22.7 3.5 %all-to-all-start.1 = ((bf16[16,64,128]{2,1,0:T(8,128)(2,1)}), bf16[16,64,128]{2,1,0:T(8,128)(2,1)S(1)}, u32[]{:S(2)}, u32[]{:S(2)}) async-start(bf16[16,64,128]{2,1,0:T(8,128)(2,1)} %shard_map.133), calls=%async_computation.1 | async-start | bytes 524288 | tf_op jit(solution)/shard_map/all_to_all | solution.py:30
  28.6 5.2 %all-to-all-done.1.own_ref = bf16[16,64,128]{2,1,0:T(8,128)(2,1)S(1)} async-done(((bf16[16,64,128]{2,1,0:T(8,128)(2,1)}), bf16[16,64,128]{2,1,0:T(8,128)(2,1)S(1)}, u32[]{:S(2)}, u32[]{:S(2)}) %all-to-all-start.1) | async-done | bytes 262176 | tf_op jit(solution)/shard_map/all_to_all | solution.py:30
  33.8 1.8 %collective-permute-start.2 = (bf16[16,64,128]{2,1,0:T(8,128)(2,1)S(1)}, bf16[16,64,128]{2,1,0:T(8,128)(2,1)S(1)}, u32[]{:S(2)}, u32[]{:S(2)}) collective-permute-start(bf16[16,64,128]{2,1,0:T(8,128)(2,1)S(1)} %all-to-all-done.1.own_ref), channel_id=1, source_target_pairs={{0,1},{1,0},{2,3},{3,2},{4,5},{5,4},{6,7},{7,6},{8,9},{9,8},{10,11... | collective-permute-start | bytes 786440 | tf_op jit(solution)/shard_map/ppermute | solution.py:26
  38.0 6.1 %all-to-all-start.2 = ((bf16[128,4,128]{2,1,0:T(4,128)(2,1)}), bf16[128,4,128]{2,1,0:T(4,128)(2,1)S(1)}, u32[]{:S(2)}, u32[]{:S(2)}) async-start(bf16[128,4,128]{2,1,0:T(4,128)(2,1)} %bitcast.7), calls=%async_computation.2 | async-start | bytes 262144 | tf_op jit(solution)/shard_map/all_to_all | solution.py:30
  45.6 8.4 %all-to-all-done.2 = bf16[128,4,128]{2,1,0:T(4,128)(2,1)S(1)} async-done(((bf16[128,4,128]{2,1,0:T(4,128)(2,1)}), bf16[128,4,128]{2,1,0:T(4,128)(2,1)S(1)}, u32[]{:S(2)}, u32[]{:S(2)}) %all-to-all-start.2) | async-done | bytes 131104 | tf_op jit(solution)/shard_map/all_to_all | solution.py:30
  55.6 4.9 %all-to-all-start.3 = ((bf16[64,64,128]{2,1,0:T(8,128)(2,1)}), bf16[64,64,128]{2,1,0:T(8,128)(2,1)S(1)}, u32[]{:S(2)}, u32[]{:S(2)}) async-start(bf16[64,64,128]{2,1,0:T(8,128)(2,1)} %get-tuple-element.104), calls=%async_computation.3 | async-start | bytes 2097152 | tf_op jit(solution)/shard_map/all_to_all | solution.py:30
  60.6 11.2 %shard_map.138.matrix_ref = bf16[16384,128]{1,0:T(8,128)(2,1)} custom-call(s32[4096]{0:T(1024)} %bitcast.37, s32[32]{0:T(128)} %slice_reduce_fusion.repeats_ref, bf16[1,2,1,64,4096]{4,3,2,1,0:T(8,128)(2,1)} %coupling_ref.1), custom_call_target="tpu_custom_call" | custom-call | bytes 31457280 | tf_op jit(solution)/shard_map/pallas_call | solution.py:50
  71.8 6.2 %all-to-all-done.3.blocks_ref.r0_ref = bf16[64,64,128]{2,1,0:T(8,128)(2,1)S(1)} async-done(((bf16[64,64,128]{2,1,0:T(8,128)(2,1)}), bf16[64,64,128]{2,1,0:T(8,128)(2,1)S(1)}, u32[]{:S(2)}, u32[]{:S(2)}) %all-to-all-start.3) | async-done | bytes 1048608 | tf_op jit(solution)/shard_map/all_to_all | solution.py:30
  77.9 2.6 %shard_map.139 = bf16[64,64,128]{2,1,0:T(8,128)(2,1)S(1)} custom-call(s32[1]{0:T(128)} %bitcast.core_ref, bf16[64,64,128]{2,1,0:T(8,128)(2,1)S(1)} %all-to-all-done.3.blocks_ref.r0_ref, bf16[64,8192]{1,0:T(8,128)(2,1)} %get-tuple-element.107.own_ref, bf16[64,8192]{1,0:T(8,128)(2,1)} %collective-permute-done.3.other_ref, ...), custom_call_target="tpu_custom_call" | custom-call | flops 134217728 | bytes 4194304 | tf_op jit(solution)/shard_map/pallas_call | solution.py:50
  80.6 2.3 %collective-permute-start.4 = (bf16[2,1,64,8192]{3,2,1,0:T(8,128)(2,1)S(1)}, bf16[2,1,64,8192]{3,2,1,0:T(8,128)(2,1)S(1)}, u32[]{:S(2)}, u32[]{:S(2)}) collective-permute-start(bf16[2,1,64,8192]{3,2,1,0:T(8,128)(2,1)S(1)} %copy-done.1), channel_id=1, source_target_pairs={{0,1},{1,0},{2,3},{3,2},{4,5},{5,4},{6,7},{7,6},{8,9},{9,8},{10,11... | collective-permute-start | bytes 6291464 | tf_op jit(solution)/shard_map/ppermute | solution.py:26
  83.1 21.5 %all_to_all.40.blocks_ref = bf16[64,64,128]{2,1,0:T(8,128)(2,1)S(1)} all-to-all(bf16[64,64,128]{2,1,0:T(8,128)(2,1)S(1)} %shard_map.139), channel_id=1, replica_groups=mesh['y'=4,'x'=4,'z'=4,'c'=2] {'y','x','z'}, dimensions={0} | all-to-all | bytes 2097152 | tf_op jit(solution)/shard_map/all_to_all | solution.py:30
  105.6 2.4 %collective-permute-start.6 = (bf16[16384,128]{1,0:T(8,128)(2,1)S(1)}, bf16[16384,128]{1,0:T(8,128)(2,1)S(1)}, u32[]{:S(2)}, u32[]{:S(2)}) collective-permute-start(bf16[16384,128]{1,0:T(8,128)(2,1)S(1)} %copy-done), channel_id=1, source_target_pairs={{0,1},{1,0},{2,3},{3,2},{4,5},{5,4},{6,7},{7,6},{8,9},{9,8},{10,11... | collective-permute-start | bytes 12582920 | tf_op jit(solution)/shard_map/ppermute | solution.py:26
  108.0 22.1 %all_to_all.41.x1_ref = bf16[64,64,128]{2,1,0:T(8,128)(2,1)S(1)} all-to-all(bf16[64,64,128]{2,1,0:T(8,128)(2,1)S(1)} %shard_map.140), channel_id=1, replica_groups=mesh['y'=4,'x'=4,'z'=4,'c'=2] {'y','x','z'}, dimensions={0} | all-to-all | bytes 2097152 | tf_op jit(solution)/shard_map/all_to_all | solution.py:30
  130.1 1.7 shard_map.141
  131.9 21.5 %all_to_all.42.x0_ref = bf16[64,64,128]{2,1,0:T(8,128)(2,1)S(1)} all-to-all(bf16[64,64,128]{2,1,0:T(8,128)(2,1)S(1)} %shard_map.141), channel_id=1, replica_groups=mesh['y'=4,'x'=4,'z'=4,'c'=2] {'y','x','z'}, dimensions={0} | all-to-all | bytes 2097152 | tf_op jit(solution)/shard_map/all_to_all | solution.py:30
  154.3 3.1 %collective-permute-start.7 = (f32[64,128]{1,0:T(8,128)S(1)}, f32[64,128]{1,0:T(8,128)S(1)}, u32[]{:S(2)}, u32[]{:S(2)}) collective-permute-start(f32[64,128]{1,0:T(8,128)S(1)} %shard_map.142), channel_id=1, source_target_pairs={{0,1},{1,0},{2,3},{3,2},{4,5},{5,4},{6,7},{7,6},{8,9},{9,8},{10,11... | collective-permute-start | bytes 98312 | tf_op jit(solution)/shard_map/ppermute | solution.py:26
  159.7 3.5 %all-to-all-start.7 = ((bf16[16,64,128]{2,1,0:T(8,128)(2,1)}), bf16[16,64,128]{2,1,0:T(8,128)(2,1)S(1)}, u32[]{:S(2)}, u32[]{:S(2)}) async-start(bf16[16,64,128]{2,1,0:T(8,128)(2,1)} %get-tuple-element.132), calls=%async_computation.7 | async-start | bytes 524288 | tf_op jit(solution)/shard_map/all_to_all | solution.py:30
  164.2 6.9 %all-to-all-done.7.own_ref = bf16[16,64,128]{2,1,0:T(8,128)(2,1)S(1)} async-done(((bf16[16,64,128]{2,1,0:T(8,128)(2,1)}), bf16[16,64,128]{2,1,0:T(8,128)(2,1)S(1)}, u32[]{:S(2)}, u32[]{:S(2)}) %all-to-all-start.7) | async-done | bytes 262176 | tf_op jit(solution)/shard_map/all_to_all | solution.py:30
  171.0 1.6 collective-permute-start.10
  (60 shorter events, 19.1 us)
Async XLA Ops:
  0.6 21.1 %copy-start.5 = (bf16[1,2,1,64,128]{4,3,2,1,0:T(8,128)(2,1)S(1)}, bf16[1,2,1,64,128]{4,3,2,1,0:T(8,128)(2,1)}, u32[]{:S(2)}) copy-start(bf16[1,2,1,64,128]{4,3,2,1,0:T(8,128)(2,1)} %rhs_ref.4) | copy-start | bytes 98308
  0.6 26.2 %copy-start.4 = (bf16[1,2,1,64,2048]{4,3,2,1,0:T(8,128)(2,1)S(1)}, bf16[1,2,1,64,2048]{4,3,2,1,0:T(8,128)(2,1)}, u32[]{:S(2)}) copy-start(bf16[1,2,1,64,2048]{4,3,2,1,0:T(8,128)(2,1)} %inverse_ref.3) | copy-start | bytes 1572868
  0.7 26.1 %copy-start.2 = (bf16[1,128,4096]{2,1,0:T(8,128)(2,1)S(1)}, bf16[1,128,4096]{2,1,0:T(8,128)(2,1)}, u32[]{:S(2)}) copy-start(bf16[1,128,4096]{2,1,0:T(8,128)(2,1)} %update_ref.3) | copy-start | bytes 3145732
  2.3 16.0 %all-to-all-start = ((bf16[16,72,128]{2,1,0:T(8,128)(2,1)}), bf16[16,72,128]{2,1,0:T(8,128)(2,1)S(1)}, u32[]{:S(2)}, u32[]{:S(2)}) async-start(bf16[16,72,128]{2,1,0:T(8,128)(2,1)} %shard_map.131), calls=%async_computation | async-start | bytes 589824 | tf_op jit(solution)/shard_map/all_to_all | solution.py:30
  11.5 15.3 %copy-start.8 = (s32[1,128,1]{1,2,0:T(1,128)S(1)}, s32[1,128,1]{1,2,0:T(1,128)}, u32[]{:S(2)}) copy-start(s32[1,128,1]{1,2,0:T(1,128)} %param.18) | copy-start | bytes 1540
  11.5 15.3 %copy-start.9 = (s32[1,128]{1,0:T(1,128)S(1)}, s32[1,128]{1,0:T(1,128)}, u32[]{:S(2)}) copy-start(s32[1,128]{1,0:T(1,128)} %slot_ref.3) | copy-start | bytes 1540
  18.3 3.4 %collective-permute-start = (bf16[16,72,128]{2,1,0:T(8,128)(2,1)S(1)}, bf16[16,72,128]{2,1,0:T(8,128)(2,1)S(1)}, u32[]{:S(2)}, u32[]{:S(2)}) collective-permute-start(bf16[16,72,128]{2,1,0:T(8,128)(2,1)S(1)} %all-to-all-done.own_ref), channel_id=1, source_target_pairs={{0,1},{1,0},{2,3},{3,2},{4,5},{5,4},{6,7},{7,6},{8,9},{9,8},{10,11... | collective-permute-start | bytes 884744 | tf_op jit(solution)/shard_map/ppermute | solution.py:26
  22.7 11.1 %all-to-all-start.1 = ((bf16[16,64,128]{2,1,0:T(8,128)(2,1)}), bf16[16,64,128]{2,1,0:T(8,128)(2,1)S(1)}, u32[]{:S(2)}, u32[]{:S(2)}) async-start(bf16[16,64,128]{2,1,0:T(8,128)(2,1)} %shard_map.133), calls=%async_computation.1 | async-start | bytes 524288 | tf_op jit(solution)/shard_map/all_to_all | solution.py:30
  26.2 2.4 %collective-permute-start.1 = (bf16[64,128]{1,0:T(8,128)(2,1)S(1)}, bf16[64,128]{1,0:T(8,128)(2,1)S(1)}, u32[]{:S(2)}, u32[]{:S(2)}) collective-permute-start(bf16[64,128]{1,0:T(8,128)(2,1)S(1)} %get-tuple-element.89), channel_id=1, source_target_pairs={{0,1},{1,0},{2,3},{3,2},{4,5},{5,4},{6,7},{7,6},{8,9},{9,8},{10,11... | collective-permute-start | bytes 49160 | tf_op jit(solution)/shard_map/ppermute | solution.py:26
  28.0 16.2 %copy-start.7 = (s32[32,128]{1,0:T(8,128)}, s32[32,128]{1,0:T(8,128)S(1)}, u32[]{:S(2)}) copy-start(s32[32,128]{1,0:T(8,128)S(1)} %get-tuple-element.85) | copy-start | bytes 49156
  33.8 3.0 %collective-permute-start.2 = (bf16[16,64,128]{2,1,0:T(8,128)(2,1)S(1)}, bf16[16,64,128]{2,1,0:T(8,128)(2,1)S(1)}, u32[]{:S(2)}, u32[]{:S(2)}) collective-permute-start(bf16[16,64,128]{2,1,0:T(8,128)(2,1)S(1)} %all-to-all-done.1.own_ref), channel_id=1, source_target_pairs={{0,1},{1,0},{2,3},{3,2},{4,5},{5,4},{6,7},{7,6},{8,9},{9,8},{10,11... | collective-permute-start | bytes 786440 | tf_op jit(solution)/shard_map/ppermute | solution.py:26
  38.0 16.0 %all-to-all-start.2 = ((bf16[128,4,128]{2,1,0:T(4,128)(2,1)}), bf16[128,4,128]{2,1,0:T(4,128)(2,1)S(1)}, u32[]{:S(2)}, u32[]{:S(2)}) async-start(bf16[128,4,128]{2,1,0:T(4,128)(2,1)} %bitcast.7), calls=%async_computation.2 | async-start | bytes 262144 | tf_op jit(solution)/shard_map/all_to_all | solution.py:30
  44.2 27.5 %collective-permute-start.3 = (bf16[64,8192]{1,0:T(8,128)(2,1)}, bf16[64,8192]{1,0:T(8,128)(2,1)}, u32[]{:S(2)}, u32[]{:S(2)}) collective-permute-start(bf16[64,8192]{1,0:T(8,128)(2,1)} %get-tuple-element.107.own_ref), channel_id=1, source_target_pairs={{0,1},{1,0},{2,3},{3,2},{4,5},{5,4},{6,7},{7,6},{8,9},{9,8},{10,11... | collective-permute-start | bytes 3145736 | tf_op jit(solution)/shard_map/ppermute | solution.py:26
  55.6 22.4 %all-to-all-start.3 = ((bf16[64,64,128]{2,1,0:T(8,128)(2,1)}), bf16[64,64,128]{2,1,0:T(8,128)(2,1)S(1)}, u32[]{:S(2)}, u32[]{:S(2)}) async-start(bf16[64,64,128]{2,1,0:T(8,128)(2,1)} %get-tuple-element.104), calls=%async_computation.3 | async-start | bytes 2097152 | tf_op jit(solution)/shard_map/all_to_all | solution.py:30
  60.5 20.1 %copy-start.1 = (bf16[2,1,64,8192]{3,2,1,0:T(8,128)(2,1)S(1)}, bf16[2,1,64,8192]{3,2,1,0:T(8,128)(2,1)}, u32[]{:S(2)}) copy-start(bf16[2,1,64,8192]{3,2,1,0:T(8,128)(2,1)} %own_ref.1) | copy-start | bytes 6291460
  80.6 25.0 %copy-start = (bf16[16384,128]{1,0:T(8,128)(2,1)S(1)}, bf16[16384,128]{1,0:T(8,128)(2,1)}, u32[]{:S(2)}) copy-start(bf16[16384,128]{1,0:T(8,128)(2,1)} %shard_map.138.matrix_ref) | copy-start | bytes 12582916
  80.6 23.9 %collective-permute-start.4 = (bf16[2,1,64,8192]{3,2,1,0:T(8,128)(2,1)S(1)}, bf16[2,1,64,8192]{3,2,1,0:T(8,128)(2,1)S(1)}, u32[]{:S(2)}, u32[]{:S(2)}) collective-permute-start(bf16[2,1,64,8192]{3,2,1,0:T(8,128)(2,1)S(1)} %copy-done.1), channel_id=1, source_target_pairs={{0,1},{1,0},{2,3},{3,2},{4,5},{5,4},{6,7},{7,6},{8,9},{9,8},{10,11... | collective-permute-start | bytes 6291464 | tf_op jit(solution)/shard_map/ppermute | solution.py:26
  83.0 21.6 %collective-permute-start.5 = (bf16[64,8192]{1,0:T(8,128)(2,1)S(1)}, bf16[64,8192]{1,0:T(8,128)(2,1)S(1)}, u32[]{:S(2)}, u32[]{:S(2)}) collective-permute-start(bf16[64,8192]{1,0:T(8,128)(2,1)S(1)} %copy-done.3), channel_id=1, source_target_pairs={{0,1},{1,0},{2,3},{3,2},{4,5},{5,4},{6,7},{7,6},{8,9},{9,8},{10,11... | collective-permute-start | bytes 3145736 | tf_op jit(solution)/shard_map/ppermute | solution.py:26
  105.6 24.5 %collective-permute-start.6 = (bf16[16384,128]{1,0:T(8,128)(2,1)S(1)}, bf16[16384,128]{1,0:T(8,128)(2,1)S(1)}, u32[]{:S(2)}, u32[]{:S(2)}) collective-permute-start(bf16[16384,128]{1,0:T(8,128)(2,1)S(1)} %copy-done), channel_id=1, source_target_pairs={{0,1},{1,0},{2,3},{3,2},{4,5},{5,4},{6,7},{7,6},{8,9},{9,8},{10,11... | collective-permute-start | bytes 12582920 | tf_op jit(solution)/shard_map/ppermute | solution.py:26
  154.3 4.0 %collective-permute-start.7 = (f32[64,128]{1,0:T(8,128)S(1)}, f32[64,128]{1,0:T(8,128)S(1)}, u32[]{:S(2)}, u32[]{:S(2)}) collective-permute-start(f32[64,128]{1,0:T(8,128)S(1)} %shard_map.142), channel_id=1, source_target_pairs={{0,1},{1,0},{2,3},{3,2},{4,5},{5,4},{6,7},{7,6},{8,9},{9,8},{10,11... | collective-permute-start | bytes 98312 | tf_op jit(solution)/shard_map/ppermute | solution.py:26
  159.1 4.1 %collective-permute-start.8 = (bf16[64,128]{1,0:T(8,128)(2,1)S(1)}, bf16[64,128]{1,0:T(8,128)(2,1)S(1)}, u32[]{:S(2)}, u32[]{:S(2)}) collective-permute-start(bf16[64,128]{1,0:T(8,128)(2,1)S(1)} %slice_bitcast_fusion.5), channel_id=1, source_target_pairs={{0,1},{1,0},{2,3},{3,2},{4,5},{5,4},{6,7},{7,6},{8,9},{9,8},{10,11... | collective-permute-start | bytes 49160 | tf_op jit(solution)/shard_map/ppermute | solution.py:26
  159.4 4.0 %collective-permute-start.9 = (bf16[64,128]{1,0:T(8,128)(2,1)S(1)}, bf16[64,128]{1,0:T(8,128)(2,1)S(1)}, u32[]{:S(2)}, u32[]{:S(2)}) collective-permute-start(bf16[64,128]{1,0:T(8,128)(2,1)S(1)} %slice_bitcast_fusion.4), channel_id=1, source_target_pairs={{0,1},{1,0},{2,3},{3,2},{4,5},{5,4},{6,7},{7,6},{8,9},{9,8},{10,11... | collective-permute-start | bytes 49160 | tf_op jit(solution)/shard_map/ppermute | solution.py:26
  159.7 11.4 %all-to-all-start.7 = ((bf16[16,64,128]{2,1,0:T(8,128)(2,1)}), bf16[16,64,128]{2,1,0:T(8,128)(2,1)S(1)}, u32[]{:S(2)}, u32[]{:S(2)}) async-start(bf16[16,64,128]{2,1,0:T(8,128)(2,1)} %get-tuple-element.132), calls=%async_computation.7 | async-start | bytes 524288 | tf_op jit(solution)/shard_map/all_to_all | solution.py:30
  171.0 2.7 %collective-permute-start.10 = (bf16[16,64,128]{2,1,0:T(8,128)(2,1)S(1)}, bf16[16,64,128]{2,1,0:T(8,128)(2,1)S(1)}, u32[]{:S(2)}, u32[]{:S(2)}) collective-permute-start(bf16[16,64,128]{2,1,0:T(8,128)(2,1)S(1)} %all-to-all-done.7.own_ref), channel_id=1, source_target_pairs={{0,1},{1,0},{2,3},{3,2},{4,5},{5,4},{6,7},{7,6},{8,9},{9,8},{10,11... | collective-permute-start | bytes 786440 | tf_op jit(solution)/shard_map/ppermute | solution.py:26
  (2 other events, 5.8 us)

commit v11 on v10

--- a/solution.py
+++ b/solution.py
@@ -555,15 +555,12 @@
         [like(piece), like((stripe, rhs)), like((stripe, rhs), F32)], [VMEM] * 3,
         limit=2, moved=MIB,
     )
-    c1_copies, x0_own, x1_own = tie((c1_copies, x0_copies[0], x1_copies[0]))
+    c1_copies, x_own = tie((c1_copies, jnp.stack([x0_copies[0], x1_copies[0]])))
     own_c1 = spread(c1_copies, PLANE)
 
-    def own_rows(half_rows):
-        pair = in_core_order(half_rows, swap(half_rows), 0).reshape(rhs, 2 * stripe)
-        rows = pair.T
-        return jnp.where(me == 0, rows[:stripe], rows[stripe:])
-
-    root_solution = jnp.stack([own_rows(x0_own), own_rows(x1_own)])[:, None]
+    pair = in_core_order(x_own, swap(x_own), 1).reshape(2, rhs, 2 * stripe)
+    rows = jnp.swapaxes(pair, 1, 2)
+    root_solution = jnp.where(me == 0, rows[:, :stripe], rows[:, stripe:])[:, None]
     own_c1, root_solution = tie((own_c1, root_solution))
     child_solution = kernel_call(
         closing_kernel, (core, own_c1, swap(own_c1), top, rest, c1),

time: 175 us -> 175 us (level)
    ppermute x11 -> x10, starting transfers between devices: 15.8 us -> 15.6 us  [swap(): return lax.ppermute(array, 'c', [(0, 1), (1, 0)])]
    ppermute x11 -> x10, waiting for transfers between devices: 3.55 us -> 3.55 us  [swap(): return lax.ppermute(array, 'c', [(0, 1), (1, 0)])]
  transfers between devices with their start and end apart: 16 -> 15, of which waited for: 8 -> 8; matrix products, arithmetic and copies ran while one was open for 3% -> 3% of each run, Pallas kernels for 9% -> 9%
where the time goes in v11:
time: 175 us; the launch traced here: 174 us
  blocking collectives  65.1 us (37%)
  starting transfers between devices  42.2 us (24%)
  waiting for transfers between devices  32.7 us (19%)
  Pallas kernels  27.1 us (15%)
  local copies, waits for them, and re-layouts  5.73 us (3%)
    all_to_all x3, blocking collectives, spread(): return lax.all_to_all(copies, axes, 0, 0)  65.1 us
    all_to_all x5, waiting for transfers between devices, spread(): return lax.all_to_all(copies, axes, 0, 0)  29.1 us
    pallas_call x15, Pallas kernels, kernel_call(): pl.pallas_call(body, out_shape=shapes, in_specs=specs, out_specs=out_spec...  27.1 us
    all_to_all x5, starting transfers between devices, spread(): return lax.all_to_all(copies, axes, 0, 0)  26.6 us
    ppermute x10, starting transfers between devices, swap(): return lax.ppermute(array, 'c', [(0, 1), (1, 0)])  15.6 us
    reshape x2, local copies, waits for them, and re-layouts, rows_of(): return lax.slice(array, start, stop).reshape(array.shape[-2], last - first)  4.17 us
    ppermute x10, waiting for transfers between devices, swap(): return lax.ppermute(array, 'c', [(0, 1), (1, 0)])  3.55 us
  transfers between devices with their start and end apart: 15, of which 8 were waited for; matrix products, arithmetic and copies ran while one was open for 3% of the time, Pallas kernels for 9%

profile of v11, /device:TPU:1, one launch (start us, length us, event | category | flops | bytes accessed | tf_op | source)
XLA Modules:
  0.0 174.3 jit_solution(14116660078647987836)
XLA Ops:
  0.7 1.6 shard_map.131
  2.3 8.4 %all-to-all-start = ((bf16[16,72,128]{2,1,0:T(8,128)(2,1)}), bf16[16,72,128]{2,1,0:T(8,128)(2,1)S(1)}, u32[]{:S(2)}, u32[]{:S(2)}) async-start(bf16[16,72,128]{2,1,0:T(8,128)(2,1)} %shard_map.131), calls=%async_computation | async-start | bytes 589824 | tf_op jit(solution)/shard_map/all_to_all | solution.py:30
  11.7 3.1 %slice_bitcast_fusion = (bf16[64,8192]{1,0:T(8,128)(2,1)}, bf16[64,8192]{1,0:T(8,128)(2,1)}) fusion(bf16[2,1,64,16384]{3,2,1,0:T(8,128)(2,1)} %param.23, bf16[2,1,64,16384]{3,2,1,0:T(8,128)(2,1)} %param.21), kind=kLoop, calls=%fused_computation | loop fusion | bytes 4194304 | tf_op jit(solution)/shard_map/reshape | solution.py:42
  15.9 2.4 %all-to-all-done.own_ref = bf16[16,72,128]{2,1,0:T(8,128)(2,1)S(1)} async-done(((bf16[16,72,128]{2,1,0:T(8,128)(2,1)}), bf16[16,72,128]{2,1,0:T(8,128)(2,1)S(1)}, u32[]{:S(2)}, u32[]{:S(2)}) %all-to-all-start) | async-done | bytes 294944 | tf_op jit(solution)/shard_map/all_to_all | solution.py:30
  18.3 2.2 %collective-permute-start = (bf16[16,72,128]{2,1,0:T(8,128)(2,1)S(1)}, bf16[16,72,128]{2,1,0:T(8,128)(2,1)S(1)}, u32[]{:S(2)}, u32[]{:S(2)}) collective-permute-start(bf16[16,72,128]{2,1,0:T(8,128)(2,1)S(1)} %all-to-all-done.own_ref), channel_id=1, source_target_pairs={{0,1},{1,0},{2,3},{3,2},{4,5},{5,4},{6,7},{7,6},{8,9},{9,8},{10,11... | collective-permute-start | bytes 884744 | tf_op jit(solution)/shard_map/ppermute | solution.py:26
  22.7 3.5 %all-to-all-start.1 = ((bf16[16,64,128]{2,1,0:T(8,128)(2,1)}), bf16[16,64,128]{2,1,0:T(8,128)(2,1)S(1)}, u32[]{:S(2)}, u32[]{:S(2)}) async-start(bf16[16,64,128]{2,1,0:T(8,128)(2,1)} %shard_map.133), calls=%async_computation.1 | async-start | bytes 524288 | tf_op jit(solution)/shard_map/all_to_all | solution.py:30
  28.6 5.2 %all-to-all-done.1.own_ref = bf16[16,64,128]{2,1,0:T(8,128)(2,1)S(1)} async-done(((bf16[16,64,128]{2,1,0:T(8,128)(2,1)}), bf16[16,64,128]{2,1,0:T(8,128)(2,1)S(1)}, u32[]{:S(2)}, u32[]{:S(2)}) %all-to-all-start.1) | async-done | bytes 262176 | tf_op jit(solution)/shard_map/all_to_all | solution.py:30
  33.8 1.8 %collective-permute-start.2 = (bf16[16,64,128]{2,1,0:T(8,128)(2,1)S(1)}, bf16[16,64,128]{2,1,0:T(8,128)(2,1)S(1)}, u32[]{:S(2)}, u32[]{:S(2)}) collective-permute-start(bf16[16,64,128]{2,1,0:T(8,128)(2,1)S(1)} %all-to-all-done.1.own_ref), channel_id=1, source_target_pairs={{0,1},{1,0},{2,3},{3,2},{4,5},{5,4},{6,7},{7,6},{8,9},{9,8},{10,11... | collective-permute-start | bytes 786440 | tf_op jit(solution)/shard_map/ppermute | solution.py:26
  38.0 6.1 %all-to-all-start.2 = ((bf16[128,4,128]{2,1,0:T(4,128)(2,1)}), bf16[128,4,128]{2,1,0:T(4,128)(2,1)S(1)}, u32[]{:S(2)}, u32[]{:S(2)}) async-start(bf16[128,4,128]{2,1,0:T(4,128)(2,1)} %bitcast.7), calls=%async_computation.2 | async-start | bytes 262144 | tf_op jit(solution)/shard_map/all_to_all | solution.py:30
  45.6 8.4 %all-to-all-done.2 = bf16[128,4,128]{2,1,0:T(4,128)(2,1)S(1)} async-done(((bf16[128,4,128]{2,1,0:T(4,128)(2,1)}), bf16[128,4,128]{2,1,0:T(4,128)(2,1)S(1)}, u32[]{:S(2)}, u32[]{:S(2)}) %all-to-all-start.2) | async-done | bytes 131104 | tf_op jit(solution)/shard_map/all_to_all | solution.py:30
  55.6 4.9 %all-to-all-start.3 = ((bf16[64,64,128]{2,1,0:T(8,128)(2,1)}), bf16[64,64,128]{2,1,0:T(8,128)(2,1)S(1)}, u32[]{:S(2)}, u32[]{:S(2)}) async-start(bf16[64,64,128]{2,1,0:T(8,128)(2,1)} %get-tuple-element.103), calls=%async_computation.3 | async-start | bytes 2097152 | tf_op jit(solution)/shard_map/all_to_all | solution.py:30
  60.5 11.2 %shard_map.138.matrix_ref = bf16[16384,128]{1,0:T(8,128)(2,1)} custom-call(s32[4096]{0:T(1024)} %bitcast.23, s32[32]{0:T(128)} %slice_reduce_fusion.repeats_ref, bf16[1,2,1,64,4096]{4,3,2,1,0:T(8,128)(2,1)} %coupling_ref.1), custom_call_target="tpu_custom_call" | custom-call | bytes 31457280 | tf_op jit(solution)/shard_map/pallas_call | solution.py:50
  71.7 6.2 %all-to-all-done.3.blocks_ref.r0_ref = bf16[64,64,128]{2,1,0:T(8,128)(2,1)S(1)} async-done(((bf16[64,64,128]{2,1,0:T(8,128)(2,1)}), bf16[64,64,128]{2,1,0:T(8,128)(2,1)S(1)}, u32[]{:S(2)}, u32[]{:S(2)}) %all-to-all-start.3) | async-done | bytes 1048608 | tf_op jit(solution)/shard_map/all_to_all | solution.py:30
  77.9 2.6 %shard_map.139 = bf16[64,64,128]{2,1,0:T(8,128)(2,1)S(1)} custom-call(s32[1]{0:T(128)} %bitcast.core_ref, bf16[64,64,128]{2,1,0:T(8,128)(2,1)S(1)} %all-to-all-done.3.blocks_ref.r0_ref, bf16[64,8192]{1,0:T(8,128)(2,1)} %get-tuple-element.106.own_ref, bf16[64,8192]{1,0:T(8,128)(2,1)} %collective-permute-done.3.other_ref, ...), custom_call_target="tpu_custom_call" | custom-call | flops 134217728 | bytes 4194304 | tf_op jit(solution)/shard_map/pallas_call | solution.py:50
  80.6 2.3 %collective-permute-start.4 = (bf16[2,1,64,8192]{3,2,1,0:T(8,128)(2,1)S(1)}, bf16[2,1,64,8192]{3,2,1,0:T(8,128)(2,1)S(1)}, u32[]{:S(2)}, u32[]{:S(2)}) collective-permute-start(bf16[2,1,64,8192]{3,2,1,0:T(8,128)(2,1)S(1)} %copy-done.1), channel_id=1, source_target_pairs={{0,1},{1,0},{2,3},{3,2},{4,5},{5,4},{6,7},{7,6},{8,9},{9,8},{10,11... | collective-permute-start | bytes 6291464 | tf_op jit(solution)/shard_map/ppermute | solution.py:26
  83.0 21.5 %all_to_all.40.blocks_ref = bf16[64,64,128]{2,1,0:T(8,128)(2,1)S(1)} all-to-all(bf16[64,64,128]{2,1,0:T(8,128)(2,1)S(1)} %shard_map.139), channel_id=1, replica_groups=mesh['y'=4,'x'=4,'z'=4,'c'=2] {'y','x','z'}, dimensions={0} | all-to-all | bytes 2097152 | tf_op jit(solution)/shard_map/all_to_all | solution.py:30
  105.6 2.4 %collective-permute-start.6 = (bf16[16384,128]{1,0:T(8,128)(2,1)S(1)}, bf16[16384,128]{1,0:T(8,128)(2,1)S(1)}, u32[]{:S(2)}, u32[]{:S(2)}) collective-permute-start(bf16[16384,128]{1,0:T(8,128)(2,1)S(1)} %copy-done), channel_id=1, source_target_pairs={{0,1},{1,0},{2,3},{3,2},{4,5},{5,4},{6,7},{7,6},{8,9},{9,8},{10,11... | collective-permute-start | bytes 12582920 | tf_op jit(solution)/shard_map/ppermute | solution.py:26
  108.0 22.1 %all_to_all.41.x1_ref = bf16[64,64,128]{2,1,0:T(8,128)(2,1)S(1)} all-to-all(bf16[64,64,128]{2,1,0:T(8,128)(2,1)S(1)} %shard_map.140), channel_id=1, replica_groups=mesh['y'=4,'x'=4,'z'=4,'c'=2] {'y','x','z'}, dimensions={0} | all-to-all | bytes 2097152 | tf_op jit(solution)/shard_map/all_to_all | solution.py:30
  130.1 1.7 shard_map.141
  131.8 21.5 %all_to_all.42.x0_ref = bf16[64,64,128]{2,1,0:T(8,128)(2,1)S(1)} all-to-all(bf16[64,64,128]{2,1,0:T(8,128)(2,1)S(1)} %shard_map.141), channel_id=1, replica_groups=mesh['y'=4,'x'=4,'z'=4,'c'=2] {'y','x','z'}, dimensions={0} | all-to-all | bytes 2097152 | tf_op jit(solution)/shard_map/all_to_all | solution.py:30
  154.3 3.1 %collective-permute-start.7 = (f32[64,128]{1,0:T(8,128)S(1)}, f32[64,128]{1,0:T(8,128)S(1)}, u32[]{:S(2)}, u32[]{:S(2)}) collective-permute-start(f32[64,128]{1,0:T(8,128)S(1)} %shard_map.142), channel_id=1, source_target_pairs={{0,1},{1,0},{2,3},{3,2},{4,5},{5,4},{6,7},{7,6},{8,9},{9,8},{10,11... | collective-permute-start | bytes 98312 | tf_op jit(solution)/shard_map/ppermute | solution.py:26
  159.4 3.5 %all-to-all-start.7 = ((bf16[16,64,128]{2,1,0:T(8,128)(2,1)}), bf16[16,64,128]{2,1,0:T(8,128)(2,1)S(1)}, u32[]{:S(2)}, u32[]{:S(2)}) async-start(bf16[16,64,128]{2,1,0:T(8,128)(2,1)} %get-tuple-element.131), calls=%async_computation.7 | async-start | bytes 524288 | tf_op jit(solution)/shard_map/all_to_all | solution.py:30
  163.7 7.0 %all-to-all-done.7.own_ref = bf16[16,64,128]{2,1,0:T(8,128)(2,1)S(1)} async-done(((bf16[16,64,128]{2,1,0:T(8,128)(2,1)}), bf16[16,64,128]{2,1,0:T(8,128)(2,1)S(1)}, u32[]{:S(2)}, u32[]{:S(2)}) %all-to-all-start.7) | async-done | bytes 262176 | tf_op jit(solution)/shard_map/all_to_all | solution.py:30
  170.7 1.6 collective-permute-start.9
  (58 shorter events, 18.7 us)
Async XLA Ops:
  0.6 21.1 %copy-start.6 = (bf16[1,2,1,64,128]{4,3,2,1,0:T(8,128)(2,1)S(1)}, bf16[1,2,1,64,128]{4,3,2,1,0:T(8,128)(2,1)}, u32[]{:S(2)}) copy-start(bf16[1,2,1,64,128]{4,3,2,1,0:T(8,128)(2,1)} %rhs_ref.4) | copy-start | bytes 98308
  0.6 26.1 %copy-start.5 = (bf16[1,2,1,64,2048]{4,3,2,1,0:T(8,128)(2,1)S(1)}, bf16[1,2,1,64,2048]{4,3,2,1,0:T(8,128)(2,1)}, u32[]{:S(2)}) copy-start(bf16[1,2,1,64,2048]{4,3,2,1,0:T(8,128)(2,1)} %inverse_ref.3) | copy-start | bytes 1572868
  0.7 26.1 %copy-start.3 = (bf16[1,128,4096]{2,1,0:T(8,128)(2,1)S(1)}, bf16[1,128,4096]{2,1,0:T(8,128)(2,1)}, u32[]{:S(2)}) copy-start(bf16[1,128,4096]{2,1,0:T(8,128)(2,1)} %update_ref.3) | copy-start | bytes 3145732
  2.3 16.0 %all-to-all-start = ((bf16[16,72,128]{2,1,0:T(8,128)(2,1)}), bf16[16,72,128]{2,1,0:T(8,128)(2,1)S(1)}, u32[]{:S(2)}, u32[]{:S(2)}) async-start(bf16[16,72,128]{2,1,0:T(8,128)(2,1)} %shard_map.131), calls=%async_computation | async-start | bytes 589824 | tf_op jit(solution)/shard_map/all_to_all | solution.py:30
  11.5 15.3 %copy-start.9 = (s32[1,128,1]{1,2,0:T(1,128)S(1)}, s32[1,128,1]{1,2,0:T(1,128)}, u32[]{:S(2)}) copy-start(s32[1,128,1]{1,2,0:T(1,128)} %param.18) | copy-start | bytes 1540
  11.5 15.3 %copy-start.10 = (s32[1,128]{1,0:T(1,128)S(1)}, s32[1,128]{1,0:T(1,128)}, u32[]{:S(2)}) copy-start(s32[1,128]{1,0:T(1,128)} %slot_ref.3) | copy-start | bytes 1540
  18.3 3.4 %collective-permute-start = (bf16[16,72,128]{2,1,0:T(8,128)(2,1)S(1)}, bf16[16,72,128]{2,1,0:T(8,128)(2,1)S(1)}, u32[]{:S(2)}, u32[]{:S(2)}) collective-permute-start(bf16[16,72,128]{2,1,0:T(8,128)(2,1)S(1)} %all-to-all-done.own_ref), channel_id=1, source_target_pairs={{0,1},{1,0},{2,3},{3,2},{4,5},{5,4},{6,7},{7,6},{8,9},{9,8},{10,11... | collective-permute-start | bytes 884744 | tf_op jit(solution)/shard_map/ppermute | solution.py:26
  22.7 11.1 %all-to-all-start.1 = ((bf16[16,64,128]{2,1,0:T(8,128)(2,1)}), bf16[16,64,128]{2,1,0:T(8,128)(2,1)S(1)}, u32[]{:S(2)}, u32[]{:S(2)}) async-start(bf16[16,64,128]{2,1,0:T(8,128)(2,1)} %shard_map.133), calls=%async_computation.1 | async-start | bytes 524288 | tf_op jit(solution)/shard_map/all_to_all | solution.py:30
  26.2 2.4 %collective-permute-start.1 = (bf16[64,128]{1,0:T(8,128)(2,1)S(1)}, bf16[64,128]{1,0:T(8,128)(2,1)S(1)}, u32[]{:S(2)}, u32[]{:S(2)}) collective-permute-start(bf16[64,128]{1,0:T(8,128)(2,1)S(1)} %get-tuple-element.88), channel_id=1, source_target_pairs={{0,1},{1,0},{2,3},{3,2},{4,5},{5,4},{6,7},{7,6},{8,9},{9,8},{10,11... | collective-permute-start | bytes 49160 | tf_op jit(solution)/shard_map/ppermute | solution.py:26
  28.0 16.2 %copy-start.8 = (s32[32,128]{1,0:T(8,128)}, s32[32,128]{1,0:T(8,128)S(1)}, u32[]{:S(2)}) copy-start(s32[32,128]{1,0:T(8,128)S(1)} %get-tuple-element.84) | copy-start | bytes 49156
  33.8 3.0 %collective-permute-start.2 = (bf16[16,64,128]{2,1,0:T(8,128)(2,1)S(1)}, bf16[16,64,128]{2,1,0:T(8,128)(2,1)S(1)}, u32[]{:S(2)}, u32[]{:S(2)}) collective-permute-start(bf16[16,64,128]{2,1,0:T(8,128)(2,1)S(1)} %all-to-all-done.1.own_ref), channel_id=1, source_target_pairs={{0,1},{1,0},{2,3},{3,2},{4,5},{5,4},{6,7},{7,6},{8,9},{9,8},{10,11... | collective-permute-start | bytes 786440 | tf_op jit(solution)/shard_map/ppermute | solution.py:26
  38.0 16.0 %all-to-all-start.2 = ((bf16[128,4,128]{2,1,0:T(4,128)(2,1)}), bf16[128,4,128]{2,1,0:T(4,128)(2,1)S(1)}, u32[]{:S(2)}, u32[]{:S(2)}) async-start(bf16[128,4,128]{2,1,0:T(4,128)(2,1)} %bitcast.7), calls=%async_computation.2 | async-start | bytes 262144 | tf_op jit(solution)/shard_map/all_to_all | solution.py:30
  44.2 27.6 %collective-permute-start.3 = (bf16[64,8192]{1,0:T(8,128)(2,1)}, bf16[64,8192]{1,0:T(8,128)(2,1)}, u32[]{:S(2)}, u32[]{:S(2)}) collective-permute-start(bf16[64,8192]{1,0:T(8,128)(2,1)} %get-tuple-element.106.own_ref), channel_id=1, source_target_pairs={{0,1},{1,0},{2,3},{3,2},{4,5},{5,4},{6,7},{7,6},{8,9},{9,8},{10,11... | collective-permute-start | bytes 3145736 | tf_op jit(solution)/shard_map/ppermute | solution.py:26
  55.6 22.4 %all-to-all-start.3 = ((bf16[64,64,128]{2,1,0:T(8,128)(2,1)}), bf16[64,64,128]{2,1,0:T(8,128)(2,1)S(1)}, u32[]{:S(2)}, u32[]{:S(2)}) async-start(bf16[64,64,128]{2,1,0:T(8,128)(2,1)} %get-tuple-element.103), calls=%async_computation.3 | async-start | bytes 2097152 | tf_op jit(solution)/shard_map/all_to_all | solution.py:30
  60.5 20.0 %copy-start.1 = (bf16[2,1,64,8192]{3,2,1,0:T(8,128)(2,1)S(1)}, bf16[2,1,64,8192]{3,2,1,0:T(8,128)(2,1)}, u32[]{:S(2)}) copy-start(bf16[2,1,64,8192]{3,2,1,0:T(8,128)(2,1)} %own_ref.1) | copy-start | bytes 6291460
  80.6 25.0 %copy-start = (bf16[16384,128]{1,0:T(8,128)(2,1)S(1)}, bf16[16384,128]{1,0:T(8,128)(2,1)}, u32[]{:S(2)}) copy-start(bf16[16384,128]{1,0:T(8,128)(2,1)} %shard_map.138.matrix_ref) | copy-start | bytes 12582916
  80.6 24.0 %collective-permute-start.4 = (bf16[2,1,64,8192]{3,2,1,0:T(8,128)(2,1)S(1)}, bf16[2,1,64,8192]{3,2,1,0:T(8,128)(2,1)S(1)}, u32[]{:S(2)}, u32[]{:S(2)}) collective-permute-start(bf16[2,1,64,8192]{3,2,1,0:T(8,128)(2,1)S(1)} %copy-done.1), channel_id=1, source_target_pairs={{0,1},{1,0},{2,3},{3,2},{4,5},{5,4},{6,7},{7,6},{8,9},{9,8},{10,11... | collective-permute-start | bytes 6291464 | tf_op jit(solution)/shard_map/ppermute | solution.py:26
  82.9 21.6 %collective-permute-start.5 = (bf16[64,8192]{1,0:T(8,128)(2,1)S(1)}, bf16[64,8192]{1,0:T(8,128)(2,1)S(1)}, u32[]{:S(2)}, u32[]{:S(2)}) collective-permute-start(bf16[64,8192]{1,0:T(8,128)(2,1)S(1)} %copy-done.4), channel_id=1, source_target_pairs={{0,1},{1,0},{2,3},{3,2},{4,5},{5,4},{6,7},{7,6},{8,9},{9,8},{10,11... | collective-permute-start | bytes 3145736 | tf_op jit(solution)/shard_map/ppermute | solution.py:26
  105.6 47.8 %copy-start.2 = (bf16[64,64,128]{2,1,0:T(8,128)(2,1)}, bf16[64,64,128]{2,1,0:T(8,128)(2,1)S(1)}, u32[]{:S(2)}) copy-start(bf16[64,64,128]{2,1,0:T(8,128)(2,1)S(1)} %shard_map.140) | copy-start | bytes 3145732
  105.6 24.5 %collective-permute-start.6 = (bf16[16384,128]{1,0:T(8,128)(2,1)S(1)}, bf16[16384,128]{1,0:T(8,128)(2,1)S(1)}, u32[]{:S(2)}, u32[]{:S(2)}) collective-permute-start(bf16[16384,128]{1,0:T(8,128)(2,1)S(1)} %copy-done), channel_id=1, source_target_pairs={{0,1},{1,0},{2,3},{3,2},{4,5},{5,4},{6,7},{7,6},{8,9},{9,8},{10,11... | collective-permute-start | bytes 12582920 | tf_op jit(solution)/shard_map/ppermute | solution.py:26
  154.3 4.0 %collective-permute-start.7 = (f32[64,128]{1,0:T(8,128)S(1)}, f32[64,128]{1,0:T(8,128)S(1)}, u32[]{:S(2)}, u32[]{:S(2)}) collective-permute-start(f32[64,128]{1,0:T(8,128)S(1)} %shard_map.142), channel_id=1, source_target_pairs={{0,1},{1,0},{2,3},{3,2},{4,5},{5,4},{6,7},{7,6},{8,9},{9,8},{10,11... | collective-permute-start | bytes 98312 | tf_op jit(solution)/shard_map/ppermute | solution.py:26
  159.1 3.8 %collective-permute-start.8 = (bf16[2,64,128]{2,1,0:T(8,128)(2,1)S(1)}, bf16[2,64,128]{2,1,0:T(8,128)(2,1)S(1)}, u32[]{:S(2)}, u32[]{:S(2)}) collective-permute-start(bf16[2,64,128]{2,1,0:T(8,128)(2,1)S(1)} %pad_maximum_fusion.1), channel_id=1, source_target_pairs={{0,1},{1,0},{2,3},{3,2},{4,5},{5,4},{6,7},{7,6},{8,9},{9,8},{10,11... | collective-permute-start | bytes 98312 | tf_op jit(solution)/shard_map/ppermute | solution.py:26
  159.4 11.3 %all-to-all-start.7 = ((bf16[16,64,128]{2,1,0:T(8,128)(2,1)}), bf16[16,64,128]{2,1,0:T(8,128)(2,1)S(1)}, u32[]{:S(2)}, u32[]{:S(2)}) async-start(bf16[16,64,128]{2,1,0:T(8,128)(2,1)} %get-tuple-element.131), calls=%async_computation.7 | async-start | bytes 524288 | tf_op jit(solution)/shard_map/all_to_all | solution.py:30
  170.7 2.8 %collective-permute-start.9 = (bf16[16,64,128]{2,1,0:T(8,128)(2,1)S(1)}, bf16[16,64,128]{2,1,0:T(8,128)(2,1)S(1)}, u32[]{:S(2)}, u32[]{:S(2)}) collective-permute-start(bf16[16,64,128]{2,1,0:T(8,128)(2,1)S(1)} %all-to-all-done.7.own_ref), channel_id=1, source_target_pairs={{0,1},{1,0},{2,3},{3,2},{4,5},{5,4},{6,7},{7,6},{8,9},{9,8},{10,11... | collective-permute-start | bytes 786440 | tf_op jit(solution)/shard_map/ppermute | solution.py:26
  (3 other events, 9.8 us)
